TPU v7x, 32 devices: a whole 2x2x4 slice. The times are simulated.
32 devices in a mesh: dp: 8 (over z, y), mp: 4 (over x, core).
Axes of the slice: x: 2, y: 2, z: 4, core: 2. Of those that a mesh axis runs over, the one named last changes fastest.
Arguments:
- tokens: bfloat16 [16, 1024, 1024], P(None, ('dp', 'mp')), may hold values from -6 to 6
- encoder: bfloat16 [16, 1024, 1024], P(None, ('dp', 'mp')), may hold values from -6 to 6
- cotangent: bfloat16 [16, 1024, 1024], P(None, ('dp', 'mp')), may hold values from -6 to 6
- lengths: int32 [16], replicated, may hold values from 1 to 1024, 8192 in all
- deal: int32 [16], replicated, may hold values from 0 to 15, each once
- attn_in: float32 [6, 1024, 1024], P(None, 'dp', 'mp'), may hold values from -0.16 to 0.16
- attn_out: float32 [2, 1024, 1024], P(None, 'mp', 'dp'), may hold values from -0.75 to 0.75
- ff_in: float32 [2, 1024, 2816], P(None, 'dp', 'mp'), may hold values from -0.1875 to 0.1875
- ff_out: float32 [2816, 1024], P('mp', 'dp'), may hold values from -0.109375 to 0.109375
- gains: float32 [3, 1024], P(None, 'dp'), may hold values from 0.5 to 1.5
- mom_attn_in: float32 [6, 1024, 1024], P(None, 'dp', 'mp'), may hold values from -6 to 6
- mom_attn_out: float32 [2, 1024, 1024], P(None, 'mp', 'dp'), may hold values from -6 to 6
- mom_ff_in: float32 [2, 1024, 2816], P(None, 'dp', 'mp'), may hold values from -6 to 6
- mom_ff_out: float32 [2816, 1024], P('mp', 'dp'), may hold values from -6 to 6
- mom_gains: float32 [3, 1024], P(None, 'dp'), may hold values from -6 to 6
- avg_attn_in: float32 [6, 1024, 1024], P(None, 'dp', 'mp'), may hold values from -0.1875 to 0.1875
- avg_attn_out: float32 [2, 1024, 1024], P(None, 'mp', 'dp'), may hold values from -0.75 to 0.75
- avg_ff_in: float32 [2, 1024, 2816], P(None, 'dp', 'mp'), may hold values from -0.1875 to 0.1875
- avg_ff_out: float32 [2816, 1024], P('mp', 'dp'), may hold values from -0.109375 to 0.109375
- avg_gains: float32 [3, 1024], P(None, 'dp'), may hold values from 0.5 to 1.5
Outputs:
- block_output: float32 [16, 1024, 1024], P(None, ('dp', 'mp'))
- grad_tokens: float32 [16, 1024, 1024], P(None, ('dp', 'mp'))
- grad_encoder: float32 [16, 1024, 1024], P(None, ('dp', 'mp'))
- grad_attn_in: float32 [6, 1024, 1024], P(None, 'dp', 'mp')
- moment_attn_in: float32 [6, 1024, 1024], P(None, 'dp', 'mp')
- average_attn_in: float32 [6, 1024, 1024], P(None, 'dp', 'mp')
- master_attn_in: float32 [6, 1024, 1024], P(None, 'dp', 'mp')
- grad_attn_out: float32 [2, 1024, 1024], P(None, 'mp', 'dp')
- moment_attn_out: float32 [2, 1024, 1024], P(None, 'mp', 'dp')
- average_attn_out: float32 [2, 1024, 1024], P(None, 'mp', 'dp')
- master_attn_out: float32 [2, 1024, 1024], P(None, 'mp', 'dp')
- grad_ff_in: float32 [2, 1024, 2816], P(None, 'dp', 'mp')
- moment_ff_in: float32 [2, 1024, 2816], P(None, 'dp', 'mp')
- average_ff_in: float32 [2, 1024, 2816], P(None, 'dp', 'mp')
- master_ff_in: float32 [2, 1024, 2816], P(None, 'dp', 'mp')
- grad_ff_out: float32 [2816, 1024], P('mp', 'dp')
- moment_ff_out: float32 [2816, 1024], P('mp', 'dp')
- average_ff_out: float32 [2816, 1024], P('mp', 'dp')
- master_ff_out: float32 [2816, 1024], P('mp', 'dp')
- grad_gains: float32 [3, 1024], P(None, 'dp')
- moment_gains: float32 [3, 1024], P(None, 'dp')
- average_gains: float32 [3, 1024], P(None, 'dp')
- master_gains: float32 [3, 1024], P(None, 'dp')
- head_maxima: float32 [16], P('mp')
- clip_factors: float32 [16], P('mp')
Inputs may be any that keep to these rules, and one draw needn't show every extreme that they name: lengths[j] counts the real tokens of slot j; positions from lengths[j] on are padding. deal holds each slot once; slot j is micro-batch j % 2 of data index j // 2.
All inputs are finite; a program needn't handle non-finite values.
Results may differ from a plain program's by a relative error of at most 0.025.
The roundings to bfloat16 on the way count: a program that leaves them out, or rounds other values in their place, can miss the bound.
Values may be sent and summed in bfloat16 or wider, within the bound.
No kernel may reach another device: no remote copies, remote signals or barrier semaphores. Data moves between devices by JAX's collectives and lax.ppermute only.
A program may use at most 256 MiB of HBM per device.

v0:
```python
import jax
import jax.numpy as jnp
from jax import lax
from jax.sharding import PartitionSpec as P

D = 1024
DK = 64


epsilon = 1e-06
clip_limit = 10.0
momentum_rate = 0.9
learn_rate = 0.01
average_rate = 0.5
neg_large = -1e30


def rms_norm(hidden, gain_vec):
    row_scale = lax.rsqrt(jnp.mean(hidden * hidden, axis=-1, keepdims=True) + epsilon)
    return hidden * row_scale * gain_vec


def gelu_product(gate_part, up_part):
    return jax.nn.gelu(gate_part, approximate=True) * up_part


def gather_rows(values):
    return lax.all_gather(values, "mp", axis=0, tiled=True)


def sum_rows(values):
    return lax.psum_scatter(values, "mp", scatter_dimension=0, tiled=True)


def split_heads(values):
    return values.reshape(values.shape[0], values.shape[1] // DK, DK)


def attend(query_h, keys_h, values_h, allowed):
    scores = jnp.einsum("qhe,khe->hqk", query_h, keys_h, preferred_element_type=jnp.float32)
    masked = jnp.where(allowed, scores, neg_large)
    row_top = jnp.max(masked, axis=-1, keepdims=True)
    expo_rows = jnp.exp(masked - row_top)
    row_total = jnp.sum(expo_rows, axis=-1, keepdims=True)
    soft_rows = expo_rows / row_total
    mixed = jnp.einsum(
        "hqk,khe->qhe", soft_rows.astype(jnp.bfloat16), values_h, preferred_element_type=jnp.float32
    )
    return (mixed, row_top + jnp.log(row_total), row_top)


def attend_back(query_h, keys_h, values_h, allowed, log_total, grad_mixed):
    scores = jnp.einsum("qhe,khe->hqk", query_h, keys_h, preferred_element_type=jnp.float32)
    soft_rows = jnp.exp(jnp.where(allowed, scores, neg_large) - log_total)
    grad_soft = jnp.einsum("qhe,khe->hqk", grad_mixed, values_h, preferred_element_type=jnp.float32)
    grad_values = jnp.einsum(
        "hqk,qhe->khe",
        soft_rows.astype(jnp.bfloat16),
        grad_mixed,
        preferred_element_type=jnp.float32,
    )
    row_dot = jnp.sum(grad_soft * soft_rows, axis=-1, keepdims=True)
    grad_scores = (soft_rows * (grad_soft - row_dot)).astype(jnp.bfloat16)
    grad_query = jnp.einsum("hqk,khe->qhe", grad_scores, keys_h, preferred_element_type=jnp.float32)
    grad_keys = jnp.einsum("hqk,qhe->khe", grad_scores, query_h, preferred_element_type=jnp.float32)
    return (grad_query, grad_keys, grad_values)


def apply_update(weight, grad_sum, moment, average, factor, grad_scale):
    grad_now = grad_sum * grad_scale
    moment_new = momentum_rate * moment + grad_now
    master_new = (weight - learn_rate * (grad_now + momentum_rate * moment_new)) * factor
    average_new = average_rate * average + (1.0 - average_rate) * master_new
    return (grad_now, moment_new, average_new, master_new)


def on_device(
    tokens,
    encoder,
    cotangent,
    lengths,
    deal,
    attn_in,
    attn_out,
    ff_in,
    ff_out,
    gains,
    mom_attn_in,
    mom_attn_out,
    mom_ff_in,
    mom_ff_out,
    mom_gains,
    avg_attn_in,
    avg_attn_out,
    avg_ff_in,
    avg_ff_out,
    avg_gains,
):
    dp_count = lax.axis_size("dp")
    mp_count = lax.axis_size("mp")
    seq_count = tokens.shape[0]
    block_rows = tokens.shape[1]
    micro_count = seq_count // dp_count
    own_rows = block_rows * dp_count
    slot_len = own_rows * mp_count
    enc_len = encoder.shape[1] * dp_count * mp_count
    mp_index = lax.axis_index("mp")
    dp_index = lax.axis_index("dp")
    inner_local = attn_in.shape[2]
    hidden_local = ff_in.shape[2]
    inverse = jnp.argsort(deal)
    tok_slots, cot_slots, enc_slots = (
        lax.all_to_all(
            jnp.take(tokens, inverse, axis=0), "dp", split_axis=0, concat_axis=1, tiled=True
        ),
        lax.all_to_all(
            jnp.take(cotangent, inverse, axis=0), "dp", split_axis=0, concat_axis=1, tiled=True
        ),
        lax.all_to_all(
            jnp.take(encoder, inverse, axis=0), "dp", split_axis=0, concat_axis=1, tiled=True
        ),
    )
    row_ids = jnp.arange(own_rows, dtype=jnp.int32)
    own_pos = (row_ids // block_rows * mp_count + mp_index) * block_rows + row_ids % block_rows
    all_ids = jnp.arange(slot_len, dtype=jnp.int32)
    local_ids = all_ids % own_rows
    all_pos = (
        local_ids // block_rows * mp_count + all_ids // own_rows
    ) * block_rows + local_ids % block_rows
    allowed = all_pos[None, :] <= all_pos[:, None]
    slot_lengths = lax.dynamic_slice_in_dim(lengths, dp_index * micro_count, micro_count)
    shard_in = attn_in.astype(jnp.bfloat16)
    shard_out = attn_out.astype(jnp.bfloat16)
    shard_ffin = ff_in.astype(jnp.bfloat16)
    shard_ffout = ff_out.astype(jnp.bfloat16)
    shard_gain = gains.astype(jnp.bfloat16)

    def micro_step(step_carry, step_items):
        grad_totals, head_max = step_carry
        tok_rows, cot_rows, enc_rows, seq_len = step_items
        fwd_weights = (
            lax.all_gather(shard_in, "dp", axis=1, tiled=True),
            lax.all_gather(shard_out, "dp", axis=2, tiled=True),
            lax.all_gather(shard_ffin, "dp", axis=1, tiled=True),
            lax.all_gather(shard_ffout, "dp", axis=1, tiled=True),
            lax.all_gather(shard_gain, "dp", axis=1, tiled=True),
        )
        w_in, w_out, f_in, f_out, gain_w = fwd_weights
        gain_f = gain_w.astype(jnp.float32)
        valid_own = (own_pos < seq_len).astype(jnp.float32)
        valid_all = all_pos < seq_len
        x_rows = tok_rows.astype(jnp.float32)
        norm_one_all = gather_rows(rms_norm(x_rows, gain_f[0]).astype(jnp.bfloat16))
        proj_qkv = jnp.einsum(
            "ld,cde->cle", norm_one_all, w_in[0:3], preferred_element_type=jnp.float32
        ).astype(jnp.bfloat16)
        heads_q = split_heads(proj_qkv[0])
        heads_k = split_heads(proj_qkv[1])
        heads_v = split_heads(proj_qkv[2])
        self_mixed, self_lse, self_top = attend(heads_q, heads_k, heads_v, allowed)
        step_top = jnp.max(jnp.where(valid_all[None, :, None], self_top, neg_large), axis=(1, 2))
        self_attn = self_mixed.reshape(slot_len, inner_local).astype(jnp.bfloat16)
        hidden_one = x_rows + sum_rows(
            jnp.dot(self_attn, w_out[0], preferred_element_type=jnp.float32)
        )
        norm_two_all = gather_rows(rms_norm(hidden_one, gain_f[1]).astype(jnp.bfloat16))
        enc_all = gather_rows(enc_rows)
        cross_q = jnp.dot(norm_two_all, w_in[3], preferred_element_type=jnp.float32).astype(
            jnp.bfloat16
        )
        cross_kv = jnp.einsum(
            "ed,cdf->cef", enc_all, w_in[4:6], preferred_element_type=jnp.float32
        ).astype(jnp.bfloat16)
        cross_out = attend(
            split_heads(cross_q), split_heads(cross_kv[0]), split_heads(cross_kv[1]), True
        )
        cross_attn = cross_out[0].reshape(slot_len, inner_local).astype(jnp.bfloat16)
        hidden_two = hidden_one + sum_rows(
            jnp.dot(cross_attn, w_out[1], preferred_element_type=jnp.float32)
        )
        norm_three_all = gather_rows(rms_norm(hidden_two, gain_f[2]).astype(jnp.bfloat16))
        gate_up = jnp.einsum(
            "ld,cdf->clf", norm_three_all, f_in, preferred_element_type=jnp.float32
        )
        inner_act = gelu_product(gate_up[0], gate_up[1]).astype(jnp.bfloat16)
        out_rows = (
            hidden_two + sum_rows(jnp.dot(inner_act, f_out, preferred_element_type=jnp.float32))
        ) * valid_own[:, None]
        bwd_weights = (
            lax.all_gather(shard_in, "dp", axis=1, tiled=True),
            lax.all_gather(shard_out, "dp", axis=2, tiled=True),
            lax.all_gather(shard_ffin, "dp", axis=1, tiled=True),
            lax.all_gather(shard_ffout, "dp", axis=1, tiled=True),
            lax.all_gather(shard_gain, "dp", axis=1, tiled=True),
        )
        w_in, w_out, f_in, f_out, gain_w = bwd_weights
        gain_f = gain_w.astype(jnp.float32)
        grad_out = cot_rows.astype(jnp.float32) * valid_own[:, None]
        grad_out_all = gather_rows(grad_out.astype(jnp.bfloat16))
        grad_f_out = jnp.einsum(
            "lf,ld->fd", inner_act, grad_out_all, preferred_element_type=jnp.float32
        )
        grad_inner = jnp.einsum(
            "ld,fd->lf", grad_out_all, f_out, preferred_element_type=jnp.float32
        )
        gelu_value, gelu_back = jax.vjp(gelu_product, gate_up[0], gate_up[1])
        grad_gate, grad_up = gelu_back(grad_inner)
        grad_gate_up = jnp.stack([grad_gate, grad_up]).astype(jnp.bfloat16)
        grad_f_in = jnp.einsum(
            "ld,clf->cdf", norm_three_all, grad_gate_up, preferred_element_type=jnp.float32
        )
        grad_norm_three = sum_rows(
            jnp.einsum("clf,cdf->ld", grad_gate_up, f_in, preferred_element_type=jnp.float32)
        )
        norm_value, norm_back = jax.vjp(rms_norm, hidden_two, gain_f[2])
        grad_h2_norm, grad_gain_three = norm_back(grad_norm_three)
        grad_hidden_two = grad_out + grad_h2_norm
        grad_co_all = gather_rows(grad_hidden_two.astype(jnp.bfloat16))
        grad_cross_out = jnp.einsum(
            "li,ld->id", cross_attn, grad_co_all, preferred_element_type=jnp.float32
        )
        grad_cross_attn = jnp.einsum(
            "ld,id->li", grad_co_all, w_out[1], preferred_element_type=jnp.float32
        ).astype(jnp.bfloat16)
        back_q, back_k, back_v = attend_back(
            split_heads(cross_q),
            split_heads(cross_kv[0]),
            split_heads(cross_kv[1]),
            True,
            cross_out[1],
            split_heads(grad_cross_attn),
        )
        grad_cross_q = back_q.reshape(slot_len, inner_local).astype(jnp.bfloat16)
        grad_cross_kv = jnp.stack(
            [back_k.reshape(enc_len, inner_local), back_v.reshape(enc_len, inner_local)]
        ).astype(jnp.bfloat16)
        grad_w_cross_q = jnp.einsum(
            "ld,li->di", norm_two_all, grad_cross_q, preferred_element_type=jnp.float32
        )
        grad_w_cross_kv = jnp.einsum(
            "ed,cei->cdi", enc_all, grad_cross_kv, preferred_element_type=jnp.float32
        )
        grad_norm_two = sum_rows(
            jnp.einsum("li,di->ld", grad_cross_q, w_in[3], preferred_element_type=jnp.float32)
        )
        grad_enc_rows = sum_rows(
            jnp.einsum("cei,cdi->ed", grad_cross_kv, w_in[4:6], preferred_element_type=jnp.float32)
        )
        norm_value, norm_back = jax.vjp(rms_norm, hidden_one, gain_f[1])
        grad_h1_norm, grad_gain_two = norm_back(grad_norm_two)
        grad_hidden_one = grad_hidden_two + grad_h1_norm
        grad_o_all = gather_rows(grad_hidden_one.astype(jnp.bfloat16))
        grad_self_out = jnp.einsum(
            "li,ld->id", self_attn, grad_o_all, preferred_element_type=jnp.float32
        )
        grad_self_attn = jnp.einsum(
            "ld,id->li", grad_o_all, w_out[0], preferred_element_type=jnp.float32
        ).astype(jnp.bfloat16)
        self_gq, self_gk, self_gv = attend_back(
            heads_q, heads_k, heads_v, allowed, self_lse, split_heads(grad_self_attn)
        )
        grad_qkv = jnp.stack(
            [
                self_gq.reshape(slot_len, inner_local),
                self_gk.reshape(slot_len, inner_local),
                self_gv.reshape(slot_len, inner_local),
            ]
        ).astype(jnp.bfloat16)
        grad_w_qkv = jnp.einsum(
            "ld,cli->cdi", norm_one_all, grad_qkv, preferred_element_type=jnp.float32
        )
        grad_norm_one = sum_rows(
            jnp.einsum("cli,cdi->ld", grad_qkv, w_in[0:3], preferred_element_type=jnp.float32)
        )
        norm_value, norm_back = jax.vjp(rms_norm, x_rows, gain_f[0])
        grad_x_norm, grad_gain_one = norm_back(grad_norm_one)
        grad_x_rows = grad_hidden_one + grad_x_norm
        grad_in_all = jnp.concatenate([grad_w_qkv, grad_w_cross_q[None], grad_w_cross_kv], axis=0)
        grad_out_w = jnp.stack([grad_self_out, grad_cross_out])
        grad_gain = jnp.stack([grad_gain_one, grad_gain_two, grad_gain_three])
        new_totals = (
            grad_totals[0] + grad_in_all,
            grad_totals[1] + grad_out_w,
            grad_totals[2] + grad_f_in,
            grad_totals[3] + grad_f_out,
            grad_totals[4] + grad_gain,
        )
        return (
            (new_totals, jnp.maximum(head_max, step_top)),
            (out_rows, grad_x_rows, grad_enc_rows),
        )

    start = (
        (
            jnp.zeros((6, D, inner_local), jnp.float32),
            jnp.zeros((2, inner_local, D), jnp.float32),
            jnp.zeros((2, D, hidden_local), jnp.float32),
            jnp.zeros((hidden_local, D), jnp.float32),
            jnp.zeros((3, D), jnp.float32),
        ),
        jnp.full((inner_local // DK,), neg_large, jnp.float32),
    )
    (grad_totals, head_max), (out_slots, grad_x_slots, grad_enc_slots) = lax.scan(
        micro_step, start, (tok_slots, cot_slots, enc_slots, slot_lengths)
    )
    output_back = lax.all_to_all(out_slots, "dp", split_axis=1, concat_axis=0, tiled=True)
    grad_x_back, grad_enc_back = (
        lax.all_to_all(grad_x_slots, "dp", split_axis=1, concat_axis=0, tiled=True),
        lax.all_to_all(grad_enc_slots, "dp", split_axis=1, concat_axis=0, tiled=True),
    )
    block_output = jnp.take(output_back, deal, axis=0)
    grad_tokens = jnp.take(grad_x_back, deal, axis=0)
    grad_encoder = jnp.take(grad_enc_back, deal, axis=0)
    gain_total = lax.psum(grad_totals[4], "mp")
    shard_grads = (
        lax.psum_scatter(grad_totals[0], "dp", scatter_dimension=1, tiled=True),
        lax.psum_scatter(grad_totals[1], "dp", scatter_dimension=2, tiled=True),
        lax.psum_scatter(grad_totals[2], "dp", scatter_dimension=1, tiled=True),
        lax.psum_scatter(grad_totals[3], "dp", scatter_dimension=1, tiled=True),
        lax.psum_scatter(gain_total, "dp", scatter_dimension=1, tiled=True),
    )
    head_peak = lax.pmax(head_max, "dp")
    clip_factors = clip_limit / jnp.maximum(head_peak, clip_limit)
    column = jnp.repeat(jnp.sqrt(clip_factors), DK)
    factor = jnp.where((jnp.arange(6) < 2)[:, None, None], column[None, None, :], 1.0)
    grad_scale = float(seq_count * slot_len) ** (-0.5)
    up_a = apply_update(attn_in, shard_grads[0], mom_attn_in, avg_attn_in, factor, grad_scale)
    up_b = apply_update(attn_out, shard_grads[1], mom_attn_out, avg_attn_out, 1.0, grad_scale)
    up_c = apply_update(ff_in, shard_grads[2], mom_ff_in, avg_ff_in, 1.0, grad_scale)
    up_d = apply_update(ff_out, shard_grads[3], mom_ff_out, avg_ff_out, 1.0, grad_scale)
    up_e = apply_update(gains, shard_grads[4], mom_gains, avg_gains, 1.0, grad_scale)
    return (
        block_output,
        grad_tokens,
        grad_encoder,
        up_a[0],
        up_a[1],
        up_a[2],
        up_a[3],
        up_b[0],
        up_b[1],
        up_b[2],
        up_b[3],
        up_c[0],
        up_c[1],
        up_c[2],
        up_c[3],
        up_d[0],
        up_d[1],
        up_d[2],
        up_d[3],
        up_e[0],
        up_e[1],
        up_e[2],
        up_e[3],
        head_peak,
        clip_factors,
    )


def solution(mesh):
    in_specs = (
        P(None, ("dp", "mp"), None),
        P(None, ("dp", "mp"), None),
        P(None, ("dp", "mp"), None),
        P(),
        P(),
        P(None, "dp", "mp"),
        P(None, "mp", "dp"),
        P(None, "dp", "mp"),
        P("mp", "dp"),
        P(None, "dp"),
        P(None, "dp", "mp"),
        P(None, "mp", "dp"),
        P(None, "dp", "mp"),
        P("mp", "dp"),
        P(None, "dp"),
        P(None, "dp", "mp"),
        P(None, "mp", "dp"),
        P(None, "dp", "mp"),
        P("mp", "dp"),
        P(None, "dp"),
    )
    out_specs = (
        P(None, ("dp", "mp"), None),
        P(None, ("dp", "mp"), None),
        P(None, ("dp", "mp"), None),
        P(None, "dp", "mp"),
        P(None, "dp", "mp"),
        P(None, "dp", "mp"),
        P(None, "dp", "mp"),
        P(None, "mp", "dp"),
        P(None, "mp", "dp"),
        P(None, "mp", "dp"),
        P(None, "mp", "dp"),
        P(None, "dp", "mp"),
        P(None, "dp", "mp"),
        P(None, "dp", "mp"),
        P(None, "dp", "mp"),
        P("mp", "dp"),
        P("mp", "dp"),
        P("mp", "dp"),
        P("mp", "dp"),
        P(None, "dp"),
        P(None, "dp"),
        P(None, "dp"),
        P(None, "dp"),
        P("mp"),
        P("mp"),
    )
    return jax.shard_map(
        on_device, mesh=mesh, in_specs=in_specs, out_specs=out_specs, check_vma=False
    )
```

profile of v0, /device:TPU:0, one launch (start us, length us, event | category | flops | bytes accessed | tf_op | source)
XLA Modules:
  0.0 2335.6 jit_solution(2610438257097573546)
XLA Ops:
  15.8 33.0 %all_to_all.108 = bf16[16,32,1024]{2,1,0:T(8,128)(2,1)S(1)} all-to-all(bf16[16,32,1024]{2,1,0:T(8,128)(2,1)S(1)} %get-tuple-element.490), channel_id=1, replica_groups=mesh['dp'=8,'mp'=4] {'dp'}, dimensions={0} | all-to-all | bytes 2097152 | tf_op jit(solution)/shard_map/all_to_all | solution.py:119
  48.7 29.1 %all_to_all.109 = bf16[16,32,1024]{2,1,0:T(8,128)(2,1)} all-to-all(bf16[16,32,1024]{2,1,0:T(8,128)(2,1)S(1)} %get-tuple-element.491), channel_id=1, replica_groups=mesh['dp'=8,'mp'=4] {'dp'}, dimensions={0} | all-to-all | bytes 2097152 | tf_op jit(solution)/shard_map/all_to_all | solution.py:116
  89.9 17.1 all-to-all-done
  107.1 1721.4 %while.29 = (s32[]{:T(128)}, f32[6,1024,256]{1,2,0:T(8,128)}, f32[2,256,1024]{2,1,0:T(8,128)}, f32[2,1024,704]{1,2,0:T(8,128)}, f32[704,1024]{1,0:T(8,128)}, /*i...) while((s32[]{:T(128)}, f32[6,1024,256]{1,2,0:T(8,128)}, ...), condition=%wide.region_25.27_spmd.clone, body=%wide.region_1.26_spmd.clone.sunk | while | flops 32826765312 | bytes 1088084352 | solution.py:303
  108.5 18.6 all_gather.99
  131.1 17.0 all-gather.18.cloned.1.call-done
  148.1 65.3 %all-gather.20.cloned.1.call-done = bf16[6,1024,256]{1,2,0:T(8,128)(2,1)} async-done(((bf16[6,128,256]{1,2,0:T(8,128)(2,1)}), bf16[6,1024,256]{1,2,0:T(8,128)(2,1)}) %all-gather.20.cloned.1.call-update) | async-done | bytes 3145744 | tf_op jit(solution)/shard_map/while/body/eval_jaxpr/all_gather | solution.py:142
  258.9 42.6 %reduce-scatter.25.cloned.1.call-done = f32[256,1024]{1,0:T(8,128)} async-done(((f32[1024,1024]{1,0:T(8,128)}), f32[256,1024]{1,0:T(8,128)}) %reduce-scatter.25.cloned.1.call-update) | async-done | bytes 1048592 | tf_op jit(solution)/shard_map/while/body/eval_jaxpr/reduce_scatter | solution.py:32
  304.5 21.6 all-gather.16.cloned.1.call-done
  329.4 21.4 all-gather.24.cloned.1.call-done
  381.1 43.9 %reduce-scatter.27.cloned.1.call-done = f32[256,1024]{1,0:T(8,128)} async-done(((f32[1024,1024]{1,0:T(8,128)}), f32[256,1024]{1,0:T(8,128)}) %reduce-scatter.27.cloned.1.call-update) | async-done | bytes 1048592 | tf_op jit(solution)/shard_map/while/body/eval_jaxpr/reduce_scatter | solution.py:32
  432.6 55.3 %all-gather.26.cloned.1.call-done = bf16[2,1024,704]{1,2,0:T(8,128)(2,1)} async-done(((bf16[2,128,704]{1,2,0:T(8,128)(2,1)}), bf16[2,1024,704]{1,2,0:T(8,128)(2,1)}) %all-gather.26.cloned.1.call-update) | async-done | bytes 2883600 | tf_op jit(solution)/shard_map/while/body/eval_jaxpr/all_gather | solution.py:144
  487.8 23.0 all-gather.28.cloned.1.call-done
  518.9 38.5 %all-gather.32.cloned.1.call-done = bf16[704,1024]{1,0:T(8,128)(2,1)} async-done(((bf16[704,128]{1,0:T(8,128)(2,1)}), bf16[704,1024]{1,0:T(8,128)(2,1)}) %all-gather.32.cloned.1.call-update) | async-done | bytes 1441808 | tf_op jit(solution)/shard_map/while/body/eval_jaxpr/all_gather | solution.py:193
  557.4 23.2 all-gather.30.cloned.1.call-done
  601.6 38.9 %reduce-scatter.29.cloned.1.call-done = f32[256,1024]{1,0:T(8,128)} async-done(((f32[1024,1024]{1,0:T(8,128)}), f32[256,1024]{1,0:T(8,128)}) %reduce-scatter.29.cloned.1.call-update) | async-done | bytes 1048592 | tf_op jit(solution)/shard_map/while/body/eval_jaxpr/reduce_scatter | solution.py:32
  642.9 44.7 %reduce-scatter.31.cloned.1.call-done = f32[256,1024]{1,0:T(8,128)} async-done(((f32[1024,1024]{1,0:T(8,128)}), f32[256,1024]{1,0:T(8,128)}) %reduce-scatter.31.cloned.1.call-update) | async-done | bytes 1048592 | tf_op jit(solution)/shard_map/while/body/eval_jaxpr/reduce_scatter | solution.py:32
  691.8 22.5 all-gather.34.cloned.1.call-done
  749.7 44.6 %reduce-scatter.33.cloned.1.call-done = f32[256,1024]{1,0:T(8,128)} async-done(((f32[1024,1024]{1,0:T(8,128)}), f32[256,1024]{1,0:T(8,128)}) %reduce-scatter.33.cloned.1.call-update) | async-done | bytes 1048592 | tf_op jit(solution)/shard_map/while/body/eval_jaxpr/reduce_scatter | solution.py:32
  825.4 19.0 multiply_reduce_fusion.19
  882.5 18.8 dynamic_update_slice.25
  909.5 18.7 dynamic_update_slice.27
  942.9 18.7 dynamic_update_slice.26
  963.5 20.5 all_gather.99
  987.9 16.3 all-gather.18.cloned.1.call-done
  1004.2 65.2 %all-gather.20.cloned.1.call-done = bf16[6,1024,256]{1,2,0:T(8,128)(2,1)} async-done(((bf16[6,128,256]{1,2,0:T(8,128)(2,1)}), bf16[6,1024,256]{1,2,0:T(8,128)(2,1)}) %all-gather.20.cloned.1.call-update) | async-done | bytes 3145744 | tf_op jit(solution)/shard_map/while/body/eval_jaxpr/all_gather | solution.py:142
  1114.8 42.6 %reduce-scatter.25.cloned.1.call-done = f32[256,1024]{1,0:T(8,128)} async-done(((f32[1024,1024]{1,0:T(8,128)}), f32[256,1024]{1,0:T(8,128)}) %reduce-scatter.25.cloned.1.call-update) | async-done | bytes 1048592 | tf_op jit(solution)/shard_map/while/body/eval_jaxpr/reduce_scatter | solution.py:32
  1160.5 21.7 all-gather.16.cloned.1.call-done
  1185.4 21.4 all-gather.24.cloned.1.call-done
  1237.0 44.0 %reduce-scatter.27.cloned.1.call-done = f32[256,1024]{1,0:T(8,128)} async-done(((f32[1024,1024]{1,0:T(8,128)}), f32[256,1024]{1,0:T(8,128)}) %reduce-scatter.27.cloned.1.call-update) | async-done | bytes 1048592 | tf_op jit(solution)/shard_map/while/body/eval_jaxpr/reduce_scatter | solution.py:32
  1288.8 55.0 %all-gather.26.cloned.1.call-done = bf16[2,1024,704]{1,2,0:T(8,128)(2,1)} async-done(((bf16[2,128,704]{1,2,0:T(8,128)(2,1)}), bf16[2,1024,704]{1,2,0:T(8,128)(2,1)}) %all-gather.26.cloned.1.call-update) | async-done | bytes 2883600 | tf_op jit(solution)/shard_map/while/body/eval_jaxpr/all_gather | solution.py:144
  1343.8 22.9 all-gather.28.cloned.1.call-done
  1374.7 38.6 %all-gather.32.cloned.1.call-done = bf16[704,1024]{1,0:T(8,128)(2,1)} async-done(((bf16[704,128]{1,0:T(8,128)(2,1)}), bf16[704,1024]{1,0:T(8,128)(2,1)}) %all-gather.32.cloned.1.call-update) | async-done | bytes 1441808 | tf_op jit(solution)/shard_map/while/body/eval_jaxpr/all_gather | solution.py:193
  1413.3 23.2 all-gather.30.cloned.1.call-done
  1457.5 38.9 %reduce-scatter.29.cloned.1.call-done = f32[256,1024]{1,0:T(8,128)} async-done(((f32[1024,1024]{1,0:T(8,128)}), f32[256,1024]{1,0:T(8,128)}) %reduce-scatter.29.cloned.1.call-update) | async-done | bytes 1048592 | tf_op jit(solution)/shard_map/while/body/eval_jaxpr/reduce_scatter | solution.py:32
  1498.8 44.7 %reduce-scatter.31.cloned.1.call-done = f32[256,1024]{1,0:T(8,128)} async-done(((f32[1024,1024]{1,0:T(8,128)}), f32[256,1024]{1,0:T(8,128)}) %reduce-scatter.31.cloned.1.call-update) | async-done | bytes 1048592 | tf_op jit(solution)/shard_map/while/body/eval_jaxpr/reduce_scatter | solution.py:32
  1547.8 22.5 all-gather.34.cloned.1.call-done
  1605.6 44.6 %reduce-scatter.33.cloned.1.call-done = f32[256,1024]{1,0:T(8,128)} async-done(((f32[1024,1024]{1,0:T(8,128)}), f32[256,1024]{1,0:T(8,128)}) %reduce-scatter.33.cloned.1.call-update) | async-done | bytes 1048592 | tf_op jit(solution)/shard_map/while/body/eval_jaxpr/reduce_scatter | solution.py:32
  1681.3 18.8 multiply_reduce_fusion.19
  1741.2 18.8 dynamic_update_slice.25
  1768.3 18.7 dynamic_update_slice.27
  1803.7 18.7 dynamic_update_slice.26
  1840.4 58.9 %all_to_all.110 = f32[2,256,1024]{2,0,1:T(2,128)} all-to-all(f32[2,256,1024]{2,0,1:T(2,128)S(1)} %copy-done.49), channel_id=1, replica_groups=mesh['dp'=8,'mp'=4] {'dp'}, dimensions={1} | all-to-all | bytes 4194304 | tf_op jit(solution)/shard_map/all_to_all | solution.py:309
  1899.3 68.7 %all_to_all.111 = f32[2,256,1024]{2,0,1:T(2,128)S(1)} all-to-all(f32[2,256,1024]{2,0,1:T(2,128)S(1)} %copy-done.50), channel_id=1, replica_groups=mesh['dp'=8,'mp'=4] {'dp'}, dimensions={1} | all-to-all | bytes 4194304 | tf_op jit(solution)/shard_map/all_to_all | solution.py:306
  1972.6 56.3 %pmax.7 = f32[4]{0:T(128)S(1)} all-reduce(f32[4]{0:T(128)S(1)} %copy-done.73), channel_id=1, replica_groups=mesh['dp'=8,'mp'=4] {'dp'}, use_global_device_ids=true, to_apply=%region_27.30 | all-reduce | flops 4 | bytes 32 | tf_op jit(solution)/shard_map/pmax | solution.py:322
  2064.2 25.3 %reduce-scatter.21.cloned.1.call-done = f32[704,128]{1,0:T(8,128)} async-done(((f32[704,1024]{1,0:T(8,128)}), f32[704,128]{1,0:T(8,128)}) %reduce-scatter.21.cloned.1.call-update) | async-done | bytes 360464 | tf_op jit(solution)/shard_map/reduce_scatter | solution.py:319
  2091.6 111.7 %reduce-scatter.19.cloned.1.call-done = f32[2,128,704]{1,2,0:T(8,128)} async-done(((f32[2,1024,704]{1,2,0:T(8,128)}), f32[2,128,704]{1,2,0:T(8,128)}) %reduce-scatter.19.cloned.1.call-update) | async-done | bytes 720912 | tf_op jit(solution)/shard_map/reduce_scatter | solution.py:318
  2206.7 118.0 %reduce-scatter.15.cloned.1.call-done = f32[6,128,256]{2,1,0:T(8,128)} async-done(((f32[6,1024,256]{2,1,0:T(8,128)}), f32[6,128,256]{2,1,0:T(8,128)}) %reduce-scatter.15.cloned.1.call-update) | async-done | bytes 786448 | tf_op jit(solution)/shard_map/reduce_scatter | solution.py:316
  (666 shorter events, 599.5 us)
Async XLA Ops:
  77.8 29.2 %all-to-all-start = ((bf16[16,32,1024]{2,1,0:T(8,128)(2,1)}), bf16[16,32,1024]{2,1,0:T(8,128)(2,1)S(1)}, u32[]{:S(2)}, u32[]{:S(2)}) async-start(bf16[16,32,1024]{2,1,0:T(8,128)(2,1)} %get-tuple-element.492), calls=%async_computation.7 | async-start | bytes 2097152 | tf_op jit(solution)/shard_map/all_to_all | solution.py:113
  107.5 321.5 %copy-start.87 = (s32[2]{0:T(128)}, s32[2]{0:T(128)S(1)}, u32[]{:S(2)}) copy-start(s32[2]{0:T(128)S(1)} %get-tuple-element.748) | copy-start | bytes 28 | tf_op jit(solution)/shard_map/while
  107.5 40.6 %all-gather.18.cloned.1.call-start = ((), (), s32[]{:S(2)}) async-start(), calls=%async_computation.24 | async-start | bytes 2621440 | tf_op jit(solution)/shard_map/while/body/eval_jaxpr/all_gather | solution.py:28
  128.2 85.3 %all-gather.20.cloned.1.call-start = ((), (), s32[]{:S(2)}) async-start(), calls=%async_computation.25 | async-start | bytes 3538944 | tf_op jit(solution)/shard_map/while/body/eval_jaxpr/all_gather | solution.py:142
  128.9 125.2 %all-gather.22.cloned.1.call-start = ((), (), s32[]{:S(2)}) async-start(), calls=%async_computation.26 | async-start | bytes 1179648 | tf_op jit(solution)/shard_map/while/body/eval_jaxpr/all_gather | solution.py:143
  129.6 171.9 %reduce-scatter.25.cloned.1.call-start = ((), (), s32[]{:S(2)}) async-start(), calls=%async_computation.27 | async-start | bytes 5242880 | tf_op jit(solution)/shard_map/while/body/eval_jaxpr/reduce_scatter | solution.py:32
  257.9 68.2 %all-gather.16.cloned.1.call-start = ((), (), s32[]{:S(2)}) async-start(), calls=%async_computation.23 | async-start | bytes 2621440 | tf_op jit(solution)/shard_map/while/body/eval_jaxpr/all_gather | solution.py:28
  258.8 91.9 %all-gather.24.cloned.1.call-start = ((), (), s32[]{:S(2)}) async-start(), calls=%async_computation.28 | async-start | bytes 2621440 | tf_op jit(solution)/shard_map/while/body/eval_jaxpr/all_gather | solution.py:28
  304.1 120.9 %reduce-scatter.27.cloned.1.call-start = ((), (), s32[]{:S(2)}) async-start(), calls=%async_computation.29 | async-start | bytes 5242880 | tf_op jit(solution)/shard_map/while/body/eval_jaxpr/reduce_scatter | solution.py:32
  380.3 107.5 %all-gather.26.cloned.1.call-start = ((), (), s32[]{:S(2)}) async-start(), calls=%async_computation.30 | async-start | bytes 3244032 | tf_op jit(solution)/shard_map/while/body/eval_jaxpr/all_gather | solution.py:144
  381.0 129.8 %all-gather.28.cloned.1.call-start = ((), (), s32[]{:S(2)}) async-start(), calls=%async_computation.31 | async-start | bytes 2621440 | tf_op jit(solution)/shard_map/while/body/eval_jaxpr/all_gather | solution.py:28
  428.4 129.0 %all-gather.32.cloned.1.call-start = ((), (), s32[]{:S(2)}) async-start(), calls=%async_computation.33 | async-start | bytes 1622016 | tf_op jit(solution)/shard_map/while/body/eval_jaxpr/all_gather | solution.py:193
  429.0 151.6 %all-gather.30.cloned.1.call-start = ((), (), s32[]{:S(2)}) async-start(), calls=%async_computation.32 | async-start | bytes 2621440 | tf_op jit(solution)/shard_map/while/body/eval_jaxpr/all_gather | solution.py:28
  432.3 208.2 %reduce-scatter.29.cloned.1.call-start = ((), (), s32[]{:S(2)}) async-start(), calls=%async_computation.34 | async-start | bytes 5242880 | tf_op jit(solution)/shard_map/while/body/eval_jaxpr/reduce_scatter | solution.py:32
  595.8 91.7 %reduce-scatter.31.cloned.1.call-start = ((), (), s32[]{:S(2)}) async-start(), calls=%async_computation.35 | async-start | bytes 5242880 | tf_op jit(solution)/shard_map/while/body/eval_jaxpr/reduce_scatter | solution.py:32
  601.5 112.7 %all-gather.34.cloned.1.call-start = ((), (), s32[]{:S(2)}) async-start(), calls=%async_computation.36 | async-start | bytes 2621440 | tf_op jit(solution)/shard_map/while/body/eval_jaxpr/all_gather | solution.py:28
  691.5 102.8 %reduce-scatter.33.cloned.1.call-start = ((), (), s32[]{:S(2)}) async-start(), calls=%async_computation.37 | async-start | bytes 5242880 | tf_op jit(solution)/shard_map/while/body/eval_jaxpr/reduce_scatter | solution.py:32
  749.6 72.6 %all-gather.36.cloned.1.call-start = ((), (), s32[]{:S(2)}) async-start(), calls=%async_computation.38 | async-start | bytes 2621440 | tf_op jit(solution)/shard_map/while/body/eval_jaxpr/all_gather | solution.py:28
  799.5 107.7 %reduce-scatter.37.cloned.1.call-start = ((), (), s32[]{:S(2)}) async-start(), calls=%async_computation.40 | async-start | bytes 5242880 | tf_op jit(solution)/shard_map/while/body/eval_jaxpr/reduce_scatter | solution.py:32
  820.1 118.5 %reduce-scatter.35.cloned.1.call-start = ((), (), s32[]{:S(2)}) async-start(), calls=%async_computation.39 | async-start | bytes 5242880 | tf_op jit(solution)/shard_map/while/body/eval_jaxpr/reduce_scatter | solution.py:32
  962.5 151.4 %copy-start.37 = (bf16[2,256,1024]{2,1,0:T(8,128)(2,1)}, bf16[2,256,1024]{2,1,0:T(8,128)(2,1)S(1)}, u32[]{:S(2)}) copy-start(bf16[2,256,1024]{2,1,0:T(8,128)(2,1)S(1)} %get-tuple-element.751) | copy-start | bytes 3145732 | tf_op jit(solution)/shard_map/while
  962.5 322.8 %copy-start.87 = (s32[2]{0:T(128)}, s32[2]{0:T(128)S(1)}, u32[]{:S(2)}) copy-start(s32[2]{0:T(128)S(1)} %get-tuple-element.748) | copy-start | bytes 28 | tf_op jit(solution)/shard_map/while
  962.5 41.7 %all-gather.18.cloned.1.call-start = ((), (), s32[]{:S(2)}) async-start(), calls=%async_computation.24 | async-start | bytes 2621440 | tf_op jit(solution)/shard_map/while/body/eval_jaxpr/all_gather | solution.py:28
  985.1 84.3 %all-gather.20.cloned.1.call-start = ((), (), s32[]{:S(2)}) async-start(), calls=%async_computation.25 | async-start | bytes 3538944 | tf_op jit(solution)/shard_map/while/body/eval_jaxpr/all_gather | solution.py:142
  985.7 124.3 %all-gather.22.cloned.1.call-start = ((), (), s32[]{:S(2)}) async-start(), calls=%async_computation.26 | async-start | bytes 1179648 | tf_op jit(solution)/shard_map/while/body/eval_jaxpr/all_gather | solution.py:143
  986.4 171.0 %reduce-scatter.25.cloned.1.call-start = ((), (), s32[]{:S(2)}) async-start(), calls=%async_computation.27 | async-start | bytes 5242880 | tf_op jit(solution)/shard_map/while/body/eval_jaxpr/reduce_scatter | solution.py:32
  1113.8 68.4 %all-gather.16.cloned.1.call-start = ((), (), s32[]{:S(2)}) async-start(), calls=%async_computation.23 | async-start | bytes 2621440 | tf_op jit(solution)/shard_map/while/body/eval_jaxpr/all_gather | solution.py:28
  1114.7 92.1 %all-gather.24.cloned.1.call-start = ((), (), s32[]{:S(2)}) async-start(), calls=%async_computation.28 | async-start | bytes 2621440 | tf_op jit(solution)/shard_map/while/body/eval_jaxpr/all_gather | solution.py:28
  1160.0 121.0 %reduce-scatter.27.cloned.1.call-start = ((), (), s32[]{:S(2)}) async-start(), calls=%async_computation.29 | async-start | bytes 5242880 | tf_op jit(solution)/shard_map/while/body/eval_jaxpr/reduce_scatter | solution.py:32
  1236.4 107.4 %all-gather.26.cloned.1.call-start = ((), (), s32[]{:S(2)}) async-start(), calls=%async_computation.30 | async-start | bytes 3244032 | tf_op jit(solution)/shard_map/while/body/eval_jaxpr/all_gather | solution.py:144
  1237.0 129.7 %all-gather.28.cloned.1.call-start = ((), (), s32[]{:S(2)}) async-start(), calls=%async_computation.31 | async-start | bytes 2621440 | tf_op jit(solution)/shard_map/while/body/eval_jaxpr/all_gather | solution.py:28
  1284.5 128.8 %all-gather.32.cloned.1.call-start = ((), (), s32[]{:S(2)}) async-start(), calls=%async_computation.33 | async-start | bytes 1622016 | tf_op jit(solution)/shard_map/while/body/eval_jaxpr/all_gather | solution.py:193
  1285.2 151.3 %all-gather.30.cloned.1.call-start = ((), (), s32[]{:S(2)}) async-start(), calls=%async_computation.32 | async-start | bytes 2621440 | tf_op jit(solution)/shard_map/while/body/eval_jaxpr/all_gather | solution.py:28
  1288.6 207.8 %reduce-scatter.29.cloned.1.call-start = ((), (), s32[]{:S(2)}) async-start(), calls=%async_computation.34 | async-start | bytes 5242880 | tf_op jit(solution)/shard_map/while/body/eval_jaxpr/reduce_scatter | solution.py:32
  1451.8 91.7 %reduce-scatter.31.cloned.1.call-start = ((), (), s32[]{:S(2)}) async-start(), calls=%async_computation.35 | async-start | bytes 5242880 | tf_op jit(solution)/shard_map/while/body/eval_jaxpr/reduce_scatter | solution.py:32
  1457.5 112.8 %all-gather.34.cloned.1.call-start = ((), (), s32[]{:S(2)}) async-start(), calls=%async_computation.36 | async-start | bytes 2621440 | tf_op jit(solution)/shard_map/while/body/eval_jaxpr/all_gather | solution.py:28
  1547.5 102.8 %reduce-scatter.33.cloned.1.call-start = ((), (), s32[]{:S(2)}) async-start(), calls=%async_computation.37 | async-start | bytes 5242880 | tf_op jit(solution)/shard_map/while/body/eval_jaxpr/reduce_scatter | solution.py:32
  1605.6 72.6 %all-gather.36.cloned.1.call-start = ((), (), s32[]{:S(2)}) async-start(), calls=%async_computation.38 | async-start | bytes 2621440 | tf_op jit(solution)/shard_map/while/body/eval_jaxpr/all_gather | solution.py:28
  1655.4 110.5 %reduce-scatter.37.cloned.1.call-start = ((), (), s32[]{:S(2)}) async-start(), calls=%async_computation.40 | async-start | bytes 5242880 | tf_op jit(solution)/shard_map/while/body/eval_jaxpr/reduce_scatter | solution.py:32
  1676.0 123.4 %reduce-scatter.35.cloned.1.call-start = ((), (), s32[]{:S(2)}) async-start(), calls=%async_computation.39 | async-start | bytes 5242880 | tf_op jit(solution)/shard_map/while/body/eval_jaxpr/reduce_scatter | solution.py:32
  1828.4 201.2 %reduce-scatter.23.cloned.1.call-start = ((), (), s32[]{:S(2)}) async-start(), calls=%async_computation.22 | async-start | bytes 589824
  1830.3 231.7 %reduce-scatter.17.cloned.1.call-start = ((), (), s32[]{:S(2)}) async-start(), calls=%async_computation.19 | async-start | bytes 2359296 | tf_op jit(solution)/shard_map/reduce_scatter | solution.py:317
  1830.8 258.6 %reduce-scatter.21.cloned.1.call-start = ((), (), s32[]{:S(2)}) async-start(), calls=%async_computation.21 | async-start | bytes 3244032 | tf_op jit(solution)/shard_map/reduce_scatter | solution.py:319
  1831.4 371.9 %reduce-scatter.19.cloned.1.call-start = ((), (), s32[]{:S(2)}) async-start(), calls=%async_computation.20 | async-start | bytes 6488064 | tf_op jit(solution)/shard_map/reduce_scatter | solution.py:318
  1832.2 492.6 %reduce-scatter.15.cloned.1.call-start = ((), (), s32[]{:S(2)}) async-start(), calls=%async_computation.18 | async-start | bytes 7077888 | tf_op jit(solution)/shard_map/reduce_scatter | solution.py:316
  1968.0 81.1 %all-to-all-start.4 = ((f32[2,256,1024]{2,0,1:T(2,128)}), f32[2,256,1024]{2,0,1:T(2,128)}, u32[]{:S(2)}, u32[]{:S(2)}) async-start(f32[2,256,1024]{2,0,1:T(2,128)} %get-tuple-element.307), calls=%async_computation.11 | async-start | bytes 4194304 | tf_op jit(solution)/shard_map/all_to_all | solution.py:308
  2091.6 233.1 %copy-start.46 = (f32[6,128,256]{2,1,0:T(8,128)S(1)}, f32[6,128,256]{2,1,0:T(8,128)}, u32[]{:S(2)}) copy-start(f32[6,128,256]{2,1,0:T(8,128)} %param.31) | copy-start | bytes 2359300
  2091.6 233.1 %copy-start.58 = (f32[6,128,256]{2,1,0:T(8,128)S(1)}, f32[6,128,256]{2,1,0:T(8,128)}, u32[]{:S(2)}) copy-start(f32[6,128,256]{2,1,0:T(8,128)} %param.41) | copy-start | bytes 2359300
  (178 other events, 2811.4 us)
Sparse Core Ops, SparseCore 0:
  128.3 19.8 all-gather.17
  150.4 63.0 all-gather.19
  216.3 37.7 all-gather.21
  258.0 43.4 reduce-scatter.24
  303.5 22.5 all-gather.15
  328.1 22.5 all-gather.23
  380.4 44.4 reduce-scatter.26
  427.8 60.0 all-gather.25
  490.0 20.7 all-gather.27
  513.5 43.8 all-gather.31
  559.6 20.9 all-gather.29
  596.0 44.4 reduce-scatter.28
  643.0 44.4 reduce-scatter.30
  691.6 22.5 all-gather.33
  749.8 44.4 reduce-scatter.32
  799.6 22.5 all-gather.35
  824.6 44.4 reduce-scatter.36
  871.7 44.4 reduce-scatter.34
  985.2 18.9 all-gather.17
  1006.3 63.0 all-gather.19
  1072.2 37.7 all-gather.21
  1113.9 43.4 reduce-scatter.24
  1159.6 22.5 all-gather.15
  1184.2 22.5 all-gather.23
  1236.5 44.4 reduce-scatter.26
  1283.7 60.0 all-gather.25
  1345.8 20.7 all-gather.27
  1369.4 43.8 all-gather.31
  1415.5 20.9 all-gather.29
  1451.9 44.4 reduce-scatter.28
  1499.0 44.4 reduce-scatter.30
  1547.6 22.5 all-gather.33
  1605.7 44.4 reduce-scatter.32
  1655.6 22.5 all-gather.35
  1680.7 44.4 reduce-scatter.36
  1727.8 44.4 reduce-scatter.34
Sparse Core Ops, SparseCore 1:
  1832.8 64.9 reduce-scatter.22
  1901.6 95.6 reduce-scatter.16
  2001.1 88.3 reduce-scatter.20
  2093.6 109.7 reduce-scatter.18
  2207.4 117.3 reduce-scatter.14
where the time goes:
time: 2350 us; the launch traced here: 2340 us
  waiting for transfers between devices  1310 us (56%)
  matrix products  358 us (15%)
  blocking collectives  291 us (12%)
  local copies, waits for them, and re-layouts  187 us (8%)
  other arithmetic  154 us (7%)
    reduce_scatter x14, waiting for transfers between devices, sum_rows(): return lax.psum_scatter(values, 'mp', scatter_dimension=0, tiled=True)  430 us
    all_gather x14, waiting for transfers between devices, gather_rows(): return lax.all_gather(values, 'mp', axis=0, tiled=True)  258 us
    all_gather x2, waiting for transfers between devices, micro_step(): lax.all_gather(shard_in, 'dp', axis=1, tiled=True)  131 us
    dynamic_update_slice x12, local copies, waits for them, and re-layouts, on_device(): lax.scan(micro_step, start, (tok_slots, cot_slots, enc_slots, slot_lengths))  122 us
    reduce_scatter x1, waiting for transfers between devices, on_device(): lax.psum_scatter(grad_totals[0], 'dp', scatter_dimension=1, tiled=True)  118 us
    reduce_scatter x1, waiting for transfers between devices, on_device(): lax.psum_scatter(grad_totals[2], 'dp', scatter_dimension=1, tiled=True)  112 us
    all_gather x2, waiting for transfers between devices, micro_step(): lax.all_gather(shard_ffin, 'dp', axis=1, tiled=True)  110 us
    all_gather x2, waiting for transfers between devices, micro_step(): lax.all_gather(shard_ffout, 'dp', axis=1, tiled=True)  77.1 us
  transfers between devices with their start and end apart: 43, of which 36 were waited for; matrix products, arithmetic and copies ran while one was open for 19% of the time, Pallas kernels for 0%

commit v1 on v0

v1 whole, which is shorter than its diff:
```python
import jax
import jax.numpy as jnp
from jax import lax
from jax.sharding import Mesh, PartitionSpec as P

D = 1024
DK = 64

epsilon = 1e-06
clip_limit = 10.0
momentum_rate = 0.9
learn_rate = 0.01
average_rate = 0.5
neg_large = -1e30
bf16 = jnp.bfloat16
f32 = jnp.float32
swap = ((0, 1), (1, 0))
chips = ("dp", "mx")


def rms_norm(hidden, gain_vec):
    row_scale = lax.rsqrt(jnp.mean(hidden * hidden, axis=-1, keepdims=True) + epsilon)
    return hidden * row_scale * gain_vec


def gelu_product(gate_part, up_part):
    return jax.nn.gelu(gate_part, approximate=True) * up_part


def nn(left, right):
    return lax.dot_general(left, right, (((1,), (0,)), ((), ())), preferred_element_type=f32)


def nt(left, right):
    return lax.dot_general(left, right, (((1,), (1,)), ((), ())), preferred_element_type=f32)


def tn(left, right):
    return lax.dot_general(left, right, (((0,), (0,)), ((), ())), preferred_element_type=f32)


def both_cores(own):
    return jnp.concatenate([own, lax.ppermute(own, "mc", swap)], axis=0)


def sum_cores(parts):
    own, other = parts
    return own + lax.ppermute(other, "mc", swap)


def split_heads(values):
    return values.reshape(values.shape[0], values.shape[1] // DK, DK)


def attend(query, keys, values, allowed):
    query_h, keys_h, values_h = split_heads(query), split_heads(keys), split_heads(values)
    scores = jnp.einsum("qhe,khe->hqk", query_h, keys_h, preferred_element_type=f32)
    masked = jnp.where(allowed, scores, neg_large)
    row_top = jnp.max(masked, axis=-1, keepdims=True)
    expo_rows = jnp.exp(masked - row_top)
    row_total = jnp.sum(expo_rows, axis=-1, keepdims=True)
    soft_rows = expo_rows / row_total
    mixed = jnp.einsum("hqk,khe->qhe", soft_rows.astype(bf16), values_h, preferred_element_type=f32)
    return (mixed.reshape(query.shape).astype(bf16), row_top + jnp.log(row_total), row_top)


def attend_back(query, keys, values, allowed, log_total, grad_mixed):
    query_h, keys_h, values_h = split_heads(query), split_heads(keys), split_heads(values)
    grad_h = split_heads(grad_mixed)
    scores = jnp.einsum("qhe,khe->hqk", query_h, keys_h, preferred_element_type=f32)
    soft_rows = jnp.exp(jnp.where(allowed, scores, neg_large) - log_total)
    grad_soft = jnp.einsum("qhe,khe->hqk", grad_h, values_h, preferred_element_type=f32)
    grad_values = jnp.einsum("hqk,qhe->khe", soft_rows.astype(bf16), grad_h, preferred_element_type=f32)
    row_dot = jnp.sum(grad_soft * soft_rows, axis=-1, keepdims=True)
    grad_scores = (soft_rows * (grad_soft - row_dot)).astype(bf16)
    grad_query = jnp.einsum("hqk,khe->qhe", grad_scores, keys_h, preferred_element_type=f32)
    grad_keys = jnp.einsum("hqk,qhe->khe", grad_scores, query_h, preferred_element_type=f32)
    return tuple(t.reshape(t.shape[0], -1).astype(bf16) for t in (grad_query, grad_keys, grad_values))


def norm_back(hidden, gain_vec, grad):
    row_scale = lax.rsqrt(jnp.mean(hidden * hidden, axis=-1, keepdims=True) + epsilon)
    z = hidden * row_scale
    grad_z = grad * gain_vec
    grad_hidden = row_scale * (grad_z - z * jnp.mean(grad_z * z, axis=-1, keepdims=True))
    return grad_hidden, jnp.sum(grad * z, axis=0)


def apply_update(weight, grad_sum, moment, average, factor, grad_scale):
    grad_now = grad_sum * grad_scale
    moment_new = momentum_rate * moment + grad_now
    master_new = (weight - learn_rate * (grad_now + momentum_rate * moment_new)) * factor
    average_new = average_rate * average + (1.0 - average_rate) * master_new
    return (grad_now, moment_new, average_new, master_new)


def flat_columns(block):
    return jnp.swapaxes(block, 0, 1).reshape(block.shape[1], -1)


def gather_chunk(local):
    own = lax.all_gather(local, "dp", axis=0, tiled=True)
    return own, lax.ppermute(own, "mx", swap)


def reduce_chunk(own, other):
    arrived = lax.ppermute(other.astype(bf16), "mx", swap)
    total = (own + arrived.astype(f32)).astype(bf16)
    return lax.psum_scatter(total, "dp", scatter_dimension=0, tiled=True).astype(f32)


def on_device(
    tokens,
    encoder,
    cotangent,
    lengths,
    deal,
    attn_in,
    attn_out,
    ff_in,
    ff_out,
    gains,
    mom_attn_in,
    mom_attn_out,
    mom_ff_in,
    mom_ff_out,
    mom_gains,
    avg_attn_in,
    avg_attn_out,
    avg_ff_in,
    avg_ff_out,
    avg_gains,
):
    seq_count, block_rows = tokens.shape[0], tokens.shape[1]
    core = lax.axis_index("mc")
    chip = lax.axis_index("dp") * lax.axis_size("mx") + lax.axis_index("mx")
    own_rows = block_rows * seq_count
    slot_len = 2 * own_rows
    heads_cols = attn_in.shape[2]
    hidden = ff_in.shape[2]
    model_rows = attn_in.shape[1]

    def to_chips(values):
        moved = lax.all_to_all(values, chips, split_axis=0, concat_axis=1, tiled=True)
        return moved.reshape(own_rows, D)

    def from_chips(rows):
        return lax.all_to_all(
            rows.reshape(1, own_rows, D), chips, split_axis=1, concat_axis=0, tiled=True
        ).astype(f32)

    seq_len = lengths[deal[chip]]
    row_ids = jnp.arange(own_rows, dtype=jnp.int32)
    lane = row_ids % block_rows
    pos_own = (row_ids // block_rows * 2 + core) * block_rows + lane
    pos_other = (row_ids // block_rows * 2 + 1 - core) * block_rows + lane
    pos = jnp.concatenate([pos_own, pos_other])
    allowed = pos[None, :] <= pos[:, None]
    valid_own = (pos_own < seq_len).astype(f32)[:, None]
    valid_all = pos < seq_len

    pad = jnp.zeros((model_rows, 125), bf16)
    chunk_a = jnp.concatenate(
        [flat_columns(attn_in[0:3].astype(bf16)), gains.astype(bf16).T, pad], axis=1
    )
    out_t = jnp.swapaxes(attn_out.astype(bf16), 1, 2)
    chunk_b = jnp.concatenate([out_t[0], flat_columns(attn_in[3:6].astype(bf16)), out_t[1]], axis=1)
    chunk_c = flat_columns(ff_in.astype(bf16))
    chunk_d = ff_out.astype(bf16).T

    tok_own = to_chips(tokens)
    got_a = gather_chunk(chunk_a)
    enc_own = to_chips(encoder)
    got_b = gather_chunk(chunk_b)
    cot_own = to_chips(cotangent)
    got_c = gather_chunk(chunk_c)
    got_d = gather_chunk(chunk_d)
    gain_f = got_a[0][:, 3 * heads_cols : 3 * heads_cols + 3].astype(f32).T

    hc = heads_cols
    w_qkv = [g[:, : 3 * hc] for g in got_a]
    w_ot = [g[:, :hc] for g in got_b]
    w_cq = [g[:, hc : 2 * hc] for g in got_b]
    w_ckv = [g[:, 2 * hc : 4 * hc] for g in got_b]
    w_cot = [g[:, 4 * hc :] for g in got_b]
    w_gu = got_c
    w_dt = got_d

    halves = lambda v: (v[:own_rows], v[own_rows:])
    x_rows = tok_own.astype(f32)
    norm_one = both_cores(rms_norm(x_rows, gain_f[0]).astype(bf16))
    qkv = [nn(norm_one, w).astype(bf16) for w in w_qkv]
    qkv = [(t[:, :hc], t[:, hc : 2 * hc], t[:, 2 * hc :]) for t in qkv]
    self_out = [attend(q, k, v, allowed) for q, k, v in qkv]
    head_top = jnp.stack(
        [jnp.max(jnp.where(valid_all[None, :, None], o[2], neg_large), axis=(1, 2)) for o in self_out]
    )
    branch = nt(self_out[0][0], w_ot[0]) + nt(self_out[1][0], w_ot[1])
    hidden_one = x_rows + sum_cores(halves(branch))
    norm_two = both_cores(rms_norm(hidden_one, gain_f[1]).astype(bf16))
    enc_all = both_cores(enc_own)
    cross_q = [nn(norm_two, w).astype(bf16) for w in w_cq]
    cross_kv = [nn(enc_all, w).astype(bf16) for w in w_ckv]
    cross_kv = [(t[:, :hc], t[:, hc:]) for t in cross_kv]
    cross_out = [attend(q, k, v, True) for q, (k, v) in zip(cross_q, cross_kv)]
    branch = nt(cross_out[0][0], w_cot[0]) + nt(cross_out[1][0], w_cot[1])
    hidden_two = hidden_one + sum_cores(halves(branch))
    norm_three = both_cores(rms_norm(hidden_two, gain_f[2]).astype(bf16))
    gate_up = [nn(norm_three, w) for w in w_gu]
    gate_up = [(t[:, :hidden], t[:, hidden:]) for t in gate_up]
    inner = [gelu_product(g, u).astype(bf16) for g, u in gate_up]
    branch = nt(inner[0], w_dt[0]) + nt(inner[1], w_dt[1])
    out_rows = (hidden_two + sum_cores(halves(branch))) * valid_own
    block_output = from_chips(out_rows.astype(bf16))

    grad_out = cot_own.astype(f32) * valid_own
    grad_out_all = both_cores(grad_out.astype(bf16))
    g_dt = [tn(grad_out_all, f) for f in inner]
    red_d = reduce_chunk(*g_dt)
    grad_gu = []
    for (g, u), w in zip(gate_up, w_dt):
        _, back = jax.vjp(gelu_product, g, u)
        dg, du = back(nn(grad_out_all, w))
        grad_gu.append(jnp.concatenate([dg.astype(bf16), du.astype(bf16)], axis=1))
    g_gu = [tn(norm_three, t) for t in grad_gu]
    red_c = reduce_chunk(*g_gu)
    grad_norm = sum_cores(halves(nt(grad_gu[0], w_gu[0]) + nt(grad_gu[1], w_gu[1])))
    grad_h, gain_three = norm_back(hidden_two, gain_f[2], grad_norm)
    grad_hidden_two = grad_out + grad_h
    grad_co = both_cores(grad_hidden_two.astype(bf16))
    g_cot = [tn(grad_co, o[0]) for o in cross_out]
    grad_ca = [nn(grad_co, w).astype(bf16) for w in w_cot]
    cross_back = [
        attend_back(q, k, v, True, o[1], d)
        for q, (k, v), o, d in zip(cross_q, cross_kv, cross_out, grad_ca)
    ]
    g_cq = [tn(norm_two, b[0]) for b in cross_back]
    d_ckv = [jnp.concatenate([b[1], b[2]], axis=1) for b in cross_back]
    g_ckv = [tn(enc_all, t) for t in d_ckv]
    red_b = reduce_chunk(*[jnp.concatenate(t, axis=1) for t in zip(g_cq, g_ckv, g_cot)])
    grad_norm = sum_cores(halves(nt(cross_back[0][0], w_cq[0]) + nt(cross_back[1][0], w_cq[1])))
    grad_enc = sum_cores(halves(nt(d_ckv[0], w_ckv[0]) + nt(d_ckv[1], w_ckv[1])))
    grad_encoder = from_chips(grad_enc.astype(bf16))
    grad_h, gain_two = norm_back(hidden_one, gain_f[1], grad_norm)
    grad_hidden_one = grad_hidden_two + grad_h
    grad_o = both_cores(grad_hidden_one.astype(bf16))
    g_ot = [tn(grad_o, o[0]) for o in self_out]
    grad_a = [nn(grad_o, w).astype(bf16) for w in w_ot]
    self_back = [
        jnp.concatenate(attend_back(q, k, v, allowed, o[1], d), axis=1)
        for (q, k, v), o, d in zip(qkv, self_out, grad_a)
    ]
    g_qkv = [tn(norm_one, t) for t in self_back]
    red_a = reduce_chunk(*[jnp.concatenate(t, axis=1) for t in zip(g_qkv, g_ot)])
    grad_norm = sum_cores(halves(nt(self_back[0], w_qkv[0]) + nt(self_back[1], w_qkv[1])))
    grad_h, gain_one = norm_back(x_rows, gain_f[0], grad_norm)
    grad_tokens = from_chips((grad_hidden_one + grad_h).astype(bf16))

    gain_total = lax.psum(jnp.stack([gain_one, gain_two, gain_three]), ("mx", "mc"))
    red_gain = lax.psum_scatter(gain_total, "dp", scatter_dimension=1, tiled=True)
    mx = lax.axis_index("mx")
    local_heads = hc // DK
    head_rows = jnp.where(mx == 0, head_top, head_top[::-1])
    head_peak = lax.dynamic_index_in_dim(lax.pmax(head_rows, chips), mx, 0, keepdims=False)

    unflat = lambda t, n: jnp.swapaxes(t.reshape(model_rows, n, -1), 0, 1)
    red_in = jnp.concatenate([unflat(red_a[:, : 3 * hc], 3), unflat(red_b[:, : 3 * hc], 3)])
    red_out = jnp.stack([red_a[:, 3 * hc :].T, red_b[:, 3 * hc :].T])
    clip_factors = clip_limit / jnp.maximum(head_peak, clip_limit)
    column = jnp.repeat(jnp.sqrt(clip_factors), DK)
    factor = jnp.where((jnp.arange(6) < 2)[:, None, None], column[None, None, :], 1.0)
    grad_scale = float(seq_count * slot_len) ** (-0.5)
    up_a = apply_update(attn_in, red_in, mom_attn_in, avg_attn_in, factor, grad_scale)
    up_b = apply_update(attn_out, red_out, mom_attn_out, avg_attn_out, 1.0, grad_scale)
    up_c = apply_update(ff_in, unflat(red_c, 2), mom_ff_in, avg_ff_in, 1.0, grad_scale)
    up_d = apply_update(ff_out, red_d.T, mom_ff_out, avg_ff_out, 1.0, grad_scale)
    up_e = apply_update(gains, red_gain, mom_gains, avg_gains, 1.0, grad_scale)
    return (
        block_output,
        grad_tokens,
        grad_encoder,
        *up_a,
        *up_b,
        *up_c,
        *up_d,
        *up_e,
        head_peak,
        clip_factors,
    )


def solution(mesh):
    dp, mp = mesh.shape["dp"], mesh.shape["mp"]
    fine = Mesh(mesh.devices.reshape(dp, mp // 2, 2), ("dp", "mx", "mc"))
    mp_axes = ("mx", "mc")
    rows = P(None, ("dp", "mx", "mc"), None)
    wide = P(None, "dp", mp_axes)
    tall = P(None, mp_axes, "dp")
    down = P(mp_axes, "dp")
    gain = P(None, "dp")
    state = (wide, tall, wide, down, gain)
    in_specs = (rows, rows, rows, P(), P(), *state, *state, *state)
    out_specs = (
        rows,
        rows,
        rows,
        *[wide] * 4,
        *[tall] * 4,
        *[wide] * 4,
        *[down] * 4,
        *[gain] * 4,
        P(mp_axes),
        P(mp_axes),
    )
    return jax.shard_map(
        on_device, mesh=fine, in_specs=in_specs, out_specs=out_specs, check_vma=False
    )
```

time: 2350 us -> 987 us (0.42)
  waiting for transfers between devices: 1310 us -> 290 us
  blocking collectives: 291 us -> 93.6 us
  local copies, waits for them, and re-layouts: 187 us -> 72.8 us
  matrix products: 358 us -> 311 us
  starting transfers between devices: 11.5 us -> 44.2 us
    reduce_scatter x18 -> x1, waiting for transfers between devices: 685 us -> 0.01 us  [reduce_chunk(): lax.psum_scatter(total, 'dp', scatter_dimension=0, tiled=True).astype(f32)]
    all_gather x22 -> x4, waiting for transfers between devices: 600 us -> 76.4 us  [gather_chunk(): own = lax.all_gather(local, 'dp', axis=0, tiled=True)]
    all_to_all x4 -> x1, blocking collectives: 190 us -> 30 us  [to_chips(): lax.all_to_all(values, chips, split_axis=0, concat_axis=1, tiled=True)]
    ppermute x0 -> x22, waiting for transfers between devices: none -> 139 us  [the longest x4 76.2 us: reduce_chunk(): arrived = lax.ppermute(other.astype(bf16), 'mx', swap)]
    dynamic_update_slice x12 -> x0, local copies, waits for them, and re-layouts: 122 us -> none  [on_device(): lax.scan(micro_step, start, (tok_slots, cot_slots, enc_slots, slot_lengths))]
    unnamed x45 -> x351, local copies, waits for them, and re-layouts: 5.26 us -> 57 us
    all_to_all x2 -> x5, waiting for transfers between devices: 17.1 us -> 65.6 us  [the longest x2 50.1 us: to_chips(): lax.all_to_all(values, chips, split_axis=0, concat_axis=1, tiled=True)]
    dot_general x66, matrix products: 358 us -> 311 us  [the longest x4 60.3 us: attend_back(): jnp.einsum('qhe,khe->hqk', grad_h, values_h, preferred_element_type=f32)]
  transfers between devices with their start and end apart: 43 -> 36, of which waited for: 36 -> 17; matrix products, arithmetic and copies ran while one was open for 19% -> 43% of each run, Pallas kernels for 0% -> 0%
where the time goes in v1:
time: 987 us; the launch traced here: 979 us
  matrix products  311 us (32%)
  waiting for transfers between devices  290 us (29%)
  other arithmetic  148 us (15%)
  blocking collectives  93.6 us (9%)
  local copies, waits for them, and re-layouts  72.8 us (7%)
  starting transfers between devices  44.2 us (4%)
  between operations  18.7 us (2%)
    all_gather x4, waiting for transfers between devices, gather_chunk(): own = lax.all_gather(local, 'dp', axis=0, tiled=True)  76.4 us
    ppermute x4, waiting for transfers between devices, reduce_chunk(): arrived = lax.ppermute(other.astype(bf16), 'mx', swap)  76.2 us
    dot_general x4, matrix products, attend_back(): jnp.einsum('qhe,khe->hqk', grad_h, values_h, preferred_element_type=f32)  60.3 us
    pmax x1, blocking collectives, on_device(): lax.pmax(head_rows, chips)  57.6 us
    unnamed x351, local copies, waits for them, and re-layouts  57 us
    ppermute x4, waiting for transfers between devices, gather_chunk(): return (own, lax.ppermute(own, 'mx', swap))  55.1 us
    dot_general x14, matrix products, nn(): lax.dot_general(left, right, (((1,), (0,)), ((), ())), preferred_element_...  50.1 us
    all_to_all x2, waiting for transfers between devices, to_chips(): lax.all_to_all(values, chips, split_axis=0, concat_axis=1, tiled=True)  50.1 us
  transfers between devices with their start and end apart: 36, of which 17 were waited for; matrix products, arithmetic and copies ran while one was open for 43% of the time, Pallas kernels for 0%

profile of v1, /device:TPU:0, one launch (start us, length us, event | category | flops | bytes accessed | tf_op | source)
XLA Modules:
  0.0 978.8 jit_solution(4755610367959535407)
XLA Ops:
  10.4 8.3 all-to-all-start
  19.6 30.9 %all-to-all-done = bf16[16,32,1024]{2,1,0:T(8,128)(2,1)S(1)} async-done(((bf16[16,32,1024]{2,1,0:T(8,128)(2,1)}), bf16[16,32,1024]{2,1,0:T(8,128)(2,1)S(1)}, u32[]{:S(2)}, u32[]{:S(2)}) %all-to-all-start) | async-done | bytes 1048608 | tf_op jit(solution)/shard_map/all_to_all | solution.py:144
  50.9 20.9 %all-gather.5.cloned.1.call-done = bf16[1024,896]{0,1:T(8,128)(2,1)} async-done(((bf16[128,896]{0,1:T(8,128)(2,1)}), bf16[1024,896]{0,1:T(8,128)(2,1)}) %all-gather.5.cloned.1.call-update) | async-done | bytes 1835024 | tf_op jit(solution)/shard_map/all_gather | solution.py:102
  81.4 8.2 fusion.153
  89.6 39.9 %all-gather.7.cloned.1.call-done = bf16[1024,1280]{0,1:T(8,128)(2,1)} async-done(((bf16[128,1280]{0,1:T(8,128)(2,1)}), bf16[1024,1280]{0,1:T(8,128)(2,1)}) %all-gather.7.cloned.1.call-update) | async-done | bytes 2621456 | tf_op jit(solution)/shard_map/all_gather | solution.py:102
  138.4 9.9 %select_reduce_fusion = (f32[4,1024]{1,0:T(4,128)}, f32[4,1024]{1,0:T(4,128)}, f32[4,1024,1024]{1,2,0:T(8,128)}) fusion(pred[1024,1024]{0,1:T(8,128)(4,1)S(1)} %broadcast_compare_fusion, f32[4,1024,1024]{1,2,0:T(8,128)S(1)} %copy-done, bf16[1024,4,64]{0,2,1:T(8,128)(2,1)} %bitcast.269, bf16[1024,4,64]{0,2,1:T(8,128)(2,1)} %bitcast.267), kind=kOutput, calls=%fused_computation.24 | convolution fusion | flops 553639936 | bytes 35684352 | tf_op jit(solution)/shard_map/qhe,khe->hqk/dot_general | solution.py:57
  148.3 9.1 fusion.1
  164.0 8.2 fusion.78
  172.2 15.8 %collective-permute-done.2 = bf16[1024,1280]{0,1:T(8,128)(2,1)} collective-permute-done((bf16[1024,1280]{0,1:T(8,128)(2,1)}, bf16[1024,1280]{0,1:T(8,128)(2,1)}, u32[]{:S(2)}, u32[]{:S(2)}) %collective-permute-start.2) | collective-permute-done | bytes 2621472 | tf_op jit(solution)/shard_map/ppermute | solution.py:103
  191.9 30.0 %all_to_all.24 = bf16[16,32,1024]{2,1,0:T(8,128)(2,1)} all-to-all(bf16[16,32,1024]{2,1,0:T(8,128)(2,1)S(1)} %copy-done.58), channel_id=1, replica_groups=mesh['dp'=8,'mx'=2,'mc'=2] {'dp','mx'}, dimensions={0} | all-to-all | bytes 2097152 | tf_op jit(solution)/shard_map/all_to_all | solution.py:144
  235.7 8.2 fusion.151
  243.9 8.0 fusion.2
  252.0 8.0 fusion.81
  262.1 8.2 fusion.152
  274.1 8.0 fusion.3
  282.2 7.5 fusion.80
  312.1 19.2 %all-to-all-done.3 = bf16[16,32,1024]{2,1,0:T(8,128)(2,1)} async-done(((bf16[16,32,1024]{2,1,0:T(8,128)(2,1)}), bf16[16,32,1024]{2,1,0:T(8,128)(2,1)}, u32[]{:S(2)}, u32[]{:S(2)}) %all-to-all-start.3) | async-done | bytes 1048608 | tf_op jit(solution)/shard_map/all_to_all | solution.py:144
  333.8 15.6 %all-gather.11.cloned.1.call-done = bf16[1024,704]{0,1:T(8,128)(2,1)} async-done(((bf16[128,704]{0,1:T(8,128)(2,1)}), bf16[1024,704]{0,1:T(8,128)(2,1)}) %all-gather.11.cloned.1.call-update) | async-done | bytes 1441808 | tf_op jit(solution)/shard_map/all_gather | solution.py:102
  356.8 20.6 %collective-permute-done.8 = bf16[1024,1408]{0,1:T(8,128)(2,1)} collective-permute-done((bf16[1024,1408]{0,1:T(8,128)(2,1)}, bf16[1024,1408]{0,1:T(8,128)(2,1)}, u32[]{:S(2)}, u32[]{:S(2)}) %collective-permute-start.8) | collective-permute-done | bytes 2883616 | tf_op jit(solution)/shard_map/ppermute | solution.py:103
  377.4 5.9 fusion.136
  388.7 18.6 %collective-permute-done.9 = bf16[1024,704]{0,1:T(8,128)(2,1)S(1)} collective-permute-done((bf16[1024,704]{0,1:T(8,128)(2,1)}, bf16[1024,704]{0,1:T(8,128)(2,1)S(1)}, u32[]{:S(2)}, u32[]{:S(2)}) %collective-permute-start.9) | collective-permute-done | bytes 1441824 | tf_op jit(solution)/shard_map/ppermute | solution.py:103
  440.0 11.2 %multiply_reduce_fusion.3 = (f32[4,1024]{1,0:T(4,128)}, f32[4,1024,1024]{1,2,0:T(8,128)}) fusion(f32[4,1024,1024]{1,2,0:T(8,128)S(1)} %bitcast.246, f32[4,1024]{1,0:T(4,128)S(1)} %log_add_fusion.3, bf16[1024,4,64]{0,2,1:T(8,128)(2,1)} %bitcast.282, bf16[1024,4,64]{0,2,1:T(8,128)(2,1)} %bitcast.291), kind=kOutput, calls=%fused_computation.10 | convolution fusion | flops 549449728 | bytes 34635776 | tf_op jit(solution)/shard_map/qhe,khe->hqk/dot_general | solution.py:72
  451.2 8.0 multiply_convert_fusion.3
  465.6 16.2 %multiply_reduce_fusion.2 = (f32[4,1024]{1,0:T(4,128)}, f32[4,1024,1024]{1,2,0:T(8,128)}) fusion(f32[4,1024,1024]{1,2,0:T(8,128)} %get-tuple-element.99, f32[4,1024]{1,0:T(4,128)S(1)} %copy-done.85, bf16[1024,4,64]{0,2,1:T(8,128)(2,1)} %bitcast.284, bf16[1024,4,64]{0,2,1:T(8,128)(2,1)} %bitcast.289), kind=kOutput, calls=%fused_computation.7 | convolution fusion | flops 549449728 | bytes 34635776 | tf_op jit(solution)/shard_map/qhe,khe->hqk/dot_general | solution.py:72
  481.7 8.1 multiply_convert_fusion.2
  506.1 7.6 convolution_convert_fusion
  514.9 21.3 %collective-permute-done.21 = bf16[1024,704]{0,1:T(8,128)(2,1)S(1)} collective-permute-done((bf16[1024,704]{0,1:T(8,128)(2,1)S(1)}, bf16[1024,704]{0,1:T(8,128)(2,1)S(1)}, u32[]{:S(2)}, u32[]{:S(2)}) %collective-permute-start.21) | collective-permute-done | bytes 1441824 | tf_op jit(solution)/shard_map/ppermute | solution.py:107
  543.9 8.3 fusion.155
  552.2 8.0 fusion.66
  562.9 8.0 fusion.69
  570.9 24.6 %multiply_reduce_fusion = (f32[4,1024]{1,0:T(4,128)S(1)}, f32[4,1024]{1,0:T(4,128)S(1)}, f32[4,1024,1024]{1,2,0:T(8,128)}) fusion(f32[4,1024,1024]{1,2,0:T(8,128)} %get-tuple-element.95, f32[4,1024]{1,0:T(4,128)S(1)} %log_add_fusion, pred[1024,1024]{0,1:T(8,128)(4,1)S(1)} %copy-done.4, f32[4,1024,1024]{1,2,0:T(8,128)} %fusion.155, ...), kind=kOutput, calls=%fused_computation.1 | convolution fusion | flops 570417152 | bytes 69271552 | tf_op jit(solution)/shard_map/qhe,khe->hqk/dot_general | solution.py:72
  595.6 29.9 %multiply_convert_fusion = (bf16[4,1024,1024]{1,2,0:T(8,128)(2,1)}, bf16[4,1024,1024]{1,2,0:T(8,128)(2,1)}) fusion(f32[4,1024,1024]{1,2,0:T(8,128)} %get-tuple-element.104, f32[4,1024,1024]{1,2,0:T(8,128)} %get-tuple-element.95, f32[4,1024]{1,0:T(4,128)S(1)} %get-tuple-element.31, f32[4,1024]{1,0:T(4,128)S(1)} %log_add_fusion, ...), kind=kLoop, calls=%fused_computation | loop fusion | flops 41943040 | bytes 85000192 | tf_op jit(solution)/shard_map/convert_element_type | solution.py:75
  625.5 6.2 convolution_convert_fusion.10
  653.9 8.1 add_convert_fusion
  663.0 6.0 convolution_convert_fusion.8
  669.1 8.8 fusion.75
  685.8 6.3 convolution_convert_fusion.9
  700.7 32.4 %collective-permute-done.19 = bf16[1024,1024]{0,1:T(8,128)(2,1)} collective-permute-done((bf16[1024,1024]{0,1:T(8,128)(2,1)}, bf16[1024,1024]{0,1:T(8,128)(2,1)}, u32[]{:S(2)}, u32[]{:S(2)}) %collective-permute-start.19) | collective-permute-done | bytes 2097184 | tf_op jit(solution)/shard_map/ppermute | solution.py:107
  757.0 7.9 reduce.4
  767.6 6.6 all-to-all-start.2
  779.7 22.5 %collective-permute-done.18 = bf16[1024,1024]{0,1:T(8,128)(2,1)} collective-permute-done((bf16[1024,1024]{0,1:T(8,128)(2,1)}, bf16[1024,1024]{0,1:T(8,128)(2,1)}, u32[]{:S(2)}, u32[]{:S(2)}) %collective-permute-start.18) | collective-permute-done | bytes 2097184 | tf_op jit(solution)/shard_map/ppermute | solution.py:107
  812.8 9.2 reduce.6
  834.6 6.8 reduce.5
  843.0 15.5 %all-to-all-done.5 = bf16[16,2,16384]{2,1,0:T(2,128)(2,1)} async-done(((bf16[16,2,16384]{2,1,0:T(2,128)(2,1)}), bf16[16,2,16384]{2,1,0:T(2,128)(2,1)}, u32[]{:S(2)}, u32[]{:S(2)}) %all-to-all-start.5) | async-done | bytes 1048608 | tf_op jit(solution)/shard_map/all_to_all | solution.py:148
  858.5 6.9 all-to-all-start.4
  865.4 57.6 %pmax.7 = f32[2,4]{1,0:T(2,128)S(1)} all-reduce(f32[2,4]{1,0:T(2,128)S(1)} %broadcast_select_fusion.1), channel_id=1, replica_groups=mesh['dp'=8,'mx'=2,'mc'=2] {'dp','mx'}, use_global_device_ids=true, to_apply=%region_22.23 | all-reduce | flops 8 | bytes 64 | tf_op jit(solution)/shard_map/pmax | solution.py:264
  940.4 5.9 psum.8
  956.5 8.9 reduce-scatter.16.cloned.1.call-done
  (553 shorter events, 284.2 us)
Async XLA Ops:
  7.2 64.6 %all-gather.5.cloned.1.call-start = ((), (), s32[]{:S(2)}) async-start(), calls=%async_computation.11 | async-start | bytes 2064384 | tf_op jit(solution)/shard_map/all_gather | solution.py:102
  10.4 40.1 %all-to-all-start = ((bf16[16,32,1024]{2,1,0:T(8,128)(2,1)}), bf16[16,32,1024]{2,1,0:T(8,128)(2,1)S(1)}, u32[]{:S(2)}, u32[]{:S(2)}) async-start(bf16[16,32,1024]{2,1,0:T(8,128)(2,1)} %param.20), calls=%async_computation | async-start | bytes 2097152 | tf_op jit(solution)/shard_map/all_to_all | solution.py:144
  18.7 110.8 %all-gather.7.cloned.1.call-start = ((), (), s32[]{:S(2)}) async-start(), calls=%async_computation.12 | async-start | bytes 2949120 | tf_op jit(solution)/shard_map/all_gather | solution.py:102
  19.6 281.5 %all-gather.9.cloned.1.call-start = ((), (), s32[]{:S(2)}) async-start(), calls=%async_computation.13 | async-start | bytes 3244032 | tf_op jit(solution)/shard_map/all_gather | solution.py:102
  50.5 30.0 %copy-start.5 = (bf16[16,32,1024]{2,1,0:T(8,128)(2,1)}, bf16[16,32,1024]{2,1,0:T(8,128)(2,1)S(1)}, u32[]{:S(2)}) copy-start(bf16[16,32,1024]{2,1,0:T(8,128)(2,1)S(1)} %all-to-all-done) | copy-start | bytes 3145732
  73.1 152.8 %copy-start.99 = (f32[1,1024]{1,0:T(1,128)}, f32[1,1024]{1,0:T(1,128)S(1)}, u32[]{:S(2)}) copy-start(f32[1,1024]{1,0:T(1,128)S(1)} %get-tuple-element.93) | copy-start | bytes 12292
  74.0 2.9 collective-permute-start
  74.1 56.9 %collective-permute-start.1 = (bf16[1024,896]{0,1:T(8,128)(2,1)}, bf16[1024,896]{0,1:T(8,128)(2,1)}, u32[]{:S(2)}, u32[]{:S(2)}) collective-permute-start(bf16[1024,896]{0,1:T(8,128)(2,1)} %all-gather.5.cloned.1.call-done), channel_id=1, source_target_pairs={{0,2},{2,0},{1,3},{3,1},{4,6},{6,4},{5,7},{7,5},{8,10},{10,8},{9,1... | collective-permute-start | bytes 5505032 | tf_op jit(solution)/shard_map/ppermute | solution.py:103
  76.4 87.6 %copy-start.3 = (pred[1024,1024]{0,1:T(8,128)(4,1)}, pred[1024,1024]{0,1:T(8,128)(4,1)S(1)}, u32[]{:S(2)}) copy-start(pred[1024,1024]{0,1:T(8,128)(4,1)S(1)} %broadcast_compare_fusion) | copy-start | bytes 3145732
  129.5 58.5 %collective-permute-start.2 = (bf16[1024,1280]{0,1:T(8,128)(2,1)}, bf16[1024,1280]{0,1:T(8,128)(2,1)}, u32[]{:S(2)}, u32[]{:S(2)}) collective-permute-start(bf16[1024,1280]{0,1:T(8,128)(2,1)} %all-gather.7.cloned.1.call-done), channel_id=1, source_target_pairs={{0,2},{2,0},{1,3},{3,1},{4,6},{6,4},{5,7},{7,5},{8,10},{10,8},{9,1... | collective-permute-start | bytes 7864328 | tf_op jit(solution)/shard_map/ppermute | solution.py:103
  189.8 32.0 %copy-start.12 = (f32[1024,1024]{1,0:T(8,128)}, f32[1024,1024]{1,0:T(8,128)S(1)}, u32[]{:S(2)}) copy-start(f32[1024,1024]{1,0:T(8,128)S(1)} %convolution_add_fusion.3) | copy-start | bytes 12582916
  189.9 32.0 %copy-start.35 = (f32[2,128,704]{1,2,0:T(8,128)S(1)}, f32[2,128,704]{1,2,0:T(8,128)}, u32[]{:S(2)}) copy-start(f32[2,128,704]{1,2,0:T(8,128)} %param.27) | copy-start | bytes 2162692
  190.0 32.9 %collective-permute-start.3 = (f32[512,1024]{1,0:T(8,128)S(1)}, f32[512,1024]{1,0:T(8,128)}, u32[]{:S(2)}, u32[]{:S(2)}) collective-permute-start(f32[512,1024]{1,0:T(8,128)S(1)} %slice.222), channel_id=1, source_target_pairs={{0,1},{1,0},{2,3},{3,2},{4,5},{5,4},{6,7},{7,6},{8,9},{9,8},{10,11... | collective-permute-start | bytes 6291464 | tf_op jit(solution)/shard_map/ppermute | solution.py:48
  221.9 4.9 collective-permute-start.4
  222.7 126.7 %all-gather.11.cloned.1.call-start = ((), (), s32[]{:S(2)}) async-start(), calls=%async_computation.14 | async-start | bytes 1622016 | tf_op jit(solution)/shard_map/all_gather | solution.py:102
  226.2 33.9 %copy-start.59 = (bf16[512,1024]{1,0:T(8,128)(2,1)}, bf16[512,1024]{1,0:T(8,128)(2,1)S(1)}, u32[]{:S(2)}) copy-start(bf16[512,1024]{1,0:T(8,128)(2,1)S(1)} %multiply_convert_fusion.9) | copy-start | bytes 3145732
  226.2 8.5 collective-permute-start.5
  234.7 47.5 %copy-start.41 = (bf16[1024,256]{0,1:T(8,128)(2,1)}, bf16[1024,256]{0,1:T(8,128)(2,1)S(1)}, u32[]{:S(2)}) copy-start(bf16[1024,256]{0,1:T(8,128)(2,1)S(1)} %get-tuple-element.85) | copy-start | bytes 1572868
  295.3 7.6 collective-permute-start.6
  296.5 34.8 %all-to-all-start.3 = ((bf16[16,32,1024]{2,1,0:T(8,128)(2,1)}), bf16[16,32,1024]{2,1,0:T(8,128)(2,1)}, u32[]{:S(2)}, u32[]{:S(2)}) async-start(bf16[16,32,1024]{2,1,0:T(8,128)(2,1)} %param.22), calls=%async_computation.3 | async-start | bytes 2097152 | tf_op jit(solution)/shard_map/all_to_all | solution.py:144
  300.8 629.1 %reduce-scatter.20.cloned.1.call-start = ((), (), s32[]{:S(2)}) async-start(), calls=%async_computation.18 | async-start | bytes 1769472
  301.1 76.3 %collective-permute-start.8 = (bf16[1024,1408]{0,1:T(8,128)(2,1)}, bf16[1024,1408]{0,1:T(8,128)(2,1)}, u32[]{:S(2)}, u32[]{:S(2)}) collective-permute-start(bf16[1024,1408]{0,1:T(8,128)(2,1)} %all-gather.9.cloned.1.call-done), channel_id=1, source_target_pairs={{0,2},{2,0},{1,3},{3,1},{4,6},{6,4},{5,7},{7,5},{8,10},{10,8},{9,1... | collective-permute-start | bytes 8650760 | tf_op jit(solution)/shard_map/ppermute | solution.py:103
  308.3 42.6 %collective-permute-start.7 = (bf16[512,1024]{1,0:T(8,128)(2,1)}, bf16[512,1024]{1,0:T(8,128)(2,1)}, u32[]{:S(2)}, u32[]{:S(2)}) collective-permute-start(bf16[512,1024]{1,0:T(8,128)(2,1)} %multiply_convert_fusion.8), channel_id=1, source_target_pairs={{0,1},{1,0},{2,3},{3,2},{4,5},{5,4},{6,7},{7,6},{8,9},{9,8},{10,11... | collective-permute-start | bytes 3145736 | tf_op jit(solution)/shard_map/ppermute | solution.py:43
  333.8 49.6 %collective-permute-start.11 = (bf16[512,1024]{1,0:T(8,128)(2,1)}, bf16[512,1024]{1,0:T(8,128)(2,1)}, u32[]{:S(2)}, u32[]{:S(2)}) collective-permute-start(bf16[512,1024]{1,0:T(8,128)(2,1)} %fusion.47), channel_id=1, source_target_pairs={{0,1},{1,0},{2,3},{3,2},{4,5},{5,4},{6,7},{7,6},{8,9},{9,8},{10,11... | collective-permute-start | bytes 3145736 | tf_op jit(solution)/shard_map/ppermute | solution.py:43
  349.4 57.9 %collective-permute-start.9 = (bf16[1024,704]{0,1:T(8,128)(2,1)}, bf16[1024,704]{0,1:T(8,128)(2,1)S(1)}, u32[]{:S(2)}, u32[]{:S(2)}) collective-permute-start(bf16[1024,704]{0,1:T(8,128)(2,1)} %all-gather.11.cloned.1.call-done), channel_id=1, source_target_pairs={{0,2},{2,0},{1,3},{3,1},{4,6},{6,4},{5,7},{7,5},{8,10},{10,8},{9,1... | collective-permute-start | bytes 4325384 | tf_op jit(solution)/shard_map/ppermute | solution.py:103
  388.7 33.3 %copy-start.143 = (bf16[1024,704]{1,0:T(8,128)(2,1)}, bf16[1024,704]{1,0:T(8,128)(2,1)S(1)}, u32[]{:S(2)}) copy-start(bf16[1024,704]{1,0:T(8,128)(2,1)S(1)} %get-tuple-element.74) | copy-start | bytes 4325380
  421.9 4.6 collective-permute-start.12
  426.0 4.3 collective-permute-start.10
  434.3 2.7 collective-permute-start.13
  497.3 5.0 collective-permute-start.14
  501.7 34.5 %collective-permute-start.21 = (bf16[1024,704]{0,1:T(8,128)(2,1)S(1)}, bf16[1024,704]{0,1:T(8,128)(2,1)S(1)}, u32[]{:S(2)}, u32[]{:S(2)}) collective-permute-start(bf16[1024,704]{0,1:T(8,128)(2,1)S(1)} %convolution_convert_fusion.4), channel_id=1, source_target_pairs={{0,2},{2,0},{1,3},{3,1},{4,6},{6,4},{5,7},{7,5},{8,10},{10,8},{9,1... | collective-permute-start | bytes 4325384 | tf_op jit(solution)/shard_map/ppermute | solution.py:107
  505.6 35.8 %collective-permute-start.15 = (bf16[512,1024]{1,0:T(8,128)(2,1)}, bf16[512,1024]{1,0:T(8,128)(2,1)S(1)}, u32[]{:S(2)}, u32[]{:S(2)}) collective-permute-start(bf16[512,1024]{1,0:T(8,128)(2,1)} %get-tuple-element.61), channel_id=1, source_target_pairs={{0,1},{1,0},{2,3},{3,2},{4,5},{5,4},{6,7},{7,6},{8,9},{9,8},{10,11... | collective-permute-start | bytes 3145736 | tf_op jit(solution)/shard_map/ppermute | solution.py:43
  506.1 30.2 %copy-start.144 = (bf16[1024,704]{1,0:T(8,128)(2,1)S(1)}, bf16[1024,704]{1,0:T(8,128)(2,1)}, u32[]{:S(2)}) copy-start(bf16[1024,704]{1,0:T(8,128)(2,1)} %copy-done.143) | copy-start | bytes 4325380
  513.7 140.2 %collective-permute-start.20 = (bf16[1024,1408]{1,0:T(8,128)(2,1)}, bf16[1024,1408]{1,0:T(8,128)(2,1)}, u32[]{:S(2)}, u32[]{:S(2)}) collective-permute-start(bf16[1024,1408]{1,0:T(8,128)(2,1)} %convolution_convert_fusion), channel_id=1, source_target_pairs={{0,2},{2,0},{1,3},{3,1},{4,6},{6,4},{5,7},{7,5},{8,10},{10,8},{9,1... | collective-permute-start | bytes 8650760 | tf_op jit(solution)/shard_map/ppermute | solution.py:107
  541.1 398.4 %reduce-scatter.22.cloned.1.call-start = ((), (), s32[]{:S(2)}) async-start(), calls=%async_computation.19 | async-start | bytes 589824
  560.2 81.1 %copy-start.137 = (bf16[4,64,1024]{2,1,0:T(8,128)(2,1)}, bf16[4,64,1024]{2,1,0:T(8,128)(2,1)S(1)}, u32[]{:S(2)}) copy-start(bf16[4,64,1024]{2,1,0:T(8,128)(2,1)S(1)} %fusion.66) | copy-start | bytes 1572868
  570.9 72.3 %copy-start.139 = (bf16[4,64,1024]{2,1,0:T(8,128)(2,1)}, bf16[4,64,1024]{2,1,0:T(8,128)(2,1)S(1)}, u32[]{:S(2)}) copy-start(bf16[4,64,1024]{2,1,0:T(8,128)(2,1)S(1)} %fusion.69) | copy-start | bytes 1572868
  595.6 29.9 %copy-start.24 = (bf16[1024,256]{0,1:T(8,128)(2,1)S(1)}, bf16[1024,256]{0,1:T(8,128)(2,1)}, u32[]{:S(2)}) copy-start(bf16[1024,256]{0,1:T(8,128)(2,1)} %get-tuple-element.78) | copy-start | bytes 1572868
  647.0 4.2 collective-permute-start.16
  653.6 293.3 %reduce-scatter.14.cloned.1.call-start = ((), (), s32[]{:S(2)}) async-start(), calls=%async_computation.15 | async-start | bytes 3244032 | tf_op jit(solution)/shard_map/reduce_scatter | solution.py:109
  662.0 289.6 %reduce-scatter.18.cloned.1.call-start = ((), (), s32[]{:S(2)}) async-start(), calls=%async_computation.17 | async-start | bytes 2359296
  685.2 48.0 %collective-permute-start.19 = (bf16[1024,1024]{0,1:T(8,128)(2,1)}, bf16[1024,1024]{0,1:T(8,128)(2,1)}, u32[]{:S(2)}, u32[]{:S(2)}) collective-permute-start(bf16[1024,1024]{0,1:T(8,128)(2,1)} %pad_maximum_fusion.10), channel_id=1, source_target_pairs={{0,2},{2,0},{1,3},{3,1},{4,6},{6,4},{5,7},{7,5},{8,10},{10,8},{9,1... | collective-permute-start | bytes 6291464 | tf_op jit(solution)/shard_map/ppermute | solution.py:107
  748.0 54.2 %collective-permute-start.18 = (bf16[1024,1024]{0,1:T(8,128)(2,1)}, bf16[1024,1024]{0,1:T(8,128)(2,1)}, u32[]{:S(2)}, u32[]{:S(2)}) collective-permute-start(bf16[1024,1024]{0,1:T(8,128)(2,1)} %pad_maximum_fusion.9), channel_id=1, source_target_pairs={{0,2},{2,0},{1,3},{3,1},{4,6},{6,4},{5,7},{7,5},{8,10},{10,8},{9,1... | collective-permute-start | bytes 6291464 | tf_op jit(solution)/shard_map/ppermute | solution.py:107
  754.7 52.6 %collective-permute-start.17 = (f32[512,1024]{1,0:T(8,128)}, f32[512,1024]{1,0:T(8,128)}, u32[]{:S(2)}, u32[]{:S(2)}) collective-permute-start(f32[512,1024]{1,0:T(8,128)} %slice.250), channel_id=1, source_target_pairs={{0,1},{1,0},{2,3},{3,2},{4,5},{5,4},{6,7},{7,6},{8,9},{9,8},{10,11... | collective-permute-start | bytes 6291464 | tf_op jit(solution)/shard_map/ppermute | solution.py:48
  767.6 56.9 %all-to-all-start.2 = ((bf16[16,2,16384]{2,1,0:T(2,128)(2,1)}), bf16[16,2,16384]{2,1,0:T(2,128)(2,1)}, u32[]{:S(2)}, u32[]{:S(2)}) async-start(bf16[16,2,16384]{2,1,0:T(2,128)(2,1)} %reshape.470), calls=%async_computation.2 | async-start | bytes 2097152 | tf_op jit(solution)/shard_map/all_to_all | solution.py:148
  774.2 191.2 %reduce-scatter.16.cloned.1.call-start = ((), (), s32[]{:S(2)}) async-start(), calls=%async_computation.16 | async-start | bytes 2359296
  824.6 33.9 %all-to-all-start.5 = ((bf16[16,2,16384]{2,1,0:T(2,128)(2,1)}), bf16[16,2,16384]{2,1,0:T(2,128)(2,1)}, u32[]{:S(2)}, u32[]{:S(2)}) async-start(bf16[16,2,16384]{2,1,0:T(2,128)(2,1)} %reshape.474), calls=%async_computation.5 | async-start | bytes 2097152 | tf_op jit(solution)/shard_map/all_to_all | solution.py:148
  858.5 95.2 %all-to-all-start.4 = ((bf16[16,2,16384]{2,1,0:T(2,128)(2,1)}), bf16[16,2,16384]{2,1,0:T(2,128)(2,1)S(1)}, u32[]{:S(2)}, u32[]{:S(2)}) async-start(bf16[16,2,16384]{2,1,0:T(2,128)(2,1)} %reshape.472), calls=%async_computation.4 | async-start | bytes 2097152 | tf_op jit(solution)/shard_map/all_to_all | solution.py:148
  (154 other events, 1091.7 us)
Sparse Core Ops, SparseCore 0:
  10.7 61.0 all-gather.4
  74.4 55.0 all-gather.6
  222.8 58.4 all-gather.8
  296.6 52.7 all-gather.10
  541.3 64.9 reduce-scatter.19
  653.7 62.0 reduce-scatter.21
  719.3 86.9 reduce-scatter.13
  809.8 84.6 reduce-scatter.17
  898.1 67.2 reduce-scatter.15

commit v2 on v1

v2 whole, which is shorter than its diff:
```python
import functools

import jax
import jax.numpy as jnp
from jax import lax
from jax.experimental import pallas as pl
from jax.experimental.layout import Layout, with_layout_constraint
from jax.experimental.pallas import tpu as pltpu
from jax.sharding import Mesh, PartitionSpec as P

D = 1024
DK = 64

epsilon = 1e-06
clip_limit = 10.0
momentum_rate = 0.9
learn_rate = 0.01
average_rate = 0.5
neg_large = -1e30
tanh_rate = 0.7978845608
tanh_cube = 0.044715
bf16 = jnp.bfloat16
f32 = jnp.float32
swap = ((0, 1), (1, 0))
chips = ("dz", "dy", "mx")


def dot(left, right, dims):
    return lax.dot_general(left, right, (dims, ((), ())), preferred_element_type=f32)


def head_lanes(block, head):
    lanes = lax.broadcasted_iota(jnp.int32, block.shape, 1)
    return jnp.where((lanes >= DK) == (head == 1), block, jnp.zeros_like(block))


def key_spans(rows, keys, start, size, causal):
    half = rows // 2
    reach = start % half + size
    return [(0, reach), (half, half + reach)] if causal and reach < half else [(0, keys)]


def total(parts):
    return functools.reduce(jnp.add, parts)


def attend_kernel(causal, size, q_ref, k_ref, v_ref, pq_ref, pk_ref, len_ref, o_ref, lse_ref, top_ref):
    rows, keys = q_ref.shape[0], k_ref.shape[0]
    tops = []
    for head in range(2):
        k, v = head_lanes(k_ref[...], head), head_lanes(v_ref[...], head)
        top = jnp.full((1, 1), neg_large, f32)
        for start in range(0, rows, size):
            r = slice(start, start + size)
            spans = key_spans(rows, keys, start, size, causal)
            q = q_ref[r, :]
            s = [dot(q, k[a:b], ((1,), (1,))) for a, b in spans]
            if causal:
                s = [jnp.where(pk_ref[:, a:b] <= pq_ref[r, :], t, neg_large) for t, (a, b) in zip(s, spans)]
            m = functools.reduce(jnp.maximum, [jnp.max(t, axis=1, keepdims=True) for t in s])
            if causal:
                real = jnp.where(pq_ref[r, :] < len_ref[0], m, neg_large)
                top = jnp.maximum(top, jnp.max(real, axis=0, keepdims=True))
            e = [jnp.exp(t - m) for t in s]
            mass = total([jnp.sum(t, axis=1, keepdims=True) for t in e])
            scale = 1.0 / mass
            mix = total([dot((t * scale).astype(bf16), v[a:b], ((1,), (0,))) for t, (a, b) in zip(e, spans)])
            if head == 0:
                o_ref[r, :] = mix.astype(bf16)
            else:
                o_ref[r, :] = (o_ref[r, :].astype(f32) + mix).astype(bf16)
            lse_ref[0, r, head : head + 1] = m + jnp.log(mass)
        tops.append(top)
    lanes = lax.broadcasted_iota(jnp.int32, (8, 128), 1)
    top_ref[0] = jnp.where(lanes == 0, tops[0], tops[1])


def attend_back_kernel(
    causal, size, q_ref, k_ref, v_ref, pq_ref, pk_ref, lse_ref, do_ref, dq_ref, dk_ref, dv_ref, dk_acc, dv_acc
):
    rows, keys = q_ref.shape[0], k_ref.shape[0]
    dk_acc[...] = jnp.zeros_like(dk_acc)
    dv_acc[...] = jnp.zeros_like(dv_acc)
    for head in range(2):
        k, v = head_lanes(k_ref[...], head), head_lanes(v_ref[...], head)
        own = slice(DK * head, DK * head + DK)
        for start in range(0, rows, size):
            r = slice(start, start + size)
            spans = key_spans(rows, keys, start, size, causal)
            q, do, lse = q_ref[r, :], do_ref[r, :], lse_ref[0, r, head : head + 1]
            soft, grad = [], []
            for a, b in spans:
                s = dot(q, k[a:b], ((1,), (1,)))
                if causal:
                    s = jnp.where(pk_ref[:, a:b] <= pq_ref[r, :], s, neg_large)
                soft.append(jnp.exp(s - lse))
                grad.append(dot(do, v[a:b], ((1,), (1,))))
            row_dot = total([jnp.sum(p * t, axis=1, keepdims=True) for p, t in zip(soft, grad)])
            q_t, do_t = q.T[own], do.T[own]
            parts = []
            for (a, b), p, t in zip(spans, soft, grad):
                ds = (p * (t - row_dot)).astype(bf16)
                parts.append(dot(ds, k[a:b], ((1,), (0,))))
                dv_acc[own, a:b] += dot(do_t, p.astype(bf16), ((1,), (0,)))
                dk_acc[own, a:b] += dot(q_t, ds, ((1,), (0,)))
            dq = total(parts)
            if head == 0:
                dq_ref[r, :] = dq.astype(bf16)
            else:
                dq_ref[r, :] = (dq_ref[r, :].astype(f32) + dq).astype(bf16)
    dk_ref[...] = dk_acc[...].T.astype(bf16)
    dv_ref[...] = dv_acc[...].T.astype(bf16)


def attend_cost(rows, keys, pairs, dots):
    return cost(0, 0)


def lane_pairs(count, first):
    return pl.BlockSpec((count, 2 * DK), lambda p: (0, first + p))


def attend(q, k, v, pos_col, pos_row, length, causal, size):
    rows, keys, pairs = q[0].shape[0], k[0].shape[0], q[2]
    mixed, lse, top = pl.pallas_call(
        functools.partial(attend_kernel, causal, size),
        grid=(pairs,),
        in_specs=[
            lane_pairs(rows, q[1]),
            lane_pairs(keys, k[1]),
            lane_pairs(keys, v[1]),
            pl.BlockSpec((rows, 1), lambda p: (0, 0)),
            pl.BlockSpec((1, keys), lambda p: (0, 0)),
            pl.BlockSpec(memory_space=pltpu.SMEM),
        ],
        out_specs=[
            lane_pairs(rows, 0),
            pl.BlockSpec((1, rows, 2), lambda p: (p, 0, 0)),
            pl.BlockSpec((1, 8, 128), lambda p: (p, 0, 0)),
        ],
        out_shape=[
            jax.ShapeDtypeStruct((rows, pairs * 2 * DK), bf16),
            jax.ShapeDtypeStruct((pairs, rows, 2), f32),
            jax.ShapeDtypeStruct((pairs, 8, 128), f32),
        ],
        cost_estimate=attend_cost(rows, keys, pairs, 2),
        name="attend",
    )(q[0], k[0], v[0], pos_col, pos_row, length)
    return mixed, lse, top[:, 0, :2].reshape(-1)


def attend_back(q, k, v, pos_col, pos_row, lse, grad, causal, size):
    rows, keys, pairs = q[0].shape[0], k[0].shape[0], q[2]
    return pl.pallas_call(
        functools.partial(attend_back_kernel, causal, size),
        grid=(pairs,),
        in_specs=[
            lane_pairs(rows, q[1]),
            lane_pairs(keys, k[1]),
            lane_pairs(keys, v[1]),
            pl.BlockSpec((rows, 1), lambda p: (0, 0)),
            pl.BlockSpec((1, keys), lambda p: (0, 0)),
            pl.BlockSpec((1, rows, 2), lambda p: (p, 0, 0)),
            lane_pairs(rows, 0),
        ],
        out_specs=[lane_pairs(rows, 0), lane_pairs(keys, 0), lane_pairs(keys, 0)],
        out_shape=[jax.ShapeDtypeStruct((n, pairs * 2 * DK), bf16) for n in (rows, keys, keys)],
        scratch_shapes=[pltpu.VMEM((2 * DK, keys), f32)] * 2,
        cost_estimate=attend_cost(rows, keys, pairs, 5),
        name="attend_back",
    )(q[0], k[0], v[0], pos_col, pos_row, lse, grad)


def apply_update(weight, grad_sum, moment, average, factor, grad_scale):
    grad_now = grad_sum * grad_scale
    moment_new = momentum_rate * moment + grad_now
    master_new = (weight - learn_rate * (grad_now + momentum_rate * moment_new)) * factor
    average_new = average_rate * average + (1.0 - average_rate) * master_new
    return (grad_now, moment_new, average_new, master_new)


def flat_columns(block):
    return jnp.swapaxes(block, 0, 1).reshape(block.shape[1], -1)


def row_major(values):
    return with_layout_constraint(values, Layout(major_to_minor=tuple(range(values.ndim))))


spec = pl.BlockSpec


def cost(flops, moved):
    return pl.CostEstimate(flops=1, bytes_accessed=1, transcendentals=0)


def reorder(parts, block, dy, to_own, keep=None):
    arrays = halves(parts)
    rows, width = arrays[0].shape[0], D
    steps = width // block // 2
    extra = [] if keep is None else [keep]
    if block % 128:
        value = total([(jnp.concatenate(p, axis=1) if isinstance(p, (list, tuple)) else p).astype(f32) for p in parts])
        value = value * (1.0 if keep is None else keep)
        axis = 2 if to_own else 1
        value = value.reshape((rows, steps, 2, block) if to_own else (rows, 2, steps, block))
        low, high = (lax.index_in_dim(value, n, axis, keepdims=False) for n in range(2))
        pair = jnp.where(dy == 0, low, high), jnp.where(dy == 0, high, low)
        return jnp.stack(pair, axis=3 - axis).reshape(rows, width).astype(bf16)

    def source(j, flag):
        if to_own:
            return j % steps * 2 + (j // steps + flag) % 2
        return j // 2 + (j % 2 + flag) % 2 * steps

    def kernel(flag_ref, *refs):
        out = refs[-1]
        whole = len(arrays) == 1
        value = refs[0] if whole else read_total(parts, refs[: len(arrays)])
        for j in range(2 * steps):
            spans = [slice(source(j, flag) * block, (source(j, flag) + 1) * block) for flag in range(2)]
            picked = jnp.where(flag_ref[0] == 0, value[:, spans[0]], value[:, spans[1]])
            if extra:
                picked = picked.astype(f32) * refs[len(arrays)][...]
            out[:, j * block : (j + 1) * block] = picked.astype(bf16)

    return pl.pallas_call(
        kernel,
        grid=(4,),
        in_specs=[
            spec(memory_space=pltpu.SMEM),
            *[by_rows(p, rows // 4) for p in [*arrays, *extra]],
        ],
        out_specs=spec((rows // 4, width), lambda i: (i, 0)),
        out_shape=jax.ShapeDtypeStruct((rows, width), bf16),
        cost_estimate=cost(0, rows * width * 4),
        name="reorder",
    )(dy[None], *arrays, *extra)


def weight_specs(weights):
    specs, arrays = [], []
    for own, other, width, place in weights:
        specs += [spec((own.shape[0], width), lambda i, place=place: (0, place))] * 2
        arrays += [own, other]
    return specs, arrays


def project(rows, weights, mode="plain", scales=()):
    own, other = rows
    half, size = own.shape[0], own.shape[0] // 2
    specs, arrays = weight_specs(weights)
    widths = [w[2] for w in weights]
    count = len(weights)
    out_widths = {"plain": widths, "gelu": widths[:1] * 3, "scale": [w for w in widths for _ in range(2)]}[mode]

    def kernel(own_ref, other_ref, *refs):
        here = pl.program_id(0) < 2
        x = jnp.where(here, own_ref[...], other_ref[...])
        split = x.shape[1] // 2
        made = []
        for j in range(count):
            low, high = refs[2 * j], refs[2 * j + 1]
            made.append(
                dot(x[:, :split], low[...], ((1,), (0,))) + dot(x[:, split:], high[...], ((1,), (0,)))
            )
        outs = refs[2 * count + len(scales) :]
        if mode == "plain":
            for out, value in zip(outs, made):
                out[...] = value.astype(bf16)
        elif mode == "gelu":
            gate, up = made
            square = gate * gate
            bend = jnp.tanh(tanh_rate * gate * (1.0 + tanh_cube * square))
            rise = 0.5 * (1.0 + bend)
            value = gate * rise
            slope = rise + 0.5 * gate * (1.0 - bend * bend) * tanh_rate * (1.0 + 3.0 * tanh_cube * square)
            outs[0][...] = (value * up).astype(bf16)
            outs[1][...] = (slope * up).astype(bf16)
            outs[2][...] = value.astype(bf16)
        else:
            for j, out in enumerate(outs):
                out[...] = (made[j // 2] * refs[2 * count + j][...].astype(f32)).astype(bf16)

    by_rows = lambda width: spec((size, width), lambda i: (i, 0))
    width_all = own.shape[1]
    return pl.pallas_call(
        kernel,
        grid=(4,),
        in_specs=[
            spec((size, width_all), lambda i: (jnp.minimum(i, 1), 0)),
            spec((size, width_all), lambda i: (jnp.maximum(i - 2, 0), 0)),
            *specs,
            *[by_rows(t.shape[1]) for t in scales],
        ],
        out_specs=[by_rows(w) for w in out_widths],
        out_shape=[jax.ShapeDtypeStruct((2 * half, w), bf16) for w in out_widths],
        cost_estimate=cost(4 * half * width_all * sum(widths), half * width_all * 4 + width_all * sum(widths) * 2),
        name="project_" + mode,
    )(own, other, *arrays, *scales)


def combine(values, weights, which):
    specs, arrays = weight_specs(weights)
    half = values[0].shape[0] // 2
    size = half // 2
    count = len(values)
    depth = weights[0][0].shape[0]

    def kernel(*refs):
        for side in range(2):
            parts = [
                dot(refs[j][...], refs[count + 2 * j + side][...], ((1,), (1,))) for j in range(count)
            ]
            refs[side - 2][...] = total(parts)

    return pl.pallas_call(
        kernel,
        grid=(2,),
        in_specs=[spec((size, v.shape[1]), lambda i: (2 * which + i, 0)) for v in values] + specs,
        out_specs=[spec((size, depth), lambda i: (i, 0))] * 2,
        out_shape=[jax.ShapeDtypeStruct((half, depth), f32)] * 2,
        cost_estimate=cost(0, 0),
        name="combine",
    )(*values, *arrays)


def weight_grad(items, part, arrived=()):
    sources = []
    for rows, _ in items:
        if not any(rows is t for t in sources):
            sources.append(rows)
    half, width = sources[0][0].shape
    size = width // 2
    steps, base = (2, 0) if part is None else (1, part)
    spans, last = [], 0
    for _, value in items:
        spans.append((last, last + value.shape[1]))
        last = spans[-1][1]
    first = len(sources) * 2

    def kernel(*refs):
        out = refs[-1]
        for (rows, _), value, (a, b) in zip(items, refs[first:], spans):
            place = [rows is t for t in sources].index(True)
            own, other = refs[2 * place], refs[2 * place + 1]
            made = dot(own[...], value[:half], ((0,), (0,))) + dot(other[...], value[half:], ((0,), (0,)))
            for (array, _, start), came in zip(arrived, refs[first + len(items) :]):
                if start <= a < start + array.shape[1]:
                    made = made + came[:, a - start : b - start].astype(f32)
            out[:, a:b] = made.astype(bf16)

    columns = spec((half, size), lambda i: (0, base + i))
    return pl.pallas_call(
        kernel,
        grid=(steps,),
        in_specs=[columns] * first
        + [spec(v.shape, lambda i: (0, 0)) for _, v in items]
        + [spec((size, a.shape[1]), lambda i, place=place: (place + i, 0)) for a, place, _ in arrived],
        out_specs=spec((size, last), lambda i: (i, 0)),
        out_shape=jax.ShapeDtypeStruct((steps * size, last), bf16),
        cost_estimate=cost(4 * half * steps * size * last, half * width * 4 + half * 4 * last),
        name="weight_grad",
    )(*[t for pair in sources for t in pair], *[v for _, v in items], *[a for a, _, _ in arrived])


def halves(parts):
    return [t for p in parts for t in (p if isinstance(p, (list, tuple)) else [p])]


def read_total(parts, refs):
    refs, read = list(refs), []
    for p in parts:
        if isinstance(p, (list, tuple)):
            read.append(jnp.concatenate([refs.pop(0)[...] for _ in p], axis=1))
        else:
            read.append(refs.pop(0)[...])
    return total([r.astype(f32) for r in read])


def by_rows(array, size=256):
    if array.shape[0] == 1:
        return spec(array.shape, lambda i: (0, 0))
    return spec((size, array.shape[1]), lambda i: (i, 0))


def add_norm(parts, gain_row):
    arrays = halves(parts)
    rows, width = arrays[0].shape[0], D

    def kernel(gain_ref, *refs):
        hidden = read_total(parts, refs[: len(arrays)])
        scale = lax.rsqrt(jnp.mean(hidden * hidden, axis=-1, keepdims=True) + epsilon)
        refs[-1][...] = (hidden * scale * gain_ref[...]).astype(bf16)
        if len(parts) > 1:
            refs[-2][...] = hidden

    kinds = [f32, bf16] if len(parts) > 1 else [bf16]
    shapes = [jax.ShapeDtypeStruct((rows, width), k) for k in kinds]
    return pl.pallas_call(
        kernel,
        grid=(rows // 256,),
        in_specs=[by_rows(gain_row), *[by_rows(p) for p in arrays]],
        out_specs=[by_rows(t) for t in shapes],
        out_shape=shapes,
        cost_estimate=cost(rows * width * 8, rows * width * 14),
        name="add_norm",
    )(gain_row, *arrays)


def norm_back(hidden, gain_row, grads, base):
    rows, width = hidden.shape
    arrays = halves(grads)

    def kernel(gain_ref, hidden_ref, base_ref, *refs):
        grad = read_total(grads, refs[: len(arrays)])
        out, low, gain_grad = refs[len(arrays) :]
        hidden = hidden_ref[...].astype(f32)
        scale = lax.rsqrt(jnp.mean(hidden * hidden, axis=-1, keepdims=True) + epsilon)
        z = hidden * scale
        grad_z = grad * gain_ref[...]
        grad_hidden = scale * (grad_z - z * jnp.mean(grad_z * z, axis=-1, keepdims=True))
        value = base_ref[...].astype(f32) + grad_hidden
        out[...] = value
        low[...] = value.astype(bf16)

        @pl.when(pl.program_id(0) == 0)
        def _():
            gain_grad[...] = jnp.zeros_like(gain_grad)

        gain_grad[...] += jnp.sum(grad * z, axis=0, keepdims=True)

    shapes = [jax.ShapeDtypeStruct((rows, width), f32), jax.ShapeDtypeStruct((rows, width), bf16)]
    return pl.pallas_call(
        kernel,
        grid=(rows // 256,),
        in_specs=[by_rows(gain_row), by_rows(hidden), by_rows(base), *[by_rows(g) for g in arrays]],
        out_specs=[*[by_rows(t) for t in shapes], spec((1, width), lambda i: (0, 0))],
        out_shape=[*shapes, jax.ShapeDtypeStruct((1, width), f32)],
        cost_estimate=cost(rows * width * 16, rows * width * 22),
        name="norm_back",
    )(gain_row, hidden, base, *arrays)


def after(value, *others):
    return lax.optimization_barrier((value, *others))[0]


def swap_cores(values):
    return lax.ppermute(values, "mc", swap)


def swap_x(values):
    return row_major(lax.ppermute(row_major(values), "mx", swap))


def swap_y(values):
    return row_major(lax.ppermute(row_major(values), "dy", swap))


def gather_part(local):
    return row_major(lax.all_gather(row_major(local), "dz", axis=0, tiled=True))


def spread(part, x_last):
    if x_last:
        high = swap_y(part)
        return (part, high), (swap_x(part), swap_x(high))
    beside = swap_x(part)
    return (part, swap_y(part)), (beside, swap_y(beside))


class Group:
    def __init__(self, x_items, y_items):
        self.own = [(r, v) for r, v, _ in (*x_items, *y_items)]
        self.own_x, self.own_y = self.own[: len(x_items)], self.own[len(x_items) :]
        self.other_x, self.other_y = ([(r, v) for r, _, v in items] for items in (x_items, y_items))

    def first(self):
        self.sent = [weight_grad(self.other_x, None), weight_grad([*self.own_y, *self.other_y], 1)]
        self.from_x, self.from_y = swap_x(self.sent[0]), swap_y(self.sent[1])
        return self.sent

    def second(self, *deps):
        self.from_x, self.from_y = after(self.from_x, *deps), after(self.from_y, *deps)
        wide_y = self.from_y.shape[1] // 2
        self.sent = [
            weight_grad(self.own_x, 1, [(self.from_x, 1, 0)]),
            weight_grad(self.other_y, 0, [(self.from_y, 0, -wide_y)]),
        ]
        self.late_y, self.late_x = swap_y(self.sent[0]), swap_x(self.sent[1])
        return self.sent

    def third(self, *deps, behind=()):
        wide_x = self.from_x.shape[1]
        late_y, late_x = after(self.late_y, *deps), after(self.late_x, *deps)
        summed = weight_grad(
            self.own, 0, [(self.from_x, 0, 0), (late_y, 0, 0), (self.from_y, 0, wide_x), (late_x, 0, wide_x)]
        )
        self.sent = [summed]
        summed = after(summed, *behind) if behind else summed
        summed = lax.psum_scatter(row_major(summed), "dz", scatter_dimension=0, tiled=True)
        self.result = summed.astype(f32)
        return self.sent


def on_device(
    tokens,
    encoder,
    cotangent,
    lengths,
    deal,
    attn_in,
    attn_out,
    ff_in,
    ff_out,
    gains,
    mom_attn_in,
    mom_attn_out,
    mom_ff_in,
    mom_ff_out,
    mom_gains,
    avg_attn_in,
    avg_attn_out,
    avg_ff_in,
    avg_ff_out,
    avg_gains,
):
    seq_count, block_rows = tokens.shape[0], tokens.shape[1]
    core = lax.axis_index("mc")
    dy = lax.axis_index("dy")
    chip = lax.axis_index(chips)
    own_rows = block_rows * seq_count
    slot_len = 2 * own_rows
    heads_cols = attn_in.shape[2]
    hidden = ff_in.shape[2]
    model_rows = attn_in.shape[1]

    def exchange(values):
        return lax.all_to_all(values, chips, split_axis=0, concat_axis=0, tiled=True)

    def to_chips(values):
        return exchange(values).reshape(own_rows, D)

    def from_chips(rows):
        return exchange(rows.reshape(seq_count, block_rows, D))

    seq_len = lengths[deal[chip]]
    row_ids = jnp.arange(own_rows, dtype=jnp.int32)
    lane = row_ids % block_rows
    pos_own = (row_ids // block_rows * 2 + core) * block_rows + lane
    pos_other = (row_ids // block_rows * 2 + 1 - core) * block_rows + lane
    pos = jnp.concatenate([pos_own, pos_other])
    places = (pos[:, None], pos[None, :])
    length = seq_len[None]
    valid_own = (pos_own < seq_len).astype(f32)[:, None]

    hc = heads_cols
    pairs = hc // (2 * DK)
    spare = -hidden % 256
    deep = hidden + spare
    widen = lambda t: jnp.pad(t.astype(bf16), ((0, 0), (0, spare)))
    out_t = jnp.swapaxes(attn_out.astype(bf16), 1, 2)
    low_in = attn_in.astype(bf16)
    pad = jnp.zeros((model_rows, 125), bf16)
    chunk_a = jnp.concatenate([*low_in[0:3], out_t[0], gains.astype(bf16).T, pad], axis=1)
    chunk_b = jnp.concatenate([*low_in[3:6], out_t[1]], axis=1)
    chunk_c = jnp.concatenate([widen(ff_in[0]), widen(ff_in[1]), widen(ff_out.T)], axis=1)

    tok_own = to_chips(tokens)
    part_a, part_b, part_c = (gather_part(t) for t in (chunk_a, chunk_b, chunk_c))
    got_a = spread(part_a, True)
    enc_own = to_chips(after(encoder, part_c))
    got_b = spread(part_b, False)
    cot_own = to_chips(cotangent)

    gain_f = jnp.concatenate([g[:, 4 * hc : 4 * hc + 3] for g in got_a[0]]).astype(f32).T
    gain_rows = [gain_f[n : n + 1] for n in range(3)]
    w_qkv = [(*g, 3 * hc, 0) for g in got_a]
    w_q, w_k, w_v, w_ot = ([(*g, hc, n) for g in got_a] for n in range(4))
    w_cq, w_ck, w_cv, w_cot = ([(*g, hc, n) for g in got_b] for n in range(4))

    def both(own):
        return own, swap_cores(own)

    def over_cores(values, weights):
        away = [swap_cores(t) for t in combine(values, weights, 1)]
        return combine(values, weights, 0), away

    x_own = reorder([after(tok_own, chunk_b, chunk_c)], model_rows, dy, True)
    norm_one = both(add_norm([x_own], gain_rows[0])[0])
    norm_one = after(norm_one[0], part_b), norm_one[1]
    qkv = [project(norm_one, [w_qkv[0]])[0]]
    qkv += project((after(norm_one[0], got_b[0][1], got_b[1][0]), norm_one[1]), [w_qkv[1]])
    self_qkv = [[(t, n * pairs, pairs) for n in range(3)] for t in qkv]
    got_c = spread(after(part_c, qkv[1]), True)
    w_g, w_u, w_dt = ([(*g, deep, n) for g in got_c] for n in range(3))
    self_qkv[1][0] = (after(qkv[1], got_b[1][1]), *self_qkv[1][0][1:])
    self_out = [attend(*t, *places, length, True, 256) for t in self_qkv]
    self_mixed = [self_out[0][0], after(self_out[1][0], part_c)]
    hidden_one, norm_two = add_norm([x_own, *over_cores(self_mixed, w_ot)], gain_rows[1])
    norm_two = both(norm_two)
    e_own = reorder([enc_own], model_rows, dy, True)
    enc_rows = both(e_own)
    cross_kv = project(enc_rows, [*w_ck, *w_cv])
    cross_q = project(norm_two, w_cq)
    cross_qkv = [
        [(t, 0, pairs) for t in (cross_q[n], cross_kv[n], cross_kv[2 + n])] for n in range(2)
    ]
    cross_qkv[1][0] = (after(cross_q[1], cross_q[0], got_c[0][1], got_c[1][0]), 0, pairs)
    cross_out = [attend(*t, *places, length, False, 512) for t in cross_qkv]
    cross_mixed = [o[0] for o in cross_out]
    hidden_two, norm_three = add_norm(
        [hidden_one, *over_cores(cross_mixed, w_cot)], gain_rows[2]
    )
    norm_three = both(norm_three)
    dy_own = reorder([cot_own], model_rows, dy, True, valid_own)
    grad_out = both(dy_own)
    inner, slope, value = zip(*[project(norm_three, list(w), "gelu") for w in zip(w_g, w_u)])

    scales = [t for pair in zip(slope, value) for t in pair]
    grad_gu = project(grad_out, w_dt, "scale", scales)
    grad_gate, grad_up = grad_gu[::2], grad_gu[1::2]
    group_c = Group([(norm_three, *grad_gate), (grad_out, *inner)], [(norm_three, *grad_up)])
    sent = group_c.first()
    parts = over_cores([after(grad_gate[0], *sent), grad_gate[1], *grad_up], [*w_g, *w_u])
    grad_two, low_two, gain_three = norm_back(hidden_two, gain_rows[2], parts, dy_own)
    grad_co = both(low_two)
    out_parts = over_cores([after(inner[0], low_two), inner[1]], w_dt)
    grad_ca = project((after(grad_co[0], out_parts[0][0]), grad_co[1]), w_cot)
    out_block = reorder([after(hidden_two, *grad_ca), *out_parts], model_rows, dy, False, valid_own)
    block_output = from_chips(out_block)
    cross_qkv[0][0] = (after(cross_q[0], out_block), 0, pairs)
    cross_back = [
        attend_back(*t, *places, o[1], d, False, 512) for t, o, d in zip(cross_qkv, cross_out, grad_ca)
    ]
    grad_cq, grad_ck, grad_cv = zip(*cross_back)
    group_b = Group(
        [(norm_two, *grad_cq), (grad_co, *[o[0] for o in cross_out])],
        [(enc_rows, *grad_ck), (enc_rows, *grad_cv)],
    )
    parts = over_cores(grad_cq, w_cq)
    sent = group_b.first()
    parts_enc = over_cores([after(grad_ck[0], *sent), grad_ck[1], *grad_cv], [*w_ck, *w_cv])
    grad_one, low_one, gain_two = norm_back(
        hidden_one, gain_rows[1], [parts[0], [after(parts[1][0], parts_enc[0][0]), parts[1][1]]], grad_two
    )
    grad_o = both(low_one)
    out_enc = reorder([parts_enc[0], [after(parts_enc[1][0], low_one), parts_enc[1][1]]], model_rows, dy, False)
    grad_encoder = from_chips(out_enc)
    sent = group_c.second(out_enc)
    grad_a = project((after(grad_o[0], *sent, block_output), grad_o[1]), w_ot)
    self_back = [attend_back(*self_qkv[0], *places, self_out[0][1], grad_a[0], True, 256)]
    sent = group_c.third(*self_back[0])
    self_back.append(attend_back(*self_qkv[1], *places, self_out[1][1], after(grad_a[1], *sent), True, 256))
    sent = group_b.second(*self_back[1])
    grad_q, grad_k, grad_v = zip(*self_back)
    group_a = Group(
        [(norm_one, *grad_q), (grad_o, *[o[0] for o in self_out])],
        [(norm_one, *grad_k), (norm_one, *grad_v)],
    )
    sent = group_a.first()
    parts = over_cores(
        [after(grad_q[0], *sent, *group_b.sent, grad_encoder), grad_q[1], *grad_k, *grad_v], [*w_q, *w_k, *w_v]
    )
    sent = group_b.third(*parts[0], behind=[group_c.result])
    _, low_tok, gain_one = norm_back(
        x_own, gain_rows[0], [[after(parts[0][0], *sent), parts[0][1]], parts[1]], grad_one
    )
    group_a.second(low_tok)
    out_tok = reorder([after(low_tok, *group_a.sent)], model_rows, dy, False)
    grad_tokens = from_chips(out_tok)
    group_a.third(out_tok, behind=[group_b.result])
    sum_a, sum_b, sum_c = group_a.result, group_b.result, group_c.result

    dp_count = seq_count // 2
    gain_part = jnp.concatenate([gain_one, gain_two, gain_three])
    gain_part = gain_part + swap_cores(gain_part)
    low, high = (gain_part[:, n * D // 2 : (n + 1) * D // 2].reshape(3, dp_count // 2, model_rows) for n in range(2))
    gain_part = jnp.stack([jnp.where(dy == 0, low, high), jnp.where(dy == 0, high, low)], axis=2)
    gain_part = jnp.swapaxes(gain_part.reshape(3, dp_count, model_rows), 0, 1)
    mx = lax.axis_index("mx")
    tops = [jnp.where(mx == n, self_out[0][2], self_out[1][2]) for n in range(2)]
    tops = jnp.broadcast_to(jnp.stack(tops)[None], (dp_count, 2, hc // DK))
    small = jnp.concatenate(
        [jnp.repeat(gain_part, 2, axis=0).reshape(dp_count * 2, -1), tops.reshape(dp_count * 2, -1)], axis=1
    )
    small = exchange(small)
    red_gain = jnp.sum(small[:, : 3 * model_rows], axis=0).reshape(3, model_rows)
    head_peak = jnp.max(small[:, 3 * model_rows :], axis=0)

    cut = lambda t, n: t[:, n * hc : (n + 1) * hc]
    red_in = jnp.stack([cut(t, n) for t in (sum_a, sum_b) for n in (0, 2, 3)])
    red_out = jnp.stack([cut(sum_a, 1).T, cut(sum_b, 1).T])
    red_ff = jnp.stack([sum_c[:, n * deep : n * deep + hidden] for n in (0, 2)])
    red_out = with_layout_constraint(red_out, Layout(major_to_minor=(0, 1, 2)))
    red_ff = with_layout_constraint(red_ff, Layout(major_to_minor=(0, 2, 1)))
    red_down = with_layout_constraint(sum_c[:, deep : deep + hidden].T, Layout(major_to_minor=(0, 1)))
    clip_factors = clip_limit / jnp.maximum(head_peak, clip_limit)
    column = jnp.repeat(jnp.sqrt(clip_factors), DK)
    factor = jnp.where((jnp.arange(6) < 2)[:, None, None], column[None, None, :], 1.0)
    grad_scale = float(seq_count * slot_len) ** (-0.5)
    up_a = apply_update(attn_in, red_in, mom_attn_in, avg_attn_in, factor, grad_scale)
    up_b = apply_update(attn_out, red_out, mom_attn_out, avg_attn_out, 1.0, grad_scale)
    up_c = apply_update(ff_in, red_ff, mom_ff_in, avg_ff_in, 1.0, grad_scale)
    up_d = apply_update(ff_out, red_down, mom_ff_out, avg_ff_out, 1.0, grad_scale)
    up_e = apply_update(gains, red_gain, mom_gains, avg_gains, 1.0, grad_scale)
    return (
        block_output.astype(f32),
        grad_tokens.astype(f32),
        grad_encoder.astype(f32),
        *up_a,
        *up_b,
        *up_c,
        *up_d,
        *up_e,
        head_peak,
        clip_factors,
    )


def solution(mesh):
    dp, mp = mesh.shape["dp"], mesh.shape["mp"]
    fine = Mesh(mesh.devices.reshape(dp // 2, 2, mp // 2, 2), ("dz", "dy", "mx", "mc"))
    dp_axes, mp_axes = ("dz", "dy"), ("mx", "mc")
    rows = P(None, (*dp_axes, *mp_axes), None)
    wide = P(None, dp_axes, mp_axes)
    tall = P(None, mp_axes, dp_axes)
    down = P(mp_axes, dp_axes)
    gain = P(None, dp_axes)
    state = (wide, tall, wide, down, gain)
    in_specs = (rows, rows, rows, P(), P(), *state, *state, *state)
    out_specs = (
        rows,
        rows,
        rows,
        *[wide] * 4,
        *[tall] * 4,
        *[wide] * 4,
        *[down] * 4,
        *[gain] * 4,
        P(mp_axes),
        P(mp_axes),
    )
    return jax.shard_map(
        on_device, mesh=fine, in_specs=in_specs, out_specs=out_specs, check_vma=False
    )
```

time: 987 us -> 730 us (0.74)
  Pallas kernels: 0 us -> 344 us
  matrix products: 311 us -> 0 us
  other arithmetic: 148 us -> 20.3 us
  blocking collectives: 93.6 us -> 0 us
  waiting for transfers between devices: 290 us -> 207 us
  starting transfers between devices: 44.2 us -> 97.2 us
  local copies, waits for them, and re-layouts: 72.8 us -> 39.4 us
    pallas_call x0 -> x58, Pallas kernels: none -> 344 us  [the longest x15 74 us: weight_grad(): pl.pallas_call(kernel, grid=(steps,), in_specs=[columns] * first + [spec(...]
    dot_general x66 -> x0, matrix products: 311 us -> none  [the longest x4 60.3 us: attend_back(): jnp.einsum('qhe,khe->hqk', grad_h, values_h, preferred_element_type=f32)]
    all_to_all x5 -> x7, waiting for transfers between devices: 65.6 us -> 0.02 us  [exchange(): lax.all_to_all(values, chips, split_axis=0, concat_axis=0, tiled=True)]
    pmax x1 -> x0, blocking collectives: 57.6 us -> none  [on_device(): lax.pmax(head_rows, chips)]
    convert_element_type x15 -> x9, other arithmetic: 65.2 us -> 8.2 us  [the longest x1 2.91 us: on_device(): grad_tokens.astype(f32)]
    ppermute x22 -> x43, waiting for transfers between devices: 139 us -> 96.7 us  [the longest x11 62.3 us: swap_x(): return row_major(lax.ppermute(row_major(values), 'mx', swap))]
    reduce_sum x9 -> x1, other arithmetic: 34.1 us -> 0.02 us  [on_device(): red_gain = jnp.sum(small[:, :3 * model_rows], axis=0).reshape(3, model_rows)]
    all_to_all x1 -> x0, blocking collectives: 30 us -> none  [to_chips(): lax.all_to_all(values, chips, split_axis=0, concat_axis=1, tiled=True)]
  transfers between devices with their start and end apart: 36 -> 56, of which waited for: 17 -> 16; matrix products, arithmetic and copies ran while one was open for 43% -> 4% of each run, Pallas kernels for 0% -> 42%
where the time goes in v2:
time: 730 us; the launch traced here: 725 us
  Pallas kernels  344 us (47%)
  waiting for transfers between devices  207 us (28%)
  starting transfers between devices  97.2 us (13%)
  local copies, waits for them, and re-layouts  39.4 us (5%)
  other arithmetic  20.3 us (3%)
  between operations  17.2 us (2%)
    all_gather x3, waiting for transfers between devices, gather_part(): return row_major(lax.all_gather(row_major(local), 'dz', axis=0, tiled=True))  95.6 us
    pallas_call x15, Pallas kernels, weight_grad(): pl.pallas_call(kernel, grid=(steps,), in_specs=[columns] * first + [spec(...  74 us
    pallas_call x14, Pallas kernels, combine(): pl.pallas_call(kernel, grid=(2,), in_specs=[spec((size, v.shape[1]), lamb...  64.3 us
    ppermute x11, waiting for transfers between devices, swap_x(): return row_major(lax.ppermute(row_major(values), 'mx', swap))  62.3 us
    all_to_all x7, starting transfers between devices, exchange(): lax.all_to_all(values, chips, split_axis=0, concat_axis=0, tiled=True)  59.3 us
    pallas_call x4, Pallas kernels, attend_back(): pl.pallas_call(functools.partial(attend_back_kernel, causal, size), grid=...  58.1 us
    pallas_call x9, Pallas kernels, project(): pl.pallas_call(kernel, grid=(4,), in_specs=[spec((size, width_all), lambd...  56.1 us
    pallas_call x4, Pallas kernels, attend(): pl.pallas_call(functools.partial(attend_kernel, causal, size), grid=(pair...  43.3 us
  transfers between devices with their start and end apart: 56, of which 16 were waited for; matrix products, arithmetic and copies ran while one was open for 4% of the time, Pallas kernels for 42%

profile of v2, /device:TPU:0, one launch (start us, length us, event | category | flops | bytes accessed | tf_op | source)
XLA Modules:
  0.0 725.1 jit_solution(2491880937612661371)
XLA Ops:
  12.8 8.3 %all-to-all-start = ((bf16[16,32,1024]{2,1,0:T(8,128)(2,1)}), bf16[16,32,1024]{2,1,0:T(8,128)(2,1)S(1)}, u32[]{:S(2)}, u32[]{:S(2)}) async-start(bf16[16,32,1024]{2,1,0:T(8,128)(2,1)} %param.20), calls=%async_computation | async-start | bytes 2097152 | tf_op jit(solution)/shard_map/all_to_all | solution.py:540
  21.1 43.8 %all-gather.4.cloned.1.call-done.refs_0_.refs_2_.refs_6_.refs_10_.refs_14_ = bf16[512,1152]{1,0:T(8,128)(2,1)} async-done(((bf16[128,1152]{1,0:T(8,128)(2,1)}), bf16[512,1152]{1,0:T(8,128)(2,1)}) %all-gather.4.cloned.1.call-update) | async-done | bytes 1179664 | tf_op jit(solution)/shard_map/all_gather | solution.py:462
  66.3 27.5 %all-gather.6.cloned.1.call-done.refs_0_.refs_4_.refs_2_.refs_8_ = bf16[512,1024]{1,0:T(8,128)(2,1)} async-done(((bf16[128,1024]{1,0:T(8,128)(2,1)}), bf16[512,1024]{1,0:T(8,128)(2,1)}) %all-gather.6.cloned.1.call-update) | async-done | bytes 1048592 | tf_op jit(solution)/shard_map/all_gather | solution.py:462
  108.2 11.9 %collective-permute-done.3.refs_2_.refs_6_.refs_4_.refs_10_ = bf16[512,1024]{1,0:T(8,128)(2,1)S(1)} collective-permute-done((bf16[512,1024]{1,0:T(8,128)(2,1)}, bf16[512,1024]{1,0:T(8,128)(2,1)S(1)}, u32[]{:S(2)}, u32[]{:S(2)}) %collective-permute-start.3) | collective-permute-done | bytes 1048608 | tf_op jit(solution)/shard_map/ppermute | solution.py:454
  121.6 24.4 %all-gather.8.cloned.1.call-done.refs_0_.refs_2_.refs_4_.refs_8_ = bf16[512,2304]{1,0:T(8,128)(2,1)} async-done(((bf16[128,2304]{1,0:T(8,128)(2,1)}), bf16[512,2304]{1,0:T(8,128)(2,1)}) %all-gather.8.cloned.1.call-update) | async-done | bytes 2359312 | tf_op jit(solution)/shard_map/all_gather | solution.py:462
  150.7 28.5 %collective-permute-done.5.refs_1_.refs_5_.refs_3_.refs_9_.refs_13_.refs_17_ = bf16[512,1152]{1,0:T(8,128)(2,1)} collective-permute-done((bf16[512,1152]{1,0:T(8,128)(2,1)}, bf16[512,1152]{1,0:T(8,128)(2,1)}, u32[]{:S(2)}, u32[]{:S(2)}) %collective-permute-start.5) | collective-permute-done | bytes 1179680 | tf_op jit(solution)/shard_map/ppermute | solution.py:454
  179.2 5.4 project_plain.7.q_ref.k_ref.v_ref
  191.8 5.4 project_plain.6.q_ref.k_ref.v_ref
  197.2 11.7 %attend.4 = (bf16[1024,256]{1,0:T(8,128)(2,1)}, f32[2,1024,2]{2,1,0:T(8,128)}, f32[2,8,128]{2,1,0:T(8,128)}) custom-call(bf16[1024,768]{1,0:T(8,128)(2,1)} %project_plain.6.q_ref.k_ref.v_ref, bf16[1024,768]{1,0:T(8,128)(2,1)} %project_plain.6.q_ref.k_ref.v_ref, bf16[1024,768]{1,0:T(8,128)(2,1)} %project_plain.6.q_ref.k_ref.v_ref, s32[1024,1]{1,0:T(8,128)} %copy.123.pq_ref, ...), custom_call_target="tpu_custom_call" | custom-call | flops 1 | bytes 1 | tf_op jit(solution)/shard_map/attend/pallas_call | solution.py:125
  208.9 11.7 %attend.5 = (bf16[1024,256]{1,0:T(8,128)(2,1)}, f32[2,1024,2]{2,1,0:T(8,128)}, f32[2,8,128]{2,1,0:T(8,128)}) custom-call(bf16[1024,768]{1,0:T(8,128)(2,1)} %project_plain.7.q_ref.k_ref.v_ref, bf16[1024,768]{1,0:T(8,128)(2,1)} %project_plain.7.q_ref.k_ref.v_ref, bf16[1024,768]{1,0:T(8,128)(2,1)} %project_plain.7.q_ref.k_ref.v_ref, s32[1024,1]{1,0:T(8,128)} %copy.123.pq_ref, ...), custom_call_target="tpu_custom_call" | custom-call | flops 1 | bytes 1 | tf_op jit(solution)/shard_map/attend/pallas_call | solution.py:125
  243.0 4.9 project_plain.8
  248.8 5.9 project_plain.9
  254.8 9.9 %attend.6 = (bf16[1024,256]{1,0:T(8,128)(2,1)}, f32[2,1024,2]{2,1,0:T(8,128)}, f32[2,8,128]{2,1,0:T(8,128)}) custom-call(bf16[1024,256]{1,0:T(8,128)(2,1)} %get-tuple-element.198.q_ref, bf16[1024,256]{1,0:T(8,128)(2,1)} %get-tuple-element.157.k_ref, bf16[1024,256]{1,0:T(8,128)(2,1)} %get-tuple-element.158.v_ref, s32[1024,1]{1,0:T(8,128)} %copy.123.pq_ref, ...), custom_call_target="tpu_custom_call" | custom-call | flops 1 | bytes 1 | tf_op jit(solution)/shard_map/attend/pallas_call | solution.py:125
  264.7 10.0 %attend.7 = (bf16[1024,256]{1,0:T(8,128)(2,1)}, f32[2,1024,2]{2,1,0:T(8,128)}, f32[2,8,128]{2,1,0:T(8,128)}) custom-call(bf16[1024,256]{1,0:T(8,128)(2,1)} %get-tuple-element.162.q_ref, bf16[1024,256]{1,0:T(8,128)(2,1)} %get-tuple-element.163.k_ref, bf16[1024,256]{1,0:T(8,128)(2,1)} %get-tuple-element.164.v_ref, s32[1024,1]{1,0:T(8,128)} %copy.123.pq_ref, ...), custom_call_target="tpu_custom_call" | custom-call | flops 1 | bytes 1 | tf_op jit(solution)/shard_map/attend/pallas_call | solution.py:125
  293.6 7.9 %project_gelu.2 = (bf16[1024,768]{1,0:T(8,128)(2,1)}, bf16[1024,768]{1,0:T(8,128)(2,1)}, bf16[1024,768]{1,0:T(8,128)(2,1)}) custom-call(bf16[512,1024]{1,0:T(8,128)(2,1)} %get-tuple-element.171.own_ref.refs_0_, bf16[512,1024]{1,0:T(8,128)(2,1)} %copy-done.2, bf16[512,2304]{1,0:T(8,128)(2,1)} %all-gather.8.cloned.1.call-done.refs_0_.refs_2_.refs_4_.refs_8_, ...), custom_call_target="tpu_custom_call" | custom-call | flops 1 | bytes 1 | tf_op jit(solution)/shard_map/project_gelu/pallas_call | solution.py:287
  305.6 8.3 %project_gelu.3 = (bf16[1024,768]{1,0:T(8,128)(2,1)}, bf16[1024,768]{1,0:T(8,128)(2,1)}, bf16[1024,768]{1,0:T(8,128)(2,1)}) custom-call(bf16[512,1024]{1,0:T(8,128)(2,1)} %get-tuple-element.171.own_ref.refs_0_, bf16[512,1024]{1,0:T(8,128)(2,1)} %copy-done.2, bf16[512,2304]{1,0:T(8,128)(2,1)} %collective-permute-done.12.refs_0_.refs_2_.refs_6_.refs_10_.refs_4_, ...), custom_call_target="tpu_custom_call" | custom-call | flops 1 | bytes 1 | tf_op jit(solution)/shard_map/project_gelu/pallas_call | solution.py:287
  314.9 8.7 %project_scale.1 = (bf16[1024,768]{1,0:T(8,128)(2,1)}, bf16[1024,768]{1,0:T(8,128)(2,1)}, bf16[1024,768]{1,0:T(8,128)(2,1)}, bf16[1024,768]{1,0:T(8,128)(2,1)}) custom-call(bf16[512,1024]{1,0:T(8,128)(2,1)} %reorder.8.own_ref.refs_2_.base_ref, bf16[512,1024]{1,0:T(8,128)(2,1)} %copy-done.3, ...), custom_call_target="tpu_custom_call" | custom-call | flops 1 | bytes 1 | tf_op jit(solution)/shard_map/project_scale/pallas_call | solution.py:287
  323.6 5.2 weight_grad.16
  328.8 7.6 %weight_grad.15 = bf16[1024,1536]{1,0:T(8,128)(2,1)} custom-call(bf16[512,1024]{1,0:T(8,128)(2,1)} %get-tuple-element.171.own_ref.refs_0_, bf16[512,1024]{1,0:T(8,128)(2,1)} %copy-done.2, bf16[512,1024]{1,0:T(8,128)(2,1)} %reorder.8.own_ref.refs_2_.base_ref, bf16[512,1024]{1,0:T(8,128)(2,1)} %copy-done.3, ...), custom_call_target="tpu_custom_call" | custom-call | flops 1 | bytes 1 | tf_op jit(solution)/shard_map/weight_grad/pallas_call | solution.py:354
  336.4 7.9 %combine.19 = (f32[512,512]{1,0:T(8,128)}, f32[512,512]{1,0:T(8,128)}) custom-call(bf16[1024,768]{1,0:T(8,128)(2,1)} %get-tuple-element.181.refs_0_.refs_4_, bf16[1024,768]{1,0:T(8,128)(2,1)} %get-tuple-element.177.refs_4_.refs_1_, bf16[1024,768]{1,0:T(8,128)(2,1)} %get-tuple-element.179.refs_2_.refs_6_, ...), custom_call_target="tpu_custom_call" | custom-call | flops 1 | bytes 1 | tf_op jit(solution)/shard_map/combine/pallas_call | solution.py:317
  345.3 7.9 %combine.18 = (f32[512,512]{1,0:T(8,128)}, f32[512,512]{1,0:T(8,128)}) custom-call(bf16[1024,768]{1,0:T(8,128)(2,1)} %get-tuple-element.181.refs_0_.refs_4_, bf16[1024,768]{1,0:T(8,128)(2,1)} %get-tuple-element.177.refs_4_.refs_1_, bf16[1024,768]{1,0:T(8,128)(2,1)} %get-tuple-element.179.refs_2_.refs_6_, ...), custom_call_target="tpu_custom_call" | custom-call | flops 1 | bytes 1 | tf_op jit(solution)/shard_map/combine/pallas_call | solution.py:317
  354.5 4.7 norm_back.3
  359.3 5.0 combine.21
  364.8 5.0 combine.20
  370.9 4.8 project_plain.10
  375.7 14.9 %attend_back.5 = (bf16[1024,256]{1,0:T(8,128)(2,1)}, bf16[1024,256]{1,0:T(8,128)(2,1)}, bf16[1024,256]{1,0:T(8,128)(2,1)}) custom-call(bf16[1024,256]{1,0:T(8,128)(2,1)} %get-tuple-element.162.q_ref, bf16[1024,256]{1,0:T(8,128)(2,1)} %get-tuple-element.163.k_ref, bf16[1024,256]{1,0:T(8,128)(2,1)} %get-tuple-element.164.v_ref, s32[1024,1]{1,0:T(8,128)} %copy.123.pq_ref, ...), custom_call_target="tpu_custom_call" | custom-call | flops 1 | bytes 1 | tf_op jit(solution)/shard_map/attend_back/pallas_call | solution.py:154
  396.6 14.6 %attend_back.4 = (bf16[1024,256]{1,0:T(8,128)(2,1)}, bf16[1024,256]{1,0:T(8,128)(2,1)}, bf16[1024,256]{1,0:T(8,128)(2,1)}) custom-call(bf16[1024,256]{1,0:T(8,128)(2,1)} %get-tuple-element.198.q_ref, bf16[1024,256]{1,0:T(8,128)(2,1)} %get-tuple-element.157.k_ref, bf16[1024,256]{1,0:T(8,128)(2,1)} %get-tuple-element.158.v_ref, s32[1024,1]{1,0:T(8,128)} %copy.123.pq_ref, ...), custom_call_target="tpu_custom_call" | custom-call | flops 1 | bytes 1 | tf_op jit(solution)/shard_map/attend_back/pallas_call | solution.py:154
  415.0 4.8 weight_grad.17
  430.2 6.1 all-to-all-start.3
  443.8 5.0 norm_back.4
  454.3 6.0 weight_grad.19
  462.2 13.7 %collective-permute-done.28.refs_3_.refs_9_ = bf16[512,1536]{1,0:T(8,128)(2,1)} collective-permute-done((bf16[512,1536]{1,0:T(8,128)(2,1)}, bf16[512,1536]{1,0:T(8,128)(2,1)}, u32[]{:S(2)}, u32[]{:S(2)}) %collective-permute-start.28) | collective-permute-done | bytes 1572896 | tf_op jit(solution)/shard_map/ppermute | solution.py:458
  482.7 4.8 project_plain.11
  487.5 14.4 %attend_back.6 = (bf16[1024,256]{1,0:T(8,128)(2,1)}, bf16[1024,256]{1,0:T(8,128)(2,1)}, bf16[1024,256]{1,0:T(8,128)(2,1)}) custom-call(bf16[1024,768]{1,0:T(8,128)(2,1)} %project_plain.6.q_ref.k_ref.v_ref, bf16[1024,768]{1,0:T(8,128)(2,1)} %project_plain.6.q_ref.k_ref.v_ref, bf16[1024,768]{1,0:T(8,128)(2,1)} %project_plain.6.q_ref.k_ref.v_ref, ...), custom_call_target="tpu_custom_call" | custom-call | flops 1 | bytes 1 | tf_op jit(solution)/shard_map/attend_back/pallas_call | solution.py:154
  501.9 8.7 %collective-permute-done.30.refs_8_ = bf16[512,1536]{1,0:T(8,128)(2,1)} collective-permute-done((bf16[512,1536]{1,0:T(8,128)(2,1)}, bf16[512,1536]{1,0:T(8,128)(2,1)}, u32[]{:S(2)}, u32[]{:S(2)}) %collective-permute-start.30) | collective-permute-done | bytes 1572896 | tf_op jit(solution)/shard_map/ppermute | solution.py:458
  510.6 8.8 %weight_grad.21 = bf16[512,2304]{1,0:T(8,128)(2,1)} custom-call(bf16[512,1024]{1,0:T(8,128)(2,1)} %get-tuple-element.171.own_ref.refs_0_, bf16[512,1024]{1,0:T(8,128)(2,1)} %copy-done.2, bf16[512,1024]{1,0:T(8,128)(2,1)} %reorder.8.own_ref.refs_2_.base_ref, bf16[512,1024]{1,0:T(8,128)(2,1)} %copy-done.3, ...), custom_call_target="tpu_custom_call" | custom-call | flops 1 | bytes 1 | tf_op jit(solution)/shard_map/weight_grad/pallas_call | solution.py:354
  519.5 6.8 all-to-all-start.4
  529.8 14.2 %attend_back.7 = (bf16[1024,256]{1,0:T(8,128)(2,1)}, bf16[1024,256]{1,0:T(8,128)(2,1)}, bf16[1024,256]{1,0:T(8,128)(2,1)}) custom-call(bf16[1024,768]{1,0:T(8,128)(2,1)} %project_plain.7.q_ref.k_ref.v_ref, bf16[1024,768]{1,0:T(8,128)(2,1)} %project_plain.7.q_ref.k_ref.v_ref, bf16[1024,768]{1,0:T(8,128)(2,1)} %project_plain.7.q_ref.k_ref.v_ref, ...), custom_call_target="tpu_custom_call" | custom-call | flops 1 | bytes 1 | tf_op jit(solution)/shard_map/attend_back/pallas_call | solution.py:154
  552.5 7.1 collective-permute-done.33.refs_4_.refs_12_
  567.5 5.7 combine.27
  578.0 5.5 combine.26
  590.9 5.6 weight_grad.26
  602.1 4.8 norm_back.5
  610.4 14.8 %all-to-all-start.6 = ((f32[16,1,388]{2,1,0:T(1,128)}), f32[16,1,388]{2,1,0:T(1,128)S(1)}, u32[]{:S(2)}, u32[]{:S(2)}) async-start(f32[16,1,388]{2,1,0:T(1,128)} %copy.140), calls=%async_computation.6 | async-start | bytes 65536 | tf_op jit(solution)/shard_map/all_to_all | solution.py:540
  635.7 14.0 %all-to-all-start.5 = ((bf16[16,32,1024]{2,1,0:T(8,128)(2,1)}), bf16[16,32,1024]{2,1,0:T(8,128)(2,1)}, u32[]{:S(2)}, u32[]{:S(2)}) async-start(bf16[16,32,1024]{2,1,0:T(8,128)(2,1)} %bitcast.101), calls=%async_computation.5 | async-start | bytes 2097152 | tf_op jit(solution)/shard_map/all_to_all | solution.py:540
  659.1 13.6 %collective-permute-done.41.refs_11_ = bf16[512,512]{1,0:T(8,128)(2,1)} collective-permute-done((bf16[512,512]{1,0:T(8,128)(2,1)}, bf16[512,512]{1,0:T(8,128)(2,1)}, u32[]{:S(2)}, u32[]{:S(2)}) %collective-permute-start.41) | collective-permute-done | bytes 524320 | tf_op jit(solution)/shard_map/ppermute | solution.py:454
  673.1 5.3 weight_grad.29
  692.4 15.0 %reduce-scatter.14.cloned.1.call-done = bf16[128,1024]{1,0:T(8,128)(2,1)} async-done(((bf16[512,1024]{1,0:T(8,128)(2,1)}), bf16[128,1024]{1,0:T(8,128)(2,1)}) %reduce-scatter.14.cloned.1.call-update) | async-done | bytes 262160
  (311 shorter events, 211.3 us)
Async XLA Ops:
  7.2 57.7 %all-gather.4.cloned.1.call-start = ((), (), s32[]{:S(2)}) async-start(), calls=%async_computation.10 | async-start | bytes 1474560 | tf_op jit(solution)/shard_map/all_gather | solution.py:462
  10.6 83.2 %all-gather.6.cloned.1.call-start = ((), (), s32[]{:S(2)}) async-start(), calls=%async_computation.11 | async-start | bytes 1310720 | tf_op jit(solution)/shard_map/all_gather | solution.py:462
  11.4 134.5 %all-gather.8.cloned.1.call-start = ((), (), s32[]{:S(2)}) async-start(), calls=%async_computation.12 | async-start | bytes 2949120 | tf_op jit(solution)/shard_map/all_gather | solution.py:462
  12.8 85.6 %all-to-all-start = ((bf16[16,32,1024]{2,1,0:T(8,128)(2,1)}), bf16[16,32,1024]{2,1,0:T(8,128)(2,1)S(1)}, u32[]{:S(2)}, u32[]{:S(2)}) async-start(bf16[16,32,1024]{2,1,0:T(8,128)(2,1)} %param.20), calls=%async_computation | async-start | bytes 2097152 | tf_op jit(solution)/shard_map/all_to_all | solution.py:540
  64.9 37.9 %collective-permute-start = (bf16[512,1152]{1,0:T(8,128)(2,1)}, bf16[512,1152]{1,0:T(8,128)(2,1)}, u32[]{:S(2)}, u32[]{:S(2)}) collective-permute-start(bf16[512,1152]{1,0:T(8,128)(2,1)} %all-gather.4.cloned.1.call-done.refs_0_.refs_2_.refs_6_.refs_10_.refs_14_), channel_id=1, source_target_pairs={{0,4},{4,0},{1,5},{5,1},{2,6},{6,2},{3,7},{7,3},{8,12},{12,8},{9,1... | collective-permute-start | bytes 3538952 | tf_op jit(solution)/shard_map/ppermute | solution.py:458
  93.8 26.3 %collective-permute-start.3 = (bf16[512,1024]{1,0:T(8,128)(2,1)}, bf16[512,1024]{1,0:T(8,128)(2,1)S(1)}, u32[]{:S(2)}, u32[]{:S(2)}) collective-permute-start(bf16[512,1024]{1,0:T(8,128)(2,1)} %all-gather.6.cloned.1.call-done.refs_0_.refs_4_.refs_2_.refs_8_), channel_id=1, source_target_pairs={{0,2},{2,0},{1,3},{3,1},{4,6},{6,4},{5,7},{7,5},{8,10},{10,8},{9,1... | collective-permute-start | bytes 3145736 | tf_op jit(solution)/shard_map/ppermute | solution.py:454
  95.3 55.4 %collective-permute-start.2 = (bf16[512,1024]{1,0:T(8,128)(2,1)}, bf16[512,1024]{1,0:T(8,128)(2,1)}, u32[]{:S(2)}, u32[]{:S(2)}) collective-permute-start(bf16[512,1024]{1,0:T(8,128)(2,1)} %all-gather.6.cloned.1.call-done.refs_0_.refs_4_.refs_2_.refs_8_), channel_id=1, source_target_pairs={{0,4},{4,0},{1,5},{5,1},{2,6},{6,2},{3,7},{7,3},{8,12},{12,8},{9,1... | collective-permute-start | bytes 3145736 | tf_op jit(solution)/shard_map/ppermute | solution.py:458
  97.8 52.9 %collective-permute-start.4 = (bf16[512,1152]{1,0:T(8,128)(2,1)}, bf16[512,1152]{1,0:T(8,128)(2,1)}, u32[]{:S(2)}, u32[]{:S(2)}) collective-permute-start(bf16[512,1152]{1,0:T(8,128)(2,1)} %all-gather.4.cloned.1.call-done.refs_0_.refs_2_.refs_6_.refs_10_.refs_14_), channel_id=1, source_target_pairs={{0,2},{2,0},{1,3},{3,1},{4,6},{6,4},{5,7},{7,5},{8,10},{10,8},{9,1... | collective-permute-start | bytes 3538952 | tf_op jit(solution)/shard_map/ppermute | solution.py:454
  103.8 75.4 %collective-permute-start.5 = (bf16[512,1152]{1,0:T(8,128)(2,1)}, bf16[512,1152]{1,0:T(8,128)(2,1)}, u32[]{:S(2)}, u32[]{:S(2)}) collective-permute-start(bf16[512,1152]{1,0:T(8,128)(2,1)} %collective-permute-done.refs_1_.refs_3_.refs_7_.refs_11_.refs_15_), channel_id=1, source_target_pairs={{0,2},{2,0},{1,3},{3,1},{4,6},{6,4},{5,7},{7,5},{8,10},{10,8},{9,1... | collective-permute-start | bytes 3538952 | tf_op jit(solution)/shard_map/ppermute | solution.py:454
  108.2 42.5 %collective-permute-start.1 = (bf16[512,1024]{1,0:T(8,128)(2,1)}, bf16[512,1024]{1,0:T(8,128)(2,1)}, u32[]{:S(2)}, u32[]{:S(2)}) collective-permute-start(bf16[512,1024]{1,0:T(8,128)(2,1)} %add_norm.3.own_ref.refs_0_), channel_id=1, source_target_pairs={{0,1},{1,0},{2,3},{3,2},{4,5},{5,4},{6,7},{7,6},{8,9},{9,8},{10,11... | collective-permute-start | bytes 3145736 | tf_op jit(solution)/shard_map/ppermute | solution.py:450
  120.1 88.8 %collective-permute-start.6 = (bf16[512,1024]{1,0:T(8,128)(2,1)S(1)}, bf16[512,1024]{1,0:T(8,128)(2,1)}, u32[]{:S(2)}, u32[]{:S(2)}) collective-permute-start(bf16[512,1024]{1,0:T(8,128)(2,1)S(1)} %collective-permute-done.3.refs_2_.refs_6_.refs_4_.refs_10_), channel_id=1, source_target_pairs={{0,4},{4,0},{1,5},{5,1},{2,6},{6,2},{3,7},{7,3},{8,12},{12,8},{9,1... | collective-permute-start | bytes 3145736 | tf_op jit(solution)/shard_map/ppermute | solution.py:458
  146.0 86.6 %all-to-all-start.1 = ((bf16[16,32,1024]{2,1,0:T(8,128)(2,1)}), bf16[16,32,1024]{2,1,0:T(8,128)(2,1)}, u32[]{:S(2)}, u32[]{:S(2)}) async-start(bf16[16,32,1024]{2,1,0:T(8,128)(2,1)} %param.21), calls=%async_computation.1 | async-start | bytes 2097152 | tf_op jit(solution)/shard_map/all_to_all | solution.py:540
  184.6 56.4 %collective-permute-start.11 = (bf16[512,2304]{1,0:T(8,128)(2,1)S(1)}, bf16[512,2304]{1,0:T(8,128)(2,1)}, u32[]{:S(2)}, u32[]{:S(2)}) collective-permute-start(bf16[512,2304]{1,0:T(8,128)(2,1)S(1)} %copy-done), channel_id=1, source_target_pairs={{0,4},{4,0},{1,5},{5,1},{2,6},{6,2},{3,7},{7,3},{8,12},{12,8},{9,1... | collective-permute-start | bytes 7077896 | tf_op jit(solution)/shard_map/ppermute | solution.py:458
  186.1 61.7 %collective-permute-start.12 = (bf16[512,2304]{1,0:T(8,128)(2,1)S(1)}, bf16[512,2304]{1,0:T(8,128)(2,1)}, u32[]{:S(2)}, u32[]{:S(2)}) collective-permute-start(bf16[512,2304]{1,0:T(8,128)(2,1)S(1)} %copy-done), channel_id=1, source_target_pairs={{0,2},{2,0},{1,3},{3,1},{4,6},{6,4},{5,7},{7,5},{8,10},{10,8},{9,1... | collective-permute-start | bytes 7077896 | tf_op jit(solution)/shard_map/ppermute | solution.py:454
  232.5 10.5 %collective-permute-start.9 = (bf16[512,1024]{1,0:T(8,128)(2,1)}, bf16[512,1024]{1,0:T(8,128)(2,1)}, u32[]{:S(2)}, u32[]{:S(2)}) collective-permute-start(bf16[512,1024]{1,0:T(8,128)(2,1)} %get-tuple-element.154.own_ref.refs_0_), channel_id=1, source_target_pairs={{0,1},{1,0},{2,3},{3,2},{4,5},{5,4},{6,7},{7,6},{8,9},{9,8},{10,11... | collective-permute-start | bytes 3145736 | tf_op jit(solution)/shard_map/ppermute | solution.py:450
  236.0 11.8 %collective-permute-start.10 = (bf16[512,1024]{1,0:T(8,128)(2,1)}, bf16[512,1024]{1,0:T(8,128)(2,1)S(1)}, u32[]{:S(2)}, u32[]{:S(2)}) collective-permute-start(bf16[512,1024]{1,0:T(8,128)(2,1)} %reorder.7.own_ref.refs_0_.refs_4_), channel_id=1, source_target_pairs={{0,1},{1,0},{2,3},{3,2},{4,5},{5,4},{6,7},{7,6},{8,9},{9,8},{10,11... | collective-permute-start | bytes 3145736 | tf_op jit(solution)/shard_map/ppermute | solution.py:450
  236.4 52.1 %all-to-all-start.2 = ((bf16[16,32,1024]{2,1,0:T(8,128)(2,1)}), bf16[16,32,1024]{2,1,0:T(8,128)(2,1)}, u32[]{:S(2)}, u32[]{:S(2)}) async-start(bf16[16,32,1024]{2,1,0:T(8,128)(2,1)} %param.22), calls=%async_computation.2 | async-start | bytes 2097152 | tf_op jit(solution)/shard_map/all_to_all | solution.py:540
  241.0 64.6 %collective-permute-start.16 = (bf16[512,2304]{1,0:T(8,128)(2,1)}, bf16[512,2304]{1,0:T(8,128)(2,1)}, u32[]{:S(2)}, u32[]{:S(2)}) collective-permute-start(bf16[512,2304]{1,0:T(8,128)(2,1)} %collective-permute-done.11.refs_1_.refs_3_.refs_5_.refs_9_), channel_id=1, source_target_pairs={{0,2},{2,0},{1,3},{3,1},{4,6},{6,4},{5,7},{7,5},{8,10},{10,8},{9,1... | collective-permute-start | bytes 7077896 | tf_op jit(solution)/shard_map/ppermute | solution.py:454
  292.2 21.6 %collective-permute-start.15 = (bf16[512,1024]{1,0:T(8,128)(2,1)}, bf16[512,1024]{1,0:T(8,128)(2,1)S(1)}, u32[]{:S(2)}, u32[]{:S(2)}) collective-permute-start(bf16[512,1024]{1,0:T(8,128)(2,1)} %reorder.8.own_ref.refs_2_.base_ref), channel_id=1, source_target_pairs={{0,1},{1,0},{2,3},{3,2},{4,5},{5,4},{6,7},{7,6},{8,9},{9,8},{10,11... | collective-permute-start | bytes 3145736 | tf_op jit(solution)/shard_map/ppermute | solution.py:450
  344.9 109.4 %collective-permute-start.25 = (bf16[1024,1536]{1,0:T(8,128)(2,1)}, bf16[1024,1536]{1,0:T(8,128)(2,1)}, u32[]{:S(2)}, u32[]{:S(2)}) collective-permute-start(bf16[1024,1536]{1,0:T(8,128)(2,1)} %weight_grad.15), channel_id=1, source_target_pairs={{0,2},{2,0},{1,3},{3,1},{4,6},{6,4},{5,7},{7,5},{8,10},{10,8},{9,1... | collective-permute-start | bytes 9437192 | tf_op jit(solution)/shard_map/ppermute | solution.py:454
  359.3 10.5 %collective-permute-start.20 = (bf16[512,1024]{1,0:T(8,128)(2,1)}, bf16[512,1024]{1,0:T(8,128)(2,1)S(1)}, u32[]{:S(2)}, u32[]{:S(2)}) collective-permute-start(bf16[512,1024]{1,0:T(8,128)(2,1)} %get-tuple-element.190.own_ref.refs_2_), channel_id=1, source_target_pairs={{0,1},{1,0},{2,3},{3,2},{4,5},{5,4},{6,7},{7,6},{8,9},{9,8},{10,11... | collective-permute-start | bytes 3145736 | tf_op jit(solution)/shard_map/ppermute | solution.py:450
  364.3 26.2 %collective-permute-start.21 = (f32[512,512]{1,0:T(8,128)}, f32[512,512]{1,0:T(8,128)S(1)}, u32[]{:S(2)}, u32[]{:S(2)}) collective-permute-start(f32[512,512]{1,0:T(8,128)} %get-tuple-element.195), channel_id=1, source_target_pairs={{0,1},{1,0},{2,3},{3,2},{4,5},{5,4},{6,7},{7,6},{8,9},{9,8},{10,11... | collective-permute-start | bytes 3145736 | tf_op jit(solution)/shard_map/ppermute | solution.py:450
  364.8 25.8 %collective-permute-start.22 = (f32[512,512]{1,0:T(8,128)}, f32[512,512]{1,0:T(8,128)S(1)}, u32[]{:S(2)}, u32[]{:S(2)}) collective-permute-start(f32[512,512]{1,0:T(8,128)} %get-tuple-element.196), channel_id=1, source_target_pairs={{0,1},{1,0},{2,3},{3,2},{4,5},{5,4},{6,7},{7,6},{8,9},{9,8},{10,11... | collective-permute-start | bytes 3145736 | tf_op jit(solution)/shard_map/ppermute | solution.py:450
  414.4 14.2 %collective-permute-start.23 = (f32[512,512]{1,0:T(8,128)}, f32[512,512]{1,0:T(8,128)S(1)}, u32[]{:S(2)}, u32[]{:S(2)}) collective-permute-start(f32[512,512]{1,0:T(8,128)} %get-tuple-element.205), channel_id=1, source_target_pairs={{0,1},{1,0},{2,3},{3,2},{4,5},{5,4},{6,7},{7,6},{8,9},{9,8},{10,11... | collective-permute-start | bytes 3145736 | tf_op jit(solution)/shard_map/ppermute | solution.py:450
  414.9 28.9 %collective-permute-start.24 = (f32[512,512]{1,0:T(8,128)}, f32[512,512]{1,0:T(8,128)}, u32[]{:S(2)}, u32[]{:S(2)}) collective-permute-start(f32[512,512]{1,0:T(8,128)} %get-tuple-element.213), channel_id=1, source_target_pairs={{0,1},{1,0},{2,3},{3,2},{4,5},{5,4},{6,7},{7,6},{8,9},{9,8},{10,11... | collective-permute-start | bytes 3145736 | tf_op jit(solution)/shard_map/ppermute | solution.py:450
  428.1 20.8 %collective-permute-start.26 = (f32[512,512]{1,0:T(8,128)}, f32[512,512]{1,0:T(8,128)S(1)}, u32[]{:S(2)}, u32[]{:S(2)}) collective-permute-start(f32[512,512]{1,0:T(8,128)} %get-tuple-element.218), channel_id=1, source_target_pairs={{0,1},{1,0},{2,3},{3,2},{4,5},{5,4},{6,7},{7,6},{8,9},{9,8},{10,11... | collective-permute-start | bytes 3145736 | tf_op jit(solution)/shard_map/ppermute | solution.py:450
  428.5 20.4 %collective-permute-start.27 = (f32[512,512]{1,0:T(8,128)}, f32[512,512]{1,0:T(8,128)S(1)}, u32[]{:S(2)}, u32[]{:S(2)}) collective-permute-start(f32[512,512]{1,0:T(8,128)} %get-tuple-element.220), channel_id=1, source_target_pairs={{0,1},{1,0},{2,3},{3,2},{4,5},{5,4},{6,7},{7,6},{8,9},{9,8},{10,11... | collective-permute-start | bytes 3145736 | tf_op jit(solution)/shard_map/ppermute | solution.py:450
  428.6 47.3 %collective-permute-start.28 = (bf16[512,1536]{1,0:T(8,128)(2,1)}, bf16[512,1536]{1,0:T(8,128)(2,1)}, u32[]{:S(2)}, u32[]{:S(2)}) collective-permute-start(bf16[512,1536]{1,0:T(8,128)(2,1)} %weight_grad.16), channel_id=1, source_target_pairs={{0,4},{4,0},{1,5},{5,1},{2,6},{6,2},{3,7},{7,3},{8,12},{12,8},{9,1... | collective-permute-start | bytes 4718600 | tf_op jit(solution)/shard_map/ppermute | solution.py:458
  430.2 51.5 %all-to-all-start.3 = ((bf16[16,32,1024]{2,1,0:T(8,128)(2,1)}), bf16[16,32,1024]{2,1,0:T(8,128)(2,1)S(1)}, u32[]{:S(2)}, u32[]{:S(2)}) async-start(bf16[16,32,1024]{2,1,0:T(8,128)(2,1)} %bitcast.25), calls=%async_computation.3 | async-start | bytes 2097152 | tf_op jit(solution)/shard_map/all_to_all | solution.py:540
  436.4 160.1 %reduce-scatter.10.cloned.1.call-start = ((), (), s32[]{:S(2)}) async-start(), calls=%async_computation.13 | async-start | bytes 2949120
  460.3 50.3 %collective-permute-start.30 = (bf16[512,1536]{1,0:T(8,128)(2,1)}, bf16[512,1536]{1,0:T(8,128)(2,1)}, u32[]{:S(2)}, u32[]{:S(2)}) collective-permute-start(bf16[512,1536]{1,0:T(8,128)(2,1)} %weight_grad.19), channel_id=1, source_target_pairs={{0,4},{4,0},{1,5},{5,1},{2,6},{6,2},{3,7},{7,3},{8,12},{12,8},{9,1... | collective-permute-start | bytes 4718600 | tf_op jit(solution)/shard_map/ppermute | solution.py:458
  462.2 19.5 %collective-permute-start.29 = (bf16[512,1024]{1,0:T(8,128)(2,1)S(1)}, bf16[512,1024]{1,0:T(8,128)(2,1)S(1)}, u32[]{:S(2)}, u32[]{:S(2)}) collective-permute-start(bf16[512,1024]{1,0:T(8,128)(2,1)S(1)} %copy-done.5), channel_id=1, source_target_pairs={{0,1},{1,0},{2,3},{3,2},{4,5},{5,4},{6,7},{7,6},{8,9},{9,8},{10,11... | collective-permute-start | bytes 3145736 | tf_op jit(solution)/shard_map/ppermute | solution.py:450
  480.1 21.8 %collective-permute-start.31 = (bf16[512,768]{1,0:T(8,128)(2,1)}, bf16[512,768]{1,0:T(8,128)(2,1)}, u32[]{:S(2)}, u32[]{:S(2)}) collective-permute-start(bf16[512,768]{1,0:T(8,128)(2,1)} %weight_grad.20), channel_id=1, source_target_pairs={{0,2},{2,0},{1,3},{3,1},{4,6},{6,4},{5,7},{7,5},{8,10},{10,8},{9,1... | collective-permute-start | bytes 2359304 | tf_op jit(solution)/shard_map/ppermute | solution.py:454
  519.5 48.0 %all-to-all-start.4 = ((bf16[16,32,1024]{2,1,0:T(8,128)(2,1)}), bf16[16,32,1024]{2,1,0:T(8,128)(2,1)S(1)}, u32[]{:S(2)}, u32[]{:S(2)}) async-start(bf16[16,32,1024]{2,1,0:T(8,128)(2,1)} %bitcast.26), calls=%async_computation.4 | async-start | bytes 2097152 | tf_op jit(solution)/shard_map/all_to_all | solution.py:540
  526.3 152.1 %reduce-scatter.12.cloned.1.call-start = ((), (), s32[]{:S(2)}) async-start(), calls=%async_computation.14 | async-start | bytes 1310720
  526.3 33.3 %collective-permute-start.33 = (bf16[512,1024]{1,0:T(8,128)(2,1)}, bf16[512,1024]{1,0:T(8,128)(2,1)S(1)}, u32[]{:S(2)}, u32[]{:S(2)}) collective-permute-start(bf16[512,1024]{1,0:T(8,128)(2,1)} %weight_grad.18), channel_id=1, source_target_pairs={{0,4},{4,0},{1,5},{5,1},{2,6},{6,2},{3,7},{7,3},{8,12},{12,8},{9,1... | collective-permute-start | bytes 3145736 | tf_op jit(solution)/shard_map/ppermute | solution.py:458
  528.3 35.7 %collective-permute-start.32 = (bf16[1024,512]{1,0:T(8,128)(2,1)}, bf16[1024,512]{1,0:T(8,128)(2,1)}, u32[]{:S(2)}, u32[]{:S(2)}) collective-permute-start(bf16[1024,512]{1,0:T(8,128)(2,1)} %weight_grad.17), channel_id=1, source_target_pairs={{0,2},{2,0},{1,3},{3,1},{4,6},{6,4},{5,7},{7,5},{8,10},{10,8},{9,1... | collective-permute-start | bytes 3145736 | tf_op jit(solution)/shard_map/ppermute | solution.py:454
  573.2 28.9 %collective-permute-start.36 = (f32[512,512]{1,0:T(8,128)}, f32[512,512]{1,0:T(8,128)}, u32[]{:S(2)}, u32[]{:S(2)}) collective-permute-start(f32[512,512]{1,0:T(8,128)} %get-tuple-element.244), channel_id=1, source_target_pairs={{0,1},{1,0},{2,3},{3,2},{4,5},{5,4},{6,7},{7,6},{8,9},{9,8},{10,11... | collective-permute-start | bytes 3145736 | tf_op jit(solution)/shard_map/ppermute | solution.py:450
  573.3 28.8 %collective-permute-start.37 = (f32[512,512]{1,0:T(8,128)}, f32[512,512]{1,0:T(8,128)}, u32[]{:S(2)}, u32[]{:S(2)}) collective-permute-start(f32[512,512]{1,0:T(8,128)} %get-tuple-element.245), channel_id=1, source_target_pairs={{0,1},{1,0},{2,3},{3,2},{4,5},{5,4},{6,7},{7,6},{8,9},{9,8},{10,11... | collective-permute-start | bytes 3145736 | tf_op jit(solution)/shard_map/ppermute | solution.py:450
  573.8 13.9 %collective-permute-start.35 = (bf16[512,512]{1,0:T(8,128)(2,1)S(1)}, bf16[512,512]{1,0:T(8,128)(2,1)S(1)}, u32[]{:S(2)}, u32[]{:S(2)}) collective-permute-start(bf16[512,512]{1,0:T(8,128)(2,1)S(1)} %copy-done.34), channel_id=1, source_target_pairs={{0,2},{2,0},{1,3},{3,1},{4,6},{6,4},{5,7},{7,5},{8,10},{10,8},{9,1... | collective-permute-start | bytes 1572872 | tf_op jit(solution)/shard_map/ppermute | solution.py:454
  575.4 14.7 %collective-permute-start.34 = (bf16[512,512]{1,0:T(8,128)(2,1)}, bf16[512,512]{1,0:T(8,128)(2,1)S(1)}, u32[]{:S(2)}, u32[]{:S(2)}) collective-permute-start(bf16[512,512]{1,0:T(8,128)(2,1)} %weight_grad.24), channel_id=1, source_target_pairs={{0,4},{4,0},{1,5},{5,1},{2,6},{6,2},{3,7},{7,3},{8,12},{12,8},{9,1... | collective-permute-start | bytes 1572872 | tf_op jit(solution)/shard_map/ppermute | solution.py:458
  598.0 27.3 %collective-permute-start.39 = (bf16[512,1024]{1,0:T(8,128)(2,1)}, bf16[512,1024]{1,0:T(8,128)(2,1)}, u32[]{:S(2)}, u32[]{:S(2)}) collective-permute-start(bf16[512,1024]{1,0:T(8,128)(2,1)} %weight_grad.23), channel_id=1, source_target_pairs={{0,4},{4,0},{1,5},{5,1},{2,6},{6,2},{3,7},{7,3},{8,12},{12,8},{9,1... | collective-permute-start | bytes 3145736 | tf_op jit(solution)/shard_map/ppermute | solution.py:458
  600.1 28.7 %collective-permute-start.38 = (bf16[1024,512]{1,0:T(8,128)(2,1)}, bf16[1024,512]{1,0:T(8,128)(2,1)}, u32[]{:S(2)}, u32[]{:S(2)}) collective-permute-start(bf16[1024,512]{1,0:T(8,128)(2,1)} %weight_grad.22), channel_id=1, source_target_pairs={{0,2},{2,0},{1,3},{3,1},{4,6},{6,4},{5,7},{7,5},{8,10},{10,8},{9,1... | collective-permute-start | bytes 3145736 | tf_op jit(solution)/shard_map/ppermute | solution.py:454
  610.4 25.3 %all-to-all-start.6 = ((f32[16,1,388]{2,1,0:T(1,128)}), f32[16,1,388]{2,1,0:T(1,128)S(1)}, u32[]{:S(2)}, u32[]{:S(2)}) async-start(f32[16,1,388]{2,1,0:T(1,128)} %copy.140), calls=%async_computation.6 | async-start | bytes 65536 | tf_op jit(solution)/shard_map/all_to_all | solution.py:540
  635.7 49.2 %all-to-all-start.5 = ((bf16[16,32,1024]{2,1,0:T(8,128)(2,1)}), bf16[16,32,1024]{2,1,0:T(8,128)(2,1)}, u32[]{:S(2)}, u32[]{:S(2)}) async-start(bf16[16,32,1024]{2,1,0:T(8,128)(2,1)} %bitcast.101), calls=%async_computation.5 | async-start | bytes 2097152 | tf_op jit(solution)/shard_map/all_to_all | solution.py:540
  649.7 57.7 %reduce-scatter.14.cloned.1.call-start = ((), (), s32[]{:S(2)}) async-start(), calls=%async_computation.15 | async-start | bytes 1310720
  649.8 23.0 %collective-permute-start.41 = (bf16[512,512]{1,0:T(8,128)(2,1)}, bf16[512,512]{1,0:T(8,128)(2,1)}, u32[]{:S(2)}, u32[]{:S(2)}) collective-permute-start(bf16[512,512]{1,0:T(8,128)(2,1)} %weight_grad.28), channel_id=1, source_target_pairs={{0,2},{2,0},{1,3},{3,1},{4,6},{6,4},{5,7},{7,5},{8,10},{10,8},{9,1... | collective-permute-start | bytes 1572872 | tf_op jit(solution)/shard_map/ppermute | solution.py:454
  651.7 21.4 %collective-permute-start.40 = (bf16[512,512]{1,0:T(8,128)(2,1)}, bf16[512,512]{1,0:T(8,128)(2,1)}, u32[]{:S(2)}, u32[]{:S(2)}) collective-permute-start(bf16[512,512]{1,0:T(8,128)(2,1)} %weight_grad.27), channel_id=1, source_target_pairs={{0,4},{4,0},{1,5},{5,1},{2,6},{6,2},{3,7},{7,3},{8,12},{12,8},{9,1... | collective-permute-start | bytes 1572872 | tf_op jit(solution)/shard_map/ppermute | solution.py:458
  (60 other events, 362.3 us)
Sparse Core Ops, SparseCore 0:
  10.8 54.0 all-gather.3
  67.0 26.7 all-gather.5
  96.0 49.9 all-gather.7
  519.6 66.7 reduce-scatter.9
  598.1 38.3 reduce-scatter.11
  680.5 26.8 reduce-scatter.13

commit v3 on v2

--- a/solution.py
+++ b/solution.py
@@ -17,6 +17,7 @@
 learn_rate = 0.01
 average_rate = 0.5
 neg_large = -1e30
+vmem_room = 24 << 20
 tanh_rate = 0.7978845608
 tanh_cube = 0.044715
 bf16 = jnp.bfloat16
@@ -143,6 +144,7 @@
             jax.ShapeDtypeStruct((pairs, rows, 2), f32),
             jax.ShapeDtypeStruct((pairs, 8, 128), f32),
         ],
+        compiler_params=pltpu.CompilerParams(vmem_limit_bytes=vmem_room),
         cost_estimate=attend_cost(rows, keys, pairs, 2),
         name="attend",
     )(q[0], k[0], v[0], pos_col, pos_row, length)
@@ -166,6 +168,7 @@
         out_specs=[lane_pairs(rows, 0), lane_pairs(keys, 0), lane_pairs(keys, 0)],
         out_shape=[jax.ShapeDtypeStruct((n, pairs * 2 * DK), bf16) for n in (rows, keys, keys)],
         scratch_shapes=[pltpu.VMEM((2 * DK, keys), f32)] * 2,
+        compiler_params=pltpu.CompilerParams(vmem_limit_bytes=vmem_room),
         cost_estimate=attend_cost(rows, keys, pairs, 5),
         name="attend_back",
     )(q[0], k[0], v[0], pos_col, pos_row, lse, grad)
@@ -233,6 +236,7 @@
         ],
         out_specs=spec((rows // 4, width), lambda i: (i, 0)),
         out_shape=jax.ShapeDtypeStruct((rows, width), bf16),
+        compiler_params=pltpu.CompilerParams(vmem_limit_bytes=vmem_room),
         cost_estimate=cost(0, rows * width * 4),
         name="reorder",
     )(dy[None], *arrays, *extra)
@@ -240,9 +244,10 @@
 
 def weight_specs(weights):
     specs, arrays = [], []
-    for own, other, width, place in weights:
-        specs += [spec((own.shape[0], width), lambda i, place=place: (0, place))] * 2
-        arrays += [own, other]
+    for own, other, width, *places in weights:
+        for array, place in zip((own, other), (places[0], places[-1])):
+            specs.append(spec((array.shape[0], width), lambda i, place=place: (0, place)))
+            arrays.append(array)
     return specs, arrays
 
 
@@ -295,6 +300,7 @@
         ],
         out_specs=[by_rows(w) for w in out_widths],
         out_shape=[jax.ShapeDtypeStruct((2 * half, w), bf16) for w in out_widths],
+        compiler_params=pltpu.CompilerParams(vmem_limit_bytes=vmem_room),
         cost_estimate=cost(4 * half * width_all * sum(widths), half * width_all * 4 + width_all * sum(widths) * 2),
         name="project_" + mode,
     )(own, other, *arrays, *scales)
@@ -320,6 +326,7 @@
         in_specs=[spec((size, v.shape[1]), lambda i: (2 * which + i, 0)) for v in values] + specs,
         out_specs=[spec((size, depth), lambda i: (i, 0))] * 2,
         out_shape=[jax.ShapeDtypeStruct((half, depth), f32)] * 2,
+        compiler_params=pltpu.CompilerParams(vmem_limit_bytes=vmem_room),
         cost_estimate=cost(0, 0),
         name="combine",
     )(*values, *arrays)
@@ -359,6 +366,7 @@
         + [spec((size, a.shape[1]), lambda i, place=place: (place + i, 0)) for a, place, _ in arrived],
         out_specs=spec((size, last), lambda i: (i, 0)),
         out_shape=jax.ShapeDtypeStruct((steps * size, last), bf16),
+        compiler_params=pltpu.CompilerParams(vmem_limit_bytes=vmem_room),
         cost_estimate=cost(4 * half * steps * size * last, half * width * 4 + half * 4 * last),
         name="weight_grad",
     )(*[t for pair in sources for t in pair], *[v for _, v in items], *[a for a, _, _ in arrived])
@@ -403,6 +411,7 @@
         in_specs=[by_rows(gain_row), *[by_rows(p) for p in arrays]],
         out_specs=[by_rows(t) for t in shapes],
         out_shape=shapes,
+        compiler_params=pltpu.CompilerParams(vmem_limit_bytes=vmem_room),
         cost_estimate=cost(rows * width * 8, rows * width * 14),
         name="add_norm",
     )(gain_row, *arrays)
@@ -437,6 +446,7 @@
         in_specs=[by_rows(gain_row), by_rows(hidden), by_rows(base), *[by_rows(g) for g in arrays]],
         out_specs=[*[by_rows(t) for t in shapes], spec((1, width), lambda i: (0, 0))],
         out_shape=[*shapes, jax.ShapeDtypeStruct((1, width), f32)],
+        compiler_params=pltpu.CompilerParams(vmem_limit_bytes=vmem_room),
         cost_estimate=cost(rows * width * 16, rows * width * 22),
         name="norm_back",
     )(gain_row, hidden, base, *arrays)
@@ -468,6 +478,14 @@
         return (part, high), (swap_x(part), swap_x(high))
     beside = swap_x(part)
     return (part, swap_y(part)), (beside, swap_y(beside))
+
+
+def pieces(value, count):
+    made = []
+    for _ in range(count):
+        made.append(value.astype(bf16))
+        value = value - made[-1].astype(f32)
+    return made
 
 
 class Group:
@@ -567,18 +585,15 @@
     chunk_b = jnp.concatenate([*low_in[3:6], out_t[1]], axis=1)
     chunk_c = jnp.concatenate([widen(ff_in[0]), widen(ff_in[1]), widen(ff_out.T)], axis=1)
 
-    tok_own = to_chips(tokens)
     part_a, part_b, part_c = (gather_part(t) for t in (chunk_a, chunk_b, chunk_c))
     got_a = spread(part_a, True)
-    enc_own = to_chips(after(encoder, part_c))
-    got_b = spread(part_b, False)
+    tok_own = to_chips(after(tokens, part_a))
     cot_own = to_chips(cotangent)
 
     gain_f = jnp.concatenate([g[:, 4 * hc : 4 * hc + 3] for g in got_a[0]]).astype(f32).T
     gain_rows = [gain_f[n : n + 1] for n in range(3)]
     w_qkv = [(*g, 3 * hc, 0) for g in got_a]
     w_q, w_k, w_v, w_ot = ([(*g, hc, n) for g in got_a] for n in range(4))
-    w_cq, w_ck, w_cv, w_cot = ([(*g, hc, n) for g in got_b] for n in range(4))
 
     def both(own):
         return own, swap_cores(own)
@@ -591,13 +606,26 @@
     norm_one = both(add_norm([x_own], gain_rows[0])[0])
     norm_one = after(norm_one[0], part_b), norm_one[1]
     qkv = [project(norm_one, [w_qkv[0]])[0]]
-    qkv += project((after(norm_one[0], got_b[0][1], got_b[1][0]), norm_one[1]), [w_qkv[1]])
-    self_qkv = [[(t, n * pairs, pairs) for n in range(3)] for t in qkv]
-    got_c = spread(after(part_c, qkv[1]), True)
-    w_g, w_u, w_dt = ([(*g, deep, n) for g in got_c] for n in range(3))
-    self_qkv[1][0] = (after(qkv[1], got_b[1][1]), *self_qkv[1][0][1:])
-    self_out = [attend(*t, *places, length, True, 256) for t in self_qkv]
-    self_mixed = [self_out[0][0], after(self_out[1][0], part_c)]
+    self_qkv = [[(qkv[0], n * pairs, pairs) for n in range(3)]]
+    self_out = [attend(*self_qkv[0], *places, length, True, 256)]
+    qkv += project((after(norm_one[0], self_out[0][0]), norm_one[1]), [w_qkv[1]])
+    self_qkv += [[(qkv[1], n * pairs, pairs) for n in range(3)]]
+    high_b, beside_b = swap_y(part_b), swap_x(part_b)
+    self_out += [attend(*self_qkv[1], *places, length, True, 256)]
+    far_b = swap_y(after(beside_b, self_out[1][0], high_b))
+    got_b = (part_b, high_b), (beside_b, far_b)
+    w_cq, w_ck, w_cv, w_cot = ([(*g, hc, n) for g in got_b] for n in range(4))
+
+    enc_own = to_chips(after(encoder, part_c, self_out[1][0]))
+    part_c = after(part_c, self_out[1][0], far_b)
+    high_c, beside_c = swap_y(part_c), swap_x(part_c)
+    far_gu, far_d = swap_x(high_c[:, : 2 * deep]), swap_y(beside_c[:, 2 * deep :])
+    w_g, w_u, w_dt = (
+        [(part_c, high_c, deep, n), (beside_c, far, deep, n, place)]
+        for n, far, place in ((0, far_gu, 0), (1, far_gu, 1), (2, far_d, 0))
+    )
+
+    self_mixed = [o[0] for o in self_out]
     hidden_one, norm_two = add_norm([x_own, *over_cores(self_mixed, w_ot)], gain_rows[1])
     norm_two = both(norm_two)
     e_own = reorder([enc_own], model_rows, dy, True)
@@ -607,7 +635,7 @@
     cross_qkv = [
         [(t, 0, pairs) for t in (cross_q[n], cross_kv[n], cross_kv[2 + n])] for n in range(2)
     ]
-    cross_qkv[1][0] = (after(cross_q[1], cross_q[0], got_c[0][1], got_c[1][0]), 0, pairs)
+    cross_qkv[0][0] = (after(cross_q[0], cross_q[1], high_c, beside_c), 0, pairs)
     cross_out = [attend(*t, *places, length, False, 512) for t in cross_qkv]
     cross_mixed = [o[0] for o in cross_out]
     hidden_two, norm_three = add_norm(
@@ -630,11 +658,12 @@
     grad_ca = project((after(grad_co[0], out_parts[0][0]), grad_co[1]), w_cot)
     out_block = reorder([after(hidden_two, *grad_ca), *out_parts], model_rows, dy, False, valid_own)
     block_output = from_chips(out_block)
-    cross_qkv[0][0] = (after(cross_q[0], out_block), 0, pairs)
-    cross_back = [
-        attend_back(*t, *places, o[1], d, False, 512) for t, o, d in zip(cross_qkv, cross_out, grad_ca)
-    ]
+    cross_back = [attend_back(*cross_qkv[0], *places, cross_out[0][1], after(grad_ca[0], out_block), False, 512)]
+    grad_late = after(grad_ca[1], group_c.from_y, *cross_back[0])
+    cross_back += [attend_back(*cross_qkv[1], *places, cross_out[1][1], grad_late, False, 512)]
     grad_cq, grad_ck, grad_cv = zip(*cross_back)
+    sent = group_c.second(*grad_cq)
+    grad_cq = (after(grad_cq[0], *sent), grad_cq[1])
     group_b = Group(
         [(norm_two, *grad_cq), (grad_co, *[o[0] for o in cross_out])],
         [(enc_rows, *grad_ck), (enc_rows, *grad_cv)],
@@ -648,12 +677,12 @@
     grad_o = both(low_one)
     out_enc = reorder([parts_enc[0], [after(parts_enc[1][0], low_one), parts_enc[1][1]]], model_rows, dy, False)
     grad_encoder = from_chips(out_enc)
-    sent = group_c.second(out_enc)
-    grad_a = project((after(grad_o[0], *sent, block_output), grad_o[1]), w_ot)
+    grad_a = project((after(grad_o[0], out_enc, block_output), grad_o[1]), w_ot)
     self_back = [attend_back(*self_qkv[0], *places, self_out[0][1], grad_a[0], True, 256)]
     sent = group_c.third(*self_back[0])
     self_back.append(attend_back(*self_qkv[1], *places, self_out[1][1], after(grad_a[1], *sent), True, 256))
     sent = group_b.second(*self_back[1])
+    self_back[1] = [*[after(t, *sent) for t in self_back[1][:2]], self_back[1][2]]
     grad_q, grad_k, grad_v = zip(*self_back)
     group_a = Group(
         [(norm_one, *grad_q), (grad_o, *[o[0] for o in self_out])],
@@ -669,30 +698,34 @@
     )
     group_a.second(low_tok)
     out_tok = reorder([after(low_tok, *group_a.sent)], model_rows, dy, False)
-    grad_tokens = from_chips(out_tok)
-    group_a.third(out_tok, behind=[group_b.result])
-    sum_a, sum_b, sum_c = group_a.result, group_b.result, group_c.result
-
     dp_count = seq_count // 2
     gain_part = jnp.concatenate([gain_one, gain_two, gain_three])
-    gain_part = gain_part + swap_cores(gain_part)
-    low, high = (gain_part[:, n * D // 2 : (n + 1) * D // 2].reshape(3, dp_count // 2, model_rows) for n in range(2))
-    gain_part = jnp.stack([jnp.where(dy == 0, low, high), jnp.where(dy == 0, high, low)], axis=2)
-    gain_part = jnp.swapaxes(gain_part.reshape(3, dp_count, model_rows), 0, 1)
+    parts = [gain_part[:, n * D // 2 : (n + 1) * D // 2].reshape(3, dp_count // 2, model_rows) for n in range(2)]
+    gain_part = jnp.stack([jnp.where(dy == 0, *parts), jnp.where(dy == 0, *parts[::-1])], axis=2)
+    gain_part = jnp.swapaxes(gain_part.reshape(3, dp_count, model_rows), 0, 1).reshape(dp_count, -1)
     mx = lax.axis_index("mx")
-    tops = [jnp.where(mx == n, self_out[0][2], self_out[1][2]) for n in range(2)]
-    tops = jnp.broadcast_to(jnp.stack(tops)[None], (dp_count, 2, hc // DK))
-    small = jnp.concatenate(
-        [jnp.repeat(gain_part, 2, axis=0).reshape(dp_count * 2, -1), tops.reshape(dp_count * 2, -1)], axis=1
-    )
-    small = exchange(small)
-    red_gain = jnp.sum(small[:, : 3 * model_rows], axis=0).reshape(3, model_rows)
-    head_peak = jnp.max(small[:, 3 * model_rows :], axis=0)
+    tops = jnp.stack([jnp.where(mx == n, self_out[0][2], self_out[1][2]) for n in range(2)])
+    tops = jnp.broadcast_to(tops[None], (dp_count, *tops.shape)).reshape(seq_count, -1)
+    small = jnp.concatenate([*pieces(jnp.repeat(gain_part, 2, axis=0), 2), *pieces(tops, 3)], axis=1)
+    small = jnp.pad(small, ((0, 0), (0, D - small.shape[1])))[:, None]
+    sent = jnp.concatenate([out_tok.reshape(seq_count, block_rows, D), small], axis=1)
+    came = exchange(sent)
+    grad_tokens, small = came[:, :block_rows], came[:, block_rows].astype(f32)
+    group_a.third(out_tok, group_b.result)
+    sum_a, sum_b, sum_c = group_a.result, group_b.result, group_c.result
+
+    small = after(small, group_a.result)
+    wide = 3 * model_rows
+    red_gain = jnp.sum(small[:, :wide] + small[:, wide : 2 * wide], axis=0).reshape(3, model_rows)
+    red_gain = red_gain + swap_cores(red_gain)
+    tops = small[:, 2 * wide : 2 * wide + 3 * (hc // DK)].reshape(seq_count, 3, -1)
+    head_peak = jnp.max(tops[:, 0] + tops[:, 1] + tops[:, 2], axis=0)
 
     cut = lambda t, n: t[:, n * hc : (n + 1) * hc]
     red_in = jnp.stack([cut(t, n) for t in (sum_a, sum_b) for n in (0, 2, 3)])
     red_out = jnp.stack([cut(sum_a, 1).T, cut(sum_b, 1).T])
     red_ff = jnp.stack([sum_c[:, n * deep : n * deep + hidden] for n in (0, 2)])
+    red_in = row_major(red_in)
     red_out = with_layout_constraint(red_out, Layout(major_to_minor=(0, 1, 2)))
     red_ff = with_layout_constraint(red_ff, Layout(major_to_minor=(0, 2, 1)))
     red_down = with_layout_constraint(sum_c[:, deep : deep + hidden].T, Layout(major_to_minor=(0, 1)))

time: 730 us -> 661 us (0.905)
  Pallas kernels: 344 us -> 244 us
  local copies, waits for them, and re-layouts: 39.4 us -> 75.3 us
  starting transfers between devices: 97.2 us -> 74.5 us
    ppermute x10 -> x11, waiting for transfers between devices: 32.4 us -> 111 us  [swap_y(): return row_major(lax.ppermute(row_major(values), 'dy', swap))]
    all_gather x3, waiting for transfers between devices: 95.6 us -> 34 us  [gather_part(): return row_major(lax.all_gather(row_major(local), 'dz', axis=0, tiled=True))]
    unnamed x125 -> x370, local copies, waits for them, and re-layouts: 31.2 us -> 65.6 us
    ppermute x11, waiting for transfers between devices: 62.3 us -> 29.5 us  [swap_x(): return row_major(lax.ppermute(row_major(values), 'mx', swap))]
    pallas_call x14, Pallas kernels: 64.3 us -> 40.2 us  [combine(): pl.pallas_call(kernel, grid=(2,), in_specs=[spec((size, v.shape[1]), lamb...]
    pallas_call x15, Pallas kernels: 74 us -> 53.2 us  [weight_grad(): pl.pallas_call(kernel, grid=(steps,), in_specs=[columns] * first + [spec(...]
    all_to_all x7 -> x6, starting transfers between devices: 59.3 us -> 39.8 us  [exchange(): lax.all_to_all(values, chips, split_axis=0, concat_axis=0, tiled=True)]
    unnamed x9, waiting for transfers between devices: 15.1 us -> 33 us
  transfers between devices with their start and end apart: 56 -> 56, of which waited for: 16 -> 18; matrix products, arithmetic and copies ran while one was open for 4% -> 5% of each run, Pallas kernels for 42% -> 34%
where the time goes in v3:
time: 661 us; the launch traced here: 649 us
  Pallas kernels  244 us (37%)
  waiting for transfers between devices  212 us (32%)
  local copies, waits for them, and re-layouts  75.3 us (11%)
  starting transfers between devices  74.5 us (11%)
  other arithmetic  24.4 us (4%)
  between operations  18.7 us (3%)
    ppermute x11, waiting for transfers between devices, swap_y(): return row_major(lax.ppermute(row_major(values), 'dy', swap))  111 us
    unnamed x370, local copies, waits for them, and re-layouts  65.6 us
    pallas_call x15, Pallas kernels, weight_grad(): pl.pallas_call(kernel, grid=(steps,), in_specs=[columns] * first + [spec(...  53.2 us
    pallas_call x4, Pallas kernels, attend_back(): pl.pallas_call(functools.partial(attend_back_kernel, causal, size), grid=...  50.5 us
    pallas_call x9, Pallas kernels, project(): pl.pallas_call(kernel, grid=(4,), in_specs=[spec((size, width_all), lambd...  42.3 us
    pallas_call x14, Pallas kernels, combine(): pl.pallas_call(kernel, grid=(2,), in_specs=[spec((size, v.shape[1]), lamb...  40.2 us
    all_to_all x6, starting transfers between devices, exchange(): lax.all_to_all(values, chips, split_axis=0, concat_axis=0, tiled=True)  39.8 us
    pallas_call x4, Pallas kernels, attend(): pl.pallas_call(functools.partial(attend_kernel, causal, size), grid=(pair...  37.5 us
  transfers between devices with their start and end apart: 56, of which 18 were waited for; matrix products, arithmetic and copies ran while one was open for 5% of the time, Pallas kernels for 34%

profile of v3, /device:TPU:0, one launch (start us, length us, event | category | flops | bytes accessed | tf_op | source)
XLA Modules:
  0.0 648.9 jit_solution(15583687449672523216)
XLA Ops:
  12.8 31.1 %all-gather.4.cloned.1.call-done.refs_0_.refs_2_.refs_6_.refs_10_.refs_14_ = bf16[512,1152]{1,0:T(8,128)(2,1)} async-done(((bf16[128,1152]{1,0:T(8,128)(2,1)}), bf16[512,1152]{1,0:T(8,128)(2,1)}) %all-gather.4.cloned.1.call-update) | async-done | bytes 1179664 | tf_op jit(solution)/shard_map/all_gather | solution.py:472
  43.9 4.9 all-to-all-start
  52.4 35.3 %collective-permute-done.refs_1_.refs_3_.refs_7_.refs_11_.refs_15_ = bf16[512,1152]{1,0:T(8,128)(2,1)} collective-permute-done((bf16[512,1152]{1,0:T(8,128)(2,1)S(1)}, bf16[512,1152]{1,0:T(8,128)(2,1)}, u32[]{:S(2)}, u32[]{:S(2)}) %collective-permute-start) | collective-permute-done | bytes 1179680 | tf_op jit(solution)/shard_map/ppermute | solution.py:468
  99.6 4.5 project_plain.6.q_ref.k_ref.v_ref
  104.2 10.0 %attend.4 = (bf16[1024,256]{1,0:T(8,128)(2,1)S(1)}, f32[2,1024,2]{2,1,0:T(8,128)S(1)}, f32[2,8,128]{2,1,0:T(8,128)S(1)}) custom-call(bf16[1024,768]{1,0:T(8,128)(2,1)S(1)} %project_plain.6.q_ref.k_ref.v_ref, bf16[1024,768]{1,0:T(8,128)(2,1)S(1)} %project_plain.6.q_ref.k_ref.v_ref, bf16[1024,768]{1,0:T(8,128)(2,1)S(1)} %project_plain.6.q_ref.k_ref.v_ref, ...), custom_call_target="tpu_custom_call" | custom-call | flops 1 | bytes 1 | tf_op jit(solution)/shard_map/attend/pallas_call | solution.py:126
  117.9 4.5 project_plain.7.q_ref.k_ref.v_ref
  122.5 10.0 %attend.5 = (bf16[1024,256]{1,0:T(8,128)(2,1)S(1)}, f32[2,1024,2]{2,1,0:T(8,128)S(1)}, f32[2,8,128]{2,1,0:T(8,128)S(1)}) custom-call(bf16[1024,768]{1,0:T(8,128)(2,1)S(1)} %project_plain.7.q_ref.k_ref.v_ref, bf16[1024,768]{1,0:T(8,128)(2,1)S(1)} %project_plain.7.q_ref.k_ref.v_ref, bf16[1024,768]{1,0:T(8,128)(2,1)S(1)} %project_plain.7.q_ref.k_ref.v_ref, ...), custom_call_target="tpu_custom_call" | custom-call | flops 1 | bytes 1 | tf_op jit(solution)/shard_map/attend/pallas_call | solution.py:126
  134.3 4.0 collective-permute-done.8.refs_2_.refs_6_.refs_4_.refs_10_
  142.1 4.8 all-to-all-start.1
  147.0 25.3 %collective-permute-done.9.refs_3_.refs_7_.refs_5_.refs_11_ = bf16[512,1024]{1,0:T(8,128)(2,1)S(1)} collective-permute-done((bf16[512,1024]{1,0:T(8,128)(2,1)S(1)}, bf16[512,1024]{1,0:T(8,128)(2,1)S(1)}, u32[]{:S(2)}, u32[]{:S(2)}) %collective-permute-start.9) | collective-permute-done | bytes 1048608 | tf_op jit(solution)/shard_map/ppermute | solution.py:468
  188.6 3.4 reorder.7.own_ref.refs_0_.refs_4_
  192.4 5.6 all-to-all-start.2
  201.8 3.8 project_plain.8
  205.7 5.0 project_plain.9
  210.7 8.8 %attend.7 = (bf16[1024,256]{1,0:T(8,128)(2,1)S(1)}, f32[2,1024,2]{2,1,0:T(8,128)S(1)}, f32[2,8,128]{2,1,0:T(8,128)}) custom-call(bf16[1024,256]{1,0:T(8,128)(2,1)S(1)} %get-tuple-element.160.q_ref, bf16[1024,256]{1,0:T(8,128)(2,1)S(1)} %get-tuple-element.167.k_ref, bf16[1024,256]{1,0:T(8,128)(2,1)S(1)} %get-tuple-element.168.v_ref, ...), custom_call_target="tpu_custom_call" | custom-call | flops 1 | bytes 1 | tf_op jit(solution)/shard_map/attend/pallas_call | solution.py:126
  220.5 12.7 %collective-permute-done.10.refs_1_.refs_3_.refs_5_.refs_9_ = bf16[512,2304]{1,0:T(8,128)(2,1)S(1)} collective-permute-done((bf16[512,2304]{1,0:T(8,128)(2,1)}, bf16[512,2304]{1,0:T(8,128)(2,1)S(1)}, u32[]{:S(2)}, u32[]{:S(2)}) %collective-permute-start.10) | collective-permute-done | bytes 2359328 | tf_op jit(solution)/shard_map/ppermute | solution.py:468
  233.9 8.8 %attend.6 = (bf16[1024,256]{1,0:T(8,128)(2,1)S(1)}, f32[2,1024,2]{2,1,0:T(8,128)S(1)}, f32[2,8,128]{2,1,0:T(8,128)}) custom-call(bf16[1024,256]{1,0:T(8,128)(2,1)S(1)} %get-tuple-element.162.q_ref, bf16[1024,256]{1,0:T(8,128)(2,1)S(1)} %get-tuple-element.164.k_ref, bf16[1024,256]{1,0:T(8,128)(2,1)S(1)} %get-tuple-element.165.v_ref, ...), custom_call_target="tpu_custom_call" | custom-call | flops 1 | bytes 1 | tf_op jit(solution)/shard_map/attend/pallas_call | solution.py:126
  259.6 5.8 project_gelu.2
  265.4 17.9 %collective-permute-done.18.refs_1_.refs_3_.refs_7_.refs_11_ = bf16[512,1536]{1,0:T(8,128)(2,1)} collective-permute-done((bf16[512,1536]{1,0:T(8,128)(2,1)}, bf16[512,1536]{1,0:T(8,128)(2,1)}, u32[]{:S(2)}, u32[]{:S(2)}) %collective-permute-start.18) | collective-permute-done | bytes 1572896 | tf_op jit(solution)/shard_map/ppermute | solution.py:464
  283.3 6.6 %project_gelu.3 = (bf16[1024,768]{1,0:T(8,128)(2,1)S(1)}, bf16[1024,768]{1,0:T(8,128)(2,1)S(1)}, bf16[1024,768]{1,0:T(8,128)(2,1)S(1)}) custom-call(bf16[512,1024]{1,0:T(8,128)(2,1)} %get-tuple-element.175.own_ref.refs_0_, bf16[512,1024]{1,0:T(8,128)(2,1)} %collective-permute-done.17.other_ref.refs_1_, ...), custom_call_target="tpu_custom_call" | custom-call | flops 1 | bytes 1 | tf_op jit(solution)/shard_map/project_gelu/pallas_call | solution.py:292
  289.9 5.6 project_scale.1
  295.5 5.7 weight_grad.15
  305.6 5.7 combine.19
  312.3 5.7 combine.18
  320.7 3.6 combine.21
  324.9 3.5 combine.20
  332.6 12.7 %attend_back.4 = (bf16[1024,256]{1,0:T(8,128)(2,1)S(1)}, bf16[1024,256]{1,0:T(8,128)(2,1)S(1)}, bf16[1024,256]{1,0:T(8,128)(2,1)S(1)}) custom-call(bf16[1024,256]{1,0:T(8,128)(2,1)S(1)} %copy-done.130, bf16[1024,256]{1,0:T(8,128)(2,1)S(1)} %copy-done.132, bf16[1024,256]{1,0:T(8,128)(2,1)S(1)} %copy-done.134, s32[1024,1]{1,0:T(8,128)S(1)} %copy-done.26, ...), custom_call_target="tpu_custom_call" | custom-call | flops 1 | bytes 1 | tf_op jit(solution)/shard_map/attend_back/pallas_call | solution.py:156
  348.3 13.1 %attend_back.5 = (bf16[1024,256]{1,0:T(8,128)(2,1)S(1)}, bf16[1024,256]{1,0:T(8,128)(2,1)S(1)}, bf16[1024,256]{1,0:T(8,128)(2,1)S(1)}) custom-call(bf16[1024,256]{1,0:T(8,128)(2,1)S(1)} %copy-done.124, bf16[1024,256]{1,0:T(8,128)(2,1)S(1)} %copy-done.126, bf16[1024,256]{1,0:T(8,128)(2,1)S(1)} %copy-done.128, s32[1024,1]{1,0:T(8,128)S(1)} %copy-done.26, ...), custom_call_target="tpu_custom_call" | custom-call | flops 1 | bytes 1 | tf_op jit(solution)/shard_map/attend_back/pallas_call | solution.py:156
  362.2 3.5 weight_grad.18
  365.7 4.9 collective-permute-done.24.refs_6_.refs_7_
  370.6 3.8 weight_grad.17
  377.0 7.6 %all-to-all-start.3 = ((bf16[16,32,1024]{2,1,0:T(8,128)(2,1)}), bf16[16,32,1024]{2,1,0:T(8,128)(2,1)}, u32[]{:S(2)}, u32[]{:S(2)}) async-start(bf16[16,32,1024]{2,1,0:T(8,128)(2,1)} %bitcast.104), calls=%async_computation.3 | async-start | bytes 2097152 | tf_op jit(solution)/shard_map/all_to_all | solution.py:558
  410.4 4.2 project_plain.11
  416.6 12.2 %attend_back.6 = (bf16[1024,256]{1,0:T(8,128)(2,1)S(1)}, bf16[1024,256]{1,0:T(8,128)(2,1)S(1)}, bf16[1024,256]{1,0:T(8,128)(2,1)S(1)}) custom-call(bf16[1024,768]{1,0:T(8,128)(2,1)S(1)} %copy-done.23, bf16[1024,768]{1,0:T(8,128)(2,1)S(1)} %copy-done.23, bf16[1024,768]{1,0:T(8,128)(2,1)S(1)} %copy-done.23, s32[1024,1]{1,0:T(8,128)S(1)} %copy-done.27, ...), custom_call_target="tpu_custom_call" | custom-call | flops 1 | bytes 1 | tf_op jit(solution)/shard_map/attend_back/pallas_call | solution.py:156
  432.0 4.7 weight_grad.21
  438.2 5.7 all-to-all-start.4
  449.7 12.4 %attend_back.7 = (bf16[1024,256]{1,0:T(8,128)(2,1)S(1)}, bf16[1024,256]{1,0:T(8,128)(2,1)S(1)}, bf16[1024,256]{1,0:T(8,128)(2,1)S(1)}) custom-call(bf16[1024,768]{1,0:T(8,128)(2,1)S(1)} %copy-done.21, bf16[1024,768]{1,0:T(8,128)(2,1)S(1)} %copy-done.21, bf16[1024,768]{1,0:T(8,128)(2,1)S(1)} %copy-done.21, s32[1024,1]{1,0:T(8,128)S(1)} %copy-done.27, ...), custom_call_target="tpu_custom_call" | custom-call | flops 1 | bytes 1 | tf_op jit(solution)/shard_map/attend_back/pallas_call | solution.py:156
  462.1 15.0 %collective-permute-done.34.refs_4_.refs_12_ = bf16[512,1024]{1,0:T(8,128)(2,1)S(1)} collective-permute-done((bf16[512,1024]{1,0:T(8,128)(2,1)}, bf16[512,1024]{1,0:T(8,128)(2,1)S(1)}, u32[]{:S(2)}, u32[]{:S(2)}) %collective-permute-start.34) | collective-permute-done | bytes 1048608 | tf_op jit(solution)/shard_map/ppermute | solution.py:468
  484.8 3.5 weight_grad.25
  488.3 3.9 weight_grad.24
  498.5 4.5 combine.27
  513.0 4.1 combine.26
  519.1 21.1 %collective-permute-done.35.refs_11_ = bf16[512,512]{1,0:T(8,128)(2,1)} collective-permute-done((bf16[512,512]{1,0:T(8,128)(2,1)}, bf16[512,512]{1,0:T(8,128)(2,1)}, u32[]{:S(2)}, u32[]{:S(2)}) %collective-permute-start.35) | collective-permute-done | bytes 524320 | tf_op jit(solution)/shard_map/ppermute | solution.py:468
  540.2 4.2 weight_grad.26
  563.1 11.1 %all-to-all-start.5 = ((bf16[16,33,1024]{2,1,0:T(8,128)(2,1)}), bf16[16,33,1024]{2,1,0:T(8,128)(2,1)}, u32[]{:S(2)}, u32[]{:S(2)}) async-start(bf16[16,33,1024]{2,1,0:T(8,128)(2,1)} %pad_maximum_fusion), calls=%async_computation.5 | async-start | bytes 2621440 | tf_op jit(solution)/shard_map/all_to_all | solution.py:558
  577.7 18.0 %reduce-scatter.12.cloned.1.call-done = bf16[128,1024]{1,0:T(8,128)(2,1)} async-done(((bf16[512,1024]{1,0:T(8,128)(2,1)}), bf16[128,1024]{1,0:T(8,128)(2,1)}) %reduce-scatter.12.cloned.1.call-update) | async-done | bytes 262160
  597.6 4.6 weight_grad.29
  618.6 14.9 %reduce-scatter.14.cloned.1.call-done = bf16[128,1024]{1,0:T(8,128)(2,1)} async-done(((bf16[512,1024]{1,0:T(8,128)(2,1)}), bf16[128,1024]{1,0:T(8,128)(2,1)}) %reduce-scatter.14.cloned.1.call-update) | async-done | bytes 262160
  (572 shorter events, 198.0 us)
Async XLA Ops:
  7.2 36.7 %all-gather.4.cloned.1.call-start = ((), (), s32[]{:S(2)}) async-start(), calls=%async_computation.9 | async-start | bytes 1474560 | tf_op jit(solution)/shard_map/all_gather | solution.py:472
  10.6 82.3 %all-gather.6.cloned.1.call-start = ((), (), s32[]{:S(2)}) async-start(), calls=%async_computation.10 | async-start | bytes 1310720 | tf_op jit(solution)/shard_map/all_gather | solution.py:472
  11.4 130.6 %all-gather.8.cloned.1.call-start = ((), (), s32[]{:S(2)}) async-start(), calls=%async_computation.11 | async-start | bytes 2949120 | tf_op jit(solution)/shard_map/all_gather | solution.py:472
  43.9 46.3 %all-to-all-start = ((bf16[16,32,1024]{2,1,0:T(8,128)(2,1)}), bf16[16,32,1024]{2,1,0:T(8,128)(2,1)S(1)}, u32[]{:S(2)}, u32[]{:S(2)}) async-start(bf16[16,32,1024]{2,1,0:T(8,128)(2,1)} %param.20), calls=%async_computation | async-start | bytes 2097152 | tf_op jit(solution)/shard_map/all_to_all | solution.py:558
  48.8 38.9 %collective-permute-start = (bf16[512,1152]{1,0:T(8,128)(2,1)S(1)}, bf16[512,1152]{1,0:T(8,128)(2,1)}, u32[]{:S(2)}, u32[]{:S(2)}) collective-permute-start(bf16[512,1152]{1,0:T(8,128)(2,1)S(1)} %copy-done.17), channel_id=1, source_target_pairs={{0,4},{4,0},{1,5},{5,1},{2,6},{6,2},{3,7},{7,3},{8,12},{12,8},{9,1... | collective-permute-start | bytes 3538952 | tf_op jit(solution)/shard_map/ppermute | solution.py:468
  50.9 65.0 %collective-permute-start.2 = (bf16[512,1152]{1,0:T(8,128)(2,1)S(1)}, bf16[512,1152]{1,0:T(8,128)(2,1)}, u32[]{:S(2)}, u32[]{:S(2)}) collective-permute-start(bf16[512,1152]{1,0:T(8,128)(2,1)S(1)} %copy-done.17), channel_id=1, source_target_pairs={{0,2},{2,0},{1,3},{3,1},{4,6},{6,4},{5,7},{7,5},{8,10},{10,8},{9,1... | collective-permute-start | bytes 3538952 | tf_op jit(solution)/shard_map/ppermute | solution.py:464
  88.7 29.2 %collective-permute-start.3 = (bf16[512,1152]{1,0:T(8,128)(2,1)}, bf16[512,1152]{1,0:T(8,128)(2,1)}, u32[]{:S(2)}, u32[]{:S(2)}) collective-permute-start(bf16[512,1152]{1,0:T(8,128)(2,1)} %collective-permute-done.refs_1_.refs_3_.refs_7_.refs_11_.refs_15_), channel_id=1, source_target_pairs={{0,2},{2,0},{1,3},{3,1},{4,6},{6,4},{5,7},{7,5},{8,10},{10,8},{9,1... | collective-permute-start | bytes 3538952 | tf_op jit(solution)/shard_map/ppermute | solution.py:464
  92.9 6.7 %collective-permute-start.1 = (bf16[512,1024]{1,0:T(8,128)(2,1)}, bf16[512,1024]{1,0:T(8,128)(2,1)}, u32[]{:S(2)}, u32[]{:S(2)}) collective-permute-start(bf16[512,1024]{1,0:T(8,128)(2,1)} %add_norm.3.own_ref.refs_0_), channel_id=1, source_target_pairs={{0,1},{1,0},{2,3},{3,2},{4,5},{5,4},{6,7},{7,6},{8,9},{9,8},{10,11... | collective-permute-start | bytes 3145736 | tf_op jit(solution)/shard_map/ppermute | solution.py:460
  92.9 41.4 %collective-permute-start.7 = (bf16[512,1024]{1,0:T(8,128)(2,1)}, bf16[512,1024]{1,0:T(8,128)(2,1)S(1)}, u32[]{:S(2)}, u32[]{:S(2)}) collective-permute-start(bf16[512,1024]{1,0:T(8,128)(2,1)} %all-gather.6.cloned.1.call-done.refs_0_.refs_4_.refs_2_.refs_8_), channel_id=1, source_target_pairs={{0,4},{4,0},{1,5},{5,1},{2,6},{6,2},{3,7},{7,3},{8,12},{12,8},{9,1... | collective-permute-start | bytes 3145736 | tf_op jit(solution)/shard_map/ppermute | solution.py:468
  94.8 43.5 %collective-permute-start.8 = (bf16[512,1024]{1,0:T(8,128)(2,1)}, bf16[512,1024]{1,0:T(8,128)(2,1)S(1)}, u32[]{:S(2)}, u32[]{:S(2)}) collective-permute-start(bf16[512,1024]{1,0:T(8,128)(2,1)} %all-gather.6.cloned.1.call-done.refs_0_.refs_4_.refs_2_.refs_8_), channel_id=1, source_target_pairs={{0,2},{2,0},{1,3},{3,1},{4,6},{6,4},{5,7},{7,5},{8,10},{10,8},{9,1... | collective-permute-start | bytes 3145736 | tf_op jit(solution)/shard_map/ppermute | solution.py:464
  138.3 34.0 %collective-permute-start.9 = (bf16[512,1024]{1,0:T(8,128)(2,1)S(1)}, bf16[512,1024]{1,0:T(8,128)(2,1)S(1)}, u32[]{:S(2)}, u32[]{:S(2)}) collective-permute-start(bf16[512,1024]{1,0:T(8,128)(2,1)S(1)} %collective-permute-done.8.refs_2_.refs_6_.refs_4_.refs_10_), channel_id=1, source_target_pairs={{0,4},{4,0},{1,5},{5,1},{2,6},{6,2},{3,7},{7,3},{8,12},{12,8},{9,1... | collective-permute-start | bytes 3145736 | tf_op jit(solution)/shard_map/ppermute | solution.py:468
  142.1 46.5 %all-to-all-start.1 = ((bf16[16,32,1024]{2,1,0:T(8,128)(2,1)}), bf16[16,32,1024]{2,1,0:T(8,128)(2,1)}, u32[]{:S(2)}, u32[]{:S(2)}) async-start(bf16[16,32,1024]{2,1,0:T(8,128)(2,1)} %param.21), calls=%async_computation.1 | async-start | bytes 2097152 | tf_op jit(solution)/shard_map/all_to_all | solution.py:558
  173.2 60.0 %collective-permute-start.10 = (bf16[512,2304]{1,0:T(8,128)(2,1)}, bf16[512,2304]{1,0:T(8,128)(2,1)S(1)}, u32[]{:S(2)}, u32[]{:S(2)}) collective-permute-start(bf16[512,2304]{1,0:T(8,128)(2,1)} %all-gather.8.cloned.1.call-done.refs_0_.refs_2_.refs_4_.refs_8_), channel_id=1, source_target_pairs={{0,4},{4,0},{1,5},{5,1},{2,6},{6,2},{3,7},{7,3},{8,12},{12,8},{9,1... | collective-permute-start | bytes 7077896 | tf_op jit(solution)/shard_map/ppermute | solution.py:468
  175.0 58.9 %collective-permute-start.11 = (bf16[512,2304]{1,0:T(8,128)(2,1)}, bf16[512,2304]{1,0:T(8,128)(2,1)}, u32[]{:S(2)}, u32[]{:S(2)}) collective-permute-start(bf16[512,2304]{1,0:T(8,128)(2,1)} %all-gather.8.cloned.1.call-done.refs_0_.refs_2_.refs_4_.refs_8_), channel_id=1, source_target_pairs={{0,2},{2,0},{1,3},{3,1},{4,6},{6,4},{5,7},{7,5},{8,10},{10,8},{9,1... | collective-permute-start | bytes 7077896 | tf_op jit(solution)/shard_map/ppermute | solution.py:464
  188.5 9.6 %collective-permute-start.6 = (bf16[512,1024]{1,0:T(8,128)(2,1)}, bf16[512,1024]{1,0:T(8,128)(2,1)}, u32[]{:S(2)}, u32[]{:S(2)}) collective-permute-start(bf16[512,1024]{1,0:T(8,128)(2,1)} %get-tuple-element.157.own_ref.refs_0_), channel_id=1, source_target_pairs={{0,1},{1,0},{2,3},{3,2},{4,5},{5,4},{6,7},{7,6},{8,9},{9,8},{10,11... | collective-permute-start | bytes 3145736 | tf_op jit(solution)/shard_map/ppermute | solution.py:460
  192.0 13.6 %collective-permute-start.12 = (bf16[512,1024]{1,0:T(8,128)(2,1)}, bf16[512,1024]{1,0:T(8,128)(2,1)}, u32[]{:S(2)}, u32[]{:S(2)}) collective-permute-start(bf16[512,1024]{1,0:T(8,128)(2,1)} %reorder.7.own_ref.refs_0_.refs_4_), channel_id=1, source_target_pairs={{0,1},{1,0},{2,3},{3,2},{4,5},{5,4},{6,7},{7,6},{8,9},{9,8},{10,11... | collective-permute-start | bytes 3145736 | tf_op jit(solution)/shard_map/ppermute | solution.py:460
  192.4 61.1 %all-to-all-start.2 = ((bf16[16,32,1024]{2,1,0:T(8,128)(2,1)}), bf16[16,32,1024]{2,1,0:T(8,128)(2,1)}, u32[]{:S(2)}, u32[]{:S(2)}) async-start(bf16[16,32,1024]{2,1,0:T(8,128)(2,1)} %param.22), calls=%async_computation.2 | async-start | bytes 2097152 | tf_op jit(solution)/shard_map/all_to_all | solution.py:558
  246.6 36.7 %collective-permute-start.18 = (bf16[512,1536]{1,0:T(8,128)(2,1)}, bf16[512,1536]{1,0:T(8,128)(2,1)}, u32[]{:S(2)}, u32[]{:S(2)}) collective-permute-start(bf16[512,1536]{1,0:T(8,128)(2,1)} %slice.156), channel_id=1, source_target_pairs={{0,2},{2,0},{1,3},{3,1},{4,6},{6,4},{5,7},{7,5},{8,10},{10,8},{9,1... | collective-permute-start | bytes 4718600 | tf_op jit(solution)/shard_map/ppermute | solution.py:464
  257.2 32.7 %collective-permute-start.15 = (bf16[512,1024]{1,0:T(8,128)(2,1)S(1)}, bf16[512,1024]{1,0:T(8,128)(2,1)S(1)}, u32[]{:S(2)}, u32[]{:S(2)}) collective-permute-start(bf16[512,1024]{1,0:T(8,128)(2,1)S(1)} %reorder.8.own_ref.refs_2_.base_ref), channel_id=1, source_target_pairs={{0,1},{1,0},{2,3},{3,2},{4,5},{5,4},{6,7},{7,6},{8,9},{9,8},{10,11... | collective-permute-start | bytes 3145736 | tf_op jit(solution)/shard_map/ppermute | solution.py:460
  259.0 30.9 %collective-permute-start.16 = (bf16[512,768]{1,0:T(8,128)(2,1)S(1)}, bf16[512,768]{1,0:T(8,128)(2,1)S(1)}, u32[]{:S(2)}, u32[]{:S(2)}) collective-permute-start(bf16[512,768]{1,0:T(8,128)(2,1)S(1)} %slice.155), channel_id=1, source_target_pairs={{0,4},{4,0},{1,5},{5,1},{2,6},{6,2},{3,7},{7,3},{8,12},{12,8},{9,1... | collective-permute-start | bytes 2359304 | tf_op jit(solution)/shard_map/ppermute | solution.py:468
  301.2 69.3 %collective-permute-start.24 = (bf16[1024,1536]{1,0:T(8,128)(2,1)S(1)}, bf16[1024,1536]{1,0:T(8,128)(2,1)S(1)}, u32[]{:S(2)}, u32[]{:S(2)}) collective-permute-start(bf16[1024,1536]{1,0:T(8,128)(2,1)S(1)} %weight_grad.15), channel_id=1, source_target_pairs={{0,2},{2,0},{1,3},{3,1},{4,6},{6,4},{5,7},{7,5},{8,10},{10,8},{9,1... | collective-permute-start | bytes 9437192 | tf_op jit(solution)/shard_map/ppermute | solution.py:464
  311.3 6.7 %collective-permute-start.19 = (f32[512,512]{1,0:T(8,128)S(1)}, f32[512,512]{1,0:T(8,128)S(1)}, u32[]{:S(2)}, u32[]{:S(2)}) collective-permute-start(f32[512,512]{1,0:T(8,128)S(1)} %get-tuple-element.188), channel_id=1, source_target_pairs={{0,1},{1,0},{2,3},{3,2},{4,5},{5,4},{6,7},{7,6},{8,9},{9,8},{10,11... | collective-permute-start | bytes 3145736 | tf_op jit(solution)/shard_map/ppermute | solution.py:460
  311.4 6.6 %collective-permute-start.20 = (f32[512,512]{1,0:T(8,128)S(1)}, f32[512,512]{1,0:T(8,128)S(1)}, u32[]{:S(2)}, u32[]{:S(2)}) collective-permute-start(f32[512,512]{1,0:T(8,128)S(1)} %get-tuple-element.189), channel_id=1, source_target_pairs={{0,1},{1,0},{2,3},{3,2},{4,5},{5,4},{6,7},{7,6},{8,9},{9,8},{10,11... | collective-permute-start | bytes 3145736 | tf_op jit(solution)/shard_map/ppermute | solution.py:460
  311.8 36.4 %collective-permute-start.25 = (bf16[512,1536]{1,0:T(8,128)(2,1)S(1)}, bf16[512,1536]{1,0:T(8,128)(2,1)S(1)}, u32[]{:S(2)}, u32[]{:S(2)}) collective-permute-start(bf16[512,1536]{1,0:T(8,128)(2,1)S(1)} %weight_grad.16), channel_id=1, source_target_pairs={{0,4},{4,0},{1,5},{5,1},{2,6},{6,2},{3,7},{7,3},{8,12},{12,8},{9,1... | collective-permute-start | bytes 4718600 | tf_op jit(solution)/shard_map/ppermute | solution.py:468
  320.7 7.6 %collective-permute-start.21 = (bf16[512,1024]{1,0:T(8,128)(2,1)S(1)}, bf16[512,1024]{1,0:T(8,128)(2,1)S(1)}, u32[]{:S(2)}, u32[]{:S(2)}) collective-permute-start(bf16[512,1024]{1,0:T(8,128)(2,1)S(1)} %get-tuple-element.194.own_ref.refs_2_), channel_id=1, source_target_pairs={{0,1},{1,0},{2,3},{3,2},{4,5},{5,4},{6,7},{7,6},{8,9},{9,8},{10,11... | collective-permute-start | bytes 3145736 | tf_op jit(solution)/shard_map/ppermute | solution.py:460
  324.3 6.4 collective-permute-start.22
  376.4 25.2 %collective-permute-start.26 = (f32[512,512]{1,0:T(8,128)}, f32[512,512]{1,0:T(8,128)}, u32[]{:S(2)}, u32[]{:S(2)}) collective-permute-start(f32[512,512]{1,0:T(8,128)} %get-tuple-element.215), channel_id=1, source_target_pairs={{0,1},{1,0},{2,3},{3,2},{4,5},{5,4},{6,7},{7,6},{8,9},{9,8},{10,11... | collective-permute-start | bytes 3145736 | tf_op jit(solution)/shard_map/ppermute | solution.py:460
  376.5 25.2 %collective-permute-start.27 = (f32[512,512]{1,0:T(8,128)}, f32[512,512]{1,0:T(8,128)}, u32[]{:S(2)}, u32[]{:S(2)}) collective-permute-start(f32[512,512]{1,0:T(8,128)} %get-tuple-element.221), channel_id=1, source_target_pairs={{0,1},{1,0},{2,3},{3,2},{4,5},{5,4},{6,7},{7,6},{8,9},{9,8},{10,11... | collective-permute-start | bytes 3145736 | tf_op jit(solution)/shard_map/ppermute | solution.py:460
  377.0 33.3 %all-to-all-start.3 = ((bf16[16,32,1024]{2,1,0:T(8,128)(2,1)}), bf16[16,32,1024]{2,1,0:T(8,128)(2,1)}, u32[]{:S(2)}, u32[]{:S(2)}) async-start(bf16[16,32,1024]{2,1,0:T(8,128)(2,1)} %bitcast.104), calls=%async_computation.3 | async-start | bytes 2097152 | tf_op jit(solution)/shard_map/all_to_all | solution.py:558
  384.6 167.3 %reduce-scatter.10.cloned.1.call-start = ((), (), s32[]{:S(2)}) async-start(), calls=%async_computation.12 | async-start | bytes 2949120
  384.7 47.3 %collective-permute-start.31 = (bf16[512,1536]{1,0:T(8,128)(2,1)}, bf16[512,1536]{1,0:T(8,128)(2,1)}, u32[]{:S(2)}, u32[]{:S(2)}) collective-permute-start(bf16[512,1536]{1,0:T(8,128)(2,1)} %copy-done.137), channel_id=1, source_target_pairs={{0,4},{4,0},{1,5},{5,1},{2,6},{6,2},{3,7},{7,3},{8,12},{12,8},{9,1... | collective-permute-start | bytes 4718600 | tf_op jit(solution)/shard_map/ppermute | solution.py:468
  398.1 10.7 %collective-permute-start.28 = (f32[512,512]{1,0:T(8,128)S(1)}, f32[512,512]{1,0:T(8,128)S(1)}, u32[]{:S(2)}, u32[]{:S(2)}) collective-permute-start(f32[512,512]{1,0:T(8,128)S(1)} %get-tuple-element.226), channel_id=1, source_target_pairs={{0,1},{1,0},{2,3},{3,2},{4,5},{5,4},{6,7},{7,6},{8,9},{9,8},{10,11... | collective-permute-start | bytes 3145736 | tf_op jit(solution)/shard_map/ppermute | solution.py:460
  398.2 10.7 %collective-permute-start.29 = (f32[512,512]{1,0:T(8,128)S(1)}, f32[512,512]{1,0:T(8,128)S(1)}, u32[]{:S(2)}, u32[]{:S(2)}) collective-permute-start(f32[512,512]{1,0:T(8,128)S(1)} %get-tuple-element.228), channel_id=1, source_target_pairs={{0,1},{1,0},{2,3},{3,2},{4,5},{5,4},{6,7},{7,6},{8,9},{9,8},{10,11... | collective-permute-start | bytes 3145736 | tf_op jit(solution)/shard_map/ppermute | solution.py:460
  407.4 23.9 %collective-permute-start.32 = (bf16[512,768]{1,0:T(8,128)(2,1)}, bf16[512,768]{1,0:T(8,128)(2,1)}, u32[]{:S(2)}, u32[]{:S(2)}) collective-permute-start(bf16[512,768]{1,0:T(8,128)(2,1)} %weight_grad.18), channel_id=1, source_target_pairs={{0,2},{2,0},{1,3},{3,1},{4,6},{6,4},{5,7},{7,5},{8,10},{10,8},{9,1... | collective-permute-start | bytes 2359304 | tf_op jit(solution)/shard_map/ppermute | solution.py:464
  438.2 54.0 %all-to-all-start.4 = ((bf16[16,32,1024]{2,1,0:T(8,128)(2,1)}), bf16[16,32,1024]{2,1,0:T(8,128)(2,1)}, u32[]{:S(2)}, u32[]{:S(2)}) async-start(bf16[16,32,1024]{2,1,0:T(8,128)(2,1)} %bitcast.105), calls=%async_computation.4 | async-start | bytes 2097152 | tf_op jit(solution)/shard_map/all_to_all | solution.py:558
  443.9 151.7 %reduce-scatter.12.cloned.1.call-start = ((), (), s32[]{:S(2)}) async-start(), calls=%async_computation.13 | async-start | bytes 1310720
  444.0 33.1 %collective-permute-start.34 = (bf16[512,1024]{1,0:T(8,128)(2,1)}, bf16[512,1024]{1,0:T(8,128)(2,1)S(1)}, u32[]{:S(2)}, u32[]{:S(2)}) collective-permute-start(bf16[512,1024]{1,0:T(8,128)(2,1)} %copy-done.138), channel_id=1, source_target_pairs={{0,4},{4,0},{1,5},{5,1},{2,6},{6,2},{3,7},{7,3},{8,12},{12,8},{9,1... | collective-permute-start | bytes 3145736 | tf_op jit(solution)/shard_map/ppermute | solution.py:468
  445.9 34.3 %collective-permute-start.33 = (bf16[1024,512]{1,0:T(8,128)(2,1)}, bf16[1024,512]{1,0:T(8,128)(2,1)S(1)}, u32[]{:S(2)}, u32[]{:S(2)}) collective-permute-start(bf16[1024,512]{1,0:T(8,128)(2,1)} %copy-done.151), channel_id=1, source_target_pairs={{0,2},{2,0},{1,3},{3,1},{4,6},{6,4},{5,7},{7,5},{8,10},{10,8},{9,1... | collective-permute-start | bytes 3145736 | tf_op jit(solution)/shard_map/ppermute | solution.py:464
  480.3 25.4 %collective-permute-start.36 = (bf16[512,512]{1,0:T(8,128)(2,1)}, bf16[512,512]{1,0:T(8,128)(2,1)}, u32[]{:S(2)}, u32[]{:S(2)}) collective-permute-start(bf16[512,512]{1,0:T(8,128)(2,1)} %weight_grad.23), channel_id=1, source_target_pairs={{0,2},{2,0},{1,3},{3,1},{4,6},{6,4},{5,7},{7,5},{8,10},{10,8},{9,1... | collective-permute-start | bytes 1572872 | tf_op jit(solution)/shard_map/ppermute | solution.py:464
  503.0 41.4 %collective-permute-start.37 = (f32[512,512]{1,0:T(8,128)}, f32[512,512]{1,0:T(8,128)}, u32[]{:S(2)}, u32[]{:S(2)}) collective-permute-start(f32[512,512]{1,0:T(8,128)} %get-tuple-element.252), channel_id=1, source_target_pairs={{0,1},{1,0},{2,3},{3,2},{4,5},{5,4},{6,7},{7,6},{8,9},{9,8},{10,11... | collective-permute-start | bytes 3145736 | tf_op jit(solution)/shard_map/ppermute | solution.py:460
  503.0 41.4 %collective-permute-start.38 = (f32[512,512]{1,0:T(8,128)}, f32[512,512]{1,0:T(8,128)}, u32[]{:S(2)}, u32[]{:S(2)}) collective-permute-start(f32[512,512]{1,0:T(8,128)} %get-tuple-element.253), channel_id=1, source_target_pairs={{0,1},{1,0},{2,3},{3,2},{4,5},{5,4},{6,7},{7,6},{8,9},{9,8},{10,11... | collective-permute-start | bytes 3145736 | tf_op jit(solution)/shard_map/ppermute | solution.py:460
  503.5 50.9 %collective-permute-start.40 = (bf16[512,1024]{1,0:T(8,128)(2,1)}, bf16[512,1024]{1,0:T(8,128)(2,1)}, u32[]{:S(2)}, u32[]{:S(2)}) collective-permute-start(bf16[512,1024]{1,0:T(8,128)(2,1)} %weight_grad.25), channel_id=1, source_target_pairs={{0,4},{4,0},{1,5},{5,1},{2,6},{6,2},{3,7},{7,3},{8,12},{12,8},{9,1... | collective-permute-start | bytes 3145736 | tf_op jit(solution)/shard_map/ppermute | solution.py:468
  504.9 53.2 %collective-permute-start.39 = (bf16[1024,512]{1,0:T(8,128)(2,1)}, bf16[1024,512]{1,0:T(8,128)(2,1)}, u32[]{:S(2)}, u32[]{:S(2)}) collective-permute-start(bf16[1024,512]{1,0:T(8,128)(2,1)} %weight_grad.24), channel_id=1, source_target_pairs={{0,2},{2,0},{1,3},{3,1},{4,6},{6,4},{5,7},{7,5},{8,10},{10,8},{9,1... | collective-permute-start | bytes 3145736 | tf_op jit(solution)/shard_map/ppermute | solution.py:464
  505.6 34.5 %collective-permute-start.35 = (bf16[512,512]{1,0:T(8,128)(2,1)}, bf16[512,512]{1,0:T(8,128)(2,1)}, u32[]{:S(2)}, u32[]{:S(2)}) collective-permute-start(bf16[512,512]{1,0:T(8,128)(2,1)} %weight_grad.22), channel_id=1, source_target_pairs={{0,4},{4,0},{1,5},{5,1},{2,6},{6,2},{3,7},{7,3},{8,12},{12,8},{9,1... | collective-permute-start | bytes 1572872 | tf_op jit(solution)/shard_map/ppermute | solution.py:468
  563.1 47.6 %all-to-all-start.5 = ((bf16[16,33,1024]{2,1,0:T(8,128)(2,1)}), bf16[16,33,1024]{2,1,0:T(8,128)(2,1)}, u32[]{:S(2)}, u32[]{:S(2)}) async-start(bf16[16,33,1024]{2,1,0:T(8,128)(2,1)} %pad_maximum_fusion), calls=%async_computation.5 | async-start | bytes 2621440 | tf_op jit(solution)/shard_map/all_to_all | solution.py:558
  574.2 59.3 %reduce-scatter.14.cloned.1.call-start = ((), (), s32[]{:S(2)}) async-start(), calls=%async_computation.14 | async-start | bytes 1310720
  574.3 23.3 %collective-permute-start.42 = (bf16[512,512]{1,0:T(8,128)(2,1)S(1)}, bf16[512,512]{1,0:T(8,128)(2,1)S(1)}, u32[]{:S(2)}, u32[]{:S(2)}) collective-permute-start(bf16[512,512]{1,0:T(8,128)(2,1)S(1)} %copy-done.155), channel_id=1, source_target_pairs={{0,2},{2,0},{1,3},{3,1},{4,6},{6,4},{5,7},{7,5},{8,10},{10,8},{9,1... | collective-permute-start | bytes 1572872 | tf_op jit(solution)/shard_map/ppermute | solution.py:464
  576.2 21.4 %collective-permute-start.41 = (bf16[512,512]{1,0:T(8,128)(2,1)}, bf16[512,512]{1,0:T(8,128)(2,1)}, u32[]{:S(2)}, u32[]{:S(2)}) collective-permute-start(bf16[512,512]{1,0:T(8,128)(2,1)} %copy-done.156), channel_id=1, source_target_pairs={{0,4},{4,0},{1,5},{5,1},{2,6},{6,2},{3,7},{7,3},{8,12},{12,8},{9,1... | collective-permute-start | bytes 1572872 | tf_op jit(solution)/shard_map/ppermute | solution.py:468
  (188 other events, 1677.8 us)
Sparse Core Ops, SparseCore 0:
  10.8 33.1 all-gather.3
  46.1 43.9 all-gather.5
  92.2 49.8 all-gather.7
  438.3 65.4 reduce-scatter.9
  554.5 41.0 reduce-scatter.11
  602.4 31.0 reduce-scatter.13

commit v4 on v3

--- a/solution.py
+++ b/solution.py
@@ -494,9 +494,10 @@
         self.own_x, self.own_y = self.own[: len(x_items)], self.own[len(x_items) :]
         self.other_x, self.other_y = ([(r, v) for r, _, v in items] for items in (x_items, y_items))
 
-    def first(self):
+    def first(self, *deps):
         self.sent = [weight_grad(self.other_x, None), weight_grad([*self.own_y, *self.other_y], 1)]
-        self.from_x, self.from_y = swap_x(self.sent[0]), swap_y(self.sent[1])
+        to_x, to_y = (after(t, *deps) if deps else t for t in self.sent)
+        self.from_x, self.from_y = swap_x(to_x), swap_y(to_y)
         return self.sent
 
     def second(self, *deps):
@@ -517,8 +518,8 @@
         )
         self.sent = [summed]
         summed = after(summed, *behind) if behind else summed
-        summed = lax.psum_scatter(row_major(summed), "dz", scatter_dimension=0, tiled=True)
-        self.result = summed.astype(f32)
+        self.low = lax.psum_scatter(row_major(summed), "dz", scatter_dimension=0, tiled=True)
+        self.result = self.low.astype(f32)
         return self.sent
 
 
@@ -688,11 +689,11 @@
         [(norm_one, *grad_q), (grad_o, *[o[0] for o in self_out])],
         [(norm_one, *grad_k), (norm_one, *grad_v)],
     )
-    sent = group_a.first()
+    sent = group_a.first(group_b.late_x, group_b.late_y)
+    sent = [*sent, *group_b.third(*sent, behind=[group_c.low])]
     parts = over_cores(
-        [after(grad_q[0], *sent, *group_b.sent, grad_encoder), grad_q[1], *grad_k, *grad_v], [*w_q, *w_k, *w_v]
-    )
-    sent = group_b.third(*parts[0], behind=[group_c.result])
+        [after(grad_q[0], *sent, grad_encoder), grad_q[1], *grad_k, *grad_v], [*w_q, *w_k, *w_v]
+    )
     _, low_tok, gain_one = norm_back(
         x_own, gain_rows[0], [[after(parts[0][0], *sent), parts[0][1]], parts[1]], grad_one
     )
@@ -711,10 +712,10 @@
     sent = jnp.concatenate([out_tok.reshape(seq_count, block_rows, D), small], axis=1)
     came = exchange(sent)
     grad_tokens, small = came[:, :block_rows], came[:, block_rows].astype(f32)
-    group_a.third(out_tok, group_b.result)
+    group_a.third(out_tok, behind=[group_b.low])
     sum_a, sum_b, sum_c = group_a.result, group_b.result, group_c.result
 
-    small = after(small, group_a.result)
+    small = after(small, group_a.low)
     wide = 3 * model_rows
     red_gain = jnp.sum(small[:, :wide] + small[:, wide : 2 * wide], axis=0).reshape(3, model_rows)
     red_gain = red_gain + swap_cores(red_gain)

time: 661 us -> 633 us (0.958)
  local copies, waits for them, and re-layouts: 75.3 us -> 63 us
  waiting for transfers between devices: 212 us -> 204 us
    ppermute x11, waiting for transfers between devices: 29.5 us -> 51.2 us  [swap_x(): return row_major(lax.ppermute(row_major(values), 'mx', swap))]
    unnamed x9, waiting for transfers between devices: 33 us -> 12.8 us
    unnamed x370 -> x334, local copies, waits for them, and re-layouts: 65.6 us -> 53.3 us
    ppermute x11, waiting for transfers between devices: 111 us -> 105 us  [swap_y(): return row_major(lax.ppermute(row_major(values), 'dy', swap))]
  transfers between devices with their start and end apart: 56 -> 56, of which waited for: 18 -> 20; matrix products, arithmetic and copies ran while one was open for 5% -> 5% of each run, Pallas kernels for 34% -> 35%
where the time goes in v4:
time: 633 us; the launch traced here: 622 us
  Pallas kernels  242 us (38%)
  waiting for transfers between devices  204 us (32%)
  starting transfers between devices  71.7 us (11%)
  local copies, waits for them, and re-layouts  63 us (10%)
  other arithmetic  22.5 us (4%)
  between operations  18.5 us (3%)
    ppermute x11, waiting for transfers between devices, swap_y(): return row_major(lax.ppermute(row_major(values), 'dy', swap))  105 us
    unnamed x334, local copies, waits for them, and re-layouts  53.3 us
    ppermute x11, waiting for transfers between devices, swap_x(): return row_major(lax.ppermute(row_major(values), 'mx', swap))  51.2 us
    pallas_call x15, Pallas kernels, weight_grad(): pl.pallas_call(kernel, grid=(steps,), in_specs=[columns] * first + [spec(...  51 us
    pallas_call x4, Pallas kernels, attend_back(): pl.pallas_call(functools.partial(attend_back_kernel, causal, size), grid=...  50.5 us
    pallas_call x9, Pallas kernels, project(): pl.pallas_call(kernel, grid=(4,), in_specs=[spec((size, width_all), lambd...  42.3 us
    pallas_call x14, Pallas kernels, combine(): pl.pallas_call(kernel, grid=(2,), in_specs=[spec((size, v.shape[1]), lamb...  40.2 us
    pallas_call x4, Pallas kernels, attend(): pl.pallas_call(functools.partial(attend_kernel, causal, size), grid=(pair...  37.5 us
  transfers between devices with their start and end apart: 56, of which 20 were waited for; matrix products, arithmetic and copies ran while one was open for 5% of the time, Pallas kernels for 35%

profile of v4, /device:TPU:0, one launch (start us, length us, event | category | flops | bytes accessed | tf_op | source)
XLA Modules:
  0.0 621.8 jit_solution(12031131620900968569)
XLA Ops:
  12.8 31.1 %all-gather.4.cloned.1.call-done.refs_0_.refs_2_.refs_6_.refs_10_.refs_14_ = bf16[512,1152]{1,0:T(8,128)(2,1)} async-done(((bf16[128,1152]{1,0:T(8,128)(2,1)}), bf16[512,1152]{1,0:T(8,128)(2,1)}) %all-gather.4.cloned.1.call-update) | async-done | bytes 1179664 | tf_op jit(solution)/shard_map/all_gather | solution.py:472
  43.9 4.9 all-to-all-start
  52.4 35.3 %collective-permute-done.refs_1_.refs_3_.refs_7_.refs_11_.refs_15_ = bf16[512,1152]{1,0:T(8,128)(2,1)} collective-permute-done((bf16[512,1152]{1,0:T(8,128)(2,1)S(1)}, bf16[512,1152]{1,0:T(8,128)(2,1)}, u32[]{:S(2)}, u32[]{:S(2)}) %collective-permute-start) | collective-permute-done | bytes 1179680 | tf_op jit(solution)/shard_map/ppermute | solution.py:468
  99.6 4.5 project_plain.6.q_ref.k_ref.v_ref
  104.2 10.0 %attend.4 = (bf16[1024,256]{1,0:T(8,128)(2,1)S(1)}, f32[2,1024,2]{2,1,0:T(8,128)S(1)}, f32[2,8,128]{2,1,0:T(8,128)S(1)}) custom-call(bf16[1024,768]{1,0:T(8,128)(2,1)S(1)} %project_plain.6.q_ref.k_ref.v_ref, bf16[1024,768]{1,0:T(8,128)(2,1)S(1)} %project_plain.6.q_ref.k_ref.v_ref, bf16[1024,768]{1,0:T(8,128)(2,1)S(1)} %project_plain.6.q_ref.k_ref.v_ref, ...), custom_call_target="tpu_custom_call" | custom-call | flops 1 | bytes 1 | tf_op jit(solution)/shard_map/attend/pallas_call | solution.py:126
  117.9 4.5 project_plain.7.q_ref.k_ref.v_ref
  122.5 10.0 %attend.5 = (bf16[1024,256]{1,0:T(8,128)(2,1)S(1)}, f32[2,1024,2]{2,1,0:T(8,128)S(1)}, f32[2,8,128]{2,1,0:T(8,128)S(1)}) custom-call(bf16[1024,768]{1,0:T(8,128)(2,1)S(1)} %project_plain.7.q_ref.k_ref.v_ref, bf16[1024,768]{1,0:T(8,128)(2,1)S(1)} %project_plain.7.q_ref.k_ref.v_ref, bf16[1024,768]{1,0:T(8,128)(2,1)S(1)} %project_plain.7.q_ref.k_ref.v_ref, ...), custom_call_target="tpu_custom_call" | custom-call | flops 1 | bytes 1 | tf_op jit(solution)/shard_map/attend/pallas_call | solution.py:126
  134.3 4.0 collective-permute-done.8.refs_2_.refs_6_.refs_4_.refs_10_
  142.1 4.8 all-to-all-start.1
  146.9 25.3 %collective-permute-done.9.refs_3_.refs_7_.refs_5_.refs_11_ = bf16[512,1024]{1,0:T(8,128)(2,1)S(1)} collective-permute-done((bf16[512,1024]{1,0:T(8,128)(2,1)S(1)}, bf16[512,1024]{1,0:T(8,128)(2,1)S(1)}, u32[]{:S(2)}, u32[]{:S(2)}) %collective-permute-start.9) | collective-permute-done | bytes 1048608 | tf_op jit(solution)/shard_map/ppermute | solution.py:468
  192.4 5.7 all-to-all-start.2
  201.7 3.8 project_plain.8
  205.7 5.0 project_plain.9
  210.7 8.8 %attend.7 = (bf16[1024,256]{1,0:T(8,128)(2,1)S(1)}, f32[2,1024,2]{2,1,0:T(8,128)S(1)}, f32[2,8,128]{2,1,0:T(8,128)}) custom-call(bf16[1024,256]{1,0:T(8,128)(2,1)S(1)} %get-tuple-element.163.q_ref, bf16[1024,256]{1,0:T(8,128)(2,1)S(1)} %get-tuple-element.170.k_ref, bf16[1024,256]{1,0:T(8,128)(2,1)S(1)} %get-tuple-element.171.v_ref, ...), custom_call_target="tpu_custom_call" | custom-call | flops 1 | bytes 1 | tf_op jit(solution)/shard_map/attend/pallas_call | solution.py:126
  220.5 12.7 %collective-permute-done.10.refs_1_.refs_3_.refs_5_.refs_9_ = bf16[512,2304]{1,0:T(8,128)(2,1)S(1)} collective-permute-done((bf16[512,2304]{1,0:T(8,128)(2,1)}, bf16[512,2304]{1,0:T(8,128)(2,1)S(1)}, u32[]{:S(2)}, u32[]{:S(2)}) %collective-permute-start.10) | collective-permute-done | bytes 2359328 | tf_op jit(solution)/shard_map/ppermute | solution.py:468
  233.9 8.8 %attend.6 = (bf16[1024,256]{1,0:T(8,128)(2,1)S(1)}, f32[2,1024,2]{2,1,0:T(8,128)S(1)}, f32[2,8,128]{2,1,0:T(8,128)}) custom-call(bf16[1024,256]{1,0:T(8,128)(2,1)S(1)} %get-tuple-element.165.q_ref, bf16[1024,256]{1,0:T(8,128)(2,1)S(1)} %get-tuple-element.167.k_ref, bf16[1024,256]{1,0:T(8,128)(2,1)S(1)} %get-tuple-element.168.v_ref, ...), custom_call_target="tpu_custom_call" | custom-call | flops 1 | bytes 1 | tf_op jit(solution)/shard_map/attend/pallas_call | solution.py:126
  259.5 5.8 project_gelu.2
  265.4 17.9 %collective-permute-done.18.refs_1_.refs_3_.refs_7_.refs_11_ = bf16[512,1536]{1,0:T(8,128)(2,1)} collective-permute-done((bf16[512,1536]{1,0:T(8,128)(2,1)}, bf16[512,1536]{1,0:T(8,128)(2,1)}, u32[]{:S(2)}, u32[]{:S(2)}) %collective-permute-start.18) | collective-permute-done | bytes 1572896 | tf_op jit(solution)/shard_map/ppermute | solution.py:464
  283.3 6.6 %project_gelu.3 = (bf16[1024,768]{1,0:T(8,128)(2,1)S(1)}, bf16[1024,768]{1,0:T(8,128)(2,1)S(1)}, bf16[1024,768]{1,0:T(8,128)(2,1)S(1)}) custom-call(bf16[512,1024]{1,0:T(8,128)(2,1)} %get-tuple-element.178.own_ref.refs_0_, bf16[512,1024]{1,0:T(8,128)(2,1)} %collective-permute-done.17.other_ref.refs_1_, ...), custom_call_target="tpu_custom_call" | custom-call | flops 1 | bytes 1 | tf_op jit(solution)/shard_map/project_gelu/pallas_call | solution.py:292
  289.9 5.6 project_scale.1
  295.5 5.7 weight_grad.15
  305.5 5.7 combine.19
  312.3 5.7 combine.18
  320.6 3.6 combine.21
  324.8 3.5 combine.20
  332.5 12.7 %attend_back.4 = (bf16[1024,256]{1,0:T(8,128)(2,1)S(1)}, bf16[1024,256]{1,0:T(8,128)(2,1)S(1)}, bf16[1024,256]{1,0:T(8,128)(2,1)S(1)}) custom-call(bf16[1024,256]{1,0:T(8,128)(2,1)S(1)} %copy-done.114, bf16[1024,256]{1,0:T(8,128)(2,1)S(1)} %copy-done.116, bf16[1024,256]{1,0:T(8,128)(2,1)S(1)} %copy-done.118, s32[1024,1]{1,0:T(8,128)S(1)} %copy-done.26, ...), custom_call_target="tpu_custom_call" | custom-call | flops 1 | bytes 1 | tf_op jit(solution)/shard_map/attend_back/pallas_call | solution.py:156
  348.2 13.1 %attend_back.5 = (bf16[1024,256]{1,0:T(8,128)(2,1)S(1)}, bf16[1024,256]{1,0:T(8,128)(2,1)S(1)}, bf16[1024,256]{1,0:T(8,128)(2,1)S(1)}) custom-call(bf16[1024,256]{1,0:T(8,128)(2,1)S(1)} %copy-done.108, bf16[1024,256]{1,0:T(8,128)(2,1)S(1)} %copy-done.110, bf16[1024,256]{1,0:T(8,128)(2,1)S(1)} %copy-done.112, s32[1024,1]{1,0:T(8,128)S(1)} %copy-done.26, ...), custom_call_target="tpu_custom_call" | custom-call | flops 1 | bytes 1 | tf_op jit(solution)/shard_map/attend_back/pallas_call | solution.py:156
  362.2 3.5 weight_grad.18
  365.6 4.9 collective-permute-done.24.refs_6_.refs_7_
  370.6 3.8 weight_grad.17
  377.0 7.6 %all-to-all-start.3 = ((bf16[16,32,1024]{2,1,0:T(8,128)(2,1)}), bf16[16,32,1024]{2,1,0:T(8,128)(2,1)}, u32[]{:S(2)}, u32[]{:S(2)}) async-start(bf16[16,32,1024]{2,1,0:T(8,128)(2,1)} %bitcast.104), calls=%async_computation.3 | async-start | bytes 2097152 | tf_op jit(solution)/shard_map/all_to_all | solution.py:559
  410.4 4.2 project_plain.11
  416.7 12.2 %attend_back.6 = (bf16[1024,256]{1,0:T(8,128)(2,1)S(1)}, bf16[1024,256]{1,0:T(8,128)(2,1)S(1)}, bf16[1024,256]{1,0:T(8,128)(2,1)S(1)}) custom-call(bf16[1024,768]{1,0:T(8,128)(2,1)S(1)} %copy-done.23, bf16[1024,768]{1,0:T(8,128)(2,1)S(1)} %copy-done.23, bf16[1024,768]{1,0:T(8,128)(2,1)S(1)} %copy-done.23, s32[1024,1]{1,0:T(8,128)S(1)} %copy-done.27, ...), custom_call_target="tpu_custom_call" | custom-call | flops 1 | bytes 1 | tf_op jit(solution)/shard_map/attend_back/pallas_call | solution.py:156
  432.0 4.7 weight_grad.21
  438.1 5.7 all-to-all-start.4
  449.6 12.4 %attend_back.7 = (bf16[1024,256]{1,0:T(8,128)(2,1)S(1)}, bf16[1024,256]{1,0:T(8,128)(2,1)S(1)}, bf16[1024,256]{1,0:T(8,128)(2,1)S(1)}) custom-call(bf16[1024,768]{1,0:T(8,128)(2,1)S(1)} %copy-done.21, bf16[1024,768]{1,0:T(8,128)(2,1)S(1)} %copy-done.21, bf16[1024,768]{1,0:T(8,128)(2,1)S(1)} %copy-done.21, s32[1024,1]{1,0:T(8,128)S(1)} %copy-done.27, ...), custom_call_target="tpu_custom_call" | custom-call | flops 1 | bytes 1 | tf_op jit(solution)/shard_map/attend_back/pallas_call | solution.py:156
  462.0 14.9 %collective-permute-done.34.refs_4_.refs_12_ = bf16[512,1024]{1,0:T(8,128)(2,1)S(1)} collective-permute-done((bf16[512,1024]{1,0:T(8,128)(2,1)}, bf16[512,1024]{1,0:T(8,128)(2,1)S(1)}, u32[]{:S(2)}, u32[]{:S(2)}) %collective-permute-start.34) | collective-permute-done | bytes 1048608 | tf_op jit(solution)/shard_map/ppermute | solution.py:468
  484.3 3.5 weight_grad.25
  487.8 4.0 weight_grad.24
  495.7 3.9 weight_grad.26
  501.7 4.7 combine.27
  512.3 3.8 combine.26
  516.2 3.5 norm_back.5
  522.9 9.6 %collective-permute-done.40.refs_4_.refs_10_ = bf16[512,1024]{1,0:T(8,128)(2,1)} collective-permute-done((bf16[512,1024]{1,0:T(8,128)(2,1)}, bf16[512,1024]{1,0:T(8,128)(2,1)}, u32[]{:S(2)}, u32[]{:S(2)}) %collective-permute-start.40) | collective-permute-done | bytes 1048608 | tf_op jit(solution)/shard_map/ppermute | solution.py:468
  540.5 7.0 %all-to-all-start.5 = ((bf16[16,33,1024]{2,1,0:T(8,128)(2,1)}), bf16[16,33,1024]{2,1,0:T(8,128)(2,1)}, u32[]{:S(2)}, u32[]{:S(2)}) async-start(bf16[16,33,1024]{2,1,0:T(8,128)(2,1)} %pad_maximum_fusion), calls=%async_computation.5 | async-start | bytes 2621440 | tf_op jit(solution)/shard_map/all_to_all | solution.py:559
  551.0 20.0 %collective-permute-done.42.refs_11_ = bf16[512,512]{1,0:T(8,128)(2,1)S(1)} collective-permute-done((bf16[512,512]{1,0:T(8,128)(2,1)S(1)}, bf16[512,512]{1,0:T(8,128)(2,1)S(1)}, u32[]{:S(2)}, u32[]{:S(2)}) %collective-permute-start.42) | collective-permute-done | bytes 524320 | tf_op jit(solution)/shard_map/ppermute | solution.py:464
  573.5 4.5 weight_grad.29
  593.7 12.7 %reduce-scatter.14.cloned.1.call-done = bf16[128,1024]{1,0:T(8,128)(2,1)} async-done(((bf16[512,1024]{1,0:T(8,128)(2,1)}), bf16[128,1024]{1,0:T(8,128)(2,1)}) %reduce-scatter.14.cloned.1.call-update) | async-done | bytes 262160
  (536 shorter events, 187.1 us)
Async XLA Ops:
  7.2 36.7 %all-gather.4.cloned.1.call-start = ((), (), s32[]{:S(2)}) async-start(), calls=%async_computation.9 | async-start | bytes 1474560 | tf_op jit(solution)/shard_map/all_gather | solution.py:472
  10.6 82.3 %all-gather.6.cloned.1.call-start = ((), (), s32[]{:S(2)}) async-start(), calls=%async_computation.10 | async-start | bytes 1310720 | tf_op jit(solution)/shard_map/all_gather | solution.py:472
  11.4 130.6 %all-gather.8.cloned.1.call-start = ((), (), s32[]{:S(2)}) async-start(), calls=%async_computation.11 | async-start | bytes 2949120 | tf_op jit(solution)/shard_map/all_gather | solution.py:472
  43.9 46.3 %all-to-all-start = ((bf16[16,32,1024]{2,1,0:T(8,128)(2,1)}), bf16[16,32,1024]{2,1,0:T(8,128)(2,1)S(1)}, u32[]{:S(2)}, u32[]{:S(2)}) async-start(bf16[16,32,1024]{2,1,0:T(8,128)(2,1)} %param.20), calls=%async_computation | async-start | bytes 2097152 | tf_op jit(solution)/shard_map/all_to_all | solution.py:559
  48.8 38.9 %collective-permute-start = (bf16[512,1152]{1,0:T(8,128)(2,1)S(1)}, bf16[512,1152]{1,0:T(8,128)(2,1)}, u32[]{:S(2)}, u32[]{:S(2)}) collective-permute-start(bf16[512,1152]{1,0:T(8,128)(2,1)S(1)} %copy-done.17), channel_id=1, source_target_pairs={{0,4},{4,0},{1,5},{5,1},{2,6},{6,2},{3,7},{7,3},{8,12},{12,8},{9,1... | collective-permute-start | bytes 3538952 | tf_op jit(solution)/shard_map/ppermute | solution.py:468
  50.9 65.0 %collective-permute-start.2 = (bf16[512,1152]{1,0:T(8,128)(2,1)S(1)}, bf16[512,1152]{1,0:T(8,128)(2,1)}, u32[]{:S(2)}, u32[]{:S(2)}) collective-permute-start(bf16[512,1152]{1,0:T(8,128)(2,1)S(1)} %copy-done.17), channel_id=1, source_target_pairs={{0,2},{2,0},{1,3},{3,1},{4,6},{6,4},{5,7},{7,5},{8,10},{10,8},{9,1... | collective-permute-start | bytes 3538952 | tf_op jit(solution)/shard_map/ppermute | solution.py:464
  88.7 29.2 %collective-permute-start.3 = (bf16[512,1152]{1,0:T(8,128)(2,1)}, bf16[512,1152]{1,0:T(8,128)(2,1)}, u32[]{:S(2)}, u32[]{:S(2)}) collective-permute-start(bf16[512,1152]{1,0:T(8,128)(2,1)} %collective-permute-done.refs_1_.refs_3_.refs_7_.refs_11_.refs_15_), channel_id=1, source_target_pairs={{0,2},{2,0},{1,3},{3,1},{4,6},{6,4},{5,7},{7,5},{8,10},{10,8},{9,1... | collective-permute-start | bytes 3538952 | tf_op jit(solution)/shard_map/ppermute | solution.py:464
  92.9 6.7 %collective-permute-start.1 = (bf16[512,1024]{1,0:T(8,128)(2,1)}, bf16[512,1024]{1,0:T(8,128)(2,1)}, u32[]{:S(2)}, u32[]{:S(2)}) collective-permute-start(bf16[512,1024]{1,0:T(8,128)(2,1)} %add_norm.3.own_ref.refs_0_), channel_id=1, source_target_pairs={{0,1},{1,0},{2,3},{3,2},{4,5},{5,4},{6,7},{7,6},{8,9},{9,8},{10,11... | collective-permute-start | bytes 3145736 | tf_op jit(solution)/shard_map/ppermute | solution.py:460
  92.9 41.3 %collective-permute-start.7 = (bf16[512,1024]{1,0:T(8,128)(2,1)}, bf16[512,1024]{1,0:T(8,128)(2,1)S(1)}, u32[]{:S(2)}, u32[]{:S(2)}) collective-permute-start(bf16[512,1024]{1,0:T(8,128)(2,1)} %all-gather.6.cloned.1.call-done.refs_0_.refs_4_.refs_2_.refs_8_), channel_id=1, source_target_pairs={{0,4},{4,0},{1,5},{5,1},{2,6},{6,2},{3,7},{7,3},{8,12},{12,8},{9,1... | collective-permute-start | bytes 3145736 | tf_op jit(solution)/shard_map/ppermute | solution.py:468
  94.8 43.5 %collective-permute-start.8 = (bf16[512,1024]{1,0:T(8,128)(2,1)}, bf16[512,1024]{1,0:T(8,128)(2,1)S(1)}, u32[]{:S(2)}, u32[]{:S(2)}) collective-permute-start(bf16[512,1024]{1,0:T(8,128)(2,1)} %all-gather.6.cloned.1.call-done.refs_0_.refs_4_.refs_2_.refs_8_), channel_id=1, source_target_pairs={{0,2},{2,0},{1,3},{3,1},{4,6},{6,4},{5,7},{7,5},{8,10},{10,8},{9,1... | collective-permute-start | bytes 3145736 | tf_op jit(solution)/shard_map/ppermute | solution.py:464
  138.3 33.9 %collective-permute-start.9 = (bf16[512,1024]{1,0:T(8,128)(2,1)S(1)}, bf16[512,1024]{1,0:T(8,128)(2,1)S(1)}, u32[]{:S(2)}, u32[]{:S(2)}) collective-permute-start(bf16[512,1024]{1,0:T(8,128)(2,1)S(1)} %collective-permute-done.8.refs_2_.refs_6_.refs_4_.refs_10_), channel_id=1, source_target_pairs={{0,4},{4,0},{1,5},{5,1},{2,6},{6,2},{3,7},{7,3},{8,12},{12,8},{9,1... | collective-permute-start | bytes 3145736 | tf_op jit(solution)/shard_map/ppermute | solution.py:468
  142.1 46.5 %all-to-all-start.1 = ((bf16[16,32,1024]{2,1,0:T(8,128)(2,1)}), bf16[16,32,1024]{2,1,0:T(8,128)(2,1)}, u32[]{:S(2)}, u32[]{:S(2)}) async-start(bf16[16,32,1024]{2,1,0:T(8,128)(2,1)} %param.21), calls=%async_computation.1 | async-start | bytes 2097152 | tf_op jit(solution)/shard_map/all_to_all | solution.py:559
  173.2 60.0 %collective-permute-start.10 = (bf16[512,2304]{1,0:T(8,128)(2,1)}, bf16[512,2304]{1,0:T(8,128)(2,1)S(1)}, u32[]{:S(2)}, u32[]{:S(2)}) collective-permute-start(bf16[512,2304]{1,0:T(8,128)(2,1)} %all-gather.8.cloned.1.call-done.refs_0_.refs_2_.refs_4_.refs_8_), channel_id=1, source_target_pairs={{0,4},{4,0},{1,5},{5,1},{2,6},{6,2},{3,7},{7,3},{8,12},{12,8},{9,1... | collective-permute-start | bytes 7077896 | tf_op jit(solution)/shard_map/ppermute | solution.py:468
  175.0 58.9 %collective-permute-start.11 = (bf16[512,2304]{1,0:T(8,128)(2,1)}, bf16[512,2304]{1,0:T(8,128)(2,1)}, u32[]{:S(2)}, u32[]{:S(2)}) collective-permute-start(bf16[512,2304]{1,0:T(8,128)(2,1)} %all-gather.8.cloned.1.call-done.refs_0_.refs_2_.refs_4_.refs_8_), channel_id=1, source_target_pairs={{0,2},{2,0},{1,3},{3,1},{4,6},{6,4},{5,7},{7,5},{8,10},{10,8},{9,1... | collective-permute-start | bytes 7077896 | tf_op jit(solution)/shard_map/ppermute | solution.py:464
  188.4 9.6 %collective-permute-start.6 = (bf16[512,1024]{1,0:T(8,128)(2,1)}, bf16[512,1024]{1,0:T(8,128)(2,1)}, u32[]{:S(2)}, u32[]{:S(2)}) collective-permute-start(bf16[512,1024]{1,0:T(8,128)(2,1)} %get-tuple-element.160.own_ref.refs_0_), channel_id=1, source_target_pairs={{0,1},{1,0},{2,3},{3,2},{4,5},{5,4},{6,7},{7,6},{8,9},{9,8},{10,11... | collective-permute-start | bytes 3145736 | tf_op jit(solution)/shard_map/ppermute | solution.py:460
  192.0 13.6 %collective-permute-start.12 = (bf16[512,1024]{1,0:T(8,128)(2,1)}, bf16[512,1024]{1,0:T(8,128)(2,1)}, u32[]{:S(2)}, u32[]{:S(2)}) collective-permute-start(bf16[512,1024]{1,0:T(8,128)(2,1)} %reorder.7.own_ref.refs_0_.refs_4_), channel_id=1, source_target_pairs={{0,1},{1,0},{2,3},{3,2},{4,5},{5,4},{6,7},{7,6},{8,9},{9,8},{10,11... | collective-permute-start | bytes 3145736 | tf_op jit(solution)/shard_map/ppermute | solution.py:460
  192.4 61.2 %all-to-all-start.2 = ((bf16[16,32,1024]{2,1,0:T(8,128)(2,1)}), bf16[16,32,1024]{2,1,0:T(8,128)(2,1)}, u32[]{:S(2)}, u32[]{:S(2)}) async-start(bf16[16,32,1024]{2,1,0:T(8,128)(2,1)} %param.22), calls=%async_computation.2 | async-start | bytes 2097152 | tf_op jit(solution)/shard_map/all_to_all | solution.py:559
  246.6 36.7 %collective-permute-start.18 = (bf16[512,1536]{1,0:T(8,128)(2,1)}, bf16[512,1536]{1,0:T(8,128)(2,1)}, u32[]{:S(2)}, u32[]{:S(2)}) collective-permute-start(bf16[512,1536]{1,0:T(8,128)(2,1)} %slice.156), channel_id=1, source_target_pairs={{0,2},{2,0},{1,3},{3,1},{4,6},{6,4},{5,7},{7,5},{8,10},{10,8},{9,1... | collective-permute-start | bytes 4718600 | tf_op jit(solution)/shard_map/ppermute | solution.py:464
  257.2 32.7 %collective-permute-start.15 = (bf16[512,1024]{1,0:T(8,128)(2,1)S(1)}, bf16[512,1024]{1,0:T(8,128)(2,1)S(1)}, u32[]{:S(2)}, u32[]{:S(2)}) collective-permute-start(bf16[512,1024]{1,0:T(8,128)(2,1)S(1)} %reorder.8.own_ref.refs_2_.base_ref), channel_id=1, source_target_pairs={{0,1},{1,0},{2,3},{3,2},{4,5},{5,4},{6,7},{7,6},{8,9},{9,8},{10,11... | collective-permute-start | bytes 3145736 | tf_op jit(solution)/shard_map/ppermute | solution.py:460
  259.0 30.9 %collective-permute-start.16 = (bf16[512,768]{1,0:T(8,128)(2,1)S(1)}, bf16[512,768]{1,0:T(8,128)(2,1)S(1)}, u32[]{:S(2)}, u32[]{:S(2)}) collective-permute-start(bf16[512,768]{1,0:T(8,128)(2,1)S(1)} %slice.155), channel_id=1, source_target_pairs={{0,4},{4,0},{1,5},{5,1},{2,6},{6,2},{3,7},{7,3},{8,12},{12,8},{9,1... | collective-permute-start | bytes 2359304 | tf_op jit(solution)/shard_map/ppermute | solution.py:468
  301.2 69.3 %collective-permute-start.24 = (bf16[1024,1536]{1,0:T(8,128)(2,1)S(1)}, bf16[1024,1536]{1,0:T(8,128)(2,1)S(1)}, u32[]{:S(2)}, u32[]{:S(2)}) collective-permute-start(bf16[1024,1536]{1,0:T(8,128)(2,1)S(1)} %weight_grad.15), channel_id=1, source_target_pairs={{0,2},{2,0},{1,3},{3,1},{4,6},{6,4},{5,7},{7,5},{8,10},{10,8},{9,1... | collective-permute-start | bytes 9437192 | tf_op jit(solution)/shard_map/ppermute | solution.py:464
  311.2 6.7 %collective-permute-start.19 = (f32[512,512]{1,0:T(8,128)S(1)}, f32[512,512]{1,0:T(8,128)S(1)}, u32[]{:S(2)}, u32[]{:S(2)}) collective-permute-start(f32[512,512]{1,0:T(8,128)S(1)} %get-tuple-element.191), channel_id=1, source_target_pairs={{0,1},{1,0},{2,3},{3,2},{4,5},{5,4},{6,7},{7,6},{8,9},{9,8},{10,11... | collective-permute-start | bytes 3145736 | tf_op jit(solution)/shard_map/ppermute | solution.py:460
  311.3 6.6 %collective-permute-start.20 = (f32[512,512]{1,0:T(8,128)S(1)}, f32[512,512]{1,0:T(8,128)S(1)}, u32[]{:S(2)}, u32[]{:S(2)}) collective-permute-start(f32[512,512]{1,0:T(8,128)S(1)} %get-tuple-element.192), channel_id=1, source_target_pairs={{0,1},{1,0},{2,3},{3,2},{4,5},{5,4},{6,7},{7,6},{8,9},{9,8},{10,11... | collective-permute-start | bytes 3145736 | tf_op jit(solution)/shard_map/ppermute | solution.py:460
  311.8 36.4 %collective-permute-start.25 = (bf16[512,1536]{1,0:T(8,128)(2,1)S(1)}, bf16[512,1536]{1,0:T(8,128)(2,1)S(1)}, u32[]{:S(2)}, u32[]{:S(2)}) collective-permute-start(bf16[512,1536]{1,0:T(8,128)(2,1)S(1)} %weight_grad.16), channel_id=1, source_target_pairs={{0,4},{4,0},{1,5},{5,1},{2,6},{6,2},{3,7},{7,3},{8,12},{12,8},{9,1... | collective-permute-start | bytes 4718600 | tf_op jit(solution)/shard_map/ppermute | solution.py:468
  320.6 7.6 %collective-permute-start.21 = (bf16[512,1024]{1,0:T(8,128)(2,1)S(1)}, bf16[512,1024]{1,0:T(8,128)(2,1)S(1)}, u32[]{:S(2)}, u32[]{:S(2)}) collective-permute-start(bf16[512,1024]{1,0:T(8,128)(2,1)S(1)} %get-tuple-element.197.own_ref.refs_2_), channel_id=1, source_target_pairs={{0,1},{1,0},{2,3},{3,2},{4,5},{5,4},{6,7},{7,6},{8,9},{9,8},{10,11... | collective-permute-start | bytes 3145736 | tf_op jit(solution)/shard_map/ppermute | solution.py:460
  324.2 6.4 %collective-permute-start.22 = (f32[512,512]{1,0:T(8,128)S(1)}, f32[512,512]{1,0:T(8,128)S(1)}, u32[]{:S(2)}, u32[]{:S(2)}) collective-permute-start(f32[512,512]{1,0:T(8,128)S(1)} %get-tuple-element.202), channel_id=1, source_target_pairs={{0,1},{1,0},{2,3},{3,2},{4,5},{5,4},{6,7},{7,6},{8,9},{9,8},{10,11... | collective-permute-start | bytes 3145736 | tf_op jit(solution)/shard_map/ppermute | solution.py:460
  376.4 25.3 %collective-permute-start.26 = (f32[512,512]{1,0:T(8,128)}, f32[512,512]{1,0:T(8,128)}, u32[]{:S(2)}, u32[]{:S(2)}) collective-permute-start(f32[512,512]{1,0:T(8,128)} %get-tuple-element.218), channel_id=1, source_target_pairs={{0,1},{1,0},{2,3},{3,2},{4,5},{5,4},{6,7},{7,6},{8,9},{9,8},{10,11... | collective-permute-start | bytes 3145736 | tf_op jit(solution)/shard_map/ppermute | solution.py:460
  376.5 25.2 %collective-permute-start.27 = (f32[512,512]{1,0:T(8,128)}, f32[512,512]{1,0:T(8,128)}, u32[]{:S(2)}, u32[]{:S(2)}) collective-permute-start(f32[512,512]{1,0:T(8,128)} %get-tuple-element.224), channel_id=1, source_target_pairs={{0,1},{1,0},{2,3},{3,2},{4,5},{5,4},{6,7},{7,6},{8,9},{9,8},{10,11... | collective-permute-start | bytes 3145736 | tf_op jit(solution)/shard_map/ppermute | solution.py:460
  377.0 33.4 %all-to-all-start.3 = ((bf16[16,32,1024]{2,1,0:T(8,128)(2,1)}), bf16[16,32,1024]{2,1,0:T(8,128)(2,1)}, u32[]{:S(2)}, u32[]{:S(2)}) async-start(bf16[16,32,1024]{2,1,0:T(8,128)(2,1)} %bitcast.104), calls=%async_computation.3 | async-start | bytes 2097152 | tf_op jit(solution)/shard_map/all_to_all | solution.py:559
  384.6 136.2 %reduce-scatter.10.cloned.1.call-start = ((), (), s32[]{:S(2)}) async-start(), calls=%async_computation.12 | async-start | bytes 2949120
  384.7 47.3 %collective-permute-start.31 = (bf16[512,1536]{1,0:T(8,128)(2,1)}, bf16[512,1536]{1,0:T(8,128)(2,1)}, u32[]{:S(2)}, u32[]{:S(2)}) collective-permute-start(bf16[512,1536]{1,0:T(8,128)(2,1)} %copy-done.121), channel_id=1, source_target_pairs={{0,4},{4,0},{1,5},{5,1},{2,6},{6,2},{3,7},{7,3},{8,12},{12,8},{9,1... | collective-permute-start | bytes 4718600 | tf_op jit(solution)/shard_map/ppermute | solution.py:468
  398.1 10.8 %collective-permute-start.28 = (f32[512,512]{1,0:T(8,128)S(1)}, f32[512,512]{1,0:T(8,128)S(1)}, u32[]{:S(2)}, u32[]{:S(2)}) collective-permute-start(f32[512,512]{1,0:T(8,128)S(1)} %get-tuple-element.229), channel_id=1, source_target_pairs={{0,1},{1,0},{2,3},{3,2},{4,5},{5,4},{6,7},{7,6},{8,9},{9,8},{10,11... | collective-permute-start | bytes 3145736 | tf_op jit(solution)/shard_map/ppermute | solution.py:460
  398.2 10.7 %collective-permute-start.29 = (f32[512,512]{1,0:T(8,128)S(1)}, f32[512,512]{1,0:T(8,128)S(1)}, u32[]{:S(2)}, u32[]{:S(2)}) collective-permute-start(f32[512,512]{1,0:T(8,128)S(1)} %get-tuple-element.231), channel_id=1, source_target_pairs={{0,1},{1,0},{2,3},{3,2},{4,5},{5,4},{6,7},{7,6},{8,9},{9,8},{10,11... | collective-permute-start | bytes 3145736 | tf_op jit(solution)/shard_map/ppermute | solution.py:460
  407.5 23.9 %collective-permute-start.32 = (bf16[512,768]{1,0:T(8,128)(2,1)}, bf16[512,768]{1,0:T(8,128)(2,1)}, u32[]{:S(2)}, u32[]{:S(2)}) collective-permute-start(bf16[512,768]{1,0:T(8,128)(2,1)} %weight_grad.18), channel_id=1, source_target_pairs={{0,2},{2,0},{1,3},{3,1},{4,6},{6,4},{5,7},{7,5},{8,10},{10,8},{9,1... | collective-permute-start | bytes 2359304 | tf_op jit(solution)/shard_map/ppermute | solution.py:464
  438.1 61.5 %all-to-all-start.4 = ((bf16[16,32,1024]{2,1,0:T(8,128)(2,1)}), bf16[16,32,1024]{2,1,0:T(8,128)(2,1)}, u32[]{:S(2)}, u32[]{:S(2)}) async-start(bf16[16,32,1024]{2,1,0:T(8,128)(2,1)} %bitcast.105), calls=%async_computation.4 | async-start | bytes 2097152 | tf_op jit(solution)/shard_map/all_to_all | solution.py:559
  443.9 134.1 %reduce-scatter.12.cloned.1.call-start = ((), (), s32[]{:S(2)}) async-start(), calls=%async_computation.13 | async-start | bytes 1310720
  443.9 33.1 %collective-permute-start.34 = (bf16[512,1024]{1,0:T(8,128)(2,1)}, bf16[512,1024]{1,0:T(8,128)(2,1)S(1)}, u32[]{:S(2)}, u32[]{:S(2)}) collective-permute-start(bf16[512,1024]{1,0:T(8,128)(2,1)} %copy-done.122), channel_id=1, source_target_pairs={{0,4},{4,0},{1,5},{5,1},{2,6},{6,2},{3,7},{7,3},{8,12},{12,8},{9,1... | collective-permute-start | bytes 3145736 | tf_op jit(solution)/shard_map/ppermute | solution.py:468
  445.9 33.3 %collective-permute-start.33 = (bf16[1024,512]{1,0:T(8,128)(2,1)}, bf16[1024,512]{1,0:T(8,128)(2,1)S(1)}, u32[]{:S(2)}, u32[]{:S(2)}) collective-permute-start(bf16[1024,512]{1,0:T(8,128)(2,1)} %copy-done.133), channel_id=1, source_target_pairs={{0,2},{2,0},{1,3},{3,1},{4,6},{6,4},{5,7},{7,5},{8,10},{10,8},{9,1... | collective-permute-start | bytes 3145736 | tf_op jit(solution)/shard_map/ppermute | solution.py:464
  479.2 14.2 %collective-permute-start.36 = (bf16[512,512]{1,0:T(8,128)(2,1)S(1)}, bf16[512,512]{1,0:T(8,128)(2,1)S(1)}, u32[]{:S(2)}, u32[]{:S(2)}) collective-permute-start(bf16[512,512]{1,0:T(8,128)(2,1)S(1)} %weight_grad.23), channel_id=1, source_target_pairs={{0,2},{2,0},{1,3},{3,1},{4,6},{6,4},{5,7},{7,5},{8,10},{10,8},{9,1... | collective-permute-start | bytes 1572872 | tf_op jit(solution)/shard_map/ppermute | solution.py:464
  482.9 12.8 %collective-permute-start.35 = (bf16[512,512]{1,0:T(8,128)(2,1)S(1)}, bf16[512,512]{1,0:T(8,128)(2,1)S(1)}, u32[]{:S(2)}, u32[]{:S(2)}) collective-permute-start(bf16[512,512]{1,0:T(8,128)(2,1)S(1)} %weight_grad.22), channel_id=1, source_target_pairs={{0,4},{4,0},{1,5},{5,1},{2,6},{6,2},{3,7},{7,3},{8,12},{12,8},{9,1... | collective-permute-start | bytes 1572872 | tf_op jit(solution)/shard_map/ppermute | solution.py:468
  506.5 9.7 %collective-permute-start.37 = (f32[512,512]{1,0:T(8,128)}, f32[512,512]{1,0:T(8,128)}, u32[]{:S(2)}, u32[]{:S(2)}) collective-permute-start(f32[512,512]{1,0:T(8,128)} %get-tuple-element.255), channel_id=1, source_target_pairs={{0,1},{1,0},{2,3},{3,2},{4,5},{5,4},{6,7},{7,6},{8,9},{9,8},{10,11... | collective-permute-start | bytes 3145736 | tf_op jit(solution)/shard_map/ppermute | solution.py:460
  506.5 9.7 %collective-permute-start.38 = (f32[512,512]{1,0:T(8,128)}, f32[512,512]{1,0:T(8,128)}, u32[]{:S(2)}, u32[]{:S(2)}) collective-permute-start(f32[512,512]{1,0:T(8,128)} %get-tuple-element.256), channel_id=1, source_target_pairs={{0,1},{1,0},{2,3},{3,2},{4,5},{5,4},{6,7},{7,6},{8,9},{9,8},{10,11... | collective-permute-start | bytes 3145736 | tf_op jit(solution)/shard_map/ppermute | solution.py:460
  507.0 25.5 %collective-permute-start.40 = (bf16[512,1024]{1,0:T(8,128)(2,1)}, bf16[512,1024]{1,0:T(8,128)(2,1)}, u32[]{:S(2)}, u32[]{:S(2)}) collective-permute-start(bf16[512,1024]{1,0:T(8,128)(2,1)} %weight_grad.25), channel_id=1, source_target_pairs={{0,4},{4,0},{1,5},{5,1},{2,6},{6,2},{3,7},{7,3},{8,12},{12,8},{9,1... | collective-permute-start | bytes 3145736 | tf_op jit(solution)/shard_map/ppermute | solution.py:468
  508.6 27.1 %collective-permute-start.39 = (bf16[1024,512]{1,0:T(8,128)(2,1)}, bf16[1024,512]{1,0:T(8,128)(2,1)}, u32[]{:S(2)}, u32[]{:S(2)}) collective-permute-start(bf16[1024,512]{1,0:T(8,128)(2,1)} %weight_grad.24), channel_id=1, source_target_pairs={{0,2},{2,0},{1,3},{3,1},{4,6},{6,4},{5,7},{7,5},{8,10},{10,8},{9,1... | collective-permute-start | bytes 3145736 | tf_op jit(solution)/shard_map/ppermute | solution.py:464
  540.5 44.2 %all-to-all-start.5 = ((bf16[16,33,1024]{2,1,0:T(8,128)(2,1)}), bf16[16,33,1024]{2,1,0:T(8,128)(2,1)}, u32[]{:S(2)}, u32[]{:S(2)}) async-start(bf16[16,33,1024]{2,1,0:T(8,128)(2,1)} %pad_maximum_fusion), calls=%async_computation.5 | async-start | bytes 2621440 | tf_op jit(solution)/shard_map/all_to_all | solution.py:559
  547.5 58.9 %reduce-scatter.14.cloned.1.call-start = ((), (), s32[]{:S(2)}) async-start(), calls=%async_computation.14 | async-start | bytes 1310720
  547.6 23.4 %collective-permute-start.42 = (bf16[512,512]{1,0:T(8,128)(2,1)S(1)}, bf16[512,512]{1,0:T(8,128)(2,1)S(1)}, u32[]{:S(2)}, u32[]{:S(2)}) collective-permute-start(bf16[512,512]{1,0:T(8,128)(2,1)S(1)} %copy-done.137), channel_id=1, source_target_pairs={{0,2},{2,0},{1,3},{3,1},{4,6},{6,4},{5,7},{7,5},{8,10},{10,8},{9,1... | collective-permute-start | bytes 1572872 | tf_op jit(solution)/shard_map/ppermute | solution.py:464
  549.5 24.0 %collective-permute-start.41 = (bf16[512,512]{1,0:T(8,128)(2,1)S(1)}, bf16[512,512]{1,0:T(8,128)(2,1)S(1)}, u32[]{:S(2)}, u32[]{:S(2)}) collective-permute-start(bf16[512,512]{1,0:T(8,128)(2,1)S(1)} %copy-done.139), channel_id=1, source_target_pairs={{0,4},{4,0},{1,5},{5,1},{2,6},{6,2},{3,7},{7,3},{8,12},{12,8},{9,1... | collective-permute-start | bytes 1572872 | tf_op jit(solution)/shard_map/ppermute | solution.py:468
  (170 other events, 1452.1 us)
Sparse Core Ops, SparseCore 0:
  10.8 33.1 all-gather.3
  46.1 43.9 all-gather.5
  92.2 49.8 all-gather.7
  438.2 65.4 reduce-scatter.9
  523.0 27.8 reduce-scatter.11
  579.2 27.1 reduce-scatter.13

commit v5 on v4

--- a/solution.py
+++ b/solution.py
@@ -494,11 +494,13 @@
         self.own_x, self.own_y = self.own[: len(x_items)], self.own[len(x_items) :]
         self.other_x, self.other_y = ([(r, v) for r, _, v in items] for items in (x_items, y_items))
 
-    def first(self, *deps):
+    def first(self):
         self.sent = [weight_grad(self.other_x, None), weight_grad([*self.own_y, *self.other_y], 1)]
+        return self.sent
+
+    def send(self, *deps):
         to_x, to_y = (after(t, *deps) if deps else t for t in self.sent)
         self.from_x, self.from_y = swap_x(to_x), swap_y(to_y)
-        return self.sent
 
     def second(self, *deps):
         self.from_x, self.from_y = after(self.from_x, *deps), after(self.from_y, *deps)
@@ -507,6 +509,7 @@
             weight_grad(self.own_x, 1, [(self.from_x, 1, 0)]),
             weight_grad(self.other_y, 0, [(self.from_y, 0, -wide_y)]),
         ]
+        self.sent2 = self.sent
         self.late_y, self.late_x = swap_y(self.sent[0]), swap_x(self.sent[1])
         return self.sent
 
@@ -617,7 +620,7 @@
     got_b = (part_b, high_b), (beside_b, far_b)
     w_cq, w_ck, w_cv, w_cot = ([(*g, hc, n) for g in got_b] for n in range(4))
 
-    enc_own = to_chips(after(encoder, part_c, self_out[1][0]))
+    enc_own = to_chips(after(encoder, self_out[0][0]))
     part_c = after(part_c, self_out[1][0], far_b)
     high_c, beside_c = swap_y(part_c), swap_x(part_c)
     far_gu, far_d = swap_x(high_c[:, : 2 * deep]), swap_y(beside_c[:, 2 * deep :])
@@ -637,7 +640,7 @@
         [(t, 0, pairs) for t in (cross_q[n], cross_kv[n], cross_kv[2 + n])] for n in range(2)
     ]
     cross_qkv[0][0] = (after(cross_q[0], cross_q[1], high_c, beside_c), 0, pairs)
-    cross_out = [attend(*t, *places, length, False, 512) for t in cross_qkv]
+    cross_out = [attend(*t, *places, length, False, 1024) for t in cross_qkv]
     cross_mixed = [o[0] for o in cross_out]
     hidden_two, norm_three = add_norm(
         [hidden_one, *over_cores(cross_mixed, w_cot)], gain_rows[2]
@@ -652,6 +655,7 @@
     grad_gate, grad_up = grad_gu[::2], grad_gu[1::2]
     group_c = Group([(norm_three, *grad_gate), (grad_out, *inner)], [(norm_three, *grad_up)])
     sent = group_c.first()
+    group_c.send()
     parts = over_cores([after(grad_gate[0], *sent), grad_gate[1], *grad_up], [*w_g, *w_u])
     grad_two, low_two, gain_three = norm_back(hidden_two, gain_rows[2], parts, dy_own)
     grad_co = both(low_two)
@@ -659,9 +663,9 @@
     grad_ca = project((after(grad_co[0], out_parts[0][0]), grad_co[1]), w_cot)
     out_block = reorder([after(hidden_two, *grad_ca), *out_parts], model_rows, dy, False, valid_own)
     block_output = from_chips(out_block)
-    cross_back = [attend_back(*cross_qkv[0], *places, cross_out[0][1], after(grad_ca[0], out_block), False, 512)]
+    cross_back = [attend_back(*cross_qkv[0], *places, cross_out[0][1], after(grad_ca[0], out_block), False, 1024)]
     grad_late = after(grad_ca[1], group_c.from_y, *cross_back[0])
-    cross_back += [attend_back(*cross_qkv[1], *places, cross_out[1][1], grad_late, False, 512)]
+    cross_back += [attend_back(*cross_qkv[1], *places, cross_out[1][1], grad_late, False, 1024)]
     grad_cq, grad_ck, grad_cv = zip(*cross_back)
     sent = group_c.second(*grad_cq)
     grad_cq = (after(grad_cq[0], *sent), grad_cq[1])
@@ -671,6 +675,7 @@
     )
     parts = over_cores(grad_cq, w_cq)
     sent = group_b.first()
+    group_b.send()
     parts_enc = over_cores([after(grad_ck[0], *sent), grad_ck[1], *grad_cv], [*w_ck, *w_cv])
     grad_one, low_one, gain_two = norm_back(
         hidden_one, gain_rows[1], [parts[0], [after(parts[1][0], parts_enc[0][0]), parts[1][1]]], grad_two
@@ -682,23 +687,24 @@
     self_back = [attend_back(*self_qkv[0], *places, self_out[0][1], grad_a[0], True, 256)]
     sent = group_c.third(*self_back[0])
     self_back.append(attend_back(*self_qkv[1], *places, self_out[1][1], after(grad_a[1], *sent), True, 256))
-    sent = group_b.second(*self_back[1])
-    self_back[1] = [*[after(t, *sent) for t in self_back[1][:2]], self_back[1][2]]
     grad_q, grad_k, grad_v = zip(*self_back)
     group_a = Group(
         [(norm_one, *grad_q), (grad_o, *[o[0] for o in self_out])],
         [(norm_one, *grad_k), (norm_one, *grad_v)],
     )
-    sent = group_a.first(group_b.late_x, group_b.late_y)
-    sent = [*sent, *group_b.third(*sent, behind=[group_c.low])]
+    sent = group_a.first()
     parts = over_cores(
-        [after(grad_q[0], *sent, grad_encoder), grad_q[1], *grad_k, *grad_v], [*w_q, *w_k, *w_v]
-    )
+        [after(grad_q[0], *sent), grad_q[1], *grad_k, *grad_v], [*w_q, *w_k, *w_v]
+    )
+    sent = group_b.second(*parts[0])
+    group_a.send(group_b.late_x, group_b.late_y)
     _, low_tok, gain_one = norm_back(
         x_own, gain_rows[0], [[after(parts[0][0], *sent), parts[0][1]], parts[1]], grad_one
     )
-    group_a.second(low_tok)
-    out_tok = reorder([after(low_tok, *group_a.sent)], model_rows, dy, False)
+    out_tok = reorder([after(low_tok, grad_encoder)], model_rows, dy, False)
+    sent = group_b.third(low_tok, behind=[group_c.low])
+    group_a.second(*sent)
+    group_a.third(behind=[group_b.low])
     dp_count = seq_count // 2
     gain_part = jnp.concatenate([gain_one, gain_two, gain_three])
     parts = [gain_part[:, n * D // 2 : (n + 1) * D // 2].reshape(3, dp_count // 2, model_rows) for n in range(2)]
@@ -710,7 +716,7 @@
     small = jnp.concatenate([*pieces(jnp.repeat(gain_part, 2, axis=0), 2), *pieces(tops, 3)], axis=1)
     small = jnp.pad(small, ((0, 0), (0, D - small.shape[1])))[:, None]
     sent = jnp.concatenate([out_tok.reshape(seq_count, block_rows, D), small], axis=1)
-    came = exchange(sent)
+    came = exchange(after(sent, *group_a.sent2))
     grad_tokens, small = came[:, :block_rows], came[:, block_rows].astype(f32)
     group_a.third(out_tok, behind=[group_b.low])
     sum_a, sum_b, sum_c = group_a.result, group_b.result, group_c.result

time: 633 us -> 618 us (0.976)
  waiting for transfers between devices: 204 us -> 191 us
    ppermute x11, waiting for transfers between devices: 105 us -> 90.5 us  [swap_y(): return row_major(lax.ppermute(row_major(values), 'dy', swap))]
    unnamed x334 -> x338, local copies, waits for them, and re-layouts: 53.3 us -> 54 us
  transfers between devices with their start and end apart: 56 -> 56, of which waited for: 20 -> 19; matrix products, arithmetic and copies ran while one was open for 5% -> 5% of each run, Pallas kernels for 35% -> 36%
where the time goes in v5:
time: 618 us; the launch traced here: 607 us
  Pallas kernels  241 us (39%)
  waiting for transfers between devices  191 us (31%)
  starting transfers between devices  70.1 us (11%)
  local copies, waits for them, and re-layouts  63.7 us (10%)
  other arithmetic  22.5 us (4%)
  between operations  18.7 us (3%)
    ppermute x11, waiting for transfers between devices, swap_y(): return row_major(lax.ppermute(row_major(values), 'dy', swap))  90.5 us
    unnamed x338, local copies, waits for them, and re-layouts  54 us
    pallas_call x15, Pallas kernels, weight_grad(): pl.pallas_call(kernel, grid=(steps,), in_specs=[columns] * first + [spec(...  53.1 us
    ppermute x11, waiting for transfers between devices, swap_x(): return row_major(lax.ppermute(row_major(values), 'mx', swap))  52.9 us
    pallas_call x4, Pallas kernels, attend_back(): pl.pallas_call(functools.partial(attend_back_kernel, causal, size), grid=...  48.9 us
    pallas_call x9, Pallas kernels, project(): pl.pallas_call(kernel, grid=(4,), in_specs=[spec((size, width_all), lambd...  42.3 us
    pallas_call x14, Pallas kernels, combine(): pl.pallas_call(kernel, grid=(2,), in_specs=[spec((size, v.shape[1]), lamb...  39.9 us
    pallas_call x4, Pallas kernels, attend(): pl.pallas_call(functools.partial(attend_kernel, causal, size), grid=(pair...  36.6 us
  transfers between devices with their start and end apart: 56, of which 19 were waited for; matrix products, arithmetic and copies ran while one was open for 5% of the time, Pallas kernels for 36%

profile of v5, /device:TPU:0, one launch (start us, length us, event | category | flops | bytes accessed | tf_op | source)
XLA Modules:
  0.0 607.2 jit_solution(3609160555792942657)
XLA Ops:
  11.8 32.1 %all-gather.4.cloned.1.call-done.refs_0_.refs_2_.refs_6_.refs_10_.refs_14_ = bf16[512,1152]{1,0:T(8,128)(2,1)} async-done(((bf16[128,1152]{1,0:T(8,128)(2,1)}), bf16[512,1152]{1,0:T(8,128)(2,1)}) %all-gather.4.cloned.1.call-update) | async-done | bytes 1179664 | tf_op jit(solution)/shard_map/all_gather | solution.py:472
  43.9 4.9 all-to-all-start
  53.4 34.3 %collective-permute-done.refs_1_.refs_3_.refs_7_.refs_11_.refs_15_ = bf16[512,1152]{1,0:T(8,128)(2,1)} collective-permute-done((bf16[512,1152]{1,0:T(8,128)(2,1)S(1)}, bf16[512,1152]{1,0:T(8,128)(2,1)}, u32[]{:S(2)}, u32[]{:S(2)}) %collective-permute-start) | collective-permute-done | bytes 1179680 | tf_op jit(solution)/shard_map/ppermute | solution.py:468
  99.6 4.5 project_plain.6.q_ref.k_ref.v_ref
  104.2 10.0 %attend.4 = (bf16[1024,256]{1,0:T(8,128)(2,1)S(1)}, f32[2,1024,2]{2,1,0:T(8,128)S(1)}, f32[2,8,128]{2,1,0:T(8,128)S(1)}) custom-call(bf16[1024,768]{1,0:T(8,128)(2,1)S(1)} %project_plain.6.q_ref.k_ref.v_ref, bf16[1024,768]{1,0:T(8,128)(2,1)S(1)} %project_plain.6.q_ref.k_ref.v_ref, bf16[1024,768]{1,0:T(8,128)(2,1)S(1)} %project_plain.6.q_ref.k_ref.v_ref, ...), custom_call_target="tpu_custom_call" | custom-call | flops 1 | bytes 1 | tf_op jit(solution)/shard_map/attend/pallas_call | solution.py:126
  117.9 4.5 project_plain.7.q_ref.k_ref.v_ref
  122.5 10.0 %attend.5 = (bf16[1024,256]{1,0:T(8,128)(2,1)S(1)}, f32[2,1024,2]{2,1,0:T(8,128)S(1)}, f32[2,8,128]{2,1,0:T(8,128)S(1)}) custom-call(bf16[1024,768]{1,0:T(8,128)(2,1)S(1)} %project_plain.7.q_ref.k_ref.v_ref, bf16[1024,768]{1,0:T(8,128)(2,1)S(1)} %project_plain.7.q_ref.k_ref.v_ref, bf16[1024,768]{1,0:T(8,128)(2,1)S(1)} %project_plain.7.q_ref.k_ref.v_ref, ...), custom_call_target="tpu_custom_call" | custom-call | flops 1 | bytes 1 | tf_op jit(solution)/shard_map/attend/pallas_call | solution.py:126
  134.3 4.0 collective-permute-done.8.refs_2_.refs_6_.refs_4_.refs_10_
  139.2 6.5 %all-to-all-start.1 = ((bf16[16,32,1024]{2,1,0:T(8,128)(2,1)}), bf16[16,32,1024]{2,1,0:T(8,128)(2,1)}, u32[]{:S(2)}, u32[]{:S(2)}) async-start(bf16[16,32,1024]{2,1,0:T(8,128)(2,1)} %param.21), calls=%async_computation.1 | async-start | bytes 2097152 | tf_op jit(solution)/shard_map/all_to_all | solution.py:562
  145.8 26.3 %collective-permute-done.9.refs_3_.refs_7_.refs_5_.refs_11_ = bf16[512,1024]{1,0:T(8,128)(2,1)S(1)} collective-permute-done((bf16[512,1024]{1,0:T(8,128)(2,1)S(1)}, bf16[512,1024]{1,0:T(8,128)(2,1)S(1)}, u32[]{:S(2)}, u32[]{:S(2)}) %collective-permute-start.9) | collective-permute-done | bytes 1048608 | tf_op jit(solution)/shard_map/ppermute | solution.py:468
  191.9 5.9 all-to-all-start.2
  201.5 3.8 project_plain.8
  205.4 5.0 project_plain.9
  210.4 8.4 %attend.7 = (bf16[1024,256]{1,0:T(8,128)(2,1)S(1)}, f32[2,1024,2]{2,1,0:T(8,128)S(1)}, f32[2,8,128]{2,1,0:T(8,128)}) custom-call(bf16[1024,256]{1,0:T(8,128)(2,1)S(1)} %get-tuple-element.162.q_ref, bf16[1024,256]{1,0:T(8,128)(2,1)S(1)} %get-tuple-element.169.k_ref, bf16[1024,256]{1,0:T(8,128)(2,1)S(1)} %get-tuple-element.170.v_ref, ...), custom_call_target="tpu_custom_call" | custom-call | flops 1 | bytes 1 | tf_op jit(solution)/shard_map/attend/pallas_call | solution.py:126
  219.8 14.0 %collective-permute-done.10.refs_1_.refs_3_.refs_5_.refs_9_ = bf16[512,2304]{1,0:T(8,128)(2,1)S(1)} collective-permute-done((bf16[512,2304]{1,0:T(8,128)(2,1)}, bf16[512,2304]{1,0:T(8,128)(2,1)S(1)}, u32[]{:S(2)}, u32[]{:S(2)}) %collective-permute-start.10) | collective-permute-done | bytes 2359328 | tf_op jit(solution)/shard_map/ppermute | solution.py:468
  235.3 8.3 %attend.6 = (bf16[1024,256]{1,0:T(8,128)(2,1)S(1)}, f32[2,1024,2]{2,1,0:T(8,128)S(1)}, f32[2,8,128]{2,1,0:T(8,128)}) custom-call(bf16[1024,256]{1,0:T(8,128)(2,1)S(1)} %get-tuple-element.164.q_ref, bf16[1024,256]{1,0:T(8,128)(2,1)S(1)} %get-tuple-element.166.k_ref, bf16[1024,256]{1,0:T(8,128)(2,1)S(1)} %get-tuple-element.167.v_ref, ...), custom_call_target="tpu_custom_call" | custom-call | flops 1 | bytes 1 | tf_op jit(solution)/shard_map/attend/pallas_call | solution.py:126
  260.3 5.8 project_gelu.2
  266.2 18.1 %collective-permute-done.18.refs_1_.refs_3_.refs_7_.refs_11_ = bf16[512,1536]{1,0:T(8,128)(2,1)} collective-permute-done((bf16[512,1536]{1,0:T(8,128)(2,1)}, bf16[512,1536]{1,0:T(8,128)(2,1)}, u32[]{:S(2)}, u32[]{:S(2)}) %collective-permute-start.18) | collective-permute-done | bytes 1572896 | tf_op jit(solution)/shard_map/ppermute | solution.py:464
  284.3 6.6 %project_gelu.3 = (bf16[1024,768]{1,0:T(8,128)(2,1)S(1)}, bf16[1024,768]{1,0:T(8,128)(2,1)S(1)}, bf16[1024,768]{1,0:T(8,128)(2,1)S(1)}) custom-call(bf16[512,1024]{1,0:T(8,128)(2,1)} %get-tuple-element.177.own_ref.refs_0_, bf16[512,1024]{1,0:T(8,128)(2,1)} %collective-permute-done.17.other_ref.refs_1_, ...), custom_call_target="tpu_custom_call" | custom-call | flops 1 | bytes 1 | tf_op jit(solution)/shard_map/project_gelu/pallas_call | solution.py:292
  290.9 5.6 project_scale.1
  296.5 5.7 weight_grad.15
  305.6 5.7 combine.19
  313.1 5.7 combine.18
  321.5 3.6 combine.21
  333.3 11.9 %attend_back.4 = (bf16[1024,256]{1,0:T(8,128)(2,1)S(1)}, bf16[1024,256]{1,0:T(8,128)(2,1)S(1)}, bf16[1024,256]{1,0:T(8,128)(2,1)S(1)}) custom-call(bf16[1024,256]{1,0:T(8,128)(2,1)S(1)} %copy-done.114, bf16[1024,256]{1,0:T(8,128)(2,1)S(1)} %copy-done.116, bf16[1024,256]{1,0:T(8,128)(2,1)S(1)} %copy-done.118, s32[1024,1]{1,0:T(8,128)S(1)} %copy-done.26, ...), custom_call_target="tpu_custom_call" | custom-call | flops 1 | bytes 1 | tf_op jit(solution)/shard_map/attend_back/pallas_call | solution.py:156
  348.3 12.3 %attend_back.5 = (bf16[1024,256]{1,0:T(8,128)(2,1)S(1)}, bf16[1024,256]{1,0:T(8,128)(2,1)S(1)}, bf16[1024,256]{1,0:T(8,128)(2,1)S(1)}) custom-call(bf16[1024,256]{1,0:T(8,128)(2,1)S(1)} %copy-done.108, bf16[1024,256]{1,0:T(8,128)(2,1)S(1)} %copy-done.110, bf16[1024,256]{1,0:T(8,128)(2,1)S(1)} %copy-done.112, s32[1024,1]{1,0:T(8,128)S(1)} %copy-done.26, ...), custom_call_target="tpu_custom_call" | custom-call | flops 1 | bytes 1 | tf_op jit(solution)/shard_map/attend_back/pallas_call | solution.py:156
  364.9 6.6 %collective-permute-done.24.refs_6_.refs_7_ = bf16[1024,1536]{1,0:T(8,128)(2,1)S(1)} collective-permute-done((bf16[1024,1536]{1,0:T(8,128)(2,1)S(1)}, bf16[1024,1536]{1,0:T(8,128)(2,1)S(1)}, u32[]{:S(2)}, u32[]{:S(2)}) %collective-permute-start.24) | collective-permute-done | bytes 3145760 | tf_op jit(solution)/shard_map/ppermute | solution.py:464
  371.6 3.8 weight_grad.17
  378.0 6.2 %all-to-all-start.3 = ((bf16[16,32,1024]{2,1,0:T(8,128)(2,1)}), bf16[16,32,1024]{2,1,0:T(8,128)(2,1)}, u32[]{:S(2)}, u32[]{:S(2)}) async-start(bf16[16,32,1024]{2,1,0:T(8,128)(2,1)} %bitcast.105), calls=%async_computation.3 | async-start | bytes 2097152 | tf_op jit(solution)/shard_map/all_to_all | solution.py:562
  410.0 4.2 project_plain.11
  416.3 12.2 %attend_back.6 = (bf16[1024,256]{1,0:T(8,128)(2,1)S(1)}, bf16[1024,256]{1,0:T(8,128)(2,1)S(1)}, bf16[1024,256]{1,0:T(8,128)(2,1)S(1)}) custom-call(bf16[1024,768]{1,0:T(8,128)(2,1)S(1)} %copy-done.23, bf16[1024,768]{1,0:T(8,128)(2,1)S(1)} %copy-done.23, bf16[1024,768]{1,0:T(8,128)(2,1)S(1)} %copy-done.23, s32[1024,1]{1,0:T(8,128)S(1)} %copy-done.27, ...), custom_call_target="tpu_custom_call" | custom-call | flops 1 | bytes 1 | tf_op jit(solution)/shard_map/attend_back/pallas_call | solution.py:156
  431.6 4.7 weight_grad.21
  439.8 5.6 all-to-all-start.4
  447.8 12.4 %attend_back.7 = (bf16[1024,256]{1,0:T(8,128)(2,1)S(1)}, bf16[1024,256]{1,0:T(8,128)(2,1)S(1)}, bf16[1024,256]{1,0:T(8,128)(2,1)S(1)}) custom-call(bf16[1024,768]{1,0:T(8,128)(2,1)S(1)} %copy-done.21, bf16[1024,768]{1,0:T(8,128)(2,1)S(1)} %copy-done.21, bf16[1024,768]{1,0:T(8,128)(2,1)S(1)} %copy-done.21, s32[1024,1]{1,0:T(8,128)S(1)} %copy-done.27, ...), custom_call_target="tpu_custom_call" | custom-call | flops 1 | bytes 1 | tf_op jit(solution)/shard_map/attend_back/pallas_call | solution.py:156
  460.2 3.5 weight_grad.22
  468.3 4.6 combine.27
  473.3 3.7 combine.26
  477.2 3.9 weight_grad.25
  487.8 8.7 %collective-permute-done.37.refs_13_ = bf16[512,512]{1,0:T(8,128)(2,1)} collective-permute-done((bf16[512,512]{1,0:T(8,128)(2,1)}, bf16[512,512]{1,0:T(8,128)(2,1)}, u32[]{:S(2)}, u32[]{:S(2)}) %collective-permute-start.37) | collective-permute-done | bytes 524320 | tf_op jit(solution)/shard_map/ppermute | solution.py:464
  496.5 3.5 collective-permute-done.38.refs_11_
  506.5 3.8 norm_back.5
  511.3 4.7 weight_grad.26
  520.1 4.4 collective-permute-done.40.refs_4_.refs_10_
  529.4 7.3 %all-to-all-start.5 = ((bf16[16,33,1024]{2,1,0:T(8,128)(2,1)}), bf16[16,33,1024]{2,1,0:T(8,128)(2,1)}, u32[]{:S(2)}, u32[]{:S(2)}) async-start(bf16[16,33,1024]{2,1,0:T(8,128)(2,1)} %pad_maximum_fusion), calls=%async_computation.5 | async-start | bytes 2621440 | tf_op jit(solution)/shard_map/all_to_all | solution.py:562
  540.1 11.8 %collective-permute-done.42.refs_11_ = bf16[512,512]{1,0:T(8,128)(2,1)S(1)} collective-permute-done((bf16[512,512]{1,0:T(8,128)(2,1)S(1)}, bf16[512,512]{1,0:T(8,128)(2,1)S(1)}, u32[]{:S(2)}, u32[]{:S(2)}) %collective-permute-start.42) | collective-permute-done | bytes 524320 | tf_op jit(solution)/shard_map/ppermute | solution.py:464
  552.0 6.0 collective-permute-done.41.refs_9_
  558.0 4.4 weight_grad.29
  579.5 12.2 %reduce-scatter.14.cloned.1.call-done = bf16[128,1024]{1,0:T(8,128)(2,1)} async-done(((bf16[512,1024]{1,0:T(8,128)(2,1)}), bf16[128,1024]{1,0:T(8,128)(2,1)}) %reduce-scatter.14.cloned.1.call-update) | async-done | bytes 262160
  (540 shorter events, 186.9 us)
Async XLA Ops:
  7.2 36.7 %all-gather.4.cloned.1.call-start = ((), (), s32[]{:S(2)}) async-start(), calls=%async_computation.9 | async-start | bytes 1474560 | tf_op jit(solution)/shard_map/all_gather | solution.py:472
  10.6 82.3 %all-gather.6.cloned.1.call-start = ((), (), s32[]{:S(2)}) async-start(), calls=%async_computation.10 | async-start | bytes 1310720 | tf_op jit(solution)/shard_map/all_gather | solution.py:472
  43.9 46.3 %all-to-all-start = ((bf16[16,32,1024]{2,1,0:T(8,128)(2,1)}), bf16[16,32,1024]{2,1,0:T(8,128)(2,1)S(1)}, u32[]{:S(2)}, u32[]{:S(2)}) async-start(bf16[16,32,1024]{2,1,0:T(8,128)(2,1)} %param.20), calls=%async_computation | async-start | bytes 2097152 | tf_op jit(solution)/shard_map/all_to_all | solution.py:562
  48.8 97.0 %all-gather.8.cloned.1.call-start = ((), (), s32[]{:S(2)}) async-start(), calls=%async_computation.11 | async-start | bytes 2949120 | tf_op jit(solution)/shard_map/all_gather | solution.py:472
  48.9 38.8 %collective-permute-start = (bf16[512,1152]{1,0:T(8,128)(2,1)S(1)}, bf16[512,1152]{1,0:T(8,128)(2,1)}, u32[]{:S(2)}, u32[]{:S(2)}) collective-permute-start(bf16[512,1152]{1,0:T(8,128)(2,1)S(1)} %copy-done.17), channel_id=1, source_target_pairs={{0,4},{4,0},{1,5},{5,1},{2,6},{6,2},{3,7},{7,3},{8,12},{12,8},{9,1... | collective-permute-start | bytes 3538952 | tf_op jit(solution)/shard_map/ppermute | solution.py:468
  51.9 64.1 %collective-permute-start.2 = (bf16[512,1152]{1,0:T(8,128)(2,1)S(1)}, bf16[512,1152]{1,0:T(8,128)(2,1)}, u32[]{:S(2)}, u32[]{:S(2)}) collective-permute-start(bf16[512,1152]{1,0:T(8,128)(2,1)S(1)} %copy-done.17), channel_id=1, source_target_pairs={{0,2},{2,0},{1,3},{3,1},{4,6},{6,4},{5,7},{7,5},{8,10},{10,8},{9,1... | collective-permute-start | bytes 3538952 | tf_op jit(solution)/shard_map/ppermute | solution.py:464
  88.7 29.2 %collective-permute-start.3 = (bf16[512,1152]{1,0:T(8,128)(2,1)}, bf16[512,1152]{1,0:T(8,128)(2,1)}, u32[]{:S(2)}, u32[]{:S(2)}) collective-permute-start(bf16[512,1152]{1,0:T(8,128)(2,1)} %collective-permute-done.refs_1_.refs_3_.refs_7_.refs_11_.refs_15_), channel_id=1, source_target_pairs={{0,2},{2,0},{1,3},{3,1},{4,6},{6,4},{5,7},{7,5},{8,10},{10,8},{9,1... | collective-permute-start | bytes 3538952 | tf_op jit(solution)/shard_map/ppermute | solution.py:464
  92.9 6.7 %collective-permute-start.1 = (bf16[512,1024]{1,0:T(8,128)(2,1)}, bf16[512,1024]{1,0:T(8,128)(2,1)}, u32[]{:S(2)}, u32[]{:S(2)}) collective-permute-start(bf16[512,1024]{1,0:T(8,128)(2,1)} %add_norm.3.own_ref.refs_0_), channel_id=1, source_target_pairs={{0,1},{1,0},{2,3},{3,2},{4,5},{5,4},{6,7},{7,6},{8,9},{9,8},{10,11... | collective-permute-start | bytes 3145736 | tf_op jit(solution)/shard_map/ppermute | solution.py:460
  92.9 41.3 %collective-permute-start.7 = (bf16[512,1024]{1,0:T(8,128)(2,1)}, bf16[512,1024]{1,0:T(8,128)(2,1)S(1)}, u32[]{:S(2)}, u32[]{:S(2)}) collective-permute-start(bf16[512,1024]{1,0:T(8,128)(2,1)} %all-gather.6.cloned.1.call-done.refs_0_.refs_4_.refs_2_.refs_8_), channel_id=1, source_target_pairs={{0,4},{4,0},{1,5},{5,1},{2,6},{6,2},{3,7},{7,3},{8,12},{12,8},{9,1... | collective-permute-start | bytes 3145736 | tf_op jit(solution)/shard_map/ppermute | solution.py:468
  94.8 43.5 %collective-permute-start.8 = (bf16[512,1024]{1,0:T(8,128)(2,1)}, bf16[512,1024]{1,0:T(8,128)(2,1)S(1)}, u32[]{:S(2)}, u32[]{:S(2)}) collective-permute-start(bf16[512,1024]{1,0:T(8,128)(2,1)} %all-gather.6.cloned.1.call-done.refs_0_.refs_4_.refs_2_.refs_8_), channel_id=1, source_target_pairs={{0,2},{2,0},{1,3},{3,1},{4,6},{6,4},{5,7},{7,5},{8,10},{10,8},{9,1... | collective-permute-start | bytes 3145736 | tf_op jit(solution)/shard_map/ppermute | solution.py:464
  138.3 33.8 %collective-permute-start.9 = (bf16[512,1024]{1,0:T(8,128)(2,1)S(1)}, bf16[512,1024]{1,0:T(8,128)(2,1)S(1)}, u32[]{:S(2)}, u32[]{:S(2)}) collective-permute-start(bf16[512,1024]{1,0:T(8,128)(2,1)S(1)} %collective-permute-done.8.refs_2_.refs_6_.refs_4_.refs_10_), channel_id=1, source_target_pairs={{0,4},{4,0},{1,5},{5,1},{2,6},{6,2},{3,7},{7,3},{8,12},{12,8},{9,1... | collective-permute-start | bytes 3145736 | tf_op jit(solution)/shard_map/ppermute | solution.py:468
  139.2 48.8 %all-to-all-start.1 = ((bf16[16,32,1024]{2,1,0:T(8,128)(2,1)}), bf16[16,32,1024]{2,1,0:T(8,128)(2,1)}, u32[]{:S(2)}, u32[]{:S(2)}) async-start(bf16[16,32,1024]{2,1,0:T(8,128)(2,1)} %param.21), calls=%async_computation.1 | async-start | bytes 2097152 | tf_op jit(solution)/shard_map/all_to_all | solution.py:562
  173.1 60.6 %collective-permute-start.10 = (bf16[512,2304]{1,0:T(8,128)(2,1)}, bf16[512,2304]{1,0:T(8,128)(2,1)S(1)}, u32[]{:S(2)}, u32[]{:S(2)}) collective-permute-start(bf16[512,2304]{1,0:T(8,128)(2,1)} %all-gather.8.cloned.1.call-done.refs_0_.refs_2_.refs_4_.refs_8_), channel_id=1, source_target_pairs={{0,4},{4,0},{1,5},{5,1},{2,6},{6,2},{3,7},{7,3},{8,12},{12,8},{9,1... | collective-permute-start | bytes 7077896 | tf_op jit(solution)/shard_map/ppermute | solution.py:468
  174.9 60.4 %collective-permute-start.11 = (bf16[512,2304]{1,0:T(8,128)(2,1)}, bf16[512,2304]{1,0:T(8,128)(2,1)}, u32[]{:S(2)}, u32[]{:S(2)}) collective-permute-start(bf16[512,2304]{1,0:T(8,128)(2,1)} %all-gather.8.cloned.1.call-done.refs_0_.refs_2_.refs_4_.refs_8_), channel_id=1, source_target_pairs={{0,2},{2,0},{1,3},{3,1},{4,6},{6,4},{5,7},{7,5},{8,10},{10,8},{9,1... | collective-permute-start | bytes 7077896 | tf_op jit(solution)/shard_map/ppermute | solution.py:464
  187.9 9.8 %collective-permute-start.6 = (bf16[512,1024]{1,0:T(8,128)(2,1)}, bf16[512,1024]{1,0:T(8,128)(2,1)}, u32[]{:S(2)}, u32[]{:S(2)}) collective-permute-start(bf16[512,1024]{1,0:T(8,128)(2,1)} %get-tuple-element.159.own_ref.refs_0_), channel_id=1, source_target_pairs={{0,1},{1,0},{2,3},{3,2},{4,5},{5,4},{6,7},{7,6},{8,9},{9,8},{10,11... | collective-permute-start | bytes 3145736 | tf_op jit(solution)/shard_map/ppermute | solution.py:460
  191.5 13.8 %collective-permute-start.12 = (bf16[512,1024]{1,0:T(8,128)(2,1)}, bf16[512,1024]{1,0:T(8,128)(2,1)}, u32[]{:S(2)}, u32[]{:S(2)}) collective-permute-start(bf16[512,1024]{1,0:T(8,128)(2,1)} %reorder.7.own_ref.refs_0_.refs_4_), channel_id=1, source_target_pairs={{0,1},{1,0},{2,3},{3,2},{4,5},{5,4},{6,7},{7,6},{8,9},{9,8},{10,11... | collective-permute-start | bytes 3145736 | tf_op jit(solution)/shard_map/ppermute | solution.py:460
  191.9 61.7 %all-to-all-start.2 = ((bf16[16,32,1024]{2,1,0:T(8,128)(2,1)}), bf16[16,32,1024]{2,1,0:T(8,128)(2,1)}, u32[]{:S(2)}, u32[]{:S(2)}) async-start(bf16[16,32,1024]{2,1,0:T(8,128)(2,1)} %param.22), calls=%async_computation.2 | async-start | bytes 2097152 | tf_op jit(solution)/shard_map/all_to_all | solution.py:562
  247.6 36.7 %collective-permute-start.18 = (bf16[512,1536]{1,0:T(8,128)(2,1)}, bf16[512,1536]{1,0:T(8,128)(2,1)}, u32[]{:S(2)}, u32[]{:S(2)}) collective-permute-start(bf16[512,1536]{1,0:T(8,128)(2,1)} %slice.156), channel_id=1, source_target_pairs={{0,2},{2,0},{1,3},{3,1},{4,6},{6,4},{5,7},{7,5},{8,10},{10,8},{9,1... | collective-permute-start | bytes 4718600 | tf_op jit(solution)/shard_map/ppermute | solution.py:464
  253.6 6.7 %collective-permute-start.17 = (bf16[512,1024]{1,0:T(8,128)(2,1)}, bf16[512,1024]{1,0:T(8,128)(2,1)}, u32[]{:S(2)}, u32[]{:S(2)}) collective-permute-start(bf16[512,1024]{1,0:T(8,128)(2,1)} %get-tuple-element.177.own_ref.refs_0_), channel_id=1, source_target_pairs={{0,1},{1,0},{2,3},{3,2},{4,5},{5,4},{6,7},{7,6},{8,9},{9,8},{10,11... | collective-permute-start | bytes 3145736 | tf_op jit(solution)/shard_map/ppermute | solution.py:460
  257.3 33.6 %collective-permute-start.15 = (bf16[512,1024]{1,0:T(8,128)(2,1)S(1)}, bf16[512,1024]{1,0:T(8,128)(2,1)S(1)}, u32[]{:S(2)}, u32[]{:S(2)}) collective-permute-start(bf16[512,1024]{1,0:T(8,128)(2,1)S(1)} %reorder.8.own_ref.refs_2_.base_ref), channel_id=1, source_target_pairs={{0,1},{1,0},{2,3},{3,2},{4,5},{5,4},{6,7},{7,6},{8,9},{9,8},{10,11... | collective-permute-start | bytes 3145736 | tf_op jit(solution)/shard_map/ppermute | solution.py:460
  259.0 31.9 %collective-permute-start.16 = (bf16[512,768]{1,0:T(8,128)(2,1)S(1)}, bf16[512,768]{1,0:T(8,128)(2,1)S(1)}, u32[]{:S(2)}, u32[]{:S(2)}) collective-permute-start(bf16[512,768]{1,0:T(8,128)(2,1)S(1)} %slice.155), channel_id=1, source_target_pairs={{0,4},{4,0},{1,5},{5,1},{2,6},{6,2},{3,7},{7,3},{8,12},{12,8},{9,1... | collective-permute-start | bytes 2359304 | tf_op jit(solution)/shard_map/ppermute | solution.py:468
  302.2 69.3 %collective-permute-start.24 = (bf16[1024,1536]{1,0:T(8,128)(2,1)S(1)}, bf16[1024,1536]{1,0:T(8,128)(2,1)S(1)}, u32[]{:S(2)}, u32[]{:S(2)}) collective-permute-start(bf16[1024,1536]{1,0:T(8,128)(2,1)S(1)} %weight_grad.15), channel_id=1, source_target_pairs={{0,2},{2,0},{1,3},{3,1},{4,6},{6,4},{5,7},{7,5},{8,10},{10,8},{9,1... | collective-permute-start | bytes 9437192 | tf_op jit(solution)/shard_map/ppermute | solution.py:464
  311.3 7.4 %collective-permute-start.19 = (f32[512,512]{1,0:T(8,128)S(1)}, f32[512,512]{1,0:T(8,128)S(1)}, u32[]{:S(2)}, u32[]{:S(2)}) collective-permute-start(f32[512,512]{1,0:T(8,128)S(1)} %get-tuple-element.190), channel_id=1, source_target_pairs={{0,1},{1,0},{2,3},{3,2},{4,5},{5,4},{6,7},{7,6},{8,9},{9,8},{10,11... | collective-permute-start | bytes 3145736 | tf_op jit(solution)/shard_map/ppermute | solution.py:460
  311.4 7.4 %collective-permute-start.20 = (f32[512,512]{1,0:T(8,128)S(1)}, f32[512,512]{1,0:T(8,128)S(1)}, u32[]{:S(2)}, u32[]{:S(2)}) collective-permute-start(f32[512,512]{1,0:T(8,128)S(1)} %get-tuple-element.191), channel_id=1, source_target_pairs={{0,1},{1,0},{2,3},{3,2},{4,5},{5,4},{6,7},{7,6},{8,9},{9,8},{10,11... | collective-permute-start | bytes 3145736 | tf_op jit(solution)/shard_map/ppermute | solution.py:460
  311.9 36.4 %collective-permute-start.25 = (bf16[512,1536]{1,0:T(8,128)(2,1)S(1)}, bf16[512,1536]{1,0:T(8,128)(2,1)S(1)}, u32[]{:S(2)}, u32[]{:S(2)}) collective-permute-start(bf16[512,1536]{1,0:T(8,128)(2,1)S(1)} %weight_grad.16), channel_id=1, source_target_pairs={{0,4},{4,0},{1,5},{5,1},{2,6},{6,2},{3,7},{7,3},{8,12},{12,8},{9,1... | collective-permute-start | bytes 4718600 | tf_op jit(solution)/shard_map/ppermute | solution.py:468
  321.5 7.6 %collective-permute-start.21 = (bf16[512,1024]{1,0:T(8,128)(2,1)S(1)}, bf16[512,1024]{1,0:T(8,128)(2,1)S(1)}, u32[]{:S(2)}, u32[]{:S(2)}) collective-permute-start(bf16[512,1024]{1,0:T(8,128)(2,1)S(1)} %get-tuple-element.196.own_ref.refs_2_), channel_id=1, source_target_pairs={{0,1},{1,0},{2,3},{3,2},{4,5},{5,4},{6,7},{7,6},{8,9},{9,8},{10,11... | collective-permute-start | bytes 3145736 | tf_op jit(solution)/shard_map/ppermute | solution.py:460
  377.4 23.9 %collective-permute-start.26 = (f32[512,512]{1,0:T(8,128)}, f32[512,512]{1,0:T(8,128)}, u32[]{:S(2)}, u32[]{:S(2)}) collective-permute-start(f32[512,512]{1,0:T(8,128)} %get-tuple-element.217), channel_id=1, source_target_pairs={{0,1},{1,0},{2,3},{3,2},{4,5},{5,4},{6,7},{7,6},{8,9},{9,8},{10,11... | collective-permute-start | bytes 3145736 | tf_op jit(solution)/shard_map/ppermute | solution.py:460
  377.5 23.8 %collective-permute-start.27 = (f32[512,512]{1,0:T(8,128)}, f32[512,512]{1,0:T(8,128)}, u32[]{:S(2)}, u32[]{:S(2)}) collective-permute-start(f32[512,512]{1,0:T(8,128)} %get-tuple-element.223), channel_id=1, source_target_pairs={{0,1},{1,0},{2,3},{3,2},{4,5},{5,4},{6,7},{7,6},{8,9},{9,8},{10,11... | collective-permute-start | bytes 3145736 | tf_op jit(solution)/shard_map/ppermute | solution.py:460
  378.0 32.0 %all-to-all-start.3 = ((bf16[16,32,1024]{2,1,0:T(8,128)(2,1)}), bf16[16,32,1024]{2,1,0:T(8,128)(2,1)}, u32[]{:S(2)}, u32[]{:S(2)}) async-start(bf16[16,32,1024]{2,1,0:T(8,128)(2,1)} %bitcast.105), calls=%async_computation.3 | async-start | bytes 2097152 | tf_op jit(solution)/shard_map/all_to_all | solution.py:562
  384.2 131.9 %reduce-scatter.10.cloned.1.call-start = ((), (), s32[]{:S(2)}) async-start(), calls=%async_computation.12 | async-start | bytes 2949120
  384.3 47.3 %collective-permute-start.31 = (bf16[512,1536]{1,0:T(8,128)(2,1)}, bf16[512,1536]{1,0:T(8,128)(2,1)}, u32[]{:S(2)}, u32[]{:S(2)}) collective-permute-start(bf16[512,1536]{1,0:T(8,128)(2,1)} %copy-done.121), channel_id=1, source_target_pairs={{0,4},{4,0},{1,5},{5,1},{2,6},{6,2},{3,7},{7,3},{8,12},{12,8},{9,1... | collective-permute-start | bytes 4718600 | tf_op jit(solution)/shard_map/ppermute | solution.py:468
  397.7 10.8 %collective-permute-start.28 = (f32[512,512]{1,0:T(8,128)S(1)}, f32[512,512]{1,0:T(8,128)S(1)}, u32[]{:S(2)}, u32[]{:S(2)}) collective-permute-start(f32[512,512]{1,0:T(8,128)S(1)} %get-tuple-element.228), channel_id=1, source_target_pairs={{0,1},{1,0},{2,3},{3,2},{4,5},{5,4},{6,7},{7,6},{8,9},{9,8},{10,11... | collective-permute-start | bytes 3145736 | tf_op jit(solution)/shard_map/ppermute | solution.py:460
  397.8 10.7 %collective-permute-start.29 = (f32[512,512]{1,0:T(8,128)S(1)}, f32[512,512]{1,0:T(8,128)S(1)}, u32[]{:S(2)}, u32[]{:S(2)}) collective-permute-start(f32[512,512]{1,0:T(8,128)S(1)} %get-tuple-element.230), channel_id=1, source_target_pairs={{0,1},{1,0},{2,3},{3,2},{4,5},{5,4},{6,7},{7,6},{8,9},{9,8},{10,11... | collective-permute-start | bytes 3145736 | tf_op jit(solution)/shard_map/ppermute | solution.py:460
  407.0 23.9 %collective-permute-start.32 = (bf16[512,768]{1,0:T(8,128)(2,1)}, bf16[512,768]{1,0:T(8,128)(2,1)}, u32[]{:S(2)}, u32[]{:S(2)}) collective-permute-start(bf16[512,768]{1,0:T(8,128)(2,1)} %weight_grad.18), channel_id=1, source_target_pairs={{0,2},{2,0},{1,3},{3,1},{4,6},{6,4},{5,7},{7,5},{8,10},{10,8},{9,1... | collective-permute-start | bytes 2359304 | tf_op jit(solution)/shard_map/ppermute | solution.py:464
  437.7 39.4 %collective-permute-start.34 = (bf16[512,1024]{1,0:T(8,128)(2,1)}, bf16[512,1024]{1,0:T(8,128)(2,1)}, u32[]{:S(2)}, u32[]{:S(2)}) collective-permute-start(bf16[512,1024]{1,0:T(8,128)(2,1)} %copy-done.123), channel_id=1, source_target_pairs={{0,4},{4,0},{1,5},{5,1},{2,6},{6,2},{3,7},{7,3},{8,12},{12,8},{9,1... | collective-permute-start | bytes 3145736 | tf_op jit(solution)/shard_map/ppermute | solution.py:468
  438.5 42.6 %collective-permute-start.33 = (bf16[1024,512]{1,0:T(8,128)(2,1)}, bf16[1024,512]{1,0:T(8,128)(2,1)}, u32[]{:S(2)}, u32[]{:S(2)}) collective-permute-start(bf16[1024,512]{1,0:T(8,128)(2,1)} %copy-done.139), channel_id=1, source_target_pairs={{0,2},{2,0},{1,3},{3,1},{4,6},{6,4},{5,7},{7,5},{8,10},{10,8},{9,1... | collective-permute-start | bytes 3145736 | tf_op jit(solution)/shard_map/ppermute | solution.py:464
  439.8 78.5 %all-to-all-start.4 = ((bf16[16,32,1024]{2,1,0:T(8,128)(2,1)}), bf16[16,32,1024]{2,1,0:T(8,128)(2,1)}, u32[]{:S(2)}, u32[]{:S(2)}) async-start(bf16[16,32,1024]{2,1,0:T(8,128)(2,1)} %bitcast.104), calls=%async_computation.4 | async-start | bytes 2097152 | tf_op jit(solution)/shard_map/all_to_all | solution.py:562
  445.4 117.0 %reduce-scatter.12.cloned.1.call-start = ((), (), s32[]{:S(2)}) async-start(), calls=%async_computation.13 | async-start | bytes 1310720
  472.8 29.6 %collective-permute-start.35 = (f32[512,512]{1,0:T(8,128)}, f32[512,512]{1,0:T(8,128)}, u32[]{:S(2)}, u32[]{:S(2)}) collective-permute-start(f32[512,512]{1,0:T(8,128)} %get-tuple-element.250), channel_id=1, source_target_pairs={{0,1},{1,0},{2,3},{3,2},{4,5},{5,4},{6,7},{7,6},{8,9},{9,8},{10,11... | collective-permute-start | bytes 3145736 | tf_op jit(solution)/shard_map/ppermute | solution.py:460
  472.8 29.6 %collective-permute-start.36 = (f32[512,512]{1,0:T(8,128)}, f32[512,512]{1,0:T(8,128)}, u32[]{:S(2)}, u32[]{:S(2)}) collective-permute-start(f32[512,512]{1,0:T(8,128)} %get-tuple-element.251), channel_id=1, source_target_pairs={{0,1},{1,0},{2,3},{3,2},{4,5},{5,4},{6,7},{7,6},{8,9},{9,8},{10,11... | collective-permute-start | bytes 3145736 | tf_op jit(solution)/shard_map/ppermute | solution.py:460
  481.1 15.4 %collective-permute-start.37 = (bf16[512,512]{1,0:T(8,128)(2,1)}, bf16[512,512]{1,0:T(8,128)(2,1)}, u32[]{:S(2)}, u32[]{:S(2)}) collective-permute-start(bf16[512,512]{1,0:T(8,128)(2,1)} %weight_grad.25), channel_id=1, source_target_pairs={{0,2},{2,0},{1,3},{3,1},{4,6},{6,4},{5,7},{7,5},{8,10},{10,8},{9,1... | collective-permute-start | bytes 1572872 | tf_op jit(solution)/shard_map/ppermute | solution.py:464
  486.0 14.0 %collective-permute-start.38 = (bf16[512,512]{1,0:T(8,128)(2,1)}, bf16[512,512]{1,0:T(8,128)(2,1)}, u32[]{:S(2)}, u32[]{:S(2)}) collective-permute-start(bf16[512,512]{1,0:T(8,128)(2,1)} %weight_grad.24), channel_id=1, source_target_pairs={{0,4},{4,0},{1,5},{5,1},{2,6},{6,2},{3,7},{7,3},{8,12},{12,8},{9,1... | collective-permute-start | bytes 1572872 | tf_op jit(solution)/shard_map/ppermute | solution.py:468
  500.1 24.4 %collective-permute-start.40 = (bf16[512,1024]{1,0:T(8,128)(2,1)}, bf16[512,1024]{1,0:T(8,128)(2,1)}, u32[]{:S(2)}, u32[]{:S(2)}) collective-permute-start(bf16[512,1024]{1,0:T(8,128)(2,1)} %copy-done.122), channel_id=1, source_target_pairs={{0,4},{4,0},{1,5},{5,1},{2,6},{6,2},{3,7},{7,3},{8,12},{12,8},{9,1... | collective-permute-start | bytes 3145736 | tf_op jit(solution)/shard_map/ppermute | solution.py:468
  501.6 25.3 %collective-permute-start.39 = (bf16[1024,512]{1,0:T(8,128)(2,1)}, bf16[1024,512]{1,0:T(8,128)(2,1)}, u32[]{:S(2)}, u32[]{:S(2)}) collective-permute-start(bf16[1024,512]{1,0:T(8,128)(2,1)} %copy-done.136), channel_id=1, source_target_pairs={{0,2},{2,0},{1,3},{3,1},{4,6},{6,4},{5,7},{7,5},{8,10},{10,8},{9,1... | collective-permute-start | bytes 3145736 | tf_op jit(solution)/shard_map/ppermute | solution.py:464
  529.4 41.2 %all-to-all-start.5 = ((bf16[16,33,1024]{2,1,0:T(8,128)(2,1)}), bf16[16,33,1024]{2,1,0:T(8,128)(2,1)}, u32[]{:S(2)}, u32[]{:S(2)}) async-start(bf16[16,33,1024]{2,1,0:T(8,128)(2,1)} %pad_maximum_fusion), calls=%async_computation.5 | async-start | bytes 2621440 | tf_op jit(solution)/shard_map/all_to_all | solution.py:562
  536.7 55.1 %reduce-scatter.14.cloned.1.call-start = ((), (), s32[]{:S(2)}) async-start(), calls=%async_computation.14 | async-start | bytes 1310720
  536.7 15.2 %collective-permute-start.42 = (bf16[512,512]{1,0:T(8,128)(2,1)S(1)}, bf16[512,512]{1,0:T(8,128)(2,1)S(1)}, u32[]{:S(2)}, u32[]{:S(2)}) collective-permute-start(bf16[512,512]{1,0:T(8,128)(2,1)S(1)} %weight_grad.28), channel_id=1, source_target_pairs={{0,2},{2,0},{1,3},{3,1},{4,6},{6,4},{5,7},{7,5},{8,10},{10,8},{9,1... | collective-permute-start | bytes 1572872 | tf_op jit(solution)/shard_map/ppermute | solution.py:464
  538.7 19.3 %collective-permute-start.41 = (bf16[512,512]{1,0:T(8,128)(2,1)S(1)}, bf16[512,512]{1,0:T(8,128)(2,1)S(1)}, u32[]{:S(2)}, u32[]{:S(2)}) collective-permute-start(bf16[512,512]{1,0:T(8,128)(2,1)S(1)} %weight_grad.27), channel_id=1, source_target_pairs={{0,4},{4,0},{1,5},{5,1},{2,6},{6,2},{3,7},{7,3},{8,12},{12,8},{9,1... | collective-permute-start | bytes 1572872 | tf_op jit(solution)/shard_map/ppermute | solution.py:468
  (172 other events, 1428.4 us)
Sparse Core Ops, SparseCore 0:
  10.8 33.1 all-gather.3
  46.1 43.9 all-gather.5
  92.2 49.8 all-gather.7
  437.8 66.0 reduce-scatter.9
  518.4 35.2 reduce-scatter.11
  563.7 28.0 reduce-scatter.13

commit v6 on v5

--- a/solution.py
+++ b/solution.py
@@ -509,7 +509,7 @@
             weight_grad(self.own_x, 1, [(self.from_x, 1, 0)]),
             weight_grad(self.other_y, 0, [(self.from_y, 0, -wide_y)]),
         ]
-        self.sent2 = self.sent
+        self.middle = self.sent
         self.late_y, self.late_x = swap_y(self.sent[0]), swap_x(self.sent[1])
         return self.sent
 
@@ -696,14 +696,14 @@
     parts = over_cores(
         [after(grad_q[0], *sent), grad_q[1], *grad_k, *grad_v], [*w_q, *w_k, *w_v]
     )
-    sent = group_b.second(*parts[0])
+    group_b.second(*parts[0])
     group_a.send(group_b.late_x, group_b.late_y)
+    sent = group_b.third(behind=[group_c.low])
     _, low_tok, gain_one = norm_back(
-        x_own, gain_rows[0], [[after(parts[0][0], *sent), parts[0][1]], parts[1]], grad_one
+        x_own, gain_rows[0], [[after(parts[0][0], *sent, group_c.low), parts[0][1]], parts[1]], grad_one
     )
     out_tok = reorder([after(low_tok, grad_encoder)], model_rows, dy, False)
-    sent = group_b.third(low_tok, behind=[group_c.low])
-    group_a.second(*sent)
+    group_a.second(low_tok)
     group_a.third(behind=[group_b.low])
     dp_count = seq_count // 2
     gain_part = jnp.concatenate([gain_one, gain_two, gain_three])
@@ -716,7 +716,7 @@
     small = jnp.concatenate([*pieces(jnp.repeat(gain_part, 2, axis=0), 2), *pieces(tops, 3)], axis=1)
     small = jnp.pad(small, ((0, 0), (0, D - small.shape[1])))[:, None]
     sent = jnp.concatenate([out_tok.reshape(seq_count, block_rows, D), small], axis=1)
-    came = exchange(after(sent, *group_a.sent2))
+    came = exchange(after(sent, *group_a.middle))
     grad_tokens, small = came[:, :block_rows], came[:, block_rows].astype(f32)
     group_a.third(out_tok, behind=[group_b.low])
     sum_a, sum_b, sum_c = group_a.result, group_b.result, group_c.result

time: 618 us -> 620 us (level)
    ppermute x11, waiting for transfers between devices: 90.5 us -> 80.7 us  [swap_y(): return row_major(lax.ppermute(row_major(values), 'dy', swap))]
    unnamed x338 -> x336, local copies, waits for them, and re-layouts: 54 us -> 58.7 us
where the time goes in v6:
time: 620 us; the launch traced here: 609 us
  Pallas kernels  239 us (39%)
  waiting for transfers between devices  189 us (30%)
  starting transfers between devices  70.7 us (11%)
  local copies, waits for them, and re-layouts  68.4 us (11%)
  other arithmetic  22.5 us (4%)
  between operations  18.6 us (3%)
    ppermute x11, waiting for transfers between devices, swap_y(): return row_major(lax.ppermute(row_major(values), 'dy', swap))  80.7 us
    unnamed x336, local copies, waits for them, and re-layouts  58.7 us
    ppermute x11, waiting for transfers between devices, swap_x(): return row_major(lax.ppermute(row_major(values), 'mx', swap))  57.3 us
    pallas_call x15, Pallas kernels, weight_grad(): pl.pallas_call(kernel, grid=(steps,), in_specs=[columns] * first + [spec(...  51.3 us
    pallas_call x4, Pallas kernels, attend_back(): pl.pallas_call(functools.partial(attend_back_kernel, causal, size), grid=...  48.9 us
    pallas_call x9, Pallas kernels, project(): pl.pallas_call(kernel, grid=(4,), in_specs=[spec((size, width_all), lambd...  42.3 us
    pallas_call x14, Pallas kernels, combine(): pl.pallas_call(kernel, grid=(2,), in_specs=[spec((size, v.shape[1]), lamb...  40.2 us
    all_to_all x6, starting transfers between devices, exchange(): lax.all_to_all(values, chips, split_axis=0, concat_axis=0, tiled=True)  36.8 us
  transfers between devices with their start and end apart: 56, of which 19 were waited for; matrix products, arithmetic and copies ran while one was open for 5% of the time, Pallas kernels for 36%

profile of v6, /device:TPU:0, one launch (start us, length us, event | category | flops | bytes accessed | tf_op | source)
XLA Modules:
  0.0 609.1 jit_solution(13268428363338995596)
XLA Ops:
  11.8 32.1 %all-gather.4.cloned.1.call-done.refs_0_.refs_2_.refs_6_.refs_10_.refs_14_ = bf16[512,1152]{1,0:T(8,128)(2,1)} async-done(((bf16[128,1152]{1,0:T(8,128)(2,1)}), bf16[512,1152]{1,0:T(8,128)(2,1)}) %all-gather.4.cloned.1.call-update) | async-done | bytes 1179664 | tf_op jit(solution)/shard_map/all_gather | solution.py:472
  43.9 4.9 all-to-all-start
  53.4 34.3 %collective-permute-done.refs_1_.refs_3_.refs_7_.refs_11_.refs_15_ = bf16[512,1152]{1,0:T(8,128)(2,1)} collective-permute-done((bf16[512,1152]{1,0:T(8,128)(2,1)S(1)}, bf16[512,1152]{1,0:T(8,128)(2,1)}, u32[]{:S(2)}, u32[]{:S(2)}) %collective-permute-start) | collective-permute-done | bytes 1179680 | tf_op jit(solution)/shard_map/ppermute | solution.py:468
  99.6 4.5 project_plain.6.q_ref.k_ref.v_ref
  104.2 10.0 %attend.4 = (bf16[1024,256]{1,0:T(8,128)(2,1)S(1)}, f32[2,1024,2]{2,1,0:T(8,128)S(1)}, f32[2,8,128]{2,1,0:T(8,128)S(1)}) custom-call(bf16[1024,768]{1,0:T(8,128)(2,1)S(1)} %project_plain.6.q_ref.k_ref.v_ref, bf16[1024,768]{1,0:T(8,128)(2,1)S(1)} %project_plain.6.q_ref.k_ref.v_ref, bf16[1024,768]{1,0:T(8,128)(2,1)S(1)} %project_plain.6.q_ref.k_ref.v_ref, ...), custom_call_target="tpu_custom_call" | custom-call | flops 1 | bytes 1 | tf_op jit(solution)/shard_map/attend/pallas_call | solution.py:126
  117.9 4.5 project_plain.7.q_ref.k_ref.v_ref
  122.5 10.0 %attend.5 = (bf16[1024,256]{1,0:T(8,128)(2,1)S(1)}, f32[2,1024,2]{2,1,0:T(8,128)S(1)}, f32[2,8,128]{2,1,0:T(8,128)S(1)}) custom-call(bf16[1024,768]{1,0:T(8,128)(2,1)S(1)} %project_plain.7.q_ref.k_ref.v_ref, bf16[1024,768]{1,0:T(8,128)(2,1)S(1)} %project_plain.7.q_ref.k_ref.v_ref, bf16[1024,768]{1,0:T(8,128)(2,1)S(1)} %project_plain.7.q_ref.k_ref.v_ref, ...), custom_call_target="tpu_custom_call" | custom-call | flops 1 | bytes 1 | tf_op jit(solution)/shard_map/attend/pallas_call | solution.py:126
  134.3 4.0 collective-permute-done.8.refs_2_.refs_6_.refs_4_.refs_10_
  139.2 6.5 %all-to-all-start.1 = ((bf16[16,32,1024]{2,1,0:T(8,128)(2,1)}), bf16[16,32,1024]{2,1,0:T(8,128)(2,1)}, u32[]{:S(2)}, u32[]{:S(2)}) async-start(bf16[16,32,1024]{2,1,0:T(8,128)(2,1)} %param.21), calls=%async_computation.1 | async-start | bytes 2097152 | tf_op jit(solution)/shard_map/all_to_all | solution.py:562
  145.8 26.3 %collective-permute-done.9.refs_3_.refs_7_.refs_5_.refs_11_ = bf16[512,1024]{1,0:T(8,128)(2,1)S(1)} collective-permute-done((bf16[512,1024]{1,0:T(8,128)(2,1)S(1)}, bf16[512,1024]{1,0:T(8,128)(2,1)S(1)}, u32[]{:S(2)}, u32[]{:S(2)}) %collective-permute-start.9) | collective-permute-done | bytes 1048608 | tf_op jit(solution)/shard_map/ppermute | solution.py:468
  188.1 3.4 reorder.7.own_ref.refs_0_.refs_4_
  191.9 5.9 all-to-all-start.2
  201.5 3.8 project_plain.8
  205.4 5.0 project_plain.9
  210.4 8.4 %attend.7 = (bf16[1024,256]{1,0:T(8,128)(2,1)S(1)}, f32[2,1024,2]{2,1,0:T(8,128)S(1)}, f32[2,8,128]{2,1,0:T(8,128)}) custom-call(bf16[1024,256]{1,0:T(8,128)(2,1)S(1)} %get-tuple-element.160.q_ref, bf16[1024,256]{1,0:T(8,128)(2,1)S(1)} %get-tuple-element.167.k_ref, bf16[1024,256]{1,0:T(8,128)(2,1)S(1)} %get-tuple-element.168.v_ref, ...), custom_call_target="tpu_custom_call" | custom-call | flops 1 | bytes 1 | tf_op jit(solution)/shard_map/attend/pallas_call | solution.py:126
  219.8 13.9 %collective-permute-done.10.refs_1_.refs_3_.refs_5_.refs_9_ = bf16[512,2304]{1,0:T(8,128)(2,1)S(1)} collective-permute-done((bf16[512,2304]{1,0:T(8,128)(2,1)}, bf16[512,2304]{1,0:T(8,128)(2,1)S(1)}, u32[]{:S(2)}, u32[]{:S(2)}) %collective-permute-start.10) | collective-permute-done | bytes 2359328 | tf_op jit(solution)/shard_map/ppermute | solution.py:468
  235.3 8.3 %attend.6 = (bf16[1024,256]{1,0:T(8,128)(2,1)S(1)}, f32[2,1024,2]{2,1,0:T(8,128)S(1)}, f32[2,8,128]{2,1,0:T(8,128)}) custom-call(bf16[1024,256]{1,0:T(8,128)(2,1)S(1)} %get-tuple-element.162.q_ref, bf16[1024,256]{1,0:T(8,128)(2,1)S(1)} %get-tuple-element.164.k_ref, bf16[1024,256]{1,0:T(8,128)(2,1)S(1)} %get-tuple-element.165.v_ref, ...), custom_call_target="tpu_custom_call" | custom-call | flops 1 | bytes 1 | tf_op jit(solution)/shard_map/attend/pallas_call | solution.py:126
  260.3 5.8 project_gelu.2
  266.2 18.1 %collective-permute-done.18.refs_1_.refs_3_.refs_7_.refs_11_ = bf16[512,1536]{1,0:T(8,128)(2,1)} collective-permute-done((bf16[512,1536]{1,0:T(8,128)(2,1)}, bf16[512,1536]{1,0:T(8,128)(2,1)}, u32[]{:S(2)}, u32[]{:S(2)}) %collective-permute-start.18) | collective-permute-done | bytes 1572896 | tf_op jit(solution)/shard_map/ppermute | solution.py:464
  284.3 6.6 %project_gelu.3 = (bf16[1024,768]{1,0:T(8,128)(2,1)S(1)}, bf16[1024,768]{1,0:T(8,128)(2,1)S(1)}, bf16[1024,768]{1,0:T(8,128)(2,1)S(1)}) custom-call(bf16[512,1024]{1,0:T(8,128)(2,1)} %get-tuple-element.175.own_ref.refs_0_, bf16[512,1024]{1,0:T(8,128)(2,1)} %collective-permute-done.17.other_ref.refs_1_, ...), custom_call_target="tpu_custom_call" | custom-call | flops 1 | bytes 1 | tf_op jit(solution)/shard_map/project_gelu/pallas_call | solution.py:292
  290.9 5.6 project_scale.1
  296.5 5.7 weight_grad.15
  305.6 5.7 combine.19
  313.1 5.7 combine.18
  321.5 3.6 combine.21
  325.6 3.5 combine.20
  333.3 11.9 %attend_back.4 = (bf16[1024,256]{1,0:T(8,128)(2,1)S(1)}, bf16[1024,256]{1,0:T(8,128)(2,1)S(1)}, bf16[1024,256]{1,0:T(8,128)(2,1)S(1)}) custom-call(bf16[1024,256]{1,0:T(8,128)(2,1)S(1)} %copy-done.112, bf16[1024,256]{1,0:T(8,128)(2,1)S(1)} %copy-done.114, bf16[1024,256]{1,0:T(8,128)(2,1)S(1)} %copy-done.116, s32[1024,1]{1,0:T(8,128)S(1)} %copy-done.26, ...), custom_call_target="tpu_custom_call" | custom-call | flops 1 | bytes 1 | tf_op jit(solution)/shard_map/attend_back/pallas_call | solution.py:156
  348.3 12.3 %attend_back.5 = (bf16[1024,256]{1,0:T(8,128)(2,1)S(1)}, bf16[1024,256]{1,0:T(8,128)(2,1)S(1)}, bf16[1024,256]{1,0:T(8,128)(2,1)S(1)}) custom-call(bf16[1024,256]{1,0:T(8,128)(2,1)S(1)} %copy-done.106, bf16[1024,256]{1,0:T(8,128)(2,1)S(1)} %copy-done.108, bf16[1024,256]{1,0:T(8,128)(2,1)S(1)} %copy-done.110, s32[1024,1]{1,0:T(8,128)S(1)} %copy-done.26, ...), custom_call_target="tpu_custom_call" | custom-call | flops 1 | bytes 1 | tf_op jit(solution)/shard_map/attend_back/pallas_call | solution.py:156
  361.4 3.5 weight_grad.18
  364.9 6.6 %collective-permute-done.24.refs_6_.refs_7_ = bf16[1024,1536]{1,0:T(8,128)(2,1)S(1)} collective-permute-done((bf16[1024,1536]{1,0:T(8,128)(2,1)S(1)}, bf16[1024,1536]{1,0:T(8,128)(2,1)S(1)}, u32[]{:S(2)}, u32[]{:S(2)}) %collective-permute-start.24) | collective-permute-done | bytes 3145760 | tf_op jit(solution)/shard_map/ppermute | solution.py:464
  371.6 3.8 weight_grad.17
  378.0 6.2 %all-to-all-start.3 = ((bf16[16,32,1024]{2,1,0:T(8,128)(2,1)}), bf16[16,32,1024]{2,1,0:T(8,128)(2,1)}, u32[]{:S(2)}, u32[]{:S(2)}) async-start(bf16[16,32,1024]{2,1,0:T(8,128)(2,1)} %bitcast.105), calls=%async_computation.3 | async-start | bytes 2097152 | tf_op jit(solution)/shard_map/all_to_all | solution.py:562
  410.0 4.2 project_plain.11
  416.3 12.4 %attend_back.6 = (bf16[1024,256]{1,0:T(8,128)(2,1)S(1)}, bf16[1024,256]{1,0:T(8,128)(2,1)S(1)}, bf16[1024,256]{1,0:T(8,128)(2,1)S(1)}) custom-call(bf16[1024,768]{1,0:T(8,128)(2,1)S(1)} %copy-done.23, bf16[1024,768]{1,0:T(8,128)(2,1)S(1)} %copy-done.23, bf16[1024,768]{1,0:T(8,128)(2,1)S(1)} %copy-done.23, s32[1024,1]{1,0:T(8,128)S(1)} %copy-done.27, ...), custom_call_target="tpu_custom_call" | custom-call | flops 1 | bytes 1 | tf_op jit(solution)/shard_map/attend_back/pallas_call | solution.py:156
  431.6 4.7 weight_grad.21
  439.8 5.6 all-to-all-start.4
  447.7 12.2 %attend_back.7 = (bf16[1024,256]{1,0:T(8,128)(2,1)S(1)}, bf16[1024,256]{1,0:T(8,128)(2,1)S(1)}, bf16[1024,256]{1,0:T(8,128)(2,1)S(1)}) custom-call(bf16[1024,768]{1,0:T(8,128)(2,1)S(1)} %copy-done.21, bf16[1024,768]{1,0:T(8,128)(2,1)S(1)} %copy-done.21, bf16[1024,768]{1,0:T(8,128)(2,1)S(1)} %copy-done.21, s32[1024,1]{1,0:T(8,128)S(1)} %copy-done.27, ...), custom_call_target="tpu_custom_call" | custom-call | flops 1 | bytes 1 | tf_op jit(solution)/shard_map/attend_back/pallas_call | solution.py:156
  460.0 4.3 weight_grad.22
  464.3 3.6 weight_grad.23
  467.9 3.8 combine.26
  481.8 4.8 combine.27
  487.2 4.6 collective-permute-done.36.refs_13_
  496.0 3.4 weight_grad.26
  500.4 3.4 reduce-scatter.10.cloned.1.call-done
  526.2 7.8 %all-to-all-start.5 = ((bf16[16,33,1024]{2,1,0:T(8,128)(2,1)}), bf16[16,33,1024]{2,1,0:T(8,128)(2,1)}, u32[]{:S(2)}, u32[]{:S(2)}) async-start(bf16[16,33,1024]{2,1,0:T(8,128)(2,1)} %pad_maximum_fusion), calls=%async_computation.5 | async-start | bytes 2621440 | tf_op jit(solution)/shard_map/all_to_all | solution.py:562
  537.5 20.4 %collective-permute-done.42.refs_11_ = bf16[512,512]{1,0:T(8,128)(2,1)S(1)} collective-permute-done((bf16[512,512]{1,0:T(8,128)(2,1)S(1)}, bf16[512,512]{1,0:T(8,128)(2,1)S(1)}, u32[]{:S(2)}, u32[]{:S(2)}) %collective-permute-start.42) | collective-permute-done | bytes 524320 | tf_op jit(solution)/shard_map/ppermute | solution.py:464
  559.5 4.4 weight_grad.29
  579.6 14.1 %reduce-scatter.14.cloned.1.call-done = bf16[128,1024]{1,0:T(8,128)(2,1)} async-done(((bf16[512,1024]{1,0:T(8,128)(2,1)}), bf16[128,1024]{1,0:T(8,128)(2,1)}) %reduce-scatter.14.cloned.1.call-update) | async-done | bytes 262160
  (538 shorter events, 186.4 us)
Async XLA Ops:
  7.2 36.7 %all-gather.4.cloned.1.call-start = ((), (), s32[]{:S(2)}) async-start(), calls=%async_computation.9 | async-start | bytes 1474560 | tf_op jit(solution)/shard_map/all_gather | solution.py:472
  10.6 82.3 %all-gather.6.cloned.1.call-start = ((), (), s32[]{:S(2)}) async-start(), calls=%async_computation.10 | async-start | bytes 1310720 | tf_op jit(solution)/shard_map/all_gather | solution.py:472
  43.9 46.3 %all-to-all-start = ((bf16[16,32,1024]{2,1,0:T(8,128)(2,1)}), bf16[16,32,1024]{2,1,0:T(8,128)(2,1)S(1)}, u32[]{:S(2)}, u32[]{:S(2)}) async-start(bf16[16,32,1024]{2,1,0:T(8,128)(2,1)} %param.20), calls=%async_computation | async-start | bytes 2097152 | tf_op jit(solution)/shard_map/all_to_all | solution.py:562
  48.8 97.0 %all-gather.8.cloned.1.call-start = ((), (), s32[]{:S(2)}) async-start(), calls=%async_computation.11 | async-start | bytes 2949120 | tf_op jit(solution)/shard_map/all_gather | solution.py:472
  48.9 38.8 %collective-permute-start = (bf16[512,1152]{1,0:T(8,128)(2,1)S(1)}, bf16[512,1152]{1,0:T(8,128)(2,1)}, u32[]{:S(2)}, u32[]{:S(2)}) collective-permute-start(bf16[512,1152]{1,0:T(8,128)(2,1)S(1)} %copy-done.17), channel_id=1, source_target_pairs={{0,4},{4,0},{1,5},{5,1},{2,6},{6,2},{3,7},{7,3},{8,12},{12,8},{9,1... | collective-permute-start | bytes 3538952 | tf_op jit(solution)/shard_map/ppermute | solution.py:468
  51.9 64.1 %collective-permute-start.2 = (bf16[512,1152]{1,0:T(8,128)(2,1)S(1)}, bf16[512,1152]{1,0:T(8,128)(2,1)}, u32[]{:S(2)}, u32[]{:S(2)}) collective-permute-start(bf16[512,1152]{1,0:T(8,128)(2,1)S(1)} %copy-done.17), channel_id=1, source_target_pairs={{0,2},{2,0},{1,3},{3,1},{4,6},{6,4},{5,7},{7,5},{8,10},{10,8},{9,1... | collective-permute-start | bytes 3538952 | tf_op jit(solution)/shard_map/ppermute | solution.py:464
  88.7 29.2 %collective-permute-start.3 = (bf16[512,1152]{1,0:T(8,128)(2,1)}, bf16[512,1152]{1,0:T(8,128)(2,1)}, u32[]{:S(2)}, u32[]{:S(2)}) collective-permute-start(bf16[512,1152]{1,0:T(8,128)(2,1)} %collective-permute-done.refs_1_.refs_3_.refs_7_.refs_11_.refs_15_), channel_id=1, source_target_pairs={{0,2},{2,0},{1,3},{3,1},{4,6},{6,4},{5,7},{7,5},{8,10},{10,8},{9,1... | collective-permute-start | bytes 3538952 | tf_op jit(solution)/shard_map/ppermute | solution.py:464
  92.9 6.7 %collective-permute-start.1 = (bf16[512,1024]{1,0:T(8,128)(2,1)}, bf16[512,1024]{1,0:T(8,128)(2,1)}, u32[]{:S(2)}, u32[]{:S(2)}) collective-permute-start(bf16[512,1024]{1,0:T(8,128)(2,1)} %add_norm.3.own_ref.refs_0_), channel_id=1, source_target_pairs={{0,1},{1,0},{2,3},{3,2},{4,5},{5,4},{6,7},{7,6},{8,9},{9,8},{10,11... | collective-permute-start | bytes 3145736 | tf_op jit(solution)/shard_map/ppermute | solution.py:460
  92.9 41.3 %collective-permute-start.7 = (bf16[512,1024]{1,0:T(8,128)(2,1)}, bf16[512,1024]{1,0:T(8,128)(2,1)S(1)}, u32[]{:S(2)}, u32[]{:S(2)}) collective-permute-start(bf16[512,1024]{1,0:T(8,128)(2,1)} %all-gather.6.cloned.1.call-done.refs_0_.refs_4_.refs_2_.refs_8_), channel_id=1, source_target_pairs={{0,4},{4,0},{1,5},{5,1},{2,6},{6,2},{3,7},{7,3},{8,12},{12,8},{9,1... | collective-permute-start | bytes 3145736 | tf_op jit(solution)/shard_map/ppermute | solution.py:468
  94.8 43.5 %collective-permute-start.8 = (bf16[512,1024]{1,0:T(8,128)(2,1)}, bf16[512,1024]{1,0:T(8,128)(2,1)S(1)}, u32[]{:S(2)}, u32[]{:S(2)}) collective-permute-start(bf16[512,1024]{1,0:T(8,128)(2,1)} %all-gather.6.cloned.1.call-done.refs_0_.refs_4_.refs_2_.refs_8_), channel_id=1, source_target_pairs={{0,2},{2,0},{1,3},{3,1},{4,6},{6,4},{5,7},{7,5},{8,10},{10,8},{9,1... | collective-permute-start | bytes 3145736 | tf_op jit(solution)/shard_map/ppermute | solution.py:464
  138.3 33.8 %collective-permute-start.9 = (bf16[512,1024]{1,0:T(8,128)(2,1)S(1)}, bf16[512,1024]{1,0:T(8,128)(2,1)S(1)}, u32[]{:S(2)}, u32[]{:S(2)}) collective-permute-start(bf16[512,1024]{1,0:T(8,128)(2,1)S(1)} %collective-permute-done.8.refs_2_.refs_6_.refs_4_.refs_10_), channel_id=1, source_target_pairs={{0,4},{4,0},{1,5},{5,1},{2,6},{6,2},{3,7},{7,3},{8,12},{12,8},{9,1... | collective-permute-start | bytes 3145736 | tf_op jit(solution)/shard_map/ppermute | solution.py:468
  139.2 48.9 %all-to-all-start.1 = ((bf16[16,32,1024]{2,1,0:T(8,128)(2,1)}), bf16[16,32,1024]{2,1,0:T(8,128)(2,1)}, u32[]{:S(2)}, u32[]{:S(2)}) async-start(bf16[16,32,1024]{2,1,0:T(8,128)(2,1)} %param.21), calls=%async_computation.1 | async-start | bytes 2097152 | tf_op jit(solution)/shard_map/all_to_all | solution.py:562
  173.1 60.6 %collective-permute-start.10 = (bf16[512,2304]{1,0:T(8,128)(2,1)}, bf16[512,2304]{1,0:T(8,128)(2,1)S(1)}, u32[]{:S(2)}, u32[]{:S(2)}) collective-permute-start(bf16[512,2304]{1,0:T(8,128)(2,1)} %all-gather.8.cloned.1.call-done.refs_0_.refs_2_.refs_4_.refs_8_), channel_id=1, source_target_pairs={{0,4},{4,0},{1,5},{5,1},{2,6},{6,2},{3,7},{7,3},{8,12},{12,8},{9,1... | collective-permute-start | bytes 7077896 | tf_op jit(solution)/shard_map/ppermute | solution.py:468
  174.9 60.4 %collective-permute-start.11 = (bf16[512,2304]{1,0:T(8,128)(2,1)}, bf16[512,2304]{1,0:T(8,128)(2,1)}, u32[]{:S(2)}, u32[]{:S(2)}) collective-permute-start(bf16[512,2304]{1,0:T(8,128)(2,1)} %all-gather.8.cloned.1.call-done.refs_0_.refs_2_.refs_4_.refs_8_), channel_id=1, source_target_pairs={{0,2},{2,0},{1,3},{3,1},{4,6},{6,4},{5,7},{7,5},{8,10},{10,8},{9,1... | collective-permute-start | bytes 7077896 | tf_op jit(solution)/shard_map/ppermute | solution.py:464
  187.9 9.8 %collective-permute-start.6 = (bf16[512,1024]{1,0:T(8,128)(2,1)}, bf16[512,1024]{1,0:T(8,128)(2,1)}, u32[]{:S(2)}, u32[]{:S(2)}) collective-permute-start(bf16[512,1024]{1,0:T(8,128)(2,1)} %get-tuple-element.157.own_ref.refs_0_), channel_id=1, source_target_pairs={{0,1},{1,0},{2,3},{3,2},{4,5},{5,4},{6,7},{7,6},{8,9},{9,8},{10,11... | collective-permute-start | bytes 3145736 | tf_op jit(solution)/shard_map/ppermute | solution.py:460
  191.5 13.8 %collective-permute-start.12 = (bf16[512,1024]{1,0:T(8,128)(2,1)}, bf16[512,1024]{1,0:T(8,128)(2,1)}, u32[]{:S(2)}, u32[]{:S(2)}) collective-permute-start(bf16[512,1024]{1,0:T(8,128)(2,1)} %reorder.7.own_ref.refs_0_.refs_4_), channel_id=1, source_target_pairs={{0,1},{1,0},{2,3},{3,2},{4,5},{5,4},{6,7},{7,6},{8,9},{9,8},{10,11... | collective-permute-start | bytes 3145736 | tf_op jit(solution)/shard_map/ppermute | solution.py:460
  191.9 61.7 %all-to-all-start.2 = ((bf16[16,32,1024]{2,1,0:T(8,128)(2,1)}), bf16[16,32,1024]{2,1,0:T(8,128)(2,1)}, u32[]{:S(2)}, u32[]{:S(2)}) async-start(bf16[16,32,1024]{2,1,0:T(8,128)(2,1)} %param.22), calls=%async_computation.2 | async-start | bytes 2097152 | tf_op jit(solution)/shard_map/all_to_all | solution.py:562
  247.6 36.7 %collective-permute-start.18 = (bf16[512,1536]{1,0:T(8,128)(2,1)}, bf16[512,1536]{1,0:T(8,128)(2,1)}, u32[]{:S(2)}, u32[]{:S(2)}) collective-permute-start(bf16[512,1536]{1,0:T(8,128)(2,1)} %slice.156), channel_id=1, source_target_pairs={{0,2},{2,0},{1,3},{3,1},{4,6},{6,4},{5,7},{7,5},{8,10},{10,8},{9,1... | collective-permute-start | bytes 4718600 | tf_op jit(solution)/shard_map/ppermute | solution.py:464
  253.6 6.7 %collective-permute-start.17 = (bf16[512,1024]{1,0:T(8,128)(2,1)}, bf16[512,1024]{1,0:T(8,128)(2,1)}, u32[]{:S(2)}, u32[]{:S(2)}) collective-permute-start(bf16[512,1024]{1,0:T(8,128)(2,1)} %get-tuple-element.175.own_ref.refs_0_), channel_id=1, source_target_pairs={{0,1},{1,0},{2,3},{3,2},{4,5},{5,4},{6,7},{7,6},{8,9},{9,8},{10,11... | collective-permute-start | bytes 3145736 | tf_op jit(solution)/shard_map/ppermute | solution.py:460
  257.3 33.6 %collective-permute-start.15 = (bf16[512,1024]{1,0:T(8,128)(2,1)S(1)}, bf16[512,1024]{1,0:T(8,128)(2,1)S(1)}, u32[]{:S(2)}, u32[]{:S(2)}) collective-permute-start(bf16[512,1024]{1,0:T(8,128)(2,1)S(1)} %reorder.8.own_ref.refs_2_.base_ref), channel_id=1, source_target_pairs={{0,1},{1,0},{2,3},{3,2},{4,5},{5,4},{6,7},{7,6},{8,9},{9,8},{10,11... | collective-permute-start | bytes 3145736 | tf_op jit(solution)/shard_map/ppermute | solution.py:460
  259.0 31.9 %collective-permute-start.16 = (bf16[512,768]{1,0:T(8,128)(2,1)S(1)}, bf16[512,768]{1,0:T(8,128)(2,1)S(1)}, u32[]{:S(2)}, u32[]{:S(2)}) collective-permute-start(bf16[512,768]{1,0:T(8,128)(2,1)S(1)} %slice.155), channel_id=1, source_target_pairs={{0,4},{4,0},{1,5},{5,1},{2,6},{6,2},{3,7},{7,3},{8,12},{12,8},{9,1... | collective-permute-start | bytes 2359304 | tf_op jit(solution)/shard_map/ppermute | solution.py:468
  302.2 69.3 %collective-permute-start.24 = (bf16[1024,1536]{1,0:T(8,128)(2,1)S(1)}, bf16[1024,1536]{1,0:T(8,128)(2,1)S(1)}, u32[]{:S(2)}, u32[]{:S(2)}) collective-permute-start(bf16[1024,1536]{1,0:T(8,128)(2,1)S(1)} %weight_grad.15), channel_id=1, source_target_pairs={{0,2},{2,0},{1,3},{3,1},{4,6},{6,4},{5,7},{7,5},{8,10},{10,8},{9,1... | collective-permute-start | bytes 9437192 | tf_op jit(solution)/shard_map/ppermute | solution.py:464
  311.3 7.5 %collective-permute-start.19 = (f32[512,512]{1,0:T(8,128)S(1)}, f32[512,512]{1,0:T(8,128)S(1)}, u32[]{:S(2)}, u32[]{:S(2)}) collective-permute-start(f32[512,512]{1,0:T(8,128)S(1)} %get-tuple-element.188), channel_id=1, source_target_pairs={{0,1},{1,0},{2,3},{3,2},{4,5},{5,4},{6,7},{7,6},{8,9},{9,8},{10,11... | collective-permute-start | bytes 3145736 | tf_op jit(solution)/shard_map/ppermute | solution.py:460
  311.4 7.4 %collective-permute-start.20 = (f32[512,512]{1,0:T(8,128)S(1)}, f32[512,512]{1,0:T(8,128)S(1)}, u32[]{:S(2)}, u32[]{:S(2)}) collective-permute-start(f32[512,512]{1,0:T(8,128)S(1)} %get-tuple-element.189), channel_id=1, source_target_pairs={{0,1},{1,0},{2,3},{3,2},{4,5},{5,4},{6,7},{7,6},{8,9},{9,8},{10,11... | collective-permute-start | bytes 3145736 | tf_op jit(solution)/shard_map/ppermute | solution.py:460
  311.9 36.4 %collective-permute-start.25 = (bf16[512,1536]{1,0:T(8,128)(2,1)S(1)}, bf16[512,1536]{1,0:T(8,128)(2,1)S(1)}, u32[]{:S(2)}, u32[]{:S(2)}) collective-permute-start(bf16[512,1536]{1,0:T(8,128)(2,1)S(1)} %weight_grad.16), channel_id=1, source_target_pairs={{0,4},{4,0},{1,5},{5,1},{2,6},{6,2},{3,7},{7,3},{8,12},{12,8},{9,1... | collective-permute-start | bytes 4718600 | tf_op jit(solution)/shard_map/ppermute | solution.py:468
  321.5 7.6 %collective-permute-start.21 = (bf16[512,1024]{1,0:T(8,128)(2,1)S(1)}, bf16[512,1024]{1,0:T(8,128)(2,1)S(1)}, u32[]{:S(2)}, u32[]{:S(2)}) collective-permute-start(bf16[512,1024]{1,0:T(8,128)(2,1)S(1)} %get-tuple-element.194.own_ref.refs_2_), channel_id=1, source_target_pairs={{0,1},{1,0},{2,3},{3,2},{4,5},{5,4},{6,7},{7,6},{8,9},{9,8},{10,11... | collective-permute-start | bytes 3145736 | tf_op jit(solution)/shard_map/ppermute | solution.py:460
  377.4 23.9 %collective-permute-start.26 = (f32[512,512]{1,0:T(8,128)}, f32[512,512]{1,0:T(8,128)}, u32[]{:S(2)}, u32[]{:S(2)}) collective-permute-start(f32[512,512]{1,0:T(8,128)} %get-tuple-element.215), channel_id=1, source_target_pairs={{0,1},{1,0},{2,3},{3,2},{4,5},{5,4},{6,7},{7,6},{8,9},{9,8},{10,11... | collective-permute-start | bytes 3145736 | tf_op jit(solution)/shard_map/ppermute | solution.py:460
  377.5 23.8 %collective-permute-start.27 = (f32[512,512]{1,0:T(8,128)}, f32[512,512]{1,0:T(8,128)}, u32[]{:S(2)}, u32[]{:S(2)}) collective-permute-start(f32[512,512]{1,0:T(8,128)} %get-tuple-element.221), channel_id=1, source_target_pairs={{0,1},{1,0},{2,3},{3,2},{4,5},{5,4},{6,7},{7,6},{8,9},{9,8},{10,11... | collective-permute-start | bytes 3145736 | tf_op jit(solution)/shard_map/ppermute | solution.py:460
  378.0 32.0 %all-to-all-start.3 = ((bf16[16,32,1024]{2,1,0:T(8,128)(2,1)}), bf16[16,32,1024]{2,1,0:T(8,128)(2,1)}, u32[]{:S(2)}, u32[]{:S(2)}) async-start(bf16[16,32,1024]{2,1,0:T(8,128)(2,1)} %bitcast.105), calls=%async_computation.3 | async-start | bytes 2097152 | tf_op jit(solution)/shard_map/all_to_all | solution.py:562
  384.2 119.7 %reduce-scatter.10.cloned.1.call-start = ((), (), s32[]{:S(2)}) async-start(), calls=%async_computation.12 | async-start | bytes 2949120
  384.2 47.3 %collective-permute-start.31 = (bf16[512,1536]{1,0:T(8,128)(2,1)}, bf16[512,1536]{1,0:T(8,128)(2,1)}, u32[]{:S(2)}, u32[]{:S(2)}) collective-permute-start(bf16[512,1536]{1,0:T(8,128)(2,1)} %copy-done.119), channel_id=1, source_target_pairs={{0,4},{4,0},{1,5},{5,1},{2,6},{6,2},{3,7},{7,3},{8,12},{12,8},{9,1... | collective-permute-start | bytes 4718600 | tf_op jit(solution)/shard_map/ppermute | solution.py:468
  397.7 10.8 %collective-permute-start.28 = (f32[512,512]{1,0:T(8,128)S(1)}, f32[512,512]{1,0:T(8,128)S(1)}, u32[]{:S(2)}, u32[]{:S(2)}) collective-permute-start(f32[512,512]{1,0:T(8,128)S(1)} %get-tuple-element.226), channel_id=1, source_target_pairs={{0,1},{1,0},{2,3},{3,2},{4,5},{5,4},{6,7},{7,6},{8,9},{9,8},{10,11... | collective-permute-start | bytes 3145736 | tf_op jit(solution)/shard_map/ppermute | solution.py:460
  397.8 10.7 %collective-permute-start.29 = (f32[512,512]{1,0:T(8,128)S(1)}, f32[512,512]{1,0:T(8,128)S(1)}, u32[]{:S(2)}, u32[]{:S(2)}) collective-permute-start(f32[512,512]{1,0:T(8,128)S(1)} %get-tuple-element.228), channel_id=1, source_target_pairs={{0,1},{1,0},{2,3},{3,2},{4,5},{5,4},{6,7},{7,6},{8,9},{9,8},{10,11... | collective-permute-start | bytes 3145736 | tf_op jit(solution)/shard_map/ppermute | solution.py:460
  407.0 24.1 %collective-permute-start.32 = (bf16[512,768]{1,0:T(8,128)(2,1)}, bf16[512,768]{1,0:T(8,128)(2,1)}, u32[]{:S(2)}, u32[]{:S(2)}) collective-permute-start(bf16[512,768]{1,0:T(8,128)(2,1)} %weight_grad.18), channel_id=1, source_target_pairs={{0,2},{2,0},{1,3},{3,1},{4,6},{6,4},{5,7},{7,5},{8,10},{10,8},{9,1... | collective-permute-start | bytes 2359304 | tf_op jit(solution)/shard_map/ppermute | solution.py:464
  437.7 35.9 %collective-permute-start.35 = (bf16[512,1024]{1,0:T(8,128)(2,1)}, bf16[512,1024]{1,0:T(8,128)(2,1)}, u32[]{:S(2)}, u32[]{:S(2)}) collective-permute-start(bf16[512,1024]{1,0:T(8,128)(2,1)} %copy-done.120), channel_id=1, source_target_pairs={{0,4},{4,0},{1,5},{5,1},{2,6},{6,2},{3,7},{7,3},{8,12},{12,8},{9,1... | collective-permute-start | bytes 3145736 | tf_op jit(solution)/shard_map/ppermute | solution.py:468
  438.5 39.6 %collective-permute-start.33 = (bf16[1024,512]{1,0:T(8,128)(2,1)}, bf16[1024,512]{1,0:T(8,128)(2,1)}, u32[]{:S(2)}, u32[]{:S(2)}) collective-permute-start(bf16[1024,512]{1,0:T(8,128)(2,1)} %copy-done.135), channel_id=1, source_target_pairs={{0,2},{2,0},{1,3},{3,1},{4,6},{6,4},{5,7},{7,5},{8,10},{10,8},{9,1... | collective-permute-start | bytes 3145736 | tf_op jit(solution)/shard_map/ppermute | solution.py:464
  439.8 75.2 %all-to-all-start.4 = ((bf16[16,32,1024]{2,1,0:T(8,128)(2,1)}), bf16[16,32,1024]{2,1,0:T(8,128)(2,1)}, u32[]{:S(2)}, u32[]{:S(2)}) async-start(bf16[16,32,1024]{2,1,0:T(8,128)(2,1)} %bitcast.104), calls=%async_computation.4 | async-start | bytes 2097152 | tf_op jit(solution)/shard_map/all_to_all | solution.py:562
  445.4 118.4 %reduce-scatter.12.cloned.1.call-start = ((), (), s32[]{:S(2)}) async-start(), calls=%async_computation.13 | async-start | bytes 1310720
  476.2 15.6 %collective-permute-start.36 = (bf16[512,512]{1,0:T(8,128)(2,1)S(1)}, bf16[512,512]{1,0:T(8,128)(2,1)S(1)}, u32[]{:S(2)}, u32[]{:S(2)}) collective-permute-start(bf16[512,512]{1,0:T(8,128)(2,1)S(1)} %weight_grad.25), channel_id=1, source_target_pairs={{0,2},{2,0},{1,3},{3,1},{4,6},{6,4},{5,7},{7,5},{8,10},{10,8},{9,1... | collective-permute-start | bytes 1572872 | tf_op jit(solution)/shard_map/ppermute | solution.py:464
  480.3 13.8 %collective-permute-start.34 = (bf16[512,512]{1,0:T(8,128)(2,1)S(1)}, bf16[512,512]{1,0:T(8,128)(2,1)S(1)}, u32[]{:S(2)}, u32[]{:S(2)}) collective-permute-start(bf16[512,512]{1,0:T(8,128)(2,1)S(1)} %weight_grad.24), channel_id=1, source_target_pairs={{0,4},{4,0},{1,5},{5,1},{2,6},{6,2},{3,7},{7,3},{8,12},{12,8},{9,1... | collective-permute-start | bytes 1572872 | tf_op jit(solution)/shard_map/ppermute | solution.py:468
  486.6 19.9 %collective-permute-start.37 = (f32[512,512]{1,0:T(8,128)}, f32[512,512]{1,0:T(8,128)}, u32[]{:S(2)}, u32[]{:S(2)}) collective-permute-start(f32[512,512]{1,0:T(8,128)} %get-tuple-element.248), channel_id=1, source_target_pairs={{0,1},{1,0},{2,3},{3,2},{4,5},{5,4},{6,7},{7,6},{8,9},{9,8},{10,11... | collective-permute-start | bytes 3145736 | tf_op jit(solution)/shard_map/ppermute | solution.py:460
  486.7 19.9 %collective-permute-start.38 = (f32[512,512]{1,0:T(8,128)}, f32[512,512]{1,0:T(8,128)}, u32[]{:S(2)}, u32[]{:S(2)}) collective-permute-start(f32[512,512]{1,0:T(8,128)} %get-tuple-element.249), channel_id=1, source_target_pairs={{0,1},{1,0},{2,3},{3,2},{4,5},{5,4},{6,7},{7,6},{8,9},{9,8},{10,11... | collective-permute-start | bytes 3145736 | tf_op jit(solution)/shard_map/ppermute | solution.py:460
  494.0 24.2 %collective-permute-start.40 = (bf16[512,1024]{1,0:T(8,128)(2,1)}, bf16[512,1024]{1,0:T(8,128)(2,1)}, u32[]{:S(2)}, u32[]{:S(2)}) collective-permute-start(bf16[512,1024]{1,0:T(8,128)(2,1)} %weight_grad.23), channel_id=1, source_target_pairs={{0,4},{4,0},{1,5},{5,1},{2,6},{6,2},{3,7},{7,3},{8,12},{12,8},{9,1... | collective-permute-start | bytes 3145736 | tf_op jit(solution)/shard_map/ppermute | solution.py:468
  495.4 25.9 %collective-permute-start.39 = (bf16[1024,512]{1,0:T(8,128)(2,1)}, bf16[1024,512]{1,0:T(8,128)(2,1)}, u32[]{:S(2)}, u32[]{:S(2)}) collective-permute-start(bf16[1024,512]{1,0:T(8,128)(2,1)} %weight_grad.22), channel_id=1, source_target_pairs={{0,2},{2,0},{1,3},{3,1},{4,6},{6,4},{5,7},{7,5},{8,10},{10,8},{9,1... | collective-permute-start | bytes 3145736 | tf_op jit(solution)/shard_map/ppermute | solution.py:464
  526.2 49.5 %all-to-all-start.5 = ((bf16[16,33,1024]{2,1,0:T(8,128)(2,1)}), bf16[16,33,1024]{2,1,0:T(8,128)(2,1)}, u32[]{:S(2)}, u32[]{:S(2)}) async-start(bf16[16,33,1024]{2,1,0:T(8,128)(2,1)} %pad_maximum_fusion), calls=%async_computation.5 | async-start | bytes 2621440 | tf_op jit(solution)/shard_map/all_to_all | solution.py:562
  534.1 59.6 %reduce-scatter.14.cloned.1.call-start = ((), (), s32[]{:S(2)}) async-start(), calls=%async_computation.14 | async-start | bytes 1310720
  534.1 23.9 %collective-permute-start.42 = (bf16[512,512]{1,0:T(8,128)(2,1)S(1)}, bf16[512,512]{1,0:T(8,128)(2,1)S(1)}, u32[]{:S(2)}, u32[]{:S(2)}) collective-permute-start(bf16[512,512]{1,0:T(8,128)(2,1)S(1)} %copy-done.137), channel_id=1, source_target_pairs={{0,2},{2,0},{1,3},{3,1},{4,6},{6,4},{5,7},{7,5},{8,10},{10,8},{9,1... | collective-permute-start | bytes 1572872 | tf_op jit(solution)/shard_map/ppermute | solution.py:464
  536.1 23.4 %collective-permute-start.41 = (bf16[512,512]{1,0:T(8,128)(2,1)}, bf16[512,512]{1,0:T(8,128)(2,1)S(1)}, u32[]{:S(2)}, u32[]{:S(2)}) collective-permute-start(bf16[512,512]{1,0:T(8,128)(2,1)} %copy-done.140), channel_id=1, source_target_pairs={{0,4},{4,0},{1,5},{5,1},{2,6},{6,2},{3,7},{7,3},{8,12},{12,8},{9,1... | collective-permute-start | bytes 1572872 | tf_op jit(solution)/shard_map/ppermute | solution.py:468
  (171 other events, 1370.0 us)
Sparse Core Ops, SparseCore 0:
  10.8 33.1 all-gather.3
  46.1 43.9 all-gather.5
  92.2 49.8 all-gather.7
  437.8 65.9 reduce-scatter.9
  506.1 29.6 reduce-scatter.11
  565.1 28.5 reduce-scatter.13

commit v7 on v6

--- a/solution.py
+++ b/solution.py
@@ -700,10 +700,10 @@
     group_a.send(group_b.late_x, group_b.late_y)
     sent = group_b.third(behind=[group_c.low])
     _, low_tok, gain_one = norm_back(
-        x_own, gain_rows[0], [[after(parts[0][0], *sent, group_c.low), parts[0][1]], parts[1]], grad_one
+        x_own, gain_rows[0], [[after(parts[0][0], *sent), parts[0][1]], parts[1]], grad_one
     )
     out_tok = reorder([after(low_tok, grad_encoder)], model_rows, dy, False)
-    group_a.second(low_tok)
+    group_a.second(low_tok, group_c.low)
     group_a.third(behind=[group_b.low])
     dp_count = seq_count // 2
     gain_part = jnp.concatenate([gain_one, gain_two, gain_three])

time: 620 us -> 632 us (1.019)
  waiting for transfers between devices: 189 us -> 198 us
    ppermute x11, waiting for transfers between devices: 80.7 us -> 88.1 us  [swap_y(): return row_major(lax.ppermute(row_major(values), 'dy', swap))]
    unnamed x336 -> x338, local copies, waits for them, and re-layouts: 58.7 us -> 60.6 us
  transfers between devices with their start and end apart: 56 -> 56, of which waited for: 19 -> 18; matrix products, arithmetic and copies ran while one was open for 5% -> 5% of each run, Pallas kernels for 36% -> 35%
where the time goes in v7:
time: 632 us; the launch traced here: 620 us
  Pallas kernels  238 us (38%)
  waiting for transfers between devices  198 us (31%)
  starting transfers between devices  72.4 us (11%)
  local copies, waits for them, and re-layouts  70.4 us (11%)
  other arithmetic  23.8 us (4%)
  between operations  18.6 us (3%)
    ppermute x11, waiting for transfers between devices, swap_y(): return row_major(lax.ppermute(row_major(values), 'dy', swap))  88.1 us
    ppermute x11, waiting for transfers between devices, swap_x(): return row_major(lax.ppermute(row_major(values), 'mx', swap))  61.6 us
    unnamed x338, local copies, waits for them, and re-layouts  60.6 us
    pallas_call x15, Pallas kernels, weight_grad(): pl.pallas_call(kernel, grid=(steps,), in_specs=[columns] * first + [spec(...  49.4 us
    pallas_call x4, Pallas kernels, attend_back(): pl.pallas_call(functools.partial(attend_back_kernel, causal, size), grid=...  48.9 us
    pallas_call x9, Pallas kernels, project(): pl.pallas_call(kernel, grid=(4,), in_specs=[spec((size, width_all), lambd...  42.3 us
    pallas_call x14, Pallas kernels, combine(): pl.pallas_call(kernel, grid=(2,), in_specs=[spec((size, v.shape[1]), lamb...  40.1 us
    all_to_all x6, starting transfers between devices, exchange(): lax.all_to_all(values, chips, split_axis=0, concat_axis=0, tiled=True)  37.8 us
  transfers between devices with their start and end apart: 56, of which 18 were waited for; matrix products, arithmetic and copies ran while one was open for 5% of the time, Pallas kernels for 35%

profile of v7, /device:TPU:0, one launch (start us, length us, event | category | flops | bytes accessed | tf_op | source)
XLA Modules:
  0.0 620.5 jit_solution(8332619024217463237)
XLA Ops:
  11.8 32.1 %all-gather.4.cloned.1.call-done.refs_0_.refs_2_.refs_6_.refs_10_.refs_14_ = bf16[512,1152]{1,0:T(8,128)(2,1)} async-done(((bf16[128,1152]{1,0:T(8,128)(2,1)}), bf16[512,1152]{1,0:T(8,128)(2,1)}) %all-gather.4.cloned.1.call-update) | async-done | bytes 1179664 | tf_op jit(solution)/shard_map/all_gather | solution.py:472
  43.9 4.9 all-to-all-start
  53.4 34.3 %collective-permute-done.refs_1_.refs_3_.refs_7_.refs_11_.refs_15_ = bf16[512,1152]{1,0:T(8,128)(2,1)} collective-permute-done((bf16[512,1152]{1,0:T(8,128)(2,1)S(1)}, bf16[512,1152]{1,0:T(8,128)(2,1)}, u32[]{:S(2)}, u32[]{:S(2)}) %collective-permute-start) | collective-permute-done | bytes 1179680 | tf_op jit(solution)/shard_map/ppermute | solution.py:468
  99.6 4.5 project_plain.6.q_ref.k_ref.v_ref
  104.2 10.0 %attend.4 = (bf16[1024,256]{1,0:T(8,128)(2,1)S(1)}, f32[2,1024,2]{2,1,0:T(8,128)S(1)}, f32[2,8,128]{2,1,0:T(8,128)S(1)}) custom-call(bf16[1024,768]{1,0:T(8,128)(2,1)S(1)} %project_plain.6.q_ref.k_ref.v_ref, bf16[1024,768]{1,0:T(8,128)(2,1)S(1)} %project_plain.6.q_ref.k_ref.v_ref, bf16[1024,768]{1,0:T(8,128)(2,1)S(1)} %project_plain.6.q_ref.k_ref.v_ref, ...), custom_call_target="tpu_custom_call" | custom-call | flops 1 | bytes 1 | tf_op jit(solution)/shard_map/attend/pallas_call | solution.py:126
  117.9 4.5 project_plain.7.q_ref.k_ref.v_ref
  122.5 10.0 %attend.5 = (bf16[1024,256]{1,0:T(8,128)(2,1)S(1)}, f32[2,1024,2]{2,1,0:T(8,128)S(1)}, f32[2,8,128]{2,1,0:T(8,128)S(1)}) custom-call(bf16[1024,768]{1,0:T(8,128)(2,1)S(1)} %project_plain.7.q_ref.k_ref.v_ref, bf16[1024,768]{1,0:T(8,128)(2,1)S(1)} %project_plain.7.q_ref.k_ref.v_ref, bf16[1024,768]{1,0:T(8,128)(2,1)S(1)} %project_plain.7.q_ref.k_ref.v_ref, ...), custom_call_target="tpu_custom_call" | custom-call | flops 1 | bytes 1 | tf_op jit(solution)/shard_map/attend/pallas_call | solution.py:126
  134.3 4.0 collective-permute-done.8.refs_2_.refs_6_.refs_4_.refs_10_
  139.2 6.5 %all-to-all-start.1 = ((bf16[16,32,1024]{2,1,0:T(8,128)(2,1)}), bf16[16,32,1024]{2,1,0:T(8,128)(2,1)}, u32[]{:S(2)}, u32[]{:S(2)}) async-start(bf16[16,32,1024]{2,1,0:T(8,128)(2,1)} %param.21), calls=%async_computation.1 | async-start | bytes 2097152 | tf_op jit(solution)/shard_map/all_to_all | solution.py:562
  145.8 26.3 %collective-permute-done.9.refs_3_.refs_7_.refs_5_.refs_11_ = bf16[512,1024]{1,0:T(8,128)(2,1)S(1)} collective-permute-done((bf16[512,1024]{1,0:T(8,128)(2,1)S(1)}, bf16[512,1024]{1,0:T(8,128)(2,1)S(1)}, u32[]{:S(2)}, u32[]{:S(2)}) %collective-permute-start.9) | collective-permute-done | bytes 1048608 | tf_op jit(solution)/shard_map/ppermute | solution.py:468
  188.1 3.4 reorder.7.own_ref.refs_0_.refs_4_
  191.9 5.9 all-to-all-start.2
  201.4 3.8 project_plain.8
  205.4 5.0 project_plain.9
  210.4 8.4 %attend.7 = (bf16[1024,256]{1,0:T(8,128)(2,1)S(1)}, f32[2,1024,2]{2,1,0:T(8,128)S(1)}, f32[2,8,128]{2,1,0:T(8,128)}) custom-call(bf16[1024,256]{1,0:T(8,128)(2,1)S(1)} %get-tuple-element.160.q_ref, bf16[1024,256]{1,0:T(8,128)(2,1)S(1)} %get-tuple-element.167.k_ref, bf16[1024,256]{1,0:T(8,128)(2,1)S(1)} %get-tuple-element.168.v_ref, ...), custom_call_target="tpu_custom_call" | custom-call | flops 1 | bytes 1 | tf_op jit(solution)/shard_map/attend/pallas_call | solution.py:126
  219.8 13.9 %collective-permute-done.10.refs_1_.refs_3_.refs_5_.refs_9_ = bf16[512,2304]{1,0:T(8,128)(2,1)S(1)} collective-permute-done((bf16[512,2304]{1,0:T(8,128)(2,1)}, bf16[512,2304]{1,0:T(8,128)(2,1)S(1)}, u32[]{:S(2)}, u32[]{:S(2)}) %collective-permute-start.10) | collective-permute-done | bytes 2359328 | tf_op jit(solution)/shard_map/ppermute | solution.py:468
  235.3 8.3 %attend.6 = (bf16[1024,256]{1,0:T(8,128)(2,1)S(1)}, f32[2,1024,2]{2,1,0:T(8,128)S(1)}, f32[2,8,128]{2,1,0:T(8,128)}) custom-call(bf16[1024,256]{1,0:T(8,128)(2,1)S(1)} %get-tuple-element.162.q_ref, bf16[1024,256]{1,0:T(8,128)(2,1)S(1)} %get-tuple-element.164.k_ref, bf16[1024,256]{1,0:T(8,128)(2,1)S(1)} %get-tuple-element.165.v_ref, ...), custom_call_target="tpu_custom_call" | custom-call | flops 1 | bytes 1 | tf_op jit(solution)/shard_map/attend/pallas_call | solution.py:126
  260.3 5.8 project_gelu.2
  266.1 18.1 %collective-permute-done.18.refs_1_.refs_3_.refs_7_.refs_11_ = bf16[512,1536]{1,0:T(8,128)(2,1)} collective-permute-done((bf16[512,1536]{1,0:T(8,128)(2,1)}, bf16[512,1536]{1,0:T(8,128)(2,1)}, u32[]{:S(2)}, u32[]{:S(2)}) %collective-permute-start.18) | collective-permute-done | bytes 1572896 | tf_op jit(solution)/shard_map/ppermute | solution.py:464
  284.3 6.6 %project_gelu.3 = (bf16[1024,768]{1,0:T(8,128)(2,1)S(1)}, bf16[1024,768]{1,0:T(8,128)(2,1)S(1)}, bf16[1024,768]{1,0:T(8,128)(2,1)S(1)}) custom-call(bf16[512,1024]{1,0:T(8,128)(2,1)} %get-tuple-element.175.own_ref.refs_0_, bf16[512,1024]{1,0:T(8,128)(2,1)} %collective-permute-done.17.other_ref.refs_1_, ...), custom_call_target="tpu_custom_call" | custom-call | flops 1 | bytes 1 | tf_op jit(solution)/shard_map/project_gelu/pallas_call | solution.py:292
  290.9 5.6 project_scale.1
  296.5 5.7 weight_grad.15
  305.6 5.7 combine.19
  313.1 5.7 combine.18
  321.5 3.6 combine.21
  325.6 3.5 combine.20
  333.3 11.9 %attend_back.4 = (bf16[1024,256]{1,0:T(8,128)(2,1)S(1)}, bf16[1024,256]{1,0:T(8,128)(2,1)S(1)}, bf16[1024,256]{1,0:T(8,128)(2,1)S(1)}) custom-call(bf16[1024,256]{1,0:T(8,128)(2,1)S(1)} %copy-done.111, bf16[1024,256]{1,0:T(8,128)(2,1)S(1)} %copy-done.113, bf16[1024,256]{1,0:T(8,128)(2,1)S(1)} %copy-done.115, s32[1024,1]{1,0:T(8,128)S(1)} %copy-done.26, ...), custom_call_target="tpu_custom_call" | custom-call | flops 1 | bytes 1 | tf_op jit(solution)/shard_map/attend_back/pallas_call | solution.py:156
  348.3 12.3 %attend_back.5 = (bf16[1024,256]{1,0:T(8,128)(2,1)S(1)}, bf16[1024,256]{1,0:T(8,128)(2,1)S(1)}, bf16[1024,256]{1,0:T(8,128)(2,1)S(1)}) custom-call(bf16[1024,256]{1,0:T(8,128)(2,1)S(1)} %copy-done.105, bf16[1024,256]{1,0:T(8,128)(2,1)S(1)} %copy-done.107, bf16[1024,256]{1,0:T(8,128)(2,1)S(1)} %copy-done.109, s32[1024,1]{1,0:T(8,128)S(1)} %copy-done.26, ...), custom_call_target="tpu_custom_call" | custom-call | flops 1 | bytes 1 | tf_op jit(solution)/shard_map/attend_back/pallas_call | solution.py:156
  361.4 3.5 weight_grad.18
  364.9 6.6 %collective-permute-done.24.refs_6_.refs_7_ = bf16[1024,1536]{1,0:T(8,128)(2,1)S(1)} collective-permute-done((bf16[1024,1536]{1,0:T(8,128)(2,1)S(1)}, bf16[1024,1536]{1,0:T(8,128)(2,1)S(1)}, u32[]{:S(2)}, u32[]{:S(2)}) %collective-permute-start.24) | collective-permute-done | bytes 3145760 | tf_op jit(solution)/shard_map/ppermute | solution.py:464
  371.6 3.8 weight_grad.17
  378.0 6.2 all-to-all-start.3
  410.0 4.2 project_plain.11
  416.3 12.4 %attend_back.6 = (bf16[1024,256]{1,0:T(8,128)(2,1)S(1)}, bf16[1024,256]{1,0:T(8,128)(2,1)S(1)}, bf16[1024,256]{1,0:T(8,128)(2,1)S(1)}) custom-call(bf16[1024,768]{1,0:T(8,128)(2,1)S(1)} %copy-done.23, bf16[1024,768]{1,0:T(8,128)(2,1)S(1)} %copy-done.23, bf16[1024,768]{1,0:T(8,128)(2,1)S(1)} %copy-done.23, s32[1024,1]{1,0:T(8,128)S(1)} %copy-done.27, ...), custom_call_target="tpu_custom_call" | custom-call | flops 1 | bytes 1 | tf_op jit(solution)/shard_map/attend_back/pallas_call | solution.py:156
  431.6 4.7 weight_grad.21
  439.8 5.6 all-to-all-start.4
  447.7 12.2 %attend_back.7 = (bf16[1024,256]{1,0:T(8,128)(2,1)S(1)}, bf16[1024,256]{1,0:T(8,128)(2,1)S(1)}, bf16[1024,256]{1,0:T(8,128)(2,1)S(1)}) custom-call(bf16[1024,768]{1,0:T(8,128)(2,1)S(1)} %copy-done.21, bf16[1024,768]{1,0:T(8,128)(2,1)S(1)} %copy-done.21, bf16[1024,768]{1,0:T(8,128)(2,1)S(1)} %copy-done.21, s32[1024,1]{1,0:T(8,128)S(1)} %copy-done.27, ...), custom_call_target="tpu_custom_call" | custom-call | flops 1 | bytes 1 | tf_op jit(solution)/shard_map/attend_back/pallas_call | solution.py:156
  460.0 3.5 weight_grad.22
  468.0 4.5 combine.27
  473.1 4.0 combine.26
  487.3 9.4 %collective-permute-done.36.refs_13_ = bf16[512,512]{1,0:T(8,128)(2,1)S(1)} collective-permute-done((bf16[512,512]{1,0:T(8,128)(2,1)S(1)}, bf16[512,512]{1,0:T(8,128)(2,1)S(1)}, u32[]{:S(2)}, u32[]{:S(2)}) %collective-permute-start.36) | collective-permute-done | bytes 524320 | tf_op jit(solution)/shard_map/ppermute | solution.py:464
  499.5 3.4 weight_grad.26
  513.6 3.5 norm_back.5
  523.3 7.8 %collective-permute-done.40.refs_4_.refs_10_ = bf16[512,1024]{1,0:T(8,128)(2,1)} collective-permute-done((bf16[512,1024]{1,0:T(8,128)(2,1)}, bf16[512,1024]{1,0:T(8,128)(2,1)}, u32[]{:S(2)}, u32[]{:S(2)}) %collective-permute-start.40) | collective-permute-done | bytes 1048608 | tf_op jit(solution)/shard_map/ppermute | solution.py:468
  537.5 8.7 %all-to-all-start.5 = ((bf16[16,33,1024]{2,1,0:T(8,128)(2,1)}), bf16[16,33,1024]{2,1,0:T(8,128)(2,1)}, u32[]{:S(2)}, u32[]{:S(2)}) async-start(bf16[16,33,1024]{2,1,0:T(8,128)(2,1)} %pad_maximum_fusion), calls=%async_computation.5 | async-start | bytes 2621440 | tf_op jit(solution)/shard_map/all_to_all | solution.py:562
  549.7 19.8 %collective-permute-done.42.refs_11_ = bf16[512,512]{1,0:T(8,128)(2,1)S(1)} collective-permute-done((bf16[512,512]{1,0:T(8,128)(2,1)S(1)}, bf16[512,512]{1,0:T(8,128)(2,1)S(1)}, u32[]{:S(2)}, u32[]{:S(2)}) %collective-permute-start.42) | collective-permute-done | bytes 524320 | tf_op jit(solution)/shard_map/ppermute | solution.py:464
  570.7 4.4 weight_grad.29
  590.9 14.2 %reduce-scatter.14.cloned.1.call-done = bf16[128,1024]{1,0:T(8,128)(2,1)} async-done(((bf16[512,1024]{1,0:T(8,128)(2,1)}), bf16[128,1024]{1,0:T(8,128)(2,1)}) %reduce-scatter.14.cloned.1.call-update) | async-done | bytes 262160
  (540 shorter events, 189.1 us)
Async XLA Ops:
  7.2 36.7 %all-gather.4.cloned.1.call-start = ((), (), s32[]{:S(2)}) async-start(), calls=%async_computation.9 | async-start | bytes 1474560 | tf_op jit(solution)/shard_map/all_gather | solution.py:472
  10.6 82.3 %all-gather.6.cloned.1.call-start = ((), (), s32[]{:S(2)}) async-start(), calls=%async_computation.10 | async-start | bytes 1310720 | tf_op jit(solution)/shard_map/all_gather | solution.py:472
  43.9 46.3 %all-to-all-start = ((bf16[16,32,1024]{2,1,0:T(8,128)(2,1)}), bf16[16,32,1024]{2,1,0:T(8,128)(2,1)S(1)}, u32[]{:S(2)}, u32[]{:S(2)}) async-start(bf16[16,32,1024]{2,1,0:T(8,128)(2,1)} %param.20), calls=%async_computation | async-start | bytes 2097152 | tf_op jit(solution)/shard_map/all_to_all | solution.py:562
  48.8 97.0 %all-gather.8.cloned.1.call-start = ((), (), s32[]{:S(2)}) async-start(), calls=%async_computation.11 | async-start | bytes 2949120 | tf_op jit(solution)/shard_map/all_gather | solution.py:472
  48.9 38.8 %collective-permute-start = (bf16[512,1152]{1,0:T(8,128)(2,1)S(1)}, bf16[512,1152]{1,0:T(8,128)(2,1)}, u32[]{:S(2)}, u32[]{:S(2)}) collective-permute-start(bf16[512,1152]{1,0:T(8,128)(2,1)S(1)} %copy-done.17), channel_id=1, source_target_pairs={{0,4},{4,0},{1,5},{5,1},{2,6},{6,2},{3,7},{7,3},{8,12},{12,8},{9,1... | collective-permute-start | bytes 3538952 | tf_op jit(solution)/shard_map/ppermute | solution.py:468
  51.9 64.1 %collective-permute-start.2 = (bf16[512,1152]{1,0:T(8,128)(2,1)S(1)}, bf16[512,1152]{1,0:T(8,128)(2,1)}, u32[]{:S(2)}, u32[]{:S(2)}) collective-permute-start(bf16[512,1152]{1,0:T(8,128)(2,1)S(1)} %copy-done.17), channel_id=1, source_target_pairs={{0,2},{2,0},{1,3},{3,1},{4,6},{6,4},{5,7},{7,5},{8,10},{10,8},{9,1... | collective-permute-start | bytes 3538952 | tf_op jit(solution)/shard_map/ppermute | solution.py:464
  88.7 29.2 %collective-permute-start.3 = (bf16[512,1152]{1,0:T(8,128)(2,1)}, bf16[512,1152]{1,0:T(8,128)(2,1)}, u32[]{:S(2)}, u32[]{:S(2)}) collective-permute-start(bf16[512,1152]{1,0:T(8,128)(2,1)} %collective-permute-done.refs_1_.refs_3_.refs_7_.refs_11_.refs_15_), channel_id=1, source_target_pairs={{0,2},{2,0},{1,3},{3,1},{4,6},{6,4},{5,7},{7,5},{8,10},{10,8},{9,1... | collective-permute-start | bytes 3538952 | tf_op jit(solution)/shard_map/ppermute | solution.py:464
  92.9 6.7 %collective-permute-start.1 = (bf16[512,1024]{1,0:T(8,128)(2,1)}, bf16[512,1024]{1,0:T(8,128)(2,1)}, u32[]{:S(2)}, u32[]{:S(2)}) collective-permute-start(bf16[512,1024]{1,0:T(8,128)(2,1)} %add_norm.3.own_ref.refs_0_), channel_id=1, source_target_pairs={{0,1},{1,0},{2,3},{3,2},{4,5},{5,4},{6,7},{7,6},{8,9},{9,8},{10,11... | collective-permute-start | bytes 3145736 | tf_op jit(solution)/shard_map/ppermute | solution.py:460
  92.9 41.3 %collective-permute-start.7 = (bf16[512,1024]{1,0:T(8,128)(2,1)}, bf16[512,1024]{1,0:T(8,128)(2,1)S(1)}, u32[]{:S(2)}, u32[]{:S(2)}) collective-permute-start(bf16[512,1024]{1,0:T(8,128)(2,1)} %all-gather.6.cloned.1.call-done.refs_0_.refs_4_.refs_2_.refs_8_), channel_id=1, source_target_pairs={{0,4},{4,0},{1,5},{5,1},{2,6},{6,2},{3,7},{7,3},{8,12},{12,8},{9,1... | collective-permute-start | bytes 3145736 | tf_op jit(solution)/shard_map/ppermute | solution.py:468
  94.8 43.5 %collective-permute-start.8 = (bf16[512,1024]{1,0:T(8,128)(2,1)}, bf16[512,1024]{1,0:T(8,128)(2,1)S(1)}, u32[]{:S(2)}, u32[]{:S(2)}) collective-permute-start(bf16[512,1024]{1,0:T(8,128)(2,1)} %all-gather.6.cloned.1.call-done.refs_0_.refs_4_.refs_2_.refs_8_), channel_id=1, source_target_pairs={{0,2},{2,0},{1,3},{3,1},{4,6},{6,4},{5,7},{7,5},{8,10},{10,8},{9,1... | collective-permute-start | bytes 3145736 | tf_op jit(solution)/shard_map/ppermute | solution.py:464
  138.3 33.8 %collective-permute-start.9 = (bf16[512,1024]{1,0:T(8,128)(2,1)S(1)}, bf16[512,1024]{1,0:T(8,128)(2,1)S(1)}, u32[]{:S(2)}, u32[]{:S(2)}) collective-permute-start(bf16[512,1024]{1,0:T(8,128)(2,1)S(1)} %collective-permute-done.8.refs_2_.refs_6_.refs_4_.refs_10_), channel_id=1, source_target_pairs={{0,4},{4,0},{1,5},{5,1},{2,6},{6,2},{3,7},{7,3},{8,12},{12,8},{9,1... | collective-permute-start | bytes 3145736 | tf_op jit(solution)/shard_map/ppermute | solution.py:468
  139.2 48.8 %all-to-all-start.1 = ((bf16[16,32,1024]{2,1,0:T(8,128)(2,1)}), bf16[16,32,1024]{2,1,0:T(8,128)(2,1)}, u32[]{:S(2)}, u32[]{:S(2)}) async-start(bf16[16,32,1024]{2,1,0:T(8,128)(2,1)} %param.21), calls=%async_computation.1 | async-start | bytes 2097152 | tf_op jit(solution)/shard_map/all_to_all | solution.py:562
  173.1 60.6 %collective-permute-start.10 = (bf16[512,2304]{1,0:T(8,128)(2,1)}, bf16[512,2304]{1,0:T(8,128)(2,1)S(1)}, u32[]{:S(2)}, u32[]{:S(2)}) collective-permute-start(bf16[512,2304]{1,0:T(8,128)(2,1)} %all-gather.8.cloned.1.call-done.refs_0_.refs_2_.refs_4_.refs_8_), channel_id=1, source_target_pairs={{0,4},{4,0},{1,5},{5,1},{2,6},{6,2},{3,7},{7,3},{8,12},{12,8},{9,1... | collective-permute-start | bytes 7077896 | tf_op jit(solution)/shard_map/ppermute | solution.py:468
  174.8 60.4 %collective-permute-start.11 = (bf16[512,2304]{1,0:T(8,128)(2,1)}, bf16[512,2304]{1,0:T(8,128)(2,1)}, u32[]{:S(2)}, u32[]{:S(2)}) collective-permute-start(bf16[512,2304]{1,0:T(8,128)(2,1)} %all-gather.8.cloned.1.call-done.refs_0_.refs_2_.refs_4_.refs_8_), channel_id=1, source_target_pairs={{0,2},{2,0},{1,3},{3,1},{4,6},{6,4},{5,7},{7,5},{8,10},{10,8},{9,1... | collective-permute-start | bytes 7077896 | tf_op jit(solution)/shard_map/ppermute | solution.py:464
  187.9 9.8 %collective-permute-start.6 = (bf16[512,1024]{1,0:T(8,128)(2,1)}, bf16[512,1024]{1,0:T(8,128)(2,1)}, u32[]{:S(2)}, u32[]{:S(2)}) collective-permute-start(bf16[512,1024]{1,0:T(8,128)(2,1)} %get-tuple-element.157.own_ref.refs_0_), channel_id=1, source_target_pairs={{0,1},{1,0},{2,3},{3,2},{4,5},{5,4},{6,7},{7,6},{8,9},{9,8},{10,11... | collective-permute-start | bytes 3145736 | tf_op jit(solution)/shard_map/ppermute | solution.py:460
  191.5 13.8 %collective-permute-start.12 = (bf16[512,1024]{1,0:T(8,128)(2,1)}, bf16[512,1024]{1,0:T(8,128)(2,1)}, u32[]{:S(2)}, u32[]{:S(2)}) collective-permute-start(bf16[512,1024]{1,0:T(8,128)(2,1)} %reorder.7.own_ref.refs_0_.refs_4_), channel_id=1, source_target_pairs={{0,1},{1,0},{2,3},{3,2},{4,5},{5,4},{6,7},{7,6},{8,9},{9,8},{10,11... | collective-permute-start | bytes 3145736 | tf_op jit(solution)/shard_map/ppermute | solution.py:460
  191.9 61.7 %all-to-all-start.2 = ((bf16[16,32,1024]{2,1,0:T(8,128)(2,1)}), bf16[16,32,1024]{2,1,0:T(8,128)(2,1)}, u32[]{:S(2)}, u32[]{:S(2)}) async-start(bf16[16,32,1024]{2,1,0:T(8,128)(2,1)} %param.22), calls=%async_computation.2 | async-start | bytes 2097152 | tf_op jit(solution)/shard_map/all_to_all | solution.py:562
  247.6 36.7 %collective-permute-start.18 = (bf16[512,1536]{1,0:T(8,128)(2,1)}, bf16[512,1536]{1,0:T(8,128)(2,1)}, u32[]{:S(2)}, u32[]{:S(2)}) collective-permute-start(bf16[512,1536]{1,0:T(8,128)(2,1)} %slice.156), channel_id=1, source_target_pairs={{0,2},{2,0},{1,3},{3,1},{4,6},{6,4},{5,7},{7,5},{8,10},{10,8},{9,1... | collective-permute-start | bytes 4718600 | tf_op jit(solution)/shard_map/ppermute | solution.py:464
  253.6 6.7 %collective-permute-start.17 = (bf16[512,1024]{1,0:T(8,128)(2,1)}, bf16[512,1024]{1,0:T(8,128)(2,1)}, u32[]{:S(2)}, u32[]{:S(2)}) collective-permute-start(bf16[512,1024]{1,0:T(8,128)(2,1)} %get-tuple-element.175.own_ref.refs_0_), channel_id=1, source_target_pairs={{0,1},{1,0},{2,3},{3,2},{4,5},{5,4},{6,7},{7,6},{8,9},{9,8},{10,11... | collective-permute-start | bytes 3145736 | tf_op jit(solution)/shard_map/ppermute | solution.py:460
  257.3 33.6 %collective-permute-start.15 = (bf16[512,1024]{1,0:T(8,128)(2,1)S(1)}, bf16[512,1024]{1,0:T(8,128)(2,1)S(1)}, u32[]{:S(2)}, u32[]{:S(2)}) collective-permute-start(bf16[512,1024]{1,0:T(8,128)(2,1)S(1)} %reorder.8.own_ref.refs_2_.base_ref), channel_id=1, source_target_pairs={{0,1},{1,0},{2,3},{3,2},{4,5},{5,4},{6,7},{7,6},{8,9},{9,8},{10,11... | collective-permute-start | bytes 3145736 | tf_op jit(solution)/shard_map/ppermute | solution.py:460
  259.0 31.9 %collective-permute-start.16 = (bf16[512,768]{1,0:T(8,128)(2,1)S(1)}, bf16[512,768]{1,0:T(8,128)(2,1)S(1)}, u32[]{:S(2)}, u32[]{:S(2)}) collective-permute-start(bf16[512,768]{1,0:T(8,128)(2,1)S(1)} %slice.155), channel_id=1, source_target_pairs={{0,4},{4,0},{1,5},{5,1},{2,6},{6,2},{3,7},{7,3},{8,12},{12,8},{9,1... | collective-permute-start | bytes 2359304 | tf_op jit(solution)/shard_map/ppermute | solution.py:468
  302.2 69.3 %collective-permute-start.24 = (bf16[1024,1536]{1,0:T(8,128)(2,1)S(1)}, bf16[1024,1536]{1,0:T(8,128)(2,1)S(1)}, u32[]{:S(2)}, u32[]{:S(2)}) collective-permute-start(bf16[1024,1536]{1,0:T(8,128)(2,1)S(1)} %weight_grad.15), channel_id=1, source_target_pairs={{0,2},{2,0},{1,3},{3,1},{4,6},{6,4},{5,7},{7,5},{8,10},{10,8},{9,1... | collective-permute-start | bytes 9437192 | tf_op jit(solution)/shard_map/ppermute | solution.py:464
  311.3 7.5 %collective-permute-start.19 = (f32[512,512]{1,0:T(8,128)S(1)}, f32[512,512]{1,0:T(8,128)S(1)}, u32[]{:S(2)}, u32[]{:S(2)}) collective-permute-start(f32[512,512]{1,0:T(8,128)S(1)} %get-tuple-element.188), channel_id=1, source_target_pairs={{0,1},{1,0},{2,3},{3,2},{4,5},{5,4},{6,7},{7,6},{8,9},{9,8},{10,11... | collective-permute-start | bytes 3145736 | tf_op jit(solution)/shard_map/ppermute | solution.py:460
  311.4 7.4 %collective-permute-start.20 = (f32[512,512]{1,0:T(8,128)S(1)}, f32[512,512]{1,0:T(8,128)S(1)}, u32[]{:S(2)}, u32[]{:S(2)}) collective-permute-start(f32[512,512]{1,0:T(8,128)S(1)} %get-tuple-element.189), channel_id=1, source_target_pairs={{0,1},{1,0},{2,3},{3,2},{4,5},{5,4},{6,7},{7,6},{8,9},{9,8},{10,11... | collective-permute-start | bytes 3145736 | tf_op jit(solution)/shard_map/ppermute | solution.py:460
  311.9 36.4 %collective-permute-start.25 = (bf16[512,1536]{1,0:T(8,128)(2,1)S(1)}, bf16[512,1536]{1,0:T(8,128)(2,1)S(1)}, u32[]{:S(2)}, u32[]{:S(2)}) collective-permute-start(bf16[512,1536]{1,0:T(8,128)(2,1)S(1)} %weight_grad.16), channel_id=1, source_target_pairs={{0,4},{4,0},{1,5},{5,1},{2,6},{6,2},{3,7},{7,3},{8,12},{12,8},{9,1... | collective-permute-start | bytes 4718600 | tf_op jit(solution)/shard_map/ppermute | solution.py:468
  321.5 7.6 %collective-permute-start.21 = (bf16[512,1024]{1,0:T(8,128)(2,1)S(1)}, bf16[512,1024]{1,0:T(8,128)(2,1)S(1)}, u32[]{:S(2)}, u32[]{:S(2)}) collective-permute-start(bf16[512,1024]{1,0:T(8,128)(2,1)S(1)} %get-tuple-element.194.own_ref.refs_2_), channel_id=1, source_target_pairs={{0,1},{1,0},{2,3},{3,2},{4,5},{5,4},{6,7},{7,6},{8,9},{9,8},{10,11... | collective-permute-start | bytes 3145736 | tf_op jit(solution)/shard_map/ppermute | solution.py:460
  377.4 23.9 %collective-permute-start.26 = (f32[512,512]{1,0:T(8,128)}, f32[512,512]{1,0:T(8,128)}, u32[]{:S(2)}, u32[]{:S(2)}) collective-permute-start(f32[512,512]{1,0:T(8,128)} %get-tuple-element.215), channel_id=1, source_target_pairs={{0,1},{1,0},{2,3},{3,2},{4,5},{5,4},{6,7},{7,6},{8,9},{9,8},{10,11... | collective-permute-start | bytes 3145736 | tf_op jit(solution)/shard_map/ppermute | solution.py:460
  377.5 23.8 %collective-permute-start.27 = (f32[512,512]{1,0:T(8,128)}, f32[512,512]{1,0:T(8,128)}, u32[]{:S(2)}, u32[]{:S(2)}) collective-permute-start(f32[512,512]{1,0:T(8,128)} %get-tuple-element.221), channel_id=1, source_target_pairs={{0,1},{1,0},{2,3},{3,2},{4,5},{5,4},{6,7},{7,6},{8,9},{9,8},{10,11... | collective-permute-start | bytes 3145736 | tf_op jit(solution)/shard_map/ppermute | solution.py:460
  378.0 32.0 %all-to-all-start.3 = ((bf16[16,32,1024]{2,1,0:T(8,128)(2,1)}), bf16[16,32,1024]{2,1,0:T(8,128)(2,1)}, u32[]{:S(2)}, u32[]{:S(2)}) async-start(bf16[16,32,1024]{2,1,0:T(8,128)(2,1)} %bitcast.105), calls=%async_computation.3 | async-start | bytes 2097152 | tf_op jit(solution)/shard_map/all_to_all | solution.py:562
  384.1 119.8 %reduce-scatter.10.cloned.1.call-start = ((), (), s32[]{:S(2)}) async-start(), calls=%async_computation.12 | async-start | bytes 2949120
  384.2 47.3 %collective-permute-start.31 = (bf16[512,1536]{1,0:T(8,128)(2,1)}, bf16[512,1536]{1,0:T(8,128)(2,1)}, u32[]{:S(2)}, u32[]{:S(2)}) collective-permute-start(bf16[512,1536]{1,0:T(8,128)(2,1)} %copy-done.118), channel_id=1, source_target_pairs={{0,4},{4,0},{1,5},{5,1},{2,6},{6,2},{3,7},{7,3},{8,12},{12,8},{9,1... | collective-permute-start | bytes 4718600 | tf_op jit(solution)/shard_map/ppermute | solution.py:468
  397.7 10.8 %collective-permute-start.28 = (f32[512,512]{1,0:T(8,128)S(1)}, f32[512,512]{1,0:T(8,128)S(1)}, u32[]{:S(2)}, u32[]{:S(2)}) collective-permute-start(f32[512,512]{1,0:T(8,128)S(1)} %get-tuple-element.226), channel_id=1, source_target_pairs={{0,1},{1,0},{2,3},{3,2},{4,5},{5,4},{6,7},{7,6},{8,9},{9,8},{10,11... | collective-permute-start | bytes 3145736 | tf_op jit(solution)/shard_map/ppermute | solution.py:460
  397.8 10.7 %collective-permute-start.29 = (f32[512,512]{1,0:T(8,128)S(1)}, f32[512,512]{1,0:T(8,128)S(1)}, u32[]{:S(2)}, u32[]{:S(2)}) collective-permute-start(f32[512,512]{1,0:T(8,128)S(1)} %get-tuple-element.228), channel_id=1, source_target_pairs={{0,1},{1,0},{2,3},{3,2},{4,5},{5,4},{6,7},{7,6},{8,9},{9,8},{10,11... | collective-permute-start | bytes 3145736 | tf_op jit(solution)/shard_map/ppermute | solution.py:460
  407.0 24.1 %collective-permute-start.32 = (bf16[512,768]{1,0:T(8,128)(2,1)}, bf16[512,768]{1,0:T(8,128)(2,1)}, u32[]{:S(2)}, u32[]{:S(2)}) collective-permute-start(bf16[512,768]{1,0:T(8,128)(2,1)} %weight_grad.18), channel_id=1, source_target_pairs={{0,2},{2,0},{1,3},{3,1},{4,6},{6,4},{5,7},{7,5},{8,10},{10,8},{9,1... | collective-permute-start | bytes 2359304 | tf_op jit(solution)/shard_map/ppermute | solution.py:464
  437.7 41.3 %collective-permute-start.35 = (bf16[512,1024]{1,0:T(8,128)(2,1)}, bf16[512,1024]{1,0:T(8,128)(2,1)}, u32[]{:S(2)}, u32[]{:S(2)}) collective-permute-start(bf16[512,1024]{1,0:T(8,128)(2,1)} %copy-done.120), channel_id=1, source_target_pairs={{0,4},{4,0},{1,5},{5,1},{2,6},{6,2},{3,7},{7,3},{8,12},{12,8},{9,1... | collective-permute-start | bytes 3145736 | tf_op jit(solution)/shard_map/ppermute | solution.py:468
  438.5 45.0 %collective-permute-start.33 = (bf16[1024,512]{1,0:T(8,128)(2,1)}, bf16[1024,512]{1,0:T(8,128)(2,1)}, u32[]{:S(2)}, u32[]{:S(2)}) collective-permute-start(bf16[1024,512]{1,0:T(8,128)(2,1)} %copy-done.136), channel_id=1, source_target_pairs={{0,2},{2,0},{1,3},{3,1},{4,6},{6,4},{5,7},{7,5},{8,10},{10,8},{9,1... | collective-permute-start | bytes 3145736 | tf_op jit(solution)/shard_map/ppermute | solution.py:464
  439.8 78.2 %all-to-all-start.4 = ((bf16[16,32,1024]{2,1,0:T(8,128)(2,1)}), bf16[16,32,1024]{2,1,0:T(8,128)(2,1)}, u32[]{:S(2)}, u32[]{:S(2)}) async-start(bf16[16,32,1024]{2,1,0:T(8,128)(2,1)} %bitcast.104), calls=%async_computation.4 | async-start | bytes 2097152 | tf_op jit(solution)/shard_map/all_to_all | solution.py:562
  445.4 129.7 %reduce-scatter.12.cloned.1.call-start = ((), (), s32[]{:S(2)}) async-start(), calls=%async_computation.13 | async-start | bytes 1310720
  472.6 37.0 %collective-permute-start.37 = (f32[512,512]{1,0:T(8,128)}, f32[512,512]{1,0:T(8,128)}, u32[]{:S(2)}, u32[]{:S(2)}) collective-permute-start(f32[512,512]{1,0:T(8,128)} %get-tuple-element.248), channel_id=1, source_target_pairs={{0,1},{1,0},{2,3},{3,2},{4,5},{5,4},{6,7},{7,6},{8,9},{9,8},{10,11... | collective-permute-start | bytes 3145736 | tf_op jit(solution)/shard_map/ppermute | solution.py:460
  472.6 37.0 %collective-permute-start.38 = (f32[512,512]{1,0:T(8,128)}, f32[512,512]{1,0:T(8,128)}, u32[]{:S(2)}, u32[]{:S(2)}) collective-permute-start(f32[512,512]{1,0:T(8,128)} %get-tuple-element.249), channel_id=1, source_target_pairs={{0,1},{1,0},{2,3},{3,2},{4,5},{5,4},{6,7},{7,6},{8,9},{9,8},{10,11... | collective-permute-start | bytes 3145736 | tf_op jit(solution)/shard_map/ppermute | solution.py:460
  481.6 15.0 %collective-permute-start.36 = (bf16[512,512]{1,0:T(8,128)(2,1)S(1)}, bf16[512,512]{1,0:T(8,128)(2,1)S(1)}, u32[]{:S(2)}, u32[]{:S(2)}) collective-permute-start(bf16[512,512]{1,0:T(8,128)(2,1)S(1)} %weight_grad.25), channel_id=1, source_target_pairs={{0,2},{2,0},{1,3},{3,1},{4,6},{6,4},{5,7},{7,5},{8,10},{10,8},{9,1... | collective-permute-start | bytes 1572872 | tf_op jit(solution)/shard_map/ppermute | solution.py:464
  485.7 13.8 %collective-permute-start.34 = (bf16[512,512]{1,0:T(8,128)(2,1)S(1)}, bf16[512,512]{1,0:T(8,128)(2,1)S(1)}, u32[]{:S(2)}, u32[]{:S(2)}) collective-permute-start(bf16[512,512]{1,0:T(8,128)(2,1)S(1)} %weight_grad.24), channel_id=1, source_target_pairs={{0,4},{4,0},{1,5},{5,1},{2,6},{6,2},{3,7},{7,3},{8,12},{12,8},{9,1... | collective-permute-start | bytes 1572872 | tf_op jit(solution)/shard_map/ppermute | solution.py:468
  506.4 24.6 %collective-permute-start.40 = (bf16[512,1024]{1,0:T(8,128)(2,1)}, bf16[512,1024]{1,0:T(8,128)(2,1)}, u32[]{:S(2)}, u32[]{:S(2)}) collective-permute-start(bf16[512,1024]{1,0:T(8,128)(2,1)} %copy-done.119), channel_id=1, source_target_pairs={{0,4},{4,0},{1,5},{5,1},{2,6},{6,2},{3,7},{7,3},{8,12},{12,8},{9,1... | collective-permute-start | bytes 3145736 | tf_op jit(solution)/shard_map/ppermute | solution.py:468
  508.0 26.2 %collective-permute-start.39 = (bf16[1024,512]{1,0:T(8,128)(2,1)}, bf16[1024,512]{1,0:T(8,128)(2,1)}, u32[]{:S(2)}, u32[]{:S(2)}) collective-permute-start(bf16[1024,512]{1,0:T(8,128)(2,1)} %copy-done.133), channel_id=1, source_target_pairs={{0,2},{2,0},{1,3},{3,1},{4,6},{6,4},{5,7},{7,5},{8,10},{10,8},{9,1... | collective-permute-start | bytes 3145736 | tf_op jit(solution)/shard_map/ppermute | solution.py:464
  537.5 49.5 %all-to-all-start.5 = ((bf16[16,33,1024]{2,1,0:T(8,128)(2,1)}), bf16[16,33,1024]{2,1,0:T(8,128)(2,1)}, u32[]{:S(2)}, u32[]{:S(2)}) async-start(bf16[16,33,1024]{2,1,0:T(8,128)(2,1)} %pad_maximum_fusion), calls=%async_computation.5 | async-start | bytes 2621440 | tf_op jit(solution)/shard_map/all_to_all | solution.py:562
  546.2 58.9 %reduce-scatter.14.cloned.1.call-start = ((), (), s32[]{:S(2)}) async-start(), calls=%async_computation.14 | async-start | bytes 1310720
  546.3 23.2 %collective-permute-start.42 = (bf16[512,512]{1,0:T(8,128)(2,1)S(1)}, bf16[512,512]{1,0:T(8,128)(2,1)S(1)}, u32[]{:S(2)}, u32[]{:S(2)}) collective-permute-start(bf16[512,512]{1,0:T(8,128)(2,1)S(1)} %copy-done.140), channel_id=1, source_target_pairs={{0,2},{2,0},{1,3},{3,1},{4,6},{6,4},{5,7},{7,5},{8,10},{10,8},{9,1... | collective-permute-start | bytes 1572872 | tf_op jit(solution)/shard_map/ppermute | solution.py:464
  548.2 22.5 %collective-permute-start.41 = (bf16[512,512]{1,0:T(8,128)(2,1)}, bf16[512,512]{1,0:T(8,128)(2,1)S(1)}, u32[]{:S(2)}, u32[]{:S(2)}) collective-permute-start(bf16[512,512]{1,0:T(8,128)(2,1)} %copy-done.141), channel_id=1, source_target_pairs={{0,4},{4,0},{1,5},{5,1},{2,6},{6,2},{3,7},{7,3},{8,12},{12,8},{9,1... | collective-permute-start | bytes 1572872 | tf_op jit(solution)/shard_map/ppermute | solution.py:468
  (172 other events, 1379.3 us)
Sparse Core Ops, SparseCore 0:
  10.8 33.1 all-gather.3
  46.1 43.9 all-gather.5
  92.2 49.8 all-gather.7
  437.8 65.9 reduce-scatter.9
  506.3 29.4 reduce-scatter.11
  576.4 28.6 reduce-scatter.13
